TPU v7x, 32 devices: a whole 2x2x4 slice. The times are simulated.
32 devices in a mesh: fsdp: 8 (over z, y), tp: 4 (over x, core).
Axes of the slice: x: 2, y: 2, z: 4, core: 2. Of those that a mesh axis runs over, the one named last changes fastest.
Arguments:
- tokens: bfloat16 [16384, 1536], P(('fsdp', 'tp')), may hold values from -6 to 6
- cotangent: bfloat16 [16384, 1536], P(('fsdp', 'tp')), may hold values from -6 to 6
- w_query: bfloat16 [1536, 1536], P('fsdp', 'tp'), may hold values from -0.15625 to 0.15625
- w_key: bfloat16 [1536, 1536], P('fsdp', 'tp'), may hold values from -0.15625 to 0.15625
- w_value: bfloat16 [1536, 1536], P('fsdp', 'tp'), may hold values from -0.15625 to 0.15625
- w_house: bfloat16 [1536, 1536], P('fsdp', 'tp'), may hold values from -0.15625 to 0.15625
- w_beta: bfloat16 [1536, 12], P('fsdp', 'tp'), may hold values from -0.15625 to 0.15625
- w_out: bfloat16 [1536, 1536], P('fsdp', 'tp'), may hold values from -0.625 to 0.625
- w_gate: bfloat16 [1536, 4096], P('fsdp', 'tp'), may hold values from -0.15625 to 0.15625
- w_up: bfloat16 [1536, 4096], P('fsdp', 'tp'), may hold values from -0.15625 to 0.15625
- w_down: bfloat16 [1536, 4096], P('fsdp', 'tp'), may hold values from -0.09375 to 0.09375
- gain_attn: bfloat16 [1536], P('fsdp'), may hold values from 0.5 to 1.5
- gain_ffn: bfloat16 [1536], P('fsdp'), may hold values from 0.5 to 1.5
- pack_index: int32 [8, 2, 1024], P('fsdp'), may hold values from 0 to 2047, as said below
- seq_start: int32 [8, 2, 1024], P('fsdp'), may hold values from 0 to 768, as said below
Outputs:
- activations: bfloat16 [16384, 1536], P(('fsdp', 'tp'))
- grad_tokens: bfloat16 [16384, 1536], P(('fsdp', 'tp'))
- grad_w_query: float32 [1536, 1536], P('fsdp', 'tp')
- grad_w_key: float32 [1536, 1536], P('fsdp', 'tp')
- grad_w_value: float32 [1536, 1536], P('fsdp', 'tp')
- grad_w_house: float32 [1536, 1536], P('fsdp', 'tp')
- grad_w_beta: float32 [1536, 12], P('fsdp', 'tp')
- grad_w_out: float32 [1536, 1536], P('fsdp', 'tp')
- grad_w_gate: float32 [1536, 4096], P('fsdp', 'tp')
- grad_w_up: float32 [1536, 4096], P('fsdp', 'tp')
- grad_w_down: float32 [1536, 4096], P('fsdp', 'tp')
- grad_gain_attn: float32 [1536], P('fsdp')
- grad_gain_ffn: float32 [1536], P('fsdp')
Inputs may be any that keep to these rules, and one draw needn't show every extreme that they name: For each group, pack_index over its 2 bins is a permutation of the group's rows; every sequence occupies a run of rows both in the bin and in tokens. `seq_start`: sequences are whole multiples of 128 rows, from 256 to 1024 long, and fill each bin exactly; some bin holds one sequence of 1024 rows.
All inputs are finite; a program needn't handle non-finite values.
Results may differ from a plain program's by a relative error of at most 0.017.
Values may be sent and summed in bfloat16 or wider, within the bound.
A program may use at most 312 MiB of HBM per device.

v0:
```python
import jax
import jax.numpy as jnp
from jax import lax
from jax.sharding import PartitionSpec as P

UT_BLOCK = 64


epsilon = 1e-06
attend_precision = lax.Precision.HIGH


def for_sending(x):
    return jax.tree.map(lambda a: a.astype(jnp.bfloat16) if a.dtype == jnp.float32 else a, x)


def path_head(query_rows, key_rows, value_rows, house_unit, beta_heads, seq_begin):
    row_count, head_dim = query_rows.shape
    blocks = row_count // UT_BLOCK
    q_blocks = query_rows.reshape(blocks, UT_BLOCK, head_dim)
    k_blocks = key_rows.reshape(blocks, UT_BLOCK, head_dim)
    w_blocks = house_unit.reshape(blocks, UT_BLOCK, head_dim)
    b_blocks = beta_heads.reshape(blocks, UT_BLOCK)
    inner_idx = jnp.arange(UT_BLOCK, dtype=jnp.int32)
    strict = inner_idx[:, None] > inner_idx[None, :]
    lower_eq = inner_idx[:, None] >= inner_idx[None, :]
    identity = jnp.broadcast_to(jnp.eye(UT_BLOCK, dtype=jnp.float32), (blocks, UT_BLOCK, UT_BLOCK))
    gram_mat = jnp.einsum("bsd,btd->bst", w_blocks, w_blocks, precision=attend_precision)
    left_mat = identity + jnp.where(strict, gram_mat * b_blocks[:, None, :], 0.0)
    right_mat = identity + jnp.where(strict, gram_mat * b_blocks[:, :, None], 0.0)
    left_inv = lax.linalg.triangular_solve(left_mat, identity, left_side=True, lower=True)
    right_inv = lax.linalg.triangular_solve(right_mat, identity, left_side=True, lower=True)
    wk_prod = jnp.einsum("bsd,bjd->bsj", w_blocks, k_blocks, precision=attend_precision)
    pushed = jnp.einsum(
        "bst,btj->bsj", left_inv, jnp.where(strict, wk_prod, 0.0), precision=attend_precision
    )
    k_end = k_blocks - jnp.einsum(
        "bsj,bsd->bjd", pushed * b_blocks[:, :, None], w_blocks, precision=attend_precision
    )
    qw_prod = jnp.where(
        lower_eq, jnp.einsum("bid,bsd->bis", q_blocks, w_blocks, precision=attend_precision), 0.0
    )
    pulled = jnp.einsum("bis,bst->bit", qw_prod, right_inv, precision=attend_precision)
    q_start = q_blocks - jnp.einsum(
        "bit,btd->bid", pulled * b_blocks[:, None, :], w_blocks, precision=attend_precision
    )
    near_scores = jnp.einsum(
        "bid,bjd->bij", q_blocks, k_blocks, precision=attend_precision
    ) - jnp.einsum(
        "bis,bsj->bij", qw_prod * b_blocks[:, None, :], pushed, precision=attend_precision
    )
    row_block = jnp.arange(row_count, dtype=jnp.int32) // UT_BLOCK

    def advance(current, block_step):
        next_block = block_step + 1
        w_next = lax.dynamic_index_in_dim(w_blocks, next_block, 0, keepdims=False)
        inv_next = lax.dynamic_index_in_dim(right_inv, next_block, 0, keepdims=False)
        b_next = lax.dynamic_index_in_dim(b_blocks, next_block, 0, keepdims=False)
        coefficient = (
            jnp.dot(
                jnp.dot(current, w_next.T, precision=attend_precision),
                inv_next,
                precision=attend_precision,
            )
            * b_next[None, :]
        )
        moved_rows = current - jnp.dot(coefficient, w_next, precision=attend_precision)
        current = jnp.where((row_block > next_block)[:, None], moved_rows, current)
        k_here = lax.dynamic_index_in_dim(k_end, block_step, 0, keepdims=False)
        return (current, jnp.dot(current, k_here.T, precision=attend_precision))

    steps_down = jnp.arange(blocks - 2, -1, -1, dtype=jnp.int32)
    final_rows, slabs = lax.scan(
        jax.checkpoint(advance), q_start.reshape(row_count, head_dim), steps_down
    )
    far_blocks = jnp.concatenate(
        [slabs[::-1], jnp.zeros((1, row_count, UT_BLOCK), jnp.float32)], axis=0
    )
    far_scores = far_blocks.transpose(1, 0, 2).reshape(row_count, row_count)
    near_full = jnp.einsum(
        "bij,bc->bicj", near_scores, jnp.eye(blocks, dtype=jnp.float32), precision=attend_precision
    ).reshape(row_count, row_count)
    same_block = row_block[:, None] == row_block[None, :]
    scores = jnp.where(same_block, near_full, far_scores) * head_dim ** (-0.5)
    columns = jnp.arange(row_count, dtype=jnp.int32)
    valid = (columns[None, :] >= seq_begin[:, None]) & (columns[None, :] <= columns[:, None])
    logits = jnp.where(valid, scores, -jnp.inf)
    row_max = jnp.max(logits, axis=1, keepdims=True)
    expos = jnp.exp(logits - row_max)
    weights_prob = expos / jnp.sum(expos, axis=1, keepdims=True)
    return jnp.dot(weights_prob, value_rows, precision=attend_precision)


def attend(query_in, keys_in, values_in, house_in, beta_in, seq_begin):
    row_count = query_in.shape[0]
    head_count = beta_in.shape[1]
    head_dim = query_in.shape[1] // head_count

    def split_heads(array_in):
        return array_in.reshape(row_count, head_count, head_dim).transpose(1, 0, 2)

    house_heads = split_heads(house_in)
    house_unit = house_heads * lax.rsqrt(
        jnp.sum(house_heads * house_heads, axis=-1, keepdims=True) + epsilon
    )
    beta_heads = (2.0 * jax.nn.sigmoid(beta_in)).T
    result = jax.vmap(path_head, in_axes=(0, 0, 0, 0, 0, None))(
        split_heads(query_in),
        split_heads(keys_in),
        split_heads(values_in),
        house_unit,
        beta_heads,
        seq_begin,
    )
    return result.transpose(1, 0, 2).reshape(row_count, head_count * head_dim)


def rows_contract(left_arr, right_arr):
    return lax.dot_general(
        left_arr, right_arr, (((0,), (0,)), ((), ())), preferred_element_type=jnp.float32
    )


def cols_contract(left_arr, right_arr):
    return lax.dot_general(
        left_arr, right_arr, (((1,), (1,)), ((), ())), preferred_element_type=jnp.float32
    )


def norm_back(grad_normed, unit_rows, scale_rows, gain_full):
    grad_unit = grad_normed * gain_full
    grad_gain = jnp.sum(grad_normed * unit_rows, axis=0)
    grad_rows = scale_rows * (
        grad_unit - unit_rows * jnp.mean(grad_unit * unit_rows, axis=1, keepdims=True)
    )
    return (grad_rows, grad_gain)


def local(
    tokens,
    cotangent,
    w_query,
    w_key,
    w_value,
    w_house,
    w_beta,
    w_out,
    w_gate,
    w_up,
    w_down,
    gain_attn,
    gain_ffn,
    pack_index,
    seq_start,
):
    full_tokens, full_cot = (
        lax.all_gather(tokens, "tp", axis=0, tiled=True),
        lax.all_gather(cotangent, "tp", axis=0, tiled=True),
    )
    packing = pack_index[0]
    begins = seq_start[0]
    bins_here = packing.shape[0]
    bin_rows = packing.shape[1]
    tp_count = lax.axis_size("tp")
    tp_rank = lax.axis_index("tp")
    share_rows = bin_rows // tp_count
    own_count = tokens.shape[0]
    model_width = tokens.shape[1]
    attn_shards = (w_query, w_key, w_value, w_house, w_beta, w_out, gain_attn)
    ffn_shards = (w_gate, w_up, w_down, gain_ffn)
    attn_owned = (w_query, w_key, w_value, w_house, w_beta, w_out)
    ffn_owned = (w_gate, w_up, w_down)
    attn_zero = tuple(
        (jnp.zeros((model_width, shard.shape[1]), jnp.float32) for shard in attn_owned)
    )
    ffn_zero = tuple((jnp.zeros((model_width, shard.shape[1]), jnp.float32) for shard in ffn_owned))
    gain_zero = (jnp.zeros((model_width,), jnp.float32), jnp.zeros((model_width,), jnp.float32))
    y_store = jnp.zeros((bins_here, share_rows, model_width), jnp.bfloat16)
    dx_store = jnp.zeros((bins_here, share_rows, model_width), jnp.bfloat16)

    def micro_step(micro_index, loop_state):
        attn_acc, ffn_acc, gain_acc, y_keep, dx_keep = loop_state
        bin_order = lax.dynamic_index_in_dim(packing, micro_index, 0, keepdims=False)
        seq_begin = lax.dynamic_index_in_dim(begins, micro_index, 0, keepdims=False)
        attn_full = (
            lax.all_gather(attn_shards[0], "fsdp", axis=0, tiled=True),
            lax.all_gather(attn_shards[1], "fsdp", axis=0, tiled=True),
            lax.all_gather(attn_shards[2], "fsdp", axis=0, tiled=True),
            lax.all_gather(attn_shards[3], "fsdp", axis=0, tiled=True),
            lax.all_gather(attn_shards[4], "fsdp", axis=0, tiled=True),
            lax.all_gather(attn_shards[5], "fsdp", axis=0, tiled=True),
            lax.all_gather(attn_shards[6], "fsdp", axis=0, tiled=True),
        )
        full_query, full_key, full_value, full_house, full_beta, full_out, gain_one = attn_full
        gain_one = gain_one.astype(jnp.float32)
        bin_tokens = jnp.take(full_tokens, bin_order, axis=0).astype(jnp.float32)
        scale_one = lax.rsqrt(jnp.mean(bin_tokens * bin_tokens, axis=1, keepdims=True) + epsilon)
        unit_one = bin_tokens * scale_one
        normed = (unit_one * gain_one).astype(jnp.bfloat16)
        query_rows = jnp.dot(normed, full_query, preferred_element_type=jnp.float32).astype(
            jnp.bfloat16
        )
        key_rows = jnp.dot(normed, full_key, preferred_element_type=jnp.float32).astype(
            jnp.bfloat16
        )
        value_rows = jnp.dot(normed, full_value, preferred_element_type=jnp.float32).astype(
            jnp.bfloat16
        )
        house_raw = jnp.dot(normed, full_house, preferred_element_type=jnp.float32).astype(
            jnp.bfloat16
        )
        beta_raw = jnp.dot(normed, full_beta, preferred_element_type=jnp.float32).astype(
            jnp.bfloat16
        )

        def attend_bin(query_in, keys_in, values_in, house_in, beta_in):
            return attend(query_in, keys_in, values_in, house_in, beta_in, seq_begin)

        mixed_f32, attend_back = jax.vjp(
            attend_bin,
            query_rows.astype(jnp.float32),
            key_rows.astype(jnp.float32),
            value_rows.astype(jnp.float32),
            house_raw.astype(jnp.float32),
            beta_raw.astype(jnp.float32),
        )
        mixed_heads = mixed_f32.astype(jnp.bfloat16)
        row_part = mixed_heads
        attn_part = lax.psum_scatter(
            cols_contract(row_part, full_out), "tp", scatter_dimension=0, tiled=True
        )
        own_start = tp_rank * share_rows
        x_own = lax.dynamic_slice_in_dim(bin_tokens, own_start, share_rows, 0)
        hidden_in = x_own + attn_part
        ffn_full = (
            lax.all_gather(ffn_shards[0], "fsdp", axis=0, tiled=True),
            lax.all_gather(ffn_shards[1], "fsdp", axis=0, tiled=True),
            lax.all_gather(ffn_shards[2], "fsdp", axis=0, tiled=True),
            lax.all_gather(ffn_shards[3], "fsdp", axis=0, tiled=True),
        )
        full_gate, full_up, full_down, gain_two = ffn_full
        gain_two = gain_two.astype(jnp.float32)
        scale_two = lax.rsqrt(jnp.mean(hidden_in * hidden_in, axis=1, keepdims=True) + epsilon)
        unit_two = hidden_in * scale_two
        normed_own = (unit_two * gain_two).astype(jnp.bfloat16)
        normed_two = lax.all_gather(normed_own, "tp", axis=0, tiled=True)
        gate_pre = jnp.dot(normed_two, full_gate, preferred_element_type=jnp.float32)
        up_part = jnp.dot(normed_two, full_up, preferred_element_type=jnp.float32)
        hidden = (jax.nn.silu(gate_pre) * up_part).astype(jnp.bfloat16)
        row_part = hidden
        ffn_part = lax.psum_scatter(
            cols_contract(row_part, full_down).astype(jnp.bfloat16),
            "tp",
            scatter_dimension=0,
            tiled=True,
        ).astype(jnp.float32)
        y_own = (hidden_in + ffn_part).astype(jnp.bfloat16)
        cot_bin = jnp.take(full_cot, bin_order, axis=0)
        cot_own = lax.dynamic_slice_in_dim(cot_bin, own_start, share_rows, 0).astype(jnp.float32)
        grad_wdown = rows_contract(cot_bin, hidden)
        grad_hidden = jnp.dot(cot_bin, full_down, preferred_element_type=jnp.float32)
        sigma_gate = jax.nn.sigmoid(gate_pre)
        grad_gate = (
            grad_hidden * up_part * sigma_gate * (1.0 + gate_pre * (1.0 - sigma_gate))
        ).astype(jnp.bfloat16)
        grad_up = (grad_hidden * jax.nn.silu(gate_pre)).astype(jnp.bfloat16)
        grad_wgate = rows_contract(normed_two, grad_gate)
        grad_wup = rows_contract(normed_two, grad_up)
        grad_normed_two = lax.psum_scatter(
            cols_contract(grad_gate, full_gate) + cols_contract(grad_up, full_up),
            "tp",
            scatter_dimension=0,
            tiled=True,
        )
        norm_two_grad, grad_gain_two = norm_back(grad_normed_two, unit_two, scale_two, gain_two)
        grad_hidden_in = cot_own + norm_two_grad
        grad_attn_full = lax.all_gather(
            grad_hidden_in.astype(jnp.bfloat16), "tp", axis=0, tiled=True
        )
        grad_wout = rows_contract(grad_attn_full, mixed_heads)
        grad_mixed = jnp.dot(grad_attn_full, full_out, preferred_element_type=jnp.float32)
        core_grads = attend_back(grad_mixed)
        grad_query = core_grads[0].astype(jnp.bfloat16)
        grad_key = core_grads[1].astype(jnp.bfloat16)
        grad_value = core_grads[2].astype(jnp.bfloat16)
        grad_house = core_grads[3].astype(jnp.bfloat16)
        grad_beta = core_grads[4].astype(jnp.bfloat16)
        grad_wquery = rows_contract(normed, grad_query)
        grad_wkey = rows_contract(normed, grad_key)
        grad_wvalue = rows_contract(normed, grad_value)
        grad_whouse = rows_contract(normed, grad_house)
        grad_wbeta = rows_contract(normed, grad_beta)
        total = cols_contract(grad_query, full_query)
        total = total + cols_contract(grad_key, full_key)
        total = total + cols_contract(grad_value, full_value)
        total = total + cols_contract(grad_house, full_house)
        grad_normed_one = lax.psum_scatter(
            (total + cols_contract(grad_beta, full_beta)).astype(jnp.bfloat16),
            "tp",
            scatter_dimension=0,
            tiled=True,
        ).astype(jnp.float32)
        unit_own = lax.dynamic_slice_in_dim(unit_one, own_start, share_rows, 0)
        scale_own = lax.dynamic_slice_in_dim(scale_one, own_start, share_rows, 0)
        norm_one_grad, grad_gain_one = norm_back(grad_normed_one, unit_own, scale_own, gain_one)
        dx_own = (grad_hidden_in + norm_one_grad).astype(jnp.bfloat16)
        attn_grads = (grad_wquery, grad_wkey, grad_wvalue, grad_whouse, grad_wbeta, grad_wout)
        ffn_grads = (grad_wgate, grad_wup, grad_wdown)
        attn_acc = jax.tree.map(jnp.add, attn_acc, attn_grads)
        ffn_acc = jax.tree.map(jnp.add, ffn_acc, ffn_grads)
        gain_acc = (gain_acc[0] + grad_gain_one, gain_acc[1] + grad_gain_two)
        y_keep = lax.dynamic_update_index_in_dim(y_keep, y_own, micro_index, 0)
        dx_keep = lax.dynamic_update_index_in_dim(dx_keep, dx_own, micro_index, 0)
        return (attn_acc, ffn_acc, gain_acc, y_keep, dx_keep)

    attn_acc, ffn_acc, gain_acc, y_store, dx_store = lax.fori_loop(
        0, bins_here, micro_step, (attn_zero, ffn_zero, gain_zero, y_store, dx_store)
    )
    attn_acc = jax.tree.map(
        lambda part: part.astype(jnp.float32),
        lax.psum_scatter(for_sending(attn_acc), "fsdp", scatter_dimension=0, tiled=True),
    )
    ffn_acc = jax.tree.map(
        lambda part: part.astype(jnp.float32),
        lax.psum_scatter(for_sending(ffn_acc), "fsdp", scatter_dimension=0, tiled=True),
    )
    gain_totals = lax.psum((gain_acc[0], gain_acc[1]), ("fsdp", "tp"))
    gain_shard = gain_attn.shape[0]
    fsdp_rank = lax.axis_index("fsdp")
    grad_gain_attn = lax.dynamic_slice_in_dim(gain_totals[0], fsdp_rank * gain_shard, gain_shard)
    grad_gain_ffn = lax.dynamic_slice_in_dim(gain_totals[1], fsdp_rank * gain_shard, gain_shard)
    full_y, full_dx = (
        lax.all_gather(y_store, "tp", axis=1, tiled=True),
        lax.all_gather(dx_store, "tp", axis=1, tiled=True),
    )
    group_rows = bins_here * bin_rows
    flat_y = full_y.reshape(group_rows, model_width)
    flat_dx = full_dx.reshape(group_rows, model_width)
    inverse = (
        jnp.zeros((group_rows,), jnp.int32)
        .at[packing.reshape(-1)]
        .set(jnp.arange(group_rows, dtype=jnp.int32))
    )
    own_slots = lax.dynamic_slice_in_dim(inverse, tp_rank * own_count, own_count)
    out_y = jnp.take(flat_y, own_slots, axis=0)
    out_dx = jnp.take(flat_dx, own_slots, axis=0)
    return (
        out_y,
        out_dx,
        attn_acc[0],
        attn_acc[1],
        attn_acc[2],
        attn_acc[3],
        attn_acc[4],
        attn_acc[5],
        ffn_acc[0],
        ffn_acc[1],
        ffn_acc[2],
        grad_gain_attn,
        grad_gain_ffn,
    )


def solution(mesh):
    placed = (
        P(("fsdp", "tp"), None),
        P(("fsdp", "tp"), None),
        P("fsdp", "tp"),
        P("fsdp", "tp"),
        P("fsdp", "tp"),
        P("fsdp", "tp"),
        P("fsdp", "tp"),
        P("fsdp", "tp"),
        P("fsdp", "tp"),
        P("fsdp", "tp"),
        P("fsdp", "tp"),
        P("fsdp"),
        P("fsdp"),
        P("fsdp", None, None),
        P("fsdp", None, None),
    )
    return jax.shard_map(
        local,
        mesh=mesh,
        in_specs=placed,
        out_specs=(
            P(("fsdp", "tp"), None),
            P(("fsdp", "tp"), None),
            P("fsdp", "tp"),
            P("fsdp", "tp"),
            P("fsdp", "tp"),
            P("fsdp", "tp"),
            P("fsdp", "tp"),
            P("fsdp", "tp"),
            P("fsdp", "tp"),
            P("fsdp", "tp"),
            P("fsdp", "tp"),
            P("fsdp"),
            P("fsdp"),
        ),
        check_vma=False,
    )
```

profile of v0, /device:TPU:0, one launch (start us, length us, event | category | flops | bytes accessed | tf_op | source)
XLA Modules:
  0.0 5376.9 jit_solution(2641941736249610359)
XLA Ops:
  8.8 49.9 all-gather.19.cloned.1.call-done
  58.7 48.0 all-gather.21.cloned.1.call-done
  106.7 4528.3 %while.197 = (s32[]{:T(128)}, f32[1536,384]{1,0:T(8,128)}, f32[1536,384]{1,0:T(8,128)}, f32[1536,384]{1,0:T(8,128)}, f32[1536,384]{1,0:T(8,128)}, /*index=5*/f32...) while((s32[]{:T(128)}, f32[1536,384]{1,0:T(8,128)}, ...), condition=%wide.region_31.35_spmd.clone, body=%wide.region_0.34_spmd.clone.sunk | while | flops 60807720960 | bytes 1838403072 | solution.py:316
  202.4 237.2 %custom-call.46 = f32[3,16,1,64,64]{3,4,2,1,0:T(8,128)S(1)} custom-call(f32[3,16,1,64,64]{4,3,2,1,0:T(8,128)} %get-tuple-element.2527), custom_call_target="InvertDiagBlocksLowerTriangular" | custom-call | tf_op jit(solution)/shard_map/while/body/eval_jaxpr/jvp(vmap())/triangular_solve/custom-call.1 | solution.py:31
  453.6 236.8 %custom-call.47 = f32[3,16,1,64,64]{3,4,2,1,0:T(8,128)S(1)} custom-call(f32[3,16,1,64,64]{4,3,2,1,0:T(8,128)} %get-tuple-element.2528), custom_call_target="InvertDiagBlocksLowerTriangular" | custom-call | tf_op jit(solution)/shard_map/while/body/eval_jaxpr/jvp(vmap())/triangular_solve/custom-call.1 | solution.py:32
  714.0 210.5 %while.198 = (s32[]{:T(128)}, f32[3,1024,128]{2,1,0:T(8,128)S(1)}, f32[15,3,1024,64]{2,3,1,0:T(8,128)}, f32[15,3,1024,128]{3,2,1,0:T(8,128)}, s32[15]{0:T(128)S(...) while((s32[]{:T(128)}, f32[3,1024,128]{2,1,0:T(8,128)S(1)}, ...), condition=%wide.region_4.6_spmd.clone, body=%wide.region_3.5_spmd.clone.sunk | while | flops 529474560 | bytes 13768237 | solution.py:73
  1095.2 35.6 reduce-scatter.34.cloned.1.call-done
  1134.9 58.8 %all-gather.41.cloned.1.call-done = bf16[1536,1024]{1,0:T(8,128)(2,1)} async-done(((bf16[192,1024]{1,0:T(8,128)(2,1)}), bf16[1536,1024]{1,0:T(8,128)(2,1)}) %all-gather.41.cloned.1.call-update) | async-done | bytes 3145744 | tf_op jit(solution)/shard_map/while/body/eval_jaxpr/all_gather | solution.py:238
  1201.9 53.2 all-gather.39.cloned.1.call-done
  1292.9 54.4 %all-gather.43.cloned.1.call-done = bf16[1536,1024]{1,0:T(8,128)(2,1)} async-done(((bf16[192,1024]{1,0:T(8,128)(2,1)}), bf16[1536,1024]{1,0:T(8,128)(2,1)}) %all-gather.43.cloned.1.call-update) | async-done | bytes 3145744 | tf_op jit(solution)/shard_map/while/body/eval_jaxpr/all_gather | solution.py:237
  1368.4 57.1 %reduce-scatter.36.cloned.1.call-done = f32[256,1536]{1,0:T(8,128)} async-done(((f32[1024,1536]{1,0:T(8,128)}), f32[256,1536]{1,0:T(8,128)}) %reduce-scatter.36.cloned.1.call-update) | async-done | bytes 1572880 | tf_op jit(solution)/shard_map/while/body/eval_jaxpr/reduce_scatter | solution.py:269
  1536.1 621.1 %while.199 = (s32[]{:T(128)}, f32[3,16,64,128]{3,2,1,0:T(8,128)}, f32[3,16,64,64]{3,2,0,1:T(8,128)}, f32[3,16,64]{2,1,0:T(8,128)S(1)}, f32[3,16,64,128]{3,2,0,1:...) while((s32[]{:T(128)}, f32[3,16,64,128]{3,2,1,0:T(8,128)}, ...), condition=%wide.region_19.21_spmd.clone, body=%wide.region_14.20_spmd.clone.sunk | while | flops 1440507136 | bytes 60679936 | solution.py:73
  2463.0 236.8 %custom-call.46 = f32[3,16,1,64,64]{3,4,2,1,0:T(8,128)S(1)} custom-call(f32[3,16,1,64,64]{4,3,2,1,0:T(8,128)} %get-tuple-element.2527), custom_call_target="InvertDiagBlocksLowerTriangular" | custom-call | tf_op jit(solution)/shard_map/while/body/eval_jaxpr/jvp(vmap())/triangular_solve/custom-call.1 | solution.py:31
  2713.8 236.8 %custom-call.47 = f32[3,16,1,64,64]{3,4,2,1,0:T(8,128)S(1)} custom-call(f32[3,16,1,64,64]{4,3,2,1,0:T(8,128)} %get-tuple-element.2528), custom_call_target="InvertDiagBlocksLowerTriangular" | custom-call | tf_op jit(solution)/shard_map/while/body/eval_jaxpr/jvp(vmap())/triangular_solve/custom-call.1 | solution.py:32
  2974.3 210.7 %while.198 = (s32[]{:T(128)}, f32[3,1024,128]{2,1,0:T(8,128)S(1)}, f32[15,3,1024,64]{2,3,1,0:T(8,128)}, f32[15,3,1024,128]{3,2,1,0:T(8,128)}, s32[15]{0:T(128)S(...) while((s32[]{:T(128)}, f32[3,1024,128]{2,1,0:T(8,128)S(1)}, ...), condition=%wide.region_4.6_spmd.clone, body=%wide.region_3.5_spmd.clone.sunk | while | flops 529474560 | bytes 13768237 | solution.py:73
  3355.8 35.4 reduce-scatter.34.cloned.1.call-done
  3395.3 58.8 %all-gather.41.cloned.1.call-done = bf16[1536,1024]{1,0:T(8,128)(2,1)} async-done(((bf16[192,1024]{1,0:T(8,128)(2,1)}), bf16[1536,1024]{1,0:T(8,128)(2,1)}) %all-gather.41.cloned.1.call-update) | async-done | bytes 3145744 | tf_op jit(solution)/shard_map/while/body/eval_jaxpr/all_gather | solution.py:238
  3462.3 53.2 all-gather.39.cloned.1.call-done
  3553.3 54.4 %all-gather.43.cloned.1.call-done = bf16[1536,1024]{1,0:T(8,128)(2,1)} async-done(((bf16[192,1024]{1,0:T(8,128)(2,1)}), bf16[1536,1024]{1,0:T(8,128)(2,1)}) %all-gather.43.cloned.1.call-update) | async-done | bytes 3145744 | tf_op jit(solution)/shard_map/while/body/eval_jaxpr/all_gather | solution.py:237
  3628.5 57.1 %reduce-scatter.36.cloned.1.call-done = f32[256,1536]{1,0:T(8,128)} async-done(((f32[1024,1536]{1,0:T(8,128)}), f32[256,1536]{1,0:T(8,128)}) %reduce-scatter.36.cloned.1.call-update) | async-done | bytes 1572880 | tf_op jit(solution)/shard_map/while/body/eval_jaxpr/reduce_scatter | solution.py:269
  3796.3 621.3 %while.199 = (s32[]{:T(128)}, f32[3,16,64,128]{3,2,1,0:T(8,128)}, f32[3,16,64,64]{3,2,0,1:T(8,128)}, f32[3,16,64]{2,1,0:T(8,128)S(1)}, f32[3,16,64,128]{3,2,0,1:...) while((s32[]{:T(128)}, f32[3,16,64,128]{3,2,1,0:T(8,128)}, ...), condition=%wide.region_19.21_spmd.clone, body=%wide.region_14.20_spmd.clone.sunk | while | flops 1440507136 | bytes 60679936 | solution.py:73
  4674.0 39.6 all-reduce.8
  4716.4 51.4 reduce-scatter.16.cloned.1.call-done
  4769.4 64.7 %reduce-scatter.18.cloned.1.call-done = bf16[192,384]{1,0:T(8,128)(2,1)} async-done(((bf16[1536,384]{1,0:T(8,128)(2,1)}), bf16[192,384]{1,0:T(8,128)(2,1)}) %reduce-scatter.18.cloned.1.call-update) | async-done | bytes 147472 | tf_op jit(solution)/shard_map/reduce_scatter | solution.py:321
  4835.7 64.9 %reduce-scatter.20.cloned.1.call-done = bf16[192,384]{1,0:T(8,128)(2,1)} async-done(((bf16[1536,384]{1,0:T(8,128)(2,1)}), bf16[192,384]{1,0:T(8,128)(2,1)}) %reduce-scatter.20.cloned.1.call-update) | async-done | bytes 147472 | tf_op jit(solution)/shard_map/reduce_scatter | solution.py:321
  4902.2 64.8 %reduce-scatter.22.cloned.1.call-done = bf16[192,384]{1,0:T(8,128)(2,1)} async-done(((bf16[1536,384]{1,0:T(8,128)(2,1)}), bf16[192,384]{1,0:T(8,128)(2,1)}) %reduce-scatter.22.cloned.1.call-update) | async-done | bytes 147472 | tf_op jit(solution)/shard_map/reduce_scatter | solution.py:321
  4968.7 64.7 %reduce-scatter.24.cloned.1.call-done = bf16[192,384]{1,0:T(8,128)(2,1)} async-done(((bf16[1536,384]{1,0:T(8,128)(2,1)}), bf16[192,384]{1,0:T(8,128)(2,1)}) %reduce-scatter.24.cloned.1.call-update) | async-done | bytes 147472 | tf_op jit(solution)/shard_map/reduce_scatter | solution.py:321
  5035.0 75.2 %reduce-scatter.26.cloned.1.call-done = bf16[192,1024]{1,0:T(8,128)(2,1)} async-done(((bf16[1536,1024]{1,0:T(8,128)(2,1)}), bf16[192,1024]{1,0:T(8,128)(2,1)}) %reduce-scatter.26.cloned.1.call-update) | async-done | bytes 393232 | tf_op jit(solution)/shard_map/reduce_scatter | solution.py:325
  5112.1 75.3 %reduce-scatter.28.cloned.1.call-done = bf16[192,1024]{1,0:T(8,128)(2,1)} async-done(((bf16[1536,1024]{1,0:T(8,128)(2,1)}), bf16[192,1024]{1,0:T(8,128)(2,1)}) %reduce-scatter.28.cloned.1.call-update) | async-done | bytes 393232 | tf_op jit(solution)/shard_map/reduce_scatter | solution.py:325
  5189.3 75.1 %reduce-scatter.30.cloned.1.call-done = bf16[192,1024]{1,0:T(8,128)(2,1)} async-done(((bf16[1536,1024]{1,0:T(8,128)(2,1)}), bf16[192,1024]{1,0:T(8,128)(2,1)}) %reduce-scatter.30.cloned.1.call-update) | async-done | bytes 393232 | tf_op jit(solution)/shard_map/reduce_scatter | solution.py:325
  5266.4 45.7 all-gather.23.cloned.1.call-done
  5319.3 41.4 all-gather.25.cloned.1.call-done
  (2641 shorter events, 2926.8 us)
Async XLA Ops:
  107.7 335.6 %all-gather.31.cloned.1.call-start = ((), (), s32[]{:S(2)}) async-start(), calls=%async_computation.28 | async-start | bytes 1327104 | tf_op jit(solution)/shard_map/while/body/eval_jaxpr/all_gather | solution.py:187
  108.3 585.9 %all-gather.27.cloned.1.call-start = ((), (), s32[]{:S(2)}) async-start(), calls=%async_computation.26 | async-start | bytes 1327104 | tf_op jit(solution)/shard_map/while/body/eval_jaxpr/all_gather | solution.py:186
  108.9 950.6 %all-gather.33.cloned.1.call-start = ((), (), s32[]{:S(2)}) async-start(), calls=%async_computation.29 | async-start | bytes 1327104 | tf_op jit(solution)/shard_map/while/body/eval_jaxpr/all_gather | solution.py:188
  109.4 960.3 %all-gather.35.cloned.1.call-start = ((), (), s32[]{:S(2)}) async-start(), calls=%async_computation.30 | async-start | bytes 1327104 | tf_op jit(solution)/shard_map/while/body/eval_jaxpr/all_gather | solution.py:191
  110.2 1020.6 %reduce-scatter.34.cloned.1.call-start = ((), (), s32[]{:S(2)}) async-start(), calls=%async_computation.31 | async-start | bytes 7864320 | tf_op jit(solution)/shard_map/while/body/eval_jaxpr/reduce_scatter | solution.py:229
  1076.0 117.8 %all-gather.41.cloned.1.call-start = ((), (), s32[]{:S(2)}) async-start(), calls=%async_computation.34 | async-start | bytes 3538944 | tf_op jit(solution)/shard_map/while/body/eval_jaxpr/all_gather | solution.py:238
  1076.7 178.4 %all-gather.39.cloned.1.call-start = ((), (), s32[]{:S(2)}) async-start(), calls=%async_computation.33 | async-start | bytes 3538944 | tf_op jit(solution)/shard_map/while/body/eval_jaxpr/all_gather | solution.py:236
  1077.3 207.2 %all-gather.37.cloned.1.call-start = ((), (), s32[]{:S(2)}) async-start(), calls=%async_computation.32 | async-start | bytes 3932160 | tf_op jit(solution)/shard_map/while/body/eval_jaxpr/all_gather | solution.py:246
  1134.2 213.0 %all-gather.43.cloned.1.call-start = ((), (), s32[]{:S(2)}) async-start(), calls=%async_computation.35 | async-start | bytes 3538944 | tf_op jit(solution)/shard_map/while/body/eval_jaxpr/all_gather | solution.py:237
  1134.8 290.6 %reduce-scatter.36.cloned.1.call-start = ((), (), s32[]{:S(2)}) async-start(), calls=%async_computation.36 | async-start | bytes 7864320 | tf_op jit(solution)/shard_map/while/body/eval_jaxpr/reduce_scatter | solution.py:269
  1431.2 902.9 %reduce-scatter.38.cloned.1.call-start = ((), (), s32[]{:S(2)}) async-start(), calls=%async_computation.38 | async-start | bytes 3932160 | tf_op jit(solution)/shard_map/while/body/eval_jaxpr/reduce_scatter | solution.py:297
  2368.0 335.6 %all-gather.31.cloned.1.call-start = ((), (), s32[]{:S(2)}) async-start(), calls=%async_computation.28 | async-start | bytes 1327104 | tf_op jit(solution)/shard_map/while/body/eval_jaxpr/all_gather | solution.py:187
  2368.6 585.9 %all-gather.27.cloned.1.call-start = ((), (), s32[]{:S(2)}) async-start(), calls=%async_computation.26 | async-start | bytes 1327104 | tf_op jit(solution)/shard_map/while/body/eval_jaxpr/all_gather | solution.py:186
  2369.3 950.6 %all-gather.33.cloned.1.call-start = ((), (), s32[]{:S(2)}) async-start(), calls=%async_computation.29 | async-start | bytes 1327104 | tf_op jit(solution)/shard_map/while/body/eval_jaxpr/all_gather | solution.py:188
  2369.9 960.3 %all-gather.35.cloned.1.call-start = ((), (), s32[]{:S(2)}) async-start(), calls=%async_computation.30 | async-start | bytes 1327104 | tf_op jit(solution)/shard_map/while/body/eval_jaxpr/all_gather | solution.py:191
  2370.6 1020.6 %reduce-scatter.34.cloned.1.call-start = ((), (), s32[]{:S(2)}) async-start(), calls=%async_computation.31 | async-start | bytes 7864320 | tf_op jit(solution)/shard_map/while/body/eval_jaxpr/reduce_scatter | solution.py:229
  3336.4 117.7 %all-gather.41.cloned.1.call-start = ((), (), s32[]{:S(2)}) async-start(), calls=%async_computation.34 | async-start | bytes 3538944 | tf_op jit(solution)/shard_map/while/body/eval_jaxpr/all_gather | solution.py:238
  3337.1 178.4 %all-gather.39.cloned.1.call-start = ((), (), s32[]{:S(2)}) async-start(), calls=%async_computation.33 | async-start | bytes 3538944 | tf_op jit(solution)/shard_map/while/body/eval_jaxpr/all_gather | solution.py:236
  3337.7 207.2 %all-gather.37.cloned.1.call-start = ((), (), s32[]{:S(2)}) async-start(), calls=%async_computation.32 | async-start | bytes 3932160 | tf_op jit(solution)/shard_map/while/body/eval_jaxpr/all_gather | solution.py:246
  3394.7 213.0 %all-gather.43.cloned.1.call-start = ((), (), s32[]{:S(2)}) async-start(), calls=%async_computation.35 | async-start | bytes 3538944 | tf_op jit(solution)/shard_map/while/body/eval_jaxpr/all_gather | solution.py:237
  3395.2 290.4 %reduce-scatter.36.cloned.1.call-start = ((), (), s32[]{:S(2)}) async-start(), calls=%async_computation.36 | async-start | bytes 7864320 | tf_op jit(solution)/shard_map/while/body/eval_jaxpr/reduce_scatter | solution.py:269
  3691.4 908.0 %reduce-scatter.38.cloned.1.call-start = ((), (), s32[]{:S(2)}) async-start(), calls=%async_computation.38 | async-start | bytes 3932160 | tf_op jit(solution)/shard_map/while/body/eval_jaxpr/reduce_scatter | solution.py:297
  4636.8 130.9 %reduce-scatter.16.cloned.1.call-start = ((), (), s32[]{:S(2)}) async-start(), calls=%async_computation.17 | async-start | bytes 1327104 | tf_op jit(solution)/shard_map/reduce_scatter | solution.py:321
  4639.9 194.2 %reduce-scatter.18.cloned.1.call-start = ((), (), s32[]{:S(2)}) async-start(), calls=%async_computation.18 | async-start | bytes 1327104 | tf_op jit(solution)/shard_map/reduce_scatter | solution.py:321
  4641.2 259.4 %reduce-scatter.20.cloned.1.call-start = ((), (), s32[]{:S(2)}) async-start(), calls=%async_computation.19 | async-start | bytes 1327104 | tf_op jit(solution)/shard_map/reduce_scatter | solution.py:321
  4644.3 322.7 %reduce-scatter.22.cloned.1.call-start = ((), (), s32[]{:S(2)}) async-start(), calls=%async_computation.20 | async-start | bytes 1327104 | tf_op jit(solution)/shard_map/reduce_scatter | solution.py:321
  4645.6 387.7 %reduce-scatter.24.cloned.1.call-start = ((), (), s32[]{:S(2)}) async-start(), calls=%async_computation.21 | async-start | bytes 1327104 | tf_op jit(solution)/shard_map/reduce_scatter | solution.py:321
  4648.5 461.6 %reduce-scatter.26.cloned.1.call-start = ((), (), s32[]{:S(2)}) async-start(), calls=%async_computation.22 | async-start | bytes 3538944 | tf_op jit(solution)/shard_map/reduce_scatter | solution.py:325
  4653.5 533.8 %reduce-scatter.28.cloned.1.call-start = ((), (), s32[]{:S(2)}) async-start(), calls=%async_computation.23 | async-start | bytes 3538944 | tf_op jit(solution)/shard_map/reduce_scatter | solution.py:325
  4658.6 605.9 %reduce-scatter.30.cloned.1.call-start = ((), (), s32[]{:S(2)}) async-start(), calls=%async_computation.24 | async-start | bytes 3538944 | tf_op jit(solution)/shard_map/reduce_scatter | solution.py:325
  4663.6 648.4 %all-gather.23.cloned.1.call-start = ((), (), s32[]{:S(2)}) async-start(), calls=%async_computation.15 | async-start | bytes 7864320 | tf_op jit(solution)/shard_map/all_gather | solution.py:333
  4664.4 696.3 %all-gather.25.cloned.1.call-start = ((), (), s32[]{:S(2)}) async-start(), calls=%async_computation.16 | async-start | bytes 7864320 | tf_op jit(solution)/shard_map/all_gather | solution.py:334
  (521 other events, 12644.7 us)
Sparse Core Ops, SparseCore 0:
  9.6 49.0 all-gather.18
  60.3 46.3 all-gather.20
  110.0 41.3 all-gather.28
  195.6 40.7 all-gather.26
  238.4 41.6 all-gather.32
  282.3 40.7 all-gather.34
  1076.1 54.6 reduce-scatter.33
  1133.2 60.4 all-gather.40
  1196.0 59.0 all-gather.38
  1286.8 60.4 all-gather.42
  1368.4 56.9 reduce-scatter.35
  2370.1 41.2 all-gather.28
  2413.5 40.1 all-gather.30
  2455.9 40.4 all-gather.26
  2498.4 41.1 all-gather.32
  2541.7 41.4 all-gather.34
  3336.5 54.6 reduce-scatter.33
  3393.6 60.4 all-gather.40
  3456.4 59.0 all-gather.38
  3547.2 60.4 all-gather.42
  3628.6 56.9 reduce-scatter.35
  4639.7 61.6 reduce-scatter.31
  4704.8 62.9 reduce-scatter.15
  4771.0 63.0 reduce-scatter.17
  4837.5 63.0 reduce-scatter.19
  4904.0 62.9 reduce-scatter.21
  4970.3 63.0 reduce-scatter.23
  5036.8 73.3 reduce-scatter.25
  5113.7 73.6 reduce-scatter.27
  5190.8 73.5 reduce-scatter.29
  5266.6 45.4 all-gather.22
  5314.2 46.3 all-gather.24
  (9 shorter events, 302.7 us)
where the time goes:
time: 5410 us; the launch traced here: 5380 us
  matrix products  1480 us (27%)
  waiting for transfers between devices  1410 us (26%)
  other arithmetic  1400 us (26%)
  local copies, waits for them, and re-layouts  715 us (13%)
  loops' own time  210 us (4%)
  blocking collectives  137 us (3%)
    another operation x4, other arithmetic, path_head(): lax.linalg.triangular_solve(right_mat, identity, left_side=True, lower=True)  478 us
    another operation x2, other arithmetic, path_head(): lax.linalg.triangular_solve(left_mat, identity, left_side=True, lower=True)  474 us
    reduce_scatter x5, waiting for transfers between devices, local(): lax.psum_scatter(for_sending(attn_acc), 'fsdp', scatter_dimension=0, tile...  310 us
    dot_general x120, matrix products, advance(): jnp.dot(coefficient, w_next, precision=attend_precision)  280 us
    dot_general x90, matrix products, advance(): return (current, jnp.dot(current, k_here.T, precision=attend_precision))  269 us
    dot_general x120, matrix products, advance(): jnp.dot(current, w_next.T, precision=attend_precision)  245 us
    dot_general x120, matrix products, advance(): jnp.dot(jnp.dot(current, w_next.T, precision=attend_precision), inv_next,...  233 us
    reduce_scatter x3, waiting for transfers between devices, local(): lax.psum_scatter(for_sending(ffn_acc), 'fsdp', scatter_dimension=0, tiled...  226 us
  transfers between devices with their start and end apart: 41, of which 28 were waited for; matrix products, arithmetic and copies ran while one was open for 36% of the time, Pallas kernels for 0%

commit v1 on v0

v1 whole, which is shorter than its diff:
```python
import functools

import jax
import jax.numpy as jnp
from jax import lax
from jax.experimental import pallas as pl
from jax.experimental.pallas import tpu as pltpu
from jax.sharding import PartitionSpec as P

BLOCK = 128
epsilon = 1e-06
bf16 = jnp.bfloat16
f32 = jnp.float32


def mm(a, b):
    return lax.dot_general(a, b, (((1,), (0,)), ((), ())), preferred_element_type=f32)


def mm_rt(a, b):
    return lax.dot_general(a, b, (((1,), (1,)), ((), ())), preferred_element_type=f32)


def mm_lt(a, b):
    return lax.dot_general(a, b, (((0,), (0,)), ((), ())), preferred_element_type=f32)


def iotas():
    rows = lax.broadcasted_iota(jnp.int32, (BLOCK, BLOCK), 0)
    cols = lax.broadcasted_iota(jnp.int32, (BLOCK, BLOCK), 1)
    return rows, cols


def strengths(u, r_col):
    uf = u.astype(f32)
    inv_sq = 1.0 / (jnp.sum(uf * uf, axis=1, keepdims=True) + epsilon)
    beta = 2.0 / (1.0 + jnp.exp(-r_col))
    return beta, inv_sq


def prep_kernel(heads, q_ref, k_ref, u_ref, r_ref, near_ref, q0_ref, kp_ref, inv_ref, t_ref):
    rows, cols = iotas()
    strict = rows > cols
    lower = rows >= cols
    diff = rows ^ cols
    eye = jnp.where(rows == cols, 1.0, 0.0).astype(f32)
    eye_b = eye.astype(bf16)
    chunks = q_ref.shape[0] // BLOCK
    items = [(c, h) for c in range(chunks) for h in range(heads)]
    state = []
    for c, h in items:
        rs, cs = pl.ds(c * BLOCK, BLOCK), pl.ds(h * BLOCK, BLOCK)
        q, k, u = q_ref[rs, cs], k_ref[rs, cs], u_ref[rs, cs]
        beta, inv_sq = strengths(u, r_ref[rs, h : h + 1].astype(f32))
        bp = beta * inv_sq
        big = mm_rt(jnp.concatenate([u, q], axis=0), jnp.concatenate([u, k], axis=0))
        gram = big[:BLOCK, :BLOCK]
        e_s = jnp.where(strict, big[:BLOCK, BLOCK:], 0.0)
        a_s = jnp.where(lower, big[BLOCK:, :BLOCK], 0.0)
        n0 = big[BLOCK:, BLOCK:]
        low = jnp.where(strict, gram * bp, 0.0)
        eu = jnp.concatenate([e_s * bp, u.astype(f32) * bp], axis=1).astype(bf16)
        state.append([q, k, u, a_s.astype(bf16), n0, low, eu, eye - jnp.where(diff < 2, low, 0.0)])
    size = 2
    while size < BLOCK:
        sel = (diff >= size) & (diff < 2 * size)
        prods = []
        for st in state:
            xb = st[7].astype(bf16)
            prods.append((xb, mm(jnp.where(sel, st[5], 0.0).astype(bf16), xb)))
        for st, (xb, y) in zip(state, prods):
            st[7] = st[7] - mm(xb, y.astype(bf16))
        size *= 2
    for (c, h), (q, k, u, a_b, n0, low, eu, x) in zip(items, state):
        rs, cs = pl.ds(c * BLOCK, BLOCK), pl.ds(h * BLOCK, BLOCK)
        xb = x.astype(bf16)
        t = mm(xb, eu).astype(bf16)
        top = mm(a_b, t)
        bot = mm_lt(u, t)
        inv_ref[c, h] = xb
        t_ref[c, h] = t
        near_ref[c, h] = n0 - top[:, :BLOCK]
        q0_ref[rs, cs] = (q.astype(f32) - top[:, BLOCK:]).astype(bf16)
        ket = mm_rt(eye_b, k) - bot[:, :BLOCK]
        kp_ref[c, h] = jnp.concatenate([ket, eye - bot[:, BLOCK:]], axis=1).astype(bf16)


def fwd_kernel(
    heads, depth, scale, first_ref, q0_ref, near_ref, kp_ref, v_ref, o_ref, linv_ref, e_ref, cur_ref, s_ref, m_ref, acc_ref
):
    i = pl.program_id(0)
    first = first_ref[i]
    rows, cols = iotas()
    lower = rows >= cols
    neg = jnp.float32(-1e30)
    for h in range(heads):
        s0 = jnp.where(lower, near_ref[0, h], neg)
        s_ref[0, h] = s0
        m_ref[h] = s0
        cur_ref[0, 0, h] = q0_ref[:, h * BLOCK : (h + 1) * BLOCK]
    for d in range(1, depth):

        @pl.when(i - d >= first)
        def _():
            j = i - d
            for h in range(heads):
                both = mm(cur_ref[0, d - 1, h], kp_ref[j, h])
                s = both[:, :BLOCK]
                s_ref[d, h] = s
                m_ref[h] = jnp.maximum(m_ref[h], s)
                if d + 1 < depth:
                    cur_ref[0, d, h] = both[:, BLOCK:].astype(bf16)

    peaks = []
    for h in range(heads):
        peak = jnp.max(m_ref[h], axis=1, keepdims=True)
        peaks.append(peak)
        e0 = jnp.exp((s_ref[0, h] - peak) * scale)
        m_ref[h] = e0
        eb = e0.astype(bf16)
        e_ref[0, 0, h] = eb
        v = v_ref[pl.ds(pl.multiple_of(i * BLOCK, BLOCK), BLOCK), h * BLOCK : (h + 1) * BLOCK]
        acc_ref[h] = mm(eb, v)
    for d in range(1, depth):

        @pl.when(i - d >= first)
        def _():
            j = i - d
            for h in range(heads):
                e = jnp.exp((s_ref[d, h] - peaks[h]) * scale)
                m_ref[h] = m_ref[h] + e
                eb = e.astype(bf16)
                e_ref[0, d, h] = eb
                v = v_ref[pl.ds(pl.multiple_of(j * BLOCK, BLOCK), BLOCK), h * BLOCK : (h + 1) * BLOCK]
                acc_ref[h] = acc_ref[h] + mm(eb, v)

    for h in range(heads):
        linv = 1.0 / jnp.sum(m_ref[h], axis=1, keepdims=True)
        cs = slice(h * BLOCK, (h + 1) * BLOCK)
        o_ref[:, cs] = (acc_ref[h] * linv).astype(bf16)
        linv_ref[:, cs] = jnp.broadcast_to(linv, (BLOCK, BLOCK))


def bwd_kernel(heads, depth, scale, last_ref, *refs):
    (do_ref, o_ref, linv_ref, q_ref, k_ref, v_ref, u_ref, r_ref, kp_ref, inv_ref, t_ref) = refs[:11]
    e_refs = refs[11 : 11 + depth]
    cur_refs = refs[11 + depth : 10 + 2 * depth]
    out_ref, dop_ref, del_ref, g_ref, dv_ref, acc_ref = refs[10 + 2 * depth :]
    j = pl.program_id(0)
    last = last_ref[j]
    rows, cols = iotas()
    strict = rows > cols
    lower = rows >= cols
    upper = rows <= cols
    total = dop_ref.shape[0]

    @pl.when(j == 0)
    def _():
        for c in range(total // BLOCK):
            rs = pl.ds(c * BLOCK, BLOCK)
            for h in range(heads):
                cs = slice(h * BLOCK, (h + 1) * BLOCK)
                dop = do_ref[rs, cs].astype(f32) * linv_ref[rs, cs]
                delta = jnp.sum(dop * o_ref[rs, cs].astype(f32), axis=1, keepdims=True)
                dop_ref[rs, cs] = dop.astype(bf16)
                del_ref[rs, cs] = jnp.broadcast_to(delta, (BLOCK, BLOCK))
                g_ref[c, h] = jnp.zeros((BLOCK, BLOCK), bf16)

    here = pl.ds(pl.multiple_of(j * BLOCK, BLOCK), BLOCK)
    near = []
    for h in range(heads):
        cs = slice(h * BLOCK, (h + 1) * BLOCK)
        dop = dop_ref[here, cs]
        e = e_refs[0][0, 0, h]
        dp = mm_rt(dop, v_ref[:, cs])
        near.append((e.astype(f32) * (dp - del_ref[here, cs]) * scale).astype(bf16))
        dv_ref[h] = mm_lt(e, dop)
        acc_ref[h] = jnp.zeros((BLOCK, 2 * BLOCK), f32)
    for d in range(1, depth):

        @pl.when(j + d <= last)
        def _():
            i = j + d
            there = pl.ds(pl.multiple_of(i * BLOCK, BLOCK), BLOCK)
            for h in range(heads):
                cs = slice(h * BLOCK, (h + 1) * BLOCK)
                dop = dop_ref[there, cs]
                e = e_refs[d][0, 0, h]
                dp = mm_rt(dop, v_ref[:, cs])
                ds = (e.astype(f32) * (dp - del_ref[there, cs]) * scale).astype(bf16)
                dv_ref[h] = dv_ref[h] + mm_lt(e, dop)
                dsg = jnp.concatenate([ds, g_ref[i, h]], axis=1)
                acc_ref[h] = acc_ref[h] + mm_lt(cur_refs[d - 1][0, 0, h], dsg)
                g_ref[i, h] = mm_rt(dsg, kp_ref[0, h]).astype(bf16)

    lane = cols
    dr_all = jnp.zeros((BLOCK, BLOCK), f32)
    width = heads * BLOCK
    for h in range(heads):
        cs = slice(h * BLOCK, (h + 1) * BLOCK)
        q, k, u = q_ref[:, cs], k_ref[:, cs], u_ref[:, cs]
        beta, inv_sq = strengths(u, r_ref[:, h : h + 1].astype(f32))
        bp = beta * inv_sq
        kq = mm_rt(u, jnp.concatenate([k, q], axis=0))
        e_s = jnp.where(strict, kq[:, :BLOCK], 0.0).astype(bf16)
        a_t = jnp.where(upper, kq[:, BLOCK:], 0.0).astype(bf16)
        dn = near[h]
        dq = g_ref[j, h]
        acc = acc_ref[h]
        bmat = jnp.concatenate([jnp.concatenate([dn, dq], axis=1), acc.astype(bf16)], axis=0)
        yz = mm(jnp.concatenate([a_t, u], axis=1), bmat).astype(bf16)
        ru = mm_rt(jnp.concatenate([e_s, u], axis=1), bmat)
        inv = inv_ref[0, h]
        left = mm_lt(inv, yz) * (-bp)
        right = -mm(inv, (ru * bp).astype(bf16))
        d_s = jnp.where(strict, -mm_rt(left.astype(bf16), t_ref[0, h]), 0.0).astype(bf16)
        d_e = jnp.where(strict, left[:, :BLOCK], 0.0).astype(bf16)
        d_at = jnp.where(upper, right[:, :BLOCK], 0.0).astype(bf16)
        d_a = d_at.astype(f32).T.astype(bf16)
        uk = jnp.concatenate([u, k], axis=0)
        uq = jnp.concatenate([u, q], axis=0)
        du = left[:, BLOCK:] + right[:, BLOCK:]
        du = du + mm(jnp.concatenate([d_s, d_e], axis=1), uk)
        d_st = d_s.astype(f32).T.astype(bf16)
        du = du + mm(jnp.concatenate([d_st, d_at], axis=1), uq)
        dq_o = dq.astype(f32) + mm(jnp.concatenate([d_a, dn], axis=1), uk)
        dk_o = acc[:, :BLOCK].T + mm_lt(jnp.concatenate([d_e, dn], axis=0), uq)
        uf = u.astype(f32)
        rad = jnp.sum(uf * du, axis=1, keepdims=True)
        du = du - (inv_sq * rad) * uf
        dr = 0.5 * rad * (1.0 - 0.5 * beta)
        dr_all = jnp.where(lane == h, dr, dr_all)
        out_ref[:, cs] = dq_o.astype(bf16)
        out_ref[:, width + h * BLOCK : width + (h + 1) * BLOCK] = dk_o.astype(bf16)
        out_ref[:, 2 * width + h * BLOCK : 2 * width + (h + 1) * BLOCK] = dv_ref[h].astype(bf16)
        out_ref[:, 3 * width + h * BLOCK : 3 * width + (h + 1) * BLOCK] = du.astype(bf16)
    out_ref[:, 4 * width :] = dr_all.astype(bf16)


def attention_prep(proj, heads):
    total = proj.shape[0]
    count = total // BLOCK
    width = heads * BLOCK
    step = 2
    wide = lambda col: pl.BlockSpec((step * BLOCK, width), lambda i: (i, col))
    tile = lambda n: pl.BlockSpec((step, heads, BLOCK, n), lambda i: (i, 0, 0, 0))
    shape = lambda n, t: jax.ShapeDtypeStruct((count, heads, BLOCK, n), t)
    return pl.pallas_call(
        functools.partial(prep_kernel, heads),
        grid=(count // step,),
        in_specs=[wide(0), wide(1), wide(3), pl.BlockSpec((step * BLOCK, BLOCK), lambda i: (i, 4 * heads))],
        out_specs=[tile(BLOCK), pl.BlockSpec((step * BLOCK, width), lambda i: (i, 0)), tile(2 * BLOCK), tile(BLOCK), tile(2 * BLOCK)],
        out_shape=[
            shape(BLOCK, f32),
            jax.ShapeDtypeStruct((total, width), bf16),
            shape(2 * BLOCK, bf16),
            shape(BLOCK, bf16),
            shape(2 * BLOCK, bf16),
        ],
        name="attn_prep",
    )(proj, proj, proj, proj)


def attention_fwd(proj, prep, first, heads, depth):
    near, q0, kp, _, _ = prep
    total = proj.shape[0]
    count = total // BLOCK
    width = heads * BLOCK
    scale = float(BLOCK) ** -0.5
    spec = pltpu.PrefetchScalarGridSpec(
        num_scalar_prefetch=1,
        grid=(count,),
        in_specs=[
            pl.BlockSpec((BLOCK, width), lambda i, f: (i, 0)),
            pl.BlockSpec((1, heads, BLOCK, BLOCK), lambda i, f: (i, 0, 0, 0)),
            pl.BlockSpec((count, heads, BLOCK, 2 * BLOCK), lambda i, f: (0, 0, 0, 0)),
            pl.BlockSpec((total, width), lambda i, f: (0, 2)),
        ],
        out_specs=[
            pl.BlockSpec((BLOCK, width), lambda i, f: (i, 0)),
            pl.BlockSpec((BLOCK, width), lambda i, f: (i, 0)),
            pl.BlockSpec((1, depth, heads, BLOCK, BLOCK), lambda i, f: (i, 0, 0, 0, 0)),
            pl.BlockSpec((1, depth - 1, heads, BLOCK, BLOCK), lambda i, f: (i, 0, 0, 0, 0)),
        ],
        scratch_shapes=[
            pltpu.VMEM((depth, heads, BLOCK, BLOCK), f32),
            pltpu.VMEM((heads, BLOCK, BLOCK), f32),
            pltpu.VMEM((heads, BLOCK, BLOCK), f32),
        ],
    )
    return pl.pallas_call(
        functools.partial(fwd_kernel, heads, depth, scale),
        grid_spec=spec,
        out_shape=[
            jax.ShapeDtypeStruct((total, width), bf16),
            jax.ShapeDtypeStruct((total, width), f32),
            jax.ShapeDtypeStruct((count, depth, heads, BLOCK, BLOCK), bf16),
            jax.ShapeDtypeStruct((count, depth - 1, heads, BLOCK, BLOCK), bf16),
        ],
        name="attn_fwd",
    )(first, q0, near, kp, proj)


def attention_bwd(proj, prep, saved, d_mixed, last, heads, depth):
    _, _, kp, inv, t_all = prep
    mixed, linv, e_all, cur_all = saved
    total = proj.shape[0]
    count = total // BLOCK
    width = heads * BLOCK
    scale = float(BLOCK) ** -0.5
    full = lambda: pl.BlockSpec((total, width), lambda j, f: (0, 0))
    wide = lambda col: pl.BlockSpec((BLOCK, width), lambda j, f: (j, col))
    tile = lambda n: pl.BlockSpec((1, heads, BLOCK, n), lambda j, f: (j, 0, 0, 0))

    def diagonal(d, slot):
        return pl.BlockSpec(
            (1, 1, heads, BLOCK, BLOCK), lambda j, f: (jnp.minimum(j + d, count - 1), slot, 0, 0, 0)
        )

    spec = pltpu.PrefetchScalarGridSpec(
        num_scalar_prefetch=1,
        grid=(count,),
        in_specs=[
            full(),
            full(),
            full(),
            wide(0),
            wide(1),
            wide(2),
            wide(3),
            pl.BlockSpec((BLOCK, BLOCK), lambda j, f: (j, 4 * heads)),
            tile(2 * BLOCK),
            tile(BLOCK),
            tile(2 * BLOCK),
        ]
        + [diagonal(d, d) for d in range(depth)]
        + [diagonal(d, d - 1) for d in range(1, depth)],
        out_specs=pl.BlockSpec((BLOCK, 4 * width + BLOCK), lambda j, f: (j, 0)),
        scratch_shapes=[
            pltpu.VMEM((total, width), bf16),
            pltpu.VMEM((total, width), f32),
            pltpu.VMEM((count, heads, BLOCK, BLOCK), bf16),
            pltpu.VMEM((heads, BLOCK, BLOCK), f32),
            pltpu.VMEM((heads, BLOCK, 2 * BLOCK), f32),
        ],
    )
    return pl.pallas_call(
        functools.partial(bwd_kernel, heads, depth, scale),
        grid_spec=spec,
        out_shape=jax.ShapeDtypeStruct((total, 4 * width + BLOCK), bf16),
        name="attn_bwd",
    )(last, d_mixed, mixed, linv, proj, proj, proj, proj, proj, kp, inv, t_all, *([e_all] * depth), *([cur_all] * (depth - 1)))


def block_tables(packing, begins):
    bins, bin_rows = packing.shape
    per_bin = bin_rows // BLOCK
    place = packing[:, ::BLOCK].reshape(-1) // BLOCK
    start = begins[:, ::BLOCK] // BLOCK + jnp.arange(bins, dtype=jnp.int32)[:, None] * per_bin
    start = start.reshape(-1)
    count = bins * per_bin
    slots = jnp.arange(count, dtype=jnp.int32)
    onehot = place[:, None] == slots[None, :]
    start_place = jnp.sum(jnp.where(start[:, None] == slots[None, :], place[None, :], 0), axis=1)
    first = jnp.sum(jnp.where(onehot, start_place[:, None], 0), axis=0).astype(jnp.int32)
    member = first[None, :] == first[:, None]
    last = jnp.max(jnp.where(member, slots[None, :], 0), axis=1).astype(jnp.int32)
    return first, last, per_bin


def rows_contract(a, b):
    return lax.dot_general(a, b, (((0,), (0,)), ((), ())), preferred_element_type=f32)


def cols_contract(a, b):
    return lax.dot_general(a, b, (((1,), (1,)), ((), ())), preferred_element_type=f32)


def unit_rows(x):
    scale = lax.rsqrt(jnp.mean(x * x, axis=1, keepdims=True) + epsilon)
    return x * scale, scale


def norm_back(grad_normed, unit, scale, gain):
    grad_unit = grad_normed * gain
    grad_gain = jnp.sum(grad_normed * unit, axis=0)
    grad_rows = scale * (grad_unit - unit * jnp.mean(grad_unit * unit, axis=1, keepdims=True))
    return grad_rows, grad_gain


def local(
    tokens,
    cotangent,
    w_query,
    w_key,
    w_value,
    w_house,
    w_beta,
    w_out,
    w_gate,
    w_up,
    w_down,
    gain_attn,
    gain_ffn,
    pack_index,
    seq_start,
):
    first, last, depth = block_tables(pack_index[0], seq_start[0])
    width = w_query.shape[1]
    heads = w_beta.shape[1]
    hidden_width = w_gate.shape[1]
    shard = w_query.shape[0]
    extras = jnp.concatenate(
        [w_beta, gain_attn[:, None], gain_ffn[:, None], jnp.zeros((shard, BLOCK - heads - 2), bf16)], axis=1
    )
    attn_pack = jnp.concatenate([w_query, w_key, w_value, w_house, extras, w_out], axis=1)
    ffn_pack = jnp.concatenate([w_gate, w_up, w_down], axis=1)
    full_tokens = lax.all_gather(tokens, "tp", axis=0, tiled=True)
    attn_full = lax.all_gather(attn_pack, "fsdp", axis=0, tiled=True)
    ffn_full = lax.all_gather(ffn_pack, "fsdp", axis=0, tiled=True)
    full_cot = lax.all_gather(cotangent, "tp", axis=0, tiled=True)
    proj_width = 4 * width + BLOCK
    w_in = attn_full[:, :proj_width]
    full_out = attn_full[:, proj_width:]
    gain_one = attn_full[:, 4 * width + heads].astype(f32)
    gain_two = attn_full[:, 4 * width + heads + 1].astype(f32)

    all_unit, _ = unit_rows(full_tokens.astype(f32))
    normed = (all_unit * gain_one).astype(bf16)
    proj = jnp.dot(normed, w_in, preferred_element_type=f32).astype(bf16)
    prep = attention_prep(proj, heads)
    saved = attention_fwd(proj, prep, first, heads, depth)
    mixed = saved[0]
    attn_part = lax.psum_scatter(
        cols_contract(mixed, full_out).astype(bf16), "tp", scatter_dimension=0, tiled=True
    ).astype(f32)
    x_own = tokens.astype(f32)
    unit_one, scale_one = unit_rows(x_own)
    hidden_in = x_own + attn_part
    unit_two, scale_two = unit_rows(hidden_in)
    normed_two = lax.all_gather((unit_two * gain_two).astype(bf16), "tp", axis=0, tiled=True)
    gate_pre = jnp.dot(normed_two, ffn_full[:, :hidden_width], preferred_element_type=f32)
    up_part = jnp.dot(normed_two, ffn_full[:, hidden_width : 2 * hidden_width], preferred_element_type=f32)
    full_down = ffn_full[:, 2 * hidden_width :]
    hidden = (jax.nn.silu(gate_pre) * up_part).astype(bf16)
    ffn_part = lax.psum_scatter(
        cols_contract(hidden, full_down).astype(bf16), "tp", scatter_dimension=0, tiled=True
    ).astype(f32)
    out_y = (hidden_in + ffn_part).astype(bf16)
    grad_hidden = jnp.dot(full_cot, full_down, preferred_element_type=f32)
    sigma = jax.nn.sigmoid(gate_pre)
    grad_gate = (grad_hidden * up_part * sigma * (1.0 + gate_pre * (1.0 - sigma))).astype(bf16)
    grad_up = (grad_hidden * jax.nn.silu(gate_pre)).astype(bf16)
    gate_up = jnp.concatenate([grad_gate, grad_up], axis=1)
    grad_two = lax.psum_scatter(
        cols_contract(gate_up, ffn_full[:, : 2 * hidden_width]).astype(bf16), "tp", scatter_dimension=0, tiled=True
    ).astype(f32)
    norm_two_grad, grad_gain_two = norm_back(grad_two, unit_two, scale_two, gain_two)
    grad_hidden_in = cotangent.astype(f32) + norm_two_grad
    grad_attn = lax.all_gather(grad_hidden_in.astype(bf16), "tp", axis=0, tiled=True)
    ffn_grads = jnp.concatenate(
        [rows_contract(normed_two, gate_up), rows_contract(full_cot, hidden)], axis=1
    ).astype(bf16)
    ffn_sum = lax.psum_scatter(ffn_grads, "fsdp", scatter_dimension=0, tiled=True).astype(f32)
    d_mixed = jnp.dot(grad_attn, full_out, preferred_element_type=f32).astype(bf16)
    d_proj = attention_bwd(proj, prep, saved, d_mixed, last, heads, depth)
    grad_one = lax.psum_scatter(
        cols_contract(d_proj, w_in).astype(bf16), "tp", scatter_dimension=0, tiled=True
    ).astype(f32)
    norm_one_grad, grad_gain_one = norm_back(grad_one, unit_one, scale_one, gain_one)
    out_dx = (grad_hidden_in + norm_one_grad).astype(bf16)
    attn_grads = jnp.concatenate(
        [rows_contract(normed, d_proj), rows_contract(grad_attn, mixed)], axis=1
    ).astype(bf16)
    attn_sum = lax.psum_scatter(attn_grads, "fsdp", scatter_dimension=0, tiled=True).astype(f32)
    gains = lax.psum(jnp.stack([grad_gain_one, grad_gain_two]), ("fsdp", "tp"))
    gains = lax.dynamic_slice_in_dim(gains, lax.axis_index("fsdp") * shard, shard, 1)
    return (
        out_y,
        out_dx,
        attn_sum[:, :width],
        attn_sum[:, width : 2 * width],
        attn_sum[:, 2 * width : 3 * width],
        attn_sum[:, 3 * width : 4 * width],
        attn_sum[:, 4 * width : 4 * width + heads],
        attn_sum[:, proj_width:],
        ffn_sum[:, :hidden_width],
        ffn_sum[:, hidden_width : 2 * hidden_width],
        ffn_sum[:, 2 * hidden_width :],
        gains[0],
        gains[1],
    )


def solution(mesh):
    rows = P(("fsdp", "tp"), None)
    weight = P("fsdp", "tp")
    return jax.shard_map(
        local,
        mesh=mesh,
        in_specs=(rows, rows) + (weight,) * 9 + (P("fsdp"), P("fsdp"), P("fsdp", None, None), P("fsdp", None, None)),
        out_specs=(rows, rows) + (weight,) * 9 + (P("fsdp"), P("fsdp")),
        check_vma=False,
    )
```

time: 5410 us -> 1130 us (0.21)
  other arithmetic: 1400 us -> 34.8 us
  matrix products: 1480 us -> 175 us
  waiting for transfers between devices: 1410 us -> 711 us
  local copies, waits for them, and re-layouts: 715 us -> 17.3 us
  loops' own time: 210 us -> 0 us
  Pallas kernels: 0 us -> 129 us
  blocking collectives: 137 us -> 39.8 us
    dot_general x568 -> x13, matrix products: 1450 us -> 175 us  [the longest x4 56.5 us: cols_contract(): lax.dot_general(a, b, (((1,), (1,)), ((), ())), preferred_element_type=f32)]
    another operation x134 -> x1, other arithmetic: 1090 us -> 0.01 us  [local(): gains = lax.psum(jnp.stack([grad_gain_one, grad_gain_two]), ('fsdp', 'tp'))]
    reduce_scatter x16 -> x6, waiting for transfers between devices: 769 us -> 335 us  [the longest x1 120 us: local(): lax.psum_scatter(attn_grads, 'fsdp', scatter_dimension=0, tiled=True)]
    all_gather x24 -> x6, waiting for transfers between devices: 633 us -> 374 us  [the longest x1 140 us: local(): ffn_full = lax.all_gather(ffn_pack, 'fsdp', axis=0, tiled=True)]
    another operation x5 -> x0, loops' own time: 210 us -> none  [the longest x4 196 us: path_head(): lax.scan(jax.checkpoint(advance), q_start.reshape(row_count, head_dim), s...]
    reshape x10 -> x1, local copies, waits for them, and re-layouts: 147 us -> 0.08 us  [block_tables(): place = packing[:, ::BLOCK].reshape(-1) // BLOCK]
    pallas_call x0 -> x3, Pallas kernels: none -> 129 us  [the longest x1 70.6 us: attention_bwd(): pl.pallas_call(functools.partial(bwd_kernel, heads, depth, scale), grid_s...]
    squeeze x60 -> x0, local copies, waits for them, and re-layouts: 108 us -> none  [path_head(): lax.scan(jax.checkpoint(advance), q_start.reshape(row_count, head_dim), s...]
  transfers between devices with their start and end apart: 41 -> 12, of which waited for: 28 -> 12; matrix products, arithmetic and copies ran while one was open for 36% -> 12% of each run, Pallas kernels for 0% -> 6%
where the time goes in v1:
time: 1130 us; the launch traced here: 1120 us
  waiting for transfers between devices  711 us (63%)
  matrix products  175 us (15%)
  Pallas kernels  129 us (11%)
  blocking collectives  39.8 us (4%)
  other arithmetic  34.8 us (3%)
  local copies, waits for them, and re-layouts  17.3 us (2%)
  between operations  14.7 us (1%)
    all_gather x1, waiting for transfers between devices, local(): ffn_full = lax.all_gather(ffn_pack, 'fsdp', axis=0, tiled=True)  140 us
    reduce_scatter x1, waiting for transfers between devices, local(): lax.psum_scatter(attn_grads, 'fsdp', scatter_dimension=0, tiled=True)  120 us
    all_gather x1, waiting for transfers between devices, local(): attn_full = lax.all_gather(attn_pack, 'fsdp', axis=0, tiled=True)  97.7 us
    pallas_call x1, Pallas kernels, attention_bwd(): pl.pallas_call(functools.partial(bwd_kernel, heads, depth, scale), grid_s...  70.6 us
    reduce_scatter x1, waiting for transfers between devices, local(): lax.psum_scatter(cols_contract(gate_up, ffn_full[:, :2 * hidden_width]).a...  58.1 us
    reduce_scatter x1, waiting for transfers between devices, local(): lax.psum_scatter(cols_contract(d_proj, w_in).astype(bf16), 'tp', scatter_...  57.1 us
    dot_general x4, matrix products, cols_contract(): lax.dot_general(a, b, (((1,), (1,)), ((), ())), preferred_element_type=f32)  56.5 us
    reduce_scatter x1, waiting for transfers between devices, local(): lax.psum_scatter(cols_contract(mixed, full_out).astype(bf16), 'tp', scatt...  53.4 us
  transfers between devices with their start and end apart: 12, of which 12 were waited for; matrix products, arithmetic and copies ran while one was open for 12% of the time, Pallas kernels for 6%

profile of v1, /device:TPU:0, one launch (start us, length us, event | category | flops | bytes accessed | tf_op | source)
XLA Modules:
  0.0 1122.1 jit_solution(13555780808790087562)
XLA Ops:
  15.1 43.6 %all-gather.7.cloned.1.call-done = bf16[2048,1536]{1,0:T(8,128)(2,1)} async-done(((bf16[512,1536]{1,0:T(8,128)(2,1)}), bf16[2048,1536]{1,0:T(8,128)(2,1)}) %all-gather.7.cloned.1.call-update) | async-done | bytes 6291472 | tf_op jit(solution)/shard_map/all_gather | solution.py:418
  58.7 4.1 fusion
  62.8 97.7 %all-gather.9.cloned.1.call-done = bf16[1536,2048]{1,0:T(8,128)(2,1)} async-done(((bf16[192,2048]{1,0:T(8,128)(2,1)}), bf16[1536,2048]{1,0:T(8,128)(2,1)}) %all-gather.9.cloned.1.call-update) | async-done | bytes 6291472 | tf_op jit(solution)/shard_map/all_gather | solution.py:419
  162.8 17.5 %convolution_convert_fusion.2.q_ref.k_ref.u_ref.r_ref.v_ref.refs_3_.refs_4_.refs_5_.refs_6_.refs_7_ = bf16[2048,1664]{1,0:T(8,128)(2,1)} fusion(bf16[1536,2048]{1,0:T(8,128)(2,1)} %all-gather.9.cloned.1.call-done, bf16[2048,1536]{1,0:T(8,128)(2,1)} %all-gather.7.cloned.1.call-done, f32[1536]{0:T(1024)S(1)} %get-tuple-element.71, f32[2048]{0:T(1024)S(1)} %add_rsqrt_fusion), kind=kOutput, calls=%fused_computation.18 | convolution fusion | flops 10484973568 | bytes 18233344 | tf_op jit(solution)/shard_map/dot_general | solution.py:430
  180.3 29.8 %attn_prep.1 = (f32[16,3,128,128]{3,2,1,0:T(8,128)}, bf16[2048,384]{1,0:T(8,128)(2,1)}, bf16[16,3,128,256]{3,2,1,0:T(8,128)(2,1)}, bf16[16,3,128,128]{3,2,1,0:T(8,128)(2,1)}, bf16[16,3,128,256]{3,2,1,0:T(8,128)(2,1)}) custom-call(bf16[2048,1664]{1,0:T(8,128)(2,1)} %convolution_convert_fusion.2.q_ref.k_ref.u_ref.r_ref.v_ref.refs_3_.refs_4_.refs_5_.refs_6_.refs_7_, ...), custom_call_target="tpu_custom_call" | custom-call | tf_op jit(solution)/shard_map/attn_prep/pallas_call | solution.py:248
  210.1 28.3 %attn_fwd.1 = (bf16[2048,384]{1,0:T(8,128)(2,1)}, f32[2048,384]{1,0:T(8,128)}, bf16[16,8,3,128,128]{4,3,2,1,0:T(8,128)(2,1)}, bf16[16,7,3,128,128]{4,3,2,1,0:T(8,128)(2,1)}) custom-call(s32[16]{0:T(128)} %select_reduce_fusion.1.first_ref, bf16[2048,384]{1,0:T(8,128)(2,1)} %get-tuple-element.22.q0_ref, f32[16,3,128,128]{3,2,1,0:T(8,128)} %get-tuple-element.23.near_ref, ...), custom_call_target="tpu_custom_call" | custom-call | tf_op jit(solution)/shard_map/attn_fwd/pallas_call | solution.py:291
  238.4 7.8 convolution_convert_fusion.1
  248.7 53.4 %reduce-scatter.7.cloned.1.call-done = bf16[512,1536]{1,0:T(8,128)(2,1)} async-done(((bf16[2048,1536]{1,0:T(8,128)(2,1)}), bf16[512,1536]{1,0:T(8,128)(2,1)}) %reduce-scatter.7.cloned.1.call-update) | async-done | bytes 1572880 | tf_op jit(solution)/shard_map/reduce_scatter | solution.py:434
  306.0 44.0 %all-gather.15.cloned.1.call-done = bf16[2048,1536]{1,0:T(8,128)(2,1)} async-done(((bf16[512,1536]{1,0:T(8,128)(2,1)}), bf16[2048,1536]{1,0:T(8,128)(2,1)}) %all-gather.15.cloned.1.call-update) | async-done | bytes 6291472 | tf_op jit(solution)/shard_map/all_gather | solution.py:421
  350.0 140.4 %all-gather.13.cloned.1.call-done = bf16[1536,3072]{1,0:T(8,128)(2,1)} async-done(((bf16[192,3072]{1,0:T(8,128)(2,1)}), bf16[1536,3072]{1,0:T(8,128)(2,1)}) %all-gather.13.cloned.1.call-update) | async-done | bytes 9437200 | tf_op jit(solution)/shard_map/all_gather | solution.py:420
  490.3 11.9 %fusion.33 = f32[1024,2048]{1,0:T(8,128)} fusion(bf16[2048,1536]{1,0:T(8,128)(2,1)} %all-gather.15.cloned.1.call-done, bf16[1536,3072]{1,0:T(8,128)(2,1)} %all-gather.13.cloned.1.call-done), kind=kOutput, calls=%fused_computation.61 | convolution fusion | flops 6442450944 | bytes 17825792 | tf_op jit(solution)/shard_map/dot_general | solution.py:450
  502.2 34.8 %all-gather.11.cloned.1.call-done = bf16[2048,1536]{1,0:T(8,128)(2,1)} async-done(((bf16[512,1536]{1,0:T(8,128)(2,1)}), bf16[2048,1536]{1,0:T(8,128)(2,1)}) %all-gather.11.cloned.1.call-update) | async-done | bytes 6291472 | tf_op jit(solution)/shard_map/all_gather | solution.py:441
  537.0 11.7 %fusion.30 = f32[2048,1024]{0,1:T(8,128)} fusion(bf16[2048,1536]{1,0:T(8,128)(2,1)} %all-gather.11.cloned.1.call-done, bf16[1536,3072]{1,0:T(8,128)(2,1)} %all-gather.13.cloned.1.call-done), kind=kOutput, calls=%fused_computation.53 | convolution fusion | flops 6442450944 | bytes 17825792 | tf_op jit(solution)/shard_map/dot_general | solution.py:442
  548.7 19.7 %fusion.5 = (bf16[2048,1024]{0,1:T(8,128)(2,1)}, bf16[2048,1024]{0,1:T(8,128)(2,1)}, bf16[2048,1024]{0,1:T(8,128)(2,1)}) fusion(f32[1024,2048]{1,0:T(8,128)} %fusion.33, f32[2048,1024]{0,1:T(8,128)} %fusion.30, bf16[2048,1536]{1,0:T(8,128)(2,1)} %all-gather.11.cloned.1.call-done, bf16[1536,3072]{1,0:T(8,128)(2,1)} %all-gather.13.cloned.1.call-done), kind=kOutput, calls=%fused_computation.11 | convolution fusion | flops 6473908224 | bytes 38797312 | tf_op jit(solution)/shard_map/dot_general | solution.py:443
  568.4 19.3 %convolution_convert_fusion.6 = bf16[2048,1536]{1,0:T(8,128)(2,1)} fusion(bf16[1536,3072]{1,0:T(8,128)(2,1)} %all-gather.13.cloned.1.call-done, bf16[2048,1024]{0,1:T(8,128)(2,1)} %get-tuple-element.78, bf16[2048,1024]{0,1:T(8,128)(2,1)} %get-tuple-element.77), kind=kOutput, calls=%fused_computation.22 | convolution fusion | flops 12904824832 | bytes 20971520 | tf_op jit(solution)/shard_map/dot_general | solution.py:376
  588.2 58.1 %reduce-scatter.11.cloned.1.call-done = bf16[512,1536]{1,0:T(8,128)(2,1)} async-done(((bf16[2048,1536]{1,0:T(8,128)(2,1)}), bf16[512,1536]{1,0:T(8,128)(2,1)}) %reduce-scatter.11.cloned.1.call-update) | async-done | bytes 1572880 | tf_op jit(solution)/shard_map/reduce_scatter | solution.py:455
  653.1 10.3 fusion.17
  663.4 16.8 %convolution_convert_fusion.3 = bf16[1536,2048]{1,0:T(8,128)(2,1)S(1)} fusion(bf16[2048,1536]{1,0:T(8,128)(2,1)} %all-gather.11.cloned.1.call-done, bf16[2048,1024]{0,1:T(8,128)(2,1)} %get-tuple-element.78, bf16[2048,1024]{0,1:T(8,128)(2,1)S(1)} %copy-done.23), kind=kOutput, calls=%fused_computation.19 | convolution fusion | flops 12904824832 | bytes 20971520 | tf_op jit(solution)/shard_map/dot_general | solution.py:372
  680.1 4.6 pad_maximum_fusion
  686.1 13.4 %all-gather.17.cloned.1.call-done = bf16[2048,1536]{1,0:T(8,128)(2,1)} async-done(((bf16[512,1536]{1,0:T(8,128)(2,1)}), bf16[2048,1536]{1,0:T(8,128)(2,1)}) %all-gather.17.cloned.1.call-update) | async-done | bytes 6291472 | tf_op jit(solution)/shard_map/all_gather | solution.py:460
  699.5 7.7 convolution_convert_fusion.9.refs_0_
  707.2 70.6 %attn_bwd.1 = bf16[2048,1664]{1,0:T(8,128)(2,1)} custom-call(s32[16]{0:T(128)} %select_reduce_fusion.last_ref, bf16[2048,384]{1,0:T(8,128)(2,1)} %convolution_convert_fusion.9.refs_0_, bf16[2048,384]{1,0:T(8,128)(2,1)} %get-tuple-element.25.refs_1_, f32[2048,384]{1,0:T(8,128)} %get-tuple-element.26.refs_2_, ...), custom_call_target="tpu_custom_call" | custom-call | tf_op jit(solution)/shard_map/attn_bwd/pallas_call | solution.py:347
  777.8 17.0 %convolution_convert_fusion.5 = bf16[2048,1536]{1,0:T(8,128)(2,1)} fusion(bf16[2048,1664]{1,0:T(8,128)(2,1)} %attn_bwd.1, bf16[1536,2048]{1,0:T(8,128)(2,1)} %all-gather.9.cloned.1.call-done), kind=kOutput, calls=%fused_computation.21 | convolution fusion | flops 10472128512 | bytes 18219008 | tf_op jit(solution)/shard_map/dot_general | solution.py:376
  796.2 6.3 convolution_convert_fusion.8
  802.5 16.3 %convolution_convert_fusion.4 = bf16[1536,1664]{1,0:T(8,128)(2,1)S(1)} fusion(bf16[2048,1664]{1,0:T(8,128)(2,1)} %attn_bwd.1, bf16[2048,1536]{1,0:T(8,128)(2,1)} %all-gather.7.cloned.1.call-done, f32[1536]{0:T(1024)S(1)} %copy-done.13, f32[2048]{0:T(1024)S(1)} %copy-done.21), kind=kOutput, calls=%fused_computation.20 | convolution fusion | flops 10484121600 | bytes 18233344 | tf_op jit(solution)/shard_map/dot_general | solution.py:372
  822.7 12.5 %convolution_convert_fusion = bf16[2048,1536]{1,0:T(8,128)(2,1)} fusion(bf16[2048,1024]{0,1:T(8,128)(2,1)} %get-tuple-element.79, bf16[1536,3072]{1,0:T(8,128)(2,1)} %all-gather.13.cloned.1.call-done), kind=kOutput, calls=%fused_computation.16 | convolution fusion | flops 6445596672 | bytes 13631488 | tf_op jit(solution)/shard_map/dot_general | solution.py:376
  835.9 30.8 %reduce-scatter.17.cloned.1.call-done = bf16[192,3072]{1,0:T(8,128)(2,1)} async-done(((bf16[1536,3072]{1,0:T(8,128)(2,1)}), bf16[192,3072]{1,0:T(8,128)(2,1)}) %reduce-scatter.17.cloned.1.call-update) | async-done | bytes 1179664 | tf_op jit(solution)/shard_map/reduce_scatter | solution.py:464
  869.3 57.1 %reduce-scatter.13.cloned.1.call-done = bf16[512,1536]{1,0:T(8,128)(2,1)} async-done(((bf16[2048,1536]{1,0:T(8,128)(2,1)}), bf16[512,1536]{1,0:T(8,128)(2,1)}) %reduce-scatter.13.cloned.1.call-update) | async-done | bytes 1572880 | tf_op jit(solution)/shard_map/reduce_scatter | solution.py:467
  929.0 119.5 %reduce-scatter.15.cloned.1.call-done = bf16[192,2048]{1,0:T(8,128)(2,1)} async-done(((bf16[1536,2048]{1,0:T(8,128)(2,1)}), bf16[192,2048]{1,0:T(8,128)(2,1)}) %reduce-scatter.15.cloned.1.call-update) | async-done | bytes 786448 | tf_op jit(solution)/shard_map/reduce_scatter | solution.py:475
  1050.0 39.8 %psum.7 = f32[2,1536]{1,0:T(2,128)S(1)} all-reduce(f32[2,1536]{1,0:T(2,128)S(1)} %pad_maximum_fusion.6), channel_id=1, replica_groups=mesh['fsdp'=8,'tp'=4] {'fsdp','tp'}, use_global_device_ids=true, to_apply=%region_16.17 | all-reduce | flops 3072 | bytes 24576 | tf_op jit(solution)/shard_map/psum | solution.py:476
  1092.8 16.5 %reduce-scatter.9.cloned.1.call-done = bf16[512,1536]{1,0:T(8,128)(2,1)} async-done(((bf16[2048,1536]{1,0:T(8,128)(2,1)}), bf16[512,1536]{1,0:T(8,128)(2,1)}) %reduce-scatter.9.cloned.1.call-update) | async-done | bytes 1572880 | tf_op jit(solution)/shard_map/reduce_scatter | solution.py:446
  1109.3 5.7 fusion.20
  (108 shorter events, 40.5 us)
Async XLA Ops:
  7.2 51.5 %all-gather.7.cloned.1.call-start = ((), (), s32[]{:S(2)}) async-start(), calls=%async_computation.6 | async-start | bytes 7864320 | tf_op jit(solution)/shard_map/all_gather | solution.py:418
  7.9 152.6 %all-gather.9.cloned.1.call-start = ((), (), s32[]{:S(2)}) async-start(), calls=%async_computation.7 | async-start | bytes 7077888 | tf_op jit(solution)/shard_map/all_gather | solution.py:419
  12.4 289.7 %reduce-scatter.7.cloned.1.call-start = ((), (), s32[]{:S(2)}) async-start(), calls=%async_computation.8 | async-start | bytes 7864320 | tf_op jit(solution)/shard_map/reduce_scatter | solution.py:434
  62.8 117.5 %copy-start.20 = (f32[2048]{0:T(1024)}, f32[2048]{0:T(1024)S(1)}, u32[]{:S(2)}) copy-start(f32[2048]{0:T(1024)S(1)} %add_rsqrt_fusion) | copy-start | bytes 24580
  162.2 487.8 %copy-start.10 = (f32[1536]{0:T(1024)}, f32[1536]{0:T(1024)S(1)}, u32[]{:S(2)}) copy-start(f32[1536]{0:T(1024)S(1)} %get-tuple-element.70) | copy-start | bytes 18436
  246.3 1.0 copy-start.7
  246.3 1.1 copy-start.8
  246.3 1.2 copy-start.9
  246.3 55.8 %copy-start = (bf16[512,1536]{1,0:T(8,128)(2,1)S(1)}, bf16[512,1536]{1,0:T(8,128)(2,1)}, u32[]{:S(2)}) copy-start(bf16[512,1536]{1,0:T(8,128)(2,1)} %param.15) | copy-start | bytes 4718596
  246.3 103.7 %all-gather.15.cloned.1.call-start = ((), (), s32[]{:S(2)}) async-start(), calls=%async_computation.12 | async-start | bytes 7864320 | tf_op jit(solution)/shard_map/all_gather | solution.py:421
  246.9 243.5 %all-gather.13.cloned.1.call-start = ((), (), s32[]{:S(2)}) async-start(), calls=%async_computation.10 | async-start | bytes 10616832 | tf_op jit(solution)/shard_map/all_gather | solution.py:420
  248.6 288.4 %all-gather.11.cloned.1.call-start = ((), (), s32[]{:S(2)}) async-start(), calls=%async_computation.9 | async-start | bytes 7864320 | tf_op jit(solution)/shard_map/all_gather | solution.py:441
  302.1 2.1 copy-start.2
  304.2 345.8 %copy-start.14 = (f32[512]{0:T(512)}, f32[512]{0:T(512)S(1)}, u32[]{:S(2)}) copy-start(f32[512]{0:T(512)S(1)} %add_rsqrt_fusion.2) | copy-start | bytes 6148
  305.9 340.3 %reduce-scatter.11.cloned.1.call-start = ((), (), s32[]{:S(2)}) async-start(), calls=%async_computation.13 | async-start | bytes 7864320 | tf_op jit(solution)/shard_map/reduce_scatter | solution.py:455
  587.8 111.8 %all-gather.17.cloned.1.call-start = ((), (), s32[]{:S(2)}) async-start(), calls=%async_computation.14 | async-start | bytes 7864320 | tf_op jit(solution)/shard_map/all_gather | solution.py:460
  646.3 4.3 copy-start.4
  646.3 4.3 copy-start.5
  653.0 213.6 %reduce-scatter.17.cloned.1.call-start = ((), (), s32[]{:S(2)}) async-start(), calls=%async_computation.17 | async-start | bytes 10616832 | tf_op jit(solution)/shard_map/reduce_scatter | solution.py:464
  653.1 10.3 copy-start.23
  684.8 241.7 %reduce-scatter.13.cloned.1.call-start = ((), (), s32[]{:S(2)}) async-start(), calls=%async_computation.15 | async-start | bytes 7864320 | tf_op jit(solution)/shard_map/reduce_scatter | solution.py:467
  794.7 1.4 copy-start.6
  794.8 7.7 copy-start.13
  794.8 7.7 copy-start.21
  794.8 253.7 %reduce-scatter.15.cloned.1.call-start = ((), (), s32[]{:S(2)}) async-start(), calls=%async_computation.16 | async-start | bytes 7077888 | tf_op jit(solution)/shard_map/reduce_scatter | solution.py:475
  822.4 286.9 %reduce-scatter.9.cloned.1.call-start = ((), (), s32[]{:S(2)}) async-start(), calls=%async_computation.11 | async-start | bytes 7864320 | tf_op jit(solution)/shard_map/reduce_scatter | solution.py:446
  835.1 0.7 copy-start.19
  835.1 91.4 %copy-start.1 = (bf16[512,1536]{1,0:T(8,128)(2,1)S(1)}, bf16[512,1536]{1,0:T(8,128)(2,1)}, u32[]{:S(2)}) copy-start(bf16[512,1536]{1,0:T(8,128)(2,1)} %param.15) | copy-start | bytes 4718596
  869.3 240.0 %copy-start.3 = (bf16[512,1536]{1,0:T(8,128)(2,1)S(1)}, bf16[512,1536]{1,0:T(8,128)(2,1)}, u32[]{:S(2)}) copy-start(bf16[512,1536]{1,0:T(8,128)(2,1)} %reduce-scatter.7.cloned.1.call-done) | copy-start | bytes 4718596
  869.3 240.0 %copy-start.11 = (f32[1536]{0:T(1024)S(1)}, f32[1536]{0:T(1024)}, u32[]{:S(2)}) copy-start(f32[1536]{0:T(1024)} %copy-done.10) | copy-start | bytes 18436
  869.3 240.0 %copy-start.15 = (f32[512]{0:T(512)S(1)}, f32[512]{0:T(512)}, u32[]{:S(2)}) copy-start(f32[512]{0:T(512)} %copy-done.14) | copy-start | bytes 6148
  869.3 240.0 %copy-start.18 = (f32[512]{0:T(512)S(1)}, f32[512]{0:T(512)}, u32[]{:S(2)}) copy-start(f32[512]{0:T(512)} %copy-done.17) | copy-start | bytes 6148
  (4 other events, 2.5 us)
Sparse Core Ops, SparseCore 0:
  9.6 49.0 all-gather.6
  61.4 99.0 all-gather.8
  246.4 55.6 reduce-scatter.6
  303.6 46.3 all-gather.14
  352.2 138.0 all-gather.12
  492.4 44.5 all-gather.10
  587.9 58.3 reduce-scatter.10
  653.1 46.3 all-gather.16
  703.1 163.4 reduce-scatter.16
  869.0 57.4 reduce-scatter.12
  930.5 117.9 reduce-scatter.14
  1051.1 58.1 reduce-scatter.8

commit v2 on v1

--- a/solution.py
+++ b/solution.py
@@ -257,6 +257,7 @@
             shape(BLOCK, bf16),
             shape(2 * BLOCK, bf16),
         ],
+        cost_estimate=pl.CostEstimate(flops=count * heads * 22 * 2 * BLOCK**3 * 4, bytes_accessed=20 * total * width, transcendentals=0),
         name="attn_prep",
     )(proj, proj, proj, proj)
 
@@ -297,6 +298,7 @@
             jax.ShapeDtypeStruct((count, depth, heads, BLOCK, BLOCK), bf16),
             jax.ShapeDtypeStruct((count, depth - 1, heads, BLOCK, BLOCK), bf16),
         ],
+        cost_estimate=pl.CostEstimate(flops=count * heads * 24 * 2 * BLOCK**3 * 4, bytes_accessed=20 * total * width, transcendentals=0),
         name="attn_fwd",
     )(first, q0, near, kp, proj)
 
@@ -348,6 +350,7 @@
         functools.partial(bwd_kernel, heads, depth, scale),
         grid_spec=spec,
         out_shape=jax.ShapeDtypeStruct((total, 4 * width + BLOCK), bf16),
+        cost_estimate=pl.CostEstimate(flops=count * heads * 60 * 2 * BLOCK**3 * 4, bytes_accessed=40 * total * width, transcendentals=0),
         name="attn_bwd",
     )(last, d_mixed, mixed, linv, proj, proj, proj, proj, proj, kp, inv, t_all, *([e_all] * depth), *([cur_all] * (depth - 1)))
 
@@ -383,9 +386,116 @@
 
 def norm_back(grad_normed, unit, scale, gain):
     grad_unit = grad_normed * gain
-    grad_gain = jnp.sum(grad_normed * unit, axis=0)
-    grad_rows = scale * (grad_unit - unit * jnp.mean(grad_unit * unit, axis=1, keepdims=True))
-    return grad_rows, grad_gain
+    return scale * (grad_unit - unit * jnp.mean(grad_unit * unit, axis=1, keepdims=True))
+
+
+def ring_order(count):
+    return list(range(0, count, 2)) + list(range(1, count, 2))[::-1]
+
+
+def ring_tables(axis):
+    count = lax.axis_size(axis)
+    order = ring_order(count)
+    place = [order.index(i) for i in range(count)]
+    right = [(order[p], order[(p + 1) % count]) for p in range(count)]
+    left = [(order[p], order[(p - 1) % count]) for p in range(count)]
+    spot = jnp.asarray(place, jnp.int32)[lax.axis_index(axis)]
+    owners = jnp.asarray(order, jnp.int32)
+    owner = lambda shift: owners[(spot + shift) % count]
+    return count, right, left, owner
+
+
+class RingGather:
+    def __init__(self, x, axis):
+        self.axis, self.x = axis, x
+        self.count, self.right, self.left, self.owner = ring_tables(axis)
+        self.moving = (x, x)
+        self.hops = []
+
+    def hop(self):
+        from_left, from_right = self.moving
+        if len(self.hops) == self.count // 2 - 1:
+            half = self.x.shape[0] // 2
+            from_left, from_right = from_left[:half], from_right[half:]
+        self.moving = (
+            lax.ppermute(from_left, self.axis, self.right),
+            lax.ppermute(from_right, self.axis, self.left),
+        )
+        self.hops.append(self.moving)
+
+    def before(self, *values):
+        held = lax.optimization_barrier((self.moving,) + values)
+        self.moving = held[0]
+        self.hops[-1] = self.moving
+        return held[1] if len(values) == 1 else held[1:]
+
+    def finish(self):
+        while len(self.hops) < self.count // 2:
+            self.hop()
+        rows = self.x.shape[0]
+        put = lax.dynamic_update_slice_in_dim
+        out = put(jnp.zeros((self.count * rows, self.x.shape[1]), self.x.dtype), self.x, self.owner(0) * rows, 0)
+        for s, (from_left, from_right) in enumerate(self.hops[:-1], 1):
+            out = put(out, from_left, self.owner(-s) * rows, 0)
+            out = put(out, from_right, self.owner(s) * rows, 0)
+        far = self.owner(self.count // 2) * rows
+        out = put(out, self.hops[-1][0], far, 0)
+        return put(out, self.hops[-1][1], far + rows // 2, 0)
+
+
+class RingScatter:
+    def __init__(self, parts, axis):
+        self.axis, self.parts = axis, parts
+        self.count, self.right, self.left, self.owner = ring_tables(axis)
+        self.rows = parts.shape[0] // self.count
+        self.top = self.count // 2
+        self.done = 0
+        half = self.rows // 2
+        self.moving = (self.piece(self.top, 0, half), self.piece(-self.top, half, half))
+
+    def piece(self, shift, start=0, size=None):
+        size = self.rows if size is None else size
+        return lax.dynamic_slice_in_dim(self.parts, self.owner(shift) * self.rows + start, size, 0)
+
+    def hop(self):
+        to_right, to_left = self.moving
+        if self.done > 0:
+            s = self.top - self.done
+            a, b = self.piece(s), self.piece(-s)
+            if self.done == 1:
+                half = self.rows // 2
+                to_right = jnp.concatenate([a[:half] + to_right, a[half:]], axis=0)
+                to_left = jnp.concatenate([b[:half], b[half:] + to_left], axis=0)
+            else:
+                to_right, to_left = a + to_right, b + to_left
+        self.moving = (lax.ppermute(to_right, self.axis, self.right), lax.ppermute(to_left, self.axis, self.left))
+        self.done += 1
+
+    def before(self, *values):
+        held = lax.optimization_barrier((self.moving,) + values)
+        self.moving = held[0]
+        return held[1] if len(values) == 1 else held[1:]
+
+    def finish(self):
+        while self.done < self.top:
+            self.hop()
+        return self.piece(0).astype(f32) + self.moving[0].astype(f32) + self.moving[1].astype(f32)
+
+
+def tp_sum(x):
+    count = lax.axis_size("tp")
+    me = lax.axis_index("tp")
+    pieces = [x] + [lax.ppermute(x, "tp", [(i, (i + s) % count) for i in range(count)]) for s in range(1, count)]
+    stacked = jnp.stack(pieces)
+    slots = (me - jnp.arange(count, dtype=jnp.int32)) % count
+    total = jnp.zeros_like(x)
+    for r in range(count):
+        total = total + jnp.sum(jnp.where((slots == r)[:, None, None], stacked, 0.0), axis=0)
+    return total
+
+
+def after(x, *others):
+    return lax.optimization_barrier((x,) + others)[0]
 
 
 def local(
@@ -416,21 +526,28 @@
     attn_pack = jnp.concatenate([w_query, w_key, w_value, w_house, extras, w_out], axis=1)
     ffn_pack = jnp.concatenate([w_gate, w_up, w_down], axis=1)
     full_tokens = lax.all_gather(tokens, "tp", axis=0, tiled=True)
-    attn_full = lax.all_gather(attn_pack, "fsdp", axis=0, tiled=True)
-    ffn_full = lax.all_gather(ffn_pack, "fsdp", axis=0, tiled=True)
-    full_cot = lax.all_gather(cotangent, "tp", axis=0, tiled=True)
+    attn_full = RingGather(attn_pack, "fsdp").finish()
+    ffn_ring = RingGather(after(ffn_pack, attn_full), "fsdp")
+    ffn_ring.hop()
+    full_cot = lax.all_gather(after(cotangent, full_tokens), "tp", axis=0, tiled=True)
     proj_width = 4 * width + BLOCK
     w_in = attn_full[:, :proj_width]
     full_out = attn_full[:, proj_width:]
-    gain_one = attn_full[:, 4 * width + heads].astype(f32)
-    gain_two = attn_full[:, 4 * width + heads + 1].astype(f32)
+    pick = (jnp.arange(BLOCK)[None, :] == heads + jnp.arange(8)[:, None]).astype(bf16)
+    gain_rows = cols_contract(pick, attn_full[:, 4 * width : proj_width])
+    gain_one, gain_two = gain_rows[0], gain_rows[1]
 
     all_unit, _ = unit_rows(full_tokens.astype(f32))
     normed = (all_unit * gain_one).astype(bf16)
     proj = jnp.dot(normed, w_in, preferred_element_type=f32).astype(bf16)
-    prep = attention_prep(proj, heads)
+    proj = ffn_ring.before(proj)
+    ffn_ring.hop()
+    prep = list(attention_prep(proj, heads))
+    prep[0] = ffn_ring.before(prep[0])
+    ffn_ring.hop()
     saved = attention_fwd(proj, prep, first, heads, depth)
-    mixed = saved[0]
+    mixed, full_cot = ffn_ring.before(saved[0], full_cot)
+    ffn_full = ffn_ring.finish()
     attn_part = lax.psum_scatter(
         cols_contract(mixed, full_out).astype(bf16), "tp", scatter_dimension=0, tiled=True
     ).astype(f32)
@@ -443,10 +560,7 @@
     up_part = jnp.dot(normed_two, ffn_full[:, hidden_width : 2 * hidden_width], preferred_element_type=f32)
     full_down = ffn_full[:, 2 * hidden_width :]
     hidden = (jax.nn.silu(gate_pre) * up_part).astype(bf16)
-    ffn_part = lax.psum_scatter(
-        cols_contract(hidden, full_down).astype(bf16), "tp", scatter_dimension=0, tiled=True
-    ).astype(f32)
-    out_y = (hidden_in + ffn_part).astype(bf16)
+    ffn_rows = cols_contract(hidden, full_down).astype(bf16)
     grad_hidden = jnp.dot(full_cot, full_down, preferred_element_type=f32)
     sigma = jax.nn.sigmoid(gate_pre)
     grad_gate = (grad_hidden * up_part * sigma * (1.0 + gate_pre * (1.0 - sigma))).astype(bf16)
@@ -455,26 +569,41 @@
     grad_two = lax.psum_scatter(
         cols_contract(gate_up, ffn_full[:, : 2 * hidden_width]).astype(bf16), "tp", scatter_dimension=0, tiled=True
     ).astype(f32)
-    norm_two_grad, grad_gain_two = norm_back(grad_two, unit_two, scale_two, gain_two)
-    grad_hidden_in = cotangent.astype(f32) + norm_two_grad
-    grad_attn = lax.all_gather(grad_hidden_in.astype(bf16), "tp", axis=0, tiled=True)
     ffn_grads = jnp.concatenate(
         [rows_contract(normed_two, gate_up), rows_contract(full_cot, hidden)], axis=1
     ).astype(bf16)
-    ffn_sum = lax.psum_scatter(ffn_grads, "fsdp", scatter_dimension=0, tiled=True).astype(f32)
+    ffn_back = RingScatter(ffn_grads, "fsdp")
+    ffn_back.hop()
+    grad_two, mixed = ffn_back.before(grad_two, mixed)
+    ffn_back.hop()
+    norm_two_grad = norm_back(grad_two, unit_two, scale_two, gain_two)
+    grad_hidden_in = cotangent.astype(f32) + norm_two_grad
+    grad_attn = lax.all_gather(grad_hidden_in.astype(bf16), "tp", axis=0, tiled=True)
+    ffn_part = lax.psum_scatter(after(ffn_rows, grad_attn), "tp", scatter_dimension=0, tiled=True).astype(f32)
+    out_y = (hidden_in + ffn_part).astype(bf16)
+    grad_out = rows_contract(grad_attn, mixed)
     d_mixed = jnp.dot(grad_attn, full_out, preferred_element_type=f32).astype(bf16)
+    d_mixed, grad_out = ffn_back.before(d_mixed, grad_out)
+    ffn_back.hop()
     d_proj = attention_bwd(proj, prep, saved, d_mixed, last, heads, depth)
+    d_proj = ffn_back.before(d_proj)
+    attn_grads = jnp.concatenate([rows_contract(normed, d_proj), grad_out], axis=1).astype(bf16)
+    attn_back = RingScatter(attn_grads, "fsdp")
+    attn_back.hop()
+    d_proj = after(d_proj, attn_grads)
     grad_one = lax.psum_scatter(
         cols_contract(d_proj, w_in).astype(bf16), "tp", scatter_dimension=0, tiled=True
     ).astype(f32)
-    norm_one_grad, grad_gain_one = norm_back(grad_one, unit_one, scale_one, gain_one)
+    norm_one_grad = norm_back(grad_one, unit_one, scale_one, gain_one)
     out_dx = (grad_hidden_in + norm_one_grad).astype(bf16)
-    attn_grads = jnp.concatenate(
-        [rows_contract(normed, d_proj), rows_contract(grad_attn, mixed)], axis=1
-    ).astype(bf16)
-    attn_sum = lax.psum_scatter(attn_grads, "fsdp", scatter_dimension=0, tiled=True).astype(f32)
-    gains = lax.psum(jnp.stack([grad_gain_one, grad_gain_two]), ("fsdp", "tp"))
-    gains = lax.dynamic_slice_in_dim(gains, lax.axis_index("fsdp") * shard, shard, 1)
+    ffn_sum = ffn_back.finish()
+    attn_sum = attn_back.finish()
+    own = lambda grads, weights: jnp.sum(grads * weights.astype(f32), axis=1)
+    own_one = own(attn_sum[:, : 4 * width], attn_pack[:, : 4 * width]) + own(
+        attn_sum[:, 4 * width : 4 * width + heads], w_beta
+    )
+    own_two = own(ffn_sum[:, : 2 * hidden_width], ffn_pack[:, : 2 * hidden_width])
+    gains = tp_sum(jnp.stack([own_one, own_two])) / jnp.stack([gain_attn, gain_ffn]).astype(f32)
     return (
         out_y,
         out_dx,

time: 1130 us -> 726 us (0.64)
  waiting for transfers between devices: 711 us -> 267 us
  blocking collectives: 39.8 us -> 0 us
  starting transfers between devices: 1.53 us -> 37 us
  local copies, waits for them, and re-layouts: 17.3 us -> 33.4 us
  Pallas kernels: 129 us -> 145 us
  between operations: 14.7 us -> 28.9 us
    all_gather x3 -> x1, waiting for transfers between devices: 282 us -> 0.02 us  [local(): lax.all_gather(after(cotangent, full_tokens), 'tp', axis=0, tiled=True)]
    reduce_scatter x3 -> x1, waiting for transfers between devices: 167 us -> 0.02 us  [local(): lax.psum_scatter(after(ffn_rows, grad_attn), 'tp', scatter_dimension=0, t...]
    ppermute x0 -> x35, waiting for transfers between devices: none -> 115 us  [the longest x8 42.4 us: hop(): lax.ppermute(from_left, self.axis, self.right)]
    reduce_scatter x1, waiting for transfers between devices: 57.1 us -> 0.01 us  [local(): lax.psum_scatter(cols_contract(d_proj, w_in).astype(bf16), 'tp', scatter_...]
    psum x1 -> x0, blocking collectives: 39.8 us -> none  [local(): gains = lax.psum(jnp.stack([grad_gain_one, grad_gain_two]), ('fsdp', 'tp'))]
    ppermute x0 -> x35, starting transfers between devices: none -> 36.4 us  [the longest x8 14.1 us: hop(): lax.ppermute(from_left, self.axis, self.right)]
    reduce_scatter x1, waiting for transfers between devices: 58.1 us -> 25.1 us  [local(): lax.psum_scatter(cols_contract(gate_up, ffn_full[:, :2 * hidden_width]).a...]
    all_gather x1, waiting for transfers between devices: 34.8 us -> 8.57 us  [local(): lax.all_gather((unit_two * gain_two).astype(bf16), 'tp', axis=0, tiled=True)]
  transfers between devices with their start and end apart: 12 -> 43, of which waited for: 12 -> 21; matrix products, arithmetic and copies ran while one was open for 12% -> 20% of each run, Pallas kernels for 6% -> 20%
where the time goes in v2:
time: 726 us; the launch traced here: 723 us
  waiting for transfers between devices  267 us (37%)
  matrix products  168 us (23%)
  Pallas kernels  145 us (20%)
  other arithmetic  43.9 us (6%)
  starting transfers between devices  37 us (5%)
  local copies, waits for them, and re-layouts  33.4 us (5%)
  between operations  28.9 us (4%)
    pallas_call x1, Pallas kernels, attention_bwd(): pl.pallas_call(functools.partial(bwd_kernel, heads, depth, scale), grid_s...  81.1 us
    dot_general x5, matrix products, cols_contract(): lax.dot_general(a, b, (((1,), (1,)), ((), ())), preferred_element_type=f32)  57.3 us
    reduce_scatter x1, waiting for transfers between devices, local(): lax.psum_scatter(cols_contract(mixed, full_out).astype(bf16), 'tp', scatt...  54.8 us
    dot_general x4, matrix products, rows_contract(): lax.dot_general(a, b, (((0,), (0,)), ((), ())), preferred_element_type=f32)  48.8 us
    ppermute x8, waiting for transfers between devices, hop(): lax.ppermute(from_left, self.axis, self.right)  42.4 us
    all_gather x1, waiting for transfers between devices, local(): lax.all_gather(grad_hidden_in.astype(bf16), 'tp', axis=0, tiled=True)  38.4 us
    ppermute x8, waiting for transfers between devices, hop(): lax.ppermute(to_right, self.axis, self.right)  36.1 us
    pallas_call x1, Pallas kernels, attention_fwd(): pl.pallas_call(functools.partial(fwd_kernel, heads, depth, scale), grid_s...  34.3 us
  transfers between devices with their start and end apart: 43, of which 21 were waited for; matrix products, arithmetic and copies ran while one was open for 20% of the time, Pallas kernels for 20%

profile of v2, /device:TPU:0, one launch (start us, length us, event | category | flops | bytes accessed | tf_op | source)
XLA Modules:
  0.0 723.5 jit_solution(8958928590511249261)
XLA Ops:
  34.9 23.8 %all-gather.5.cloned.1.call-done = bf16[2048,1536]{1,0:T(8,128)(2,1)} async-done(((bf16[512,1536]{1,0:T(8,128)(2,1)}), bf16[2048,1536]{1,0:T(8,128)(2,1)}) %all-gather.5.cloned.1.call-update) | async-done | bytes 6291472 | tf_op jit(solution)/shard_map/all_gather | solution.py:528
  66.1 14.0 %collective-permute-done.4 = bf16[192,2048]{1,0:T(8,128)(2,1)S(1)} collective-permute-done((bf16[192,2048]{1,0:T(8,128)(2,1)}, bf16[192,2048]{1,0:T(8,128)(2,1)S(1)}, u32[]{:S(2)}, u32[]{:S(2)}) %collective-permute-start.4) | collective-permute-done | bytes 786464 | tf_op jit(solution)/shard_map/ppermute | solution.py:421
  82.4 8.3 %collective-permute-done.6 = bf16[96,2048]{1,0:T(8,128)(2,1)S(1)} collective-permute-done((bf16[96,2048]{1,0:T(8,128)(2,1)S(1)}, bf16[96,2048]{1,0:T(8,128)(2,1)S(1)}, u32[]{:S(2)}, u32[]{:S(2)}) %collective-permute-start.6) | collective-permute-done | bytes 393248 | tf_op jit(solution)/shard_map/ppermute | solution.py:421
  95.8 14.0 %convolution_convert_fusion.2.q_ref.k_ref.u_ref.r_ref.v_ref.refs_3_.refs_4_.refs_5_.refs_6_.refs_7_ = bf16[2048,1664]{1,0:T(8,128)(2,1)} fusion(bf16[1536,2048]{1,0:T(8,128)(2,1)S(1)} %constant_dynamic-update-slice_fusion.9, bf16[2048,1536]{1,0:T(8,128)(2,1)S(1)} %bitcast.39, f32[1536]{0:T(1024)S(1)} %get-tuple-element.123, f32[2048]{0:T(1024)S(1)} %add_rsqrt_fusion), kind=kOutput, calls=%fused_computation.41 | convolution fusion | flops 10484973568 | bytes 18235392 | tf_op jit(solution)/shard_map/dot_general | solution.py:542
  109.8 8.6 %collective-permute-done.8 = bf16[192,3072]{1,0:T(8,128)(2,1)S(1)} collective-permute-done((bf16[192,3072]{1,0:T(8,128)(2,1)S(1)}, bf16[192,3072]{1,0:T(8,128)(2,1)S(1)}, u32[]{:S(2)}, u32[]{:S(2)}) %collective-permute-start.8) | collective-permute-done | bytes 1179680 | tf_op jit(solution)/shard_map/ppermute | solution.py:421
  121.8 29.9 %attn_prep.1 = (f32[16,3,128,128]{3,2,1,0:T(8,128)}, bf16[2048,384]{1,0:T(8,128)(2,1)}, bf16[16,3,128,256]{3,2,1,0:T(8,128)(2,1)}, bf16[16,3,128,128]{3,2,1,0:T(8,128)(2,1)}, bf16[16,3,128,256]{3,2,1,0:T(8,128)(2,1)}) custom-call(bf16[2048,1664]{1,0:T(8,128)(2,1)} %convolution_convert_fusion.2.q_ref.k_ref.u_ref.r_ref.v_ref.refs_3_.refs_4_.refs_5_.refs_6_.refs_7_, ...), custom_call_target="tpu_custom_call" | custom-call | flops 17716740096 | bytes 15728640 | tf_op jit(solution)/shard_map/attn_prep/pallas_call | solution.py:248
  154.2 34.3 %attn_fwd.1 = (bf16[2048,384]{1,0:T(8,128)(2,1)}, f32[2048,384]{1,0:T(8,128)}, bf16[16,8,3,128,128]{4,3,2,1,0:T(8,128)(2,1)}, bf16[16,7,3,128,128]{4,3,2,1,0:T(8,128)(2,1)}) custom-call(s32[16]{0:T(128)} %select_reduce_fusion.5.first_ref, bf16[2048,384]{1,0:T(8,128)(2,1)} %get-tuple-element.54.q0_ref, f32[16,3,128,128]{3,2,1,0:T(8,128)} %get-tuple-element.55.near_ref, ...), custom_call_target="tpu_custom_call" | custom-call | flops 19327352832 | bytes 15728640 | tf_op jit(solution)/shard_map/attn_fwd/pallas_call | solution.py:292
  188.6 8.3 %convolution_convert_fusion.1 = bf16[2048,1536]{1,0:T(8,128)(2,1)} fusion(bf16[2048,384]{1,0:T(8,128)(2,1)} %get-tuple-element.67.refs_1_, bf16[1536,2048]{1,0:T(8,128)(2,1)} %copy-done.13), kind=kOutput, calls=%fused_computation.40 | convolution fusion | flops 2419064832 | bytes 9043968 | tf_op jit(solution)/shard_map/dot_general | solution.py:379
  197.0 54.8 %reduce-scatter.5.cloned.1.call-done = bf16[512,1536]{1,0:T(8,128)(2,1)} async-done(((bf16[2048,1536]{1,0:T(8,128)(2,1)}), bf16[512,1536]{1,0:T(8,128)(2,1)}) %reduce-scatter.5.cloned.1.call-update) | async-done | bytes 1572880 | tf_op jit(solution)/shard_map/reduce_scatter | solution.py:551
  268.6 9.8 %collective-permute-done.14 = bf16[96,3072]{1,0:T(8,128)(2,1)S(1)} collective-permute-done((bf16[96,3072]{1,0:T(8,128)(2,1)S(1)}, bf16[96,3072]{1,0:T(8,128)(2,1)S(1)}, u32[]{:S(2)}, u32[]{:S(2)}) %collective-permute-start.14) | collective-permute-done | bytes 589856 | tf_op jit(solution)/shard_map/ppermute | solution.py:421
  284.7 9.0 %fusion.20 = f32[2048,1024]{0,1:T(8,128)} fusion(bf16[2048,1536]{1,0:T(8,128)(2,1)S(1)} %bitcast.49, bf16[1536,3072]{1,0:T(8,128)(2,1)S(1)} %constant_dynamic-update-slice_fusion.1), kind=kOutput, calls=%fused_computation.82 | convolution fusion | flops 6442450944 | bytes 17825792 | tf_op jit(solution)/shard_map/dot_general | solution.py:564
  293.6 8.6 %all-gather.9.cloned.1.call-done = bf16[2048,1536]{1,0:T(8,128)(2,1)} async-done(((bf16[512,1536]{1,0:T(8,128)(2,1)}), bf16[2048,1536]{1,0:T(8,128)(2,1)}) %all-gather.9.cloned.1.call-update) | async-done | bytes 6291472 | tf_op jit(solution)/shard_map/all_gather | solution.py:558
  302.2 11.7 %fusion.15 = f32[2048,1024]{0,1:T(8,128)} fusion(bf16[2048,1536]{1,0:T(8,128)(2,1)} %all-gather.9.cloned.1.call-done, bf16[1536,3072]{1,0:T(8,128)(2,1)} %copy-done.12), kind=kOutput, calls=%fused_computation.70 | convolution fusion | flops 6442450944 | bytes 17825792 | tf_op jit(solution)/shard_map/dot_general | solution.py:560
  314.0 19.8 %multiply_convert_fusion.1 = (bf16[2048,1024]{0,1:T(8,128)(2,1)}, bf16[2048,1024]{0,1:T(8,128)(2,1)}, bf16[2048,1024]{0,1:T(8,128)(2,1)}) fusion(f32[2048,1024]{0,1:T(8,128)} %fusion.20, f32[2048,1024]{0,1:T(8,128)} %fusion.15, bf16[2048,1536]{1,0:T(8,128)(2,1)} %all-gather.9.cloned.1.call-done, bf16[1536,3072]{1,0:T(8,128)(2,1)} %copy-done.12), kind=kOutput, calls=%fused_computation.35 | convolution fusion | flops 6473908224 | bytes 38797312 | tf_op jit(solution)/shard_map/dot_general | solution.py:559
  333.8 19.1 %convolution_convert_fusion.5 = bf16[2048,1536]{1,0:T(8,128)(2,1)} fusion(bf16[1536,3072]{1,0:T(8,128)(2,1)} %copy-done.12, bf16[2048,1024]{0,1:T(8,128)(2,1)} %get-tuple-element.128, bf16[2048,1024]{0,1:T(8,128)(2,1)} %get-tuple-element.127), kind=kOutput, calls=%fused_computation.44 | convolution fusion | flops 12904824832 | bytes 20971520 | tf_op jit(solution)/shard_map/dot_general | solution.py:379
  353.7 10.7 %convolution_convert_fusion.7 = bf16[1536,1024]{1,0:T(8,128)(2,1)S(1)} fusion(bf16[2048,1536]{1,0:T(8,128)(2,1)} %all-gather.7.cloned.1.call-done, bf16[2048,1024]{0,1:T(8,128)(2,1)} %get-tuple-element.129), kind=kOutput, calls=%fused_computation.61 | convolution fusion | flops 6444023808 | bytes 13631488 | tf_op jit(solution)/shard_map/dot_general | solution.py:375
  364.4 16.9 %convolution_convert_fusion.6 = bf16[1536,2048]{1,0:T(8,128)(2,1)S(1)} fusion(bf16[2048,1536]{1,0:T(8,128)(2,1)} %all-gather.9.cloned.1.call-done, bf16[2048,1024]{0,1:T(8,128)(2,1)} %get-tuple-element.128, bf16[2048,1024]{0,1:T(8,128)(2,1)S(1)} %copy-done.46), kind=kOutput, calls=%fused_computation.45 | convolution fusion | flops 12904824832 | bytes 20971520 | tf_op jit(solution)/shard_map/dot_general | solution.py:375
  386.4 25.1 %reduce-scatter.7.cloned.1.call-done = bf16[512,1536]{1,0:T(8,128)(2,1)} async-done(((bf16[2048,1536]{1,0:T(8,128)(2,1)}), bf16[512,1536]{1,0:T(8,128)(2,1)}) %reduce-scatter.7.cloned.1.call-update) | async-done | bytes 1572880 | tf_op jit(solution)/shard_map/reduce_scatter | solution.py:569
  426.7 38.4 %all-gather.11.cloned.1.call-done = bf16[2048,1536]{1,0:T(8,128)(2,1)} async-done(((bf16[512,1536]{1,0:T(8,128)(2,1)}), bf16[2048,1536]{1,0:T(8,128)(2,1)}) %all-gather.11.cloned.1.call-update) | async-done | bytes 6291472 | tf_op jit(solution)/shard_map/all_gather | solution.py:581
  465.1 7.8 %convolution_convert_fusion.8.refs_0_ = bf16[2048,384]{1,0:T(8,128)(2,1)} fusion(bf16[2048,1536]{1,0:T(8,128)(2,1)} %all-gather.11.cloned.1.call-done, bf16[1536,2048]{1,0:T(8,128)(2,1)} %copy-done.13), kind=kOutput, calls=%fused_computation.80 | convolution fusion | flops 2416705536 | bytes 9043968 | tf_op jit(solution)/shard_map/dot_general | solution.py:585
  472.9 4.6 fusion.70
  477.5 4.4 fusion.35
  484.1 81.1 %attn_bwd.1 = bf16[2048,1664]{1,0:T(8,128)(2,1)} custom-call(s32[16]{0:T(128)} %select_reduce_fusion.4.last_ref, bf16[2048,384]{1,0:T(8,128)(2,1)} %convolution_convert_fusion.8.refs_0_, bf16[2048,384]{1,0:T(8,128)(2,1)} %get-tuple-element.67.refs_1_, f32[2048,384]{1,0:T(8,128)} %get-tuple-element.71.refs_2_, ...), custom_call_target="tpu_custom_call" | custom-call | flops 48318382080 | bytes 31457280 | tf_op jit(solution)/shard_map/attn_bwd/pallas_call | solution.py:349
  565.2 17.0 %convolution_convert_fusion.3 = bf16[2048,1536]{1,0:T(8,128)(2,1)} fusion(bf16[2048,1664]{1,0:T(8,128)(2,1)} %attn_bwd.1, bf16[1536,2048]{1,0:T(8,128)(2,1)} %copy-done.13), kind=kOutput, calls=%fused_computation.42 | convolution fusion | flops 10472128512 | bytes 18219008 | tf_op jit(solution)/shard_map/dot_general | solution.py:379
  582.5 12.6 %convolution_convert_fusion = bf16[2048,1536]{1,0:T(8,128)(2,1)} fusion(bf16[2048,1024]{0,1:T(8,128)(2,1)} %get-tuple-element.129, bf16[1536,3072]{1,0:T(8,128)(2,1)} %copy-done.12), kind=kOutput, calls=%fused_computation.39 | convolution fusion | flops 6445596672 | bytes 13631488 | tf_op jit(solution)/shard_map/dot_general | solution.py:379
  595.8 16.5 %convolution_convert_fusion.4 = bf16[1536,1664]{1,0:T(8,128)(2,1)S(1)} fusion(bf16[2048,1664]{1,0:T(8,128)(2,1)} %attn_bwd.1, bf16[2048,1536]{1,0:T(8,128)(2,1)} %all-gather.5.cloned.1.call-done, f32[1536]{0:T(1024)S(1)} %copy-done.31, f32[2048]{0:T(1024)S(1)} %copy-done.40), kind=kOutput, calls=%fused_computation.43 | convolution fusion | flops 10484121600 | bytes 18233344 | tf_op jit(solution)/shard_map/dot_general | solution.py:375
  614.8 8.1 %collective-permute-done.22 = bf16[96,2048]{1,0:T(8,128)(2,1)S(1)} collective-permute-done((bf16[96,2048]{1,0:T(8,128)(2,1)S(1)}, bf16[96,2048]{1,0:T(8,128)(2,1)S(1)}, u32[]{:S(2)}, u32[]{:S(2)}) %collective-permute-start.22) | collective-permute-done | bytes 393248 | tf_op jit(solution)/shard_map/ppermute | solution.py:471
  625.2 15.7 %collective-permute-done.23 = bf16[192,2048]{1,0:T(8,128)(2,1)S(1)} collective-permute-done((bf16[192,2048]{1,0:T(8,128)(2,1)S(1)}, bf16[192,2048]{1,0:T(8,128)(2,1)S(1)}, u32[]{:S(2)}, u32[]{:S(2)}) %collective-permute-start.23) | collective-permute-done | bytes 786464 | tf_op jit(solution)/shard_map/ppermute | solution.py:471
  651.6 12.3 %collective-permute-done.24 = bf16[192,2048]{1,0:T(8,128)(2,1)} collective-permute-done((bf16[192,2048]{1,0:T(8,128)(2,1)}, bf16[192,2048]{1,0:T(8,128)(2,1)}, u32[]{:S(2)}, u32[]{:S(2)}) %collective-permute-start.24) | collective-permute-done | bytes 786464 | tf_op jit(solution)/shard_map/ppermute | solution.py:471
  669.0 20.5 %collective-permute-done.31 = bf16[192,3072]{1,0:T(8,128)(2,1)} collective-permute-done((bf16[192,3072]{1,0:T(8,128)(2,1)}, bf16[192,3072]{1,0:T(8,128)(2,1)}, u32[]{:S(2)}, u32[]{:S(2)}) %collective-permute-start.31) | collective-permute-done | bytes 1179680 | tf_op jit(solution)/shard_map/ppermute | solution.py:471
  693.6 9.1 %collective-permute-done.29 = bf16[192,2048]{1,0:T(8,128)(2,1)S(1)} collective-permute-done((bf16[192,2048]{1,0:T(8,128)(2,1)S(1)}, bf16[192,2048]{1,0:T(8,128)(2,1)S(1)}, u32[]{:S(2)}, u32[]{:S(2)}) %collective-permute-start.29) | collective-permute-done | bytes 786464 | tf_op jit(solution)/shard_map/ppermute | solution.py:471
  710.3 5.9 fusion.13
  (287 shorter events, 113.9 us)
Async XLA Ops:
  7.2 51.5 %all-gather.5.cloned.1.call-start = ((), (), s32[]{:S(2)}) async-start(), calls=%async_computation.4 | async-start | bytes 7864320 | tf_op jit(solution)/shard_map/all_gather | solution.py:528
  7.9 180.6 %all-gather.7.cloned.1.call-start = ((), (), s32[]{:S(2)}) async-start(), calls=%async_computation.5 | async-start | bytes 7864320 | tf_op jit(solution)/shard_map/all_gather | solution.py:532
  11.7 20.6 %collective-permute-start = (bf16[192,2048]{1,0:T(8,128)(2,1)S(1)}, bf16[192,2048]{1,0:T(8,128)(2,1)S(1)}, u32[]{:S(2)}, u32[]{:S(2)}) collective-permute-start(bf16[192,2048]{1,0:T(8,128)(2,1)S(1)} %concatenate.36), channel_id=1, source_target_pairs={{0,8},{8,16},{16,24},{24,28},{28,20},{20,12},{12,4},{4,0},{1,9},{9... | collective-permute-start | bytes 2359304 | tf_op jit(solution)/shard_map/ppermute | solution.py:421
  14.8 19.3 %collective-permute-start.1 = (bf16[192,2048]{1,0:T(8,128)(2,1)S(1)}, bf16[192,2048]{1,0:T(8,128)(2,1)}, u32[]{:S(2)}, u32[]{:S(2)}) collective-permute-start(bf16[192,2048]{1,0:T(8,128)(2,1)S(1)} %concatenate.36), channel_id=1, source_target_pairs={{0,4},{8,0},{16,8},{24,16},{28,24},{20,28},{12,20},{4,12},{1,5},{9... | collective-permute-start | bytes 2359304 | tf_op jit(solution)/shard_map/ppermute | solution.py:422
  32.2 27.8 %collective-permute-start.2 = (bf16[192,2048]{1,0:T(8,128)(2,1)S(1)}, bf16[192,2048]{1,0:T(8,128)(2,1)}, u32[]{:S(2)}, u32[]{:S(2)}) collective-permute-start(bf16[192,2048]{1,0:T(8,128)(2,1)S(1)} %collective-permute-done), channel_id=1, source_target_pairs={{0,8},{8,16},{16,24},{24,28},{28,20},{20,12},{12,4},{4,0},{1,9},{9... | collective-permute-start | bytes 2359304 | tf_op jit(solution)/shard_map/ppermute | solution.py:421
  34.0 27.6 %collective-permute-start.3 = (bf16[192,2048]{1,0:T(8,128)(2,1)}, bf16[192,2048]{1,0:T(8,128)(2,1)}, u32[]{:S(2)}, u32[]{:S(2)}) collective-permute-start(bf16[192,2048]{1,0:T(8,128)(2,1)} %collective-permute-done.1), channel_id=1, source_target_pairs={{0,4},{8,0},{16,8},{24,16},{28,24},{20,28},{12,20},{4,12},{1,5},{9... | collective-permute-start | bytes 2359304 | tf_op jit(solution)/shard_map/ppermute | solution.py:422
  58.8 193.0 %reduce-scatter.5.cloned.1.call-start = ((), (), s32[]{:S(2)}) async-start(), calls=%async_computation.6 | async-start | bytes 7864320 | tf_op jit(solution)/shard_map/reduce_scatter | solution.py:551
  60.1 20.0 %collective-permute-start.4 = (bf16[192,2048]{1,0:T(8,128)(2,1)}, bf16[192,2048]{1,0:T(8,128)(2,1)S(1)}, u32[]{:S(2)}, u32[]{:S(2)}) collective-permute-start(bf16[192,2048]{1,0:T(8,128)(2,1)} %collective-permute-done.2), channel_id=1, source_target_pairs={{0,8},{8,16},{16,24},{24,28},{28,20},{20,12},{12,4},{4,0},{1,9},{9... | collective-permute-start | bytes 2359304 | tf_op jit(solution)/shard_map/ppermute | solution.py:421
  61.6 20.0 %collective-permute-start.5 = (bf16[192,2048]{1,0:T(8,128)(2,1)}, bf16[192,2048]{1,0:T(8,128)(2,1)S(1)}, u32[]{:S(2)}, u32[]{:S(2)}) collective-permute-start(bf16[192,2048]{1,0:T(8,128)(2,1)} %collective-permute-done.3), channel_id=1, source_target_pairs={{0,4},{8,0},{16,8},{24,16},{28,24},{20,28},{12,20},{4,12},{1,5},{9... | collective-permute-start | bytes 2359304 | tf_op jit(solution)/shard_map/ppermute | solution.py:422
  92.0 26.4 %collective-permute-start.8 = (bf16[192,3072]{1,0:T(8,128)(2,1)S(1)}, bf16[192,3072]{1,0:T(8,128)(2,1)S(1)}, u32[]{:S(2)}, u32[]{:S(2)}) collective-permute-start(bf16[192,3072]{1,0:T(8,128)(2,1)S(1)} %pad_maximum_fusion.4), channel_id=1, source_target_pairs={{0,8},{8,16},{16,24},{24,28},{28,20},{20,12},{12,4},{4,0},{1,9},{9... | collective-permute-start | bytes 3538952 | tf_op jit(solution)/shard_map/ppermute | solution.py:421
  93.6 26.2 %collective-permute-start.9 = (bf16[192,3072]{1,0:T(8,128)(2,1)S(1)}, bf16[192,3072]{1,0:T(8,128)(2,1)}, u32[]{:S(2)}, u32[]{:S(2)}) collective-permute-start(bf16[192,3072]{1,0:T(8,128)(2,1)S(1)} %pad_maximum_fusion.4), channel_id=1, source_target_pairs={{0,4},{8,0},{16,8},{24,16},{28,24},{20,28},{12,20},{4,12},{1,5},{9... | collective-permute-start | bytes 3538952 | tf_op jit(solution)/shard_map/ppermute | solution.py:422
  119.7 31.9 %collective-permute-start.10 = (bf16[192,3072]{1,0:T(8,128)(2,1)S(1)}, bf16[192,3072]{1,0:T(8,128)(2,1)}, u32[]{:S(2)}, u32[]{:S(2)}) collective-permute-start(bf16[192,3072]{1,0:T(8,128)(2,1)S(1)} %collective-permute-done.8), channel_id=1, source_target_pairs={{0,8},{8,16},{16,24},{24,28},{28,20},{20,12},{12,4},{4,0},{1,9},{9... | collective-permute-start | bytes 3538952 | tf_op jit(solution)/shard_map/ppermute | solution.py:421
  121.2 30.4 %collective-permute-start.11 = (bf16[192,3072]{1,0:T(8,128)(2,1)}, bf16[192,3072]{1,0:T(8,128)(2,1)}, u32[]{:S(2)}, u32[]{:S(2)}) collective-permute-start(bf16[192,3072]{1,0:T(8,128)(2,1)} %collective-permute-done.9), channel_id=1, source_target_pairs={{0,4},{8,0},{16,8},{24,16},{28,24},{20,28},{12,20},{4,12},{1,5},{9... | collective-permute-start | bytes 3538952 | tf_op jit(solution)/shard_map/ppermute | solution.py:422
  151.7 36.9 %collective-permute-start.12 = (bf16[192,3072]{1,0:T(8,128)(2,1)}, bf16[192,3072]{1,0:T(8,128)(2,1)S(1)}, u32[]{:S(2)}, u32[]{:S(2)}) collective-permute-start(bf16[192,3072]{1,0:T(8,128)(2,1)} %collective-permute-done.10), channel_id=1, source_target_pairs={{0,8},{8,16},{16,24},{24,28},{28,20},{20,12},{12,4},{4,0},{1,9},{9... | collective-permute-start | bytes 3538952 | tf_op jit(solution)/shard_map/ppermute | solution.py:421
  153.2 35.4 %collective-permute-start.13 = (bf16[192,3072]{1,0:T(8,128)(2,1)}, bf16[192,3072]{1,0:T(8,128)(2,1)}, u32[]{:S(2)}, u32[]{:S(2)}) collective-permute-start(bf16[192,3072]{1,0:T(8,128)(2,1)} %collective-permute-done.11), channel_id=1, source_target_pairs={{0,4},{8,0},{16,8},{24,16},{28,24},{20,28},{12,20},{4,12},{1,5},{9... | collective-permute-start | bytes 3538952 | tf_op jit(solution)/shard_map/ppermute | solution.py:422
  196.9 105.3 %all-gather.9.cloned.1.call-start = ((), (), s32[]{:S(2)}) async-start(), calls=%async_computation.7 | async-start | bytes 7864320 | tf_op jit(solution)/shard_map/all_gather | solution.py:558
  255.7 155.8 %reduce-scatter.7.cloned.1.call-start = ((), (), s32[]{:S(2)}) async-start(), calls=%async_computation.8 | async-start | bytes 7864320 | tf_op jit(solution)/shard_map/reduce_scatter | solution.py:569
  353.0 112.1 %all-gather.11.cloned.1.call-start = ((), (), s32[]{:S(2)}) async-start(), calls=%async_computation.9 | async-start | bytes 7864320 | tf_op jit(solution)/shard_map/all_gather | solution.py:581
  384.4 29.1 %collective-permute-start.16 = (bf16[96,3072]{1,0:T(8,128)(2,1)}, bf16[96,3072]{1,0:T(8,128)(2,1)}, u32[]{:S(2)}, u32[]{:S(2)}) collective-permute-start(bf16[96,3072]{1,0:T(8,128)(2,1)} %get-tuple-element.137), channel_id=1, source_target_pairs={{0,8},{8,16},{16,24},{24,28},{28,20},{20,12},{12,4},{4,0},{1,9},{9... | collective-permute-start | bytes 1769480 | tf_op jit(solution)/shard_map/ppermute | solution.py:471
  385.9 27.6 %collective-permute-start.17 = (bf16[96,3072]{1,0:T(8,128)(2,1)}, bf16[96,3072]{1,0:T(8,128)(2,1)}, u32[]{:S(2)}, u32[]{:S(2)}) collective-permute-start(bf16[96,3072]{1,0:T(8,128)(2,1)} %get-tuple-element.136), channel_id=1, source_target_pairs={{0,4},{8,0},{16,8},{24,16},{28,24},{20,28},{12,20},{4,12},{1,5},{9... | collective-permute-start | bytes 1769480 | tf_op jit(solution)/shard_map/ppermute | solution.py:471
  418.5 289.5 %reduce-scatter.11.cloned.1.call-start = ((), (), s32[]{:S(2)}) async-start(), calls=%async_computation.11 | async-start | bytes 7864320 | tf_op jit(solution)/shard_map/reduce_scatter | solution.py:594
  423.4 54.1 %collective-permute-start.18 = (bf16[192,3072]{1,0:T(8,128)(2,1)}, bf16[192,3072]{1,0:T(8,128)(2,1)}, u32[]{:S(2)}, u32[]{:S(2)}) collective-permute-start(bf16[192,3072]{1,0:T(8,128)(2,1)} %pad_maximum_fusion.5), channel_id=1, source_target_pairs={{0,8},{8,16},{16,24},{24,28},{28,20},{20,12},{12,4},{4,0},{1,9},{9... | collective-permute-start | bytes 3538952 | tf_op jit(solution)/shard_map/ppermute | solution.py:471
  426.0 51.5 %collective-permute-start.19 = (bf16[192,3072]{1,0:T(8,128)(2,1)}, bf16[192,3072]{1,0:T(8,128)(2,1)}, u32[]{:S(2)}, u32[]{:S(2)}) collective-permute-start(bf16[192,3072]{1,0:T(8,128)(2,1)} %pad_maximum_fusion.6), channel_id=1, source_target_pairs={{0,4},{8,0},{16,8},{24,16},{28,24},{20,28},{12,20},{4,12},{1,5},{9... | collective-permute-start | bytes 3538952 | tf_op jit(solution)/shard_map/ppermute | solution.py:471
  481.9 83.3 %collective-permute-start.20 = (bf16[192,3072]{1,0:T(8,128)(2,1)}, bf16[192,3072]{1,0:T(8,128)(2,1)}, u32[]{:S(2)}, u32[]{:S(2)}) collective-permute-start(bf16[192,3072]{1,0:T(8,128)(2,1)} %get-tuple-element.133), channel_id=1, source_target_pairs={{0,8},{8,16},{16,24},{24,28},{28,20},{20,12},{12,4},{4,0},{1,9},{9... | collective-permute-start | bytes 3538952 | tf_op jit(solution)/shard_map/ppermute | solution.py:471
  483.3 81.8 %collective-permute-start.21 = (bf16[192,3072]{1,0:T(8,128)(2,1)}, bf16[192,3072]{1,0:T(8,128)(2,1)}, u32[]{:S(2)}, u32[]{:S(2)}) collective-permute-start(bf16[192,3072]{1,0:T(8,128)(2,1)} %get-tuple-element.132), channel_id=1, source_target_pairs={{0,4},{8,0},{16,8},{24,16},{28,24},{20,28},{12,20},{4,12},{1,5},{9... | collective-permute-start | bytes 3538952 | tf_op jit(solution)/shard_map/ppermute | solution.py:471
  582.2 128.1 %reduce-scatter.9.cloned.1.call-start = ((), (), s32[]{:S(2)}) async-start(), calls=%async_computation.10 | async-start | bytes 7864320 | tf_op jit(solution)/shard_map/reduce_scatter | solution.py:582
  643.1 20.8 %collective-permute-start.24 = (bf16[192,2048]{1,0:T(8,128)(2,1)}, bf16[192,2048]{1,0:T(8,128)(2,1)}, u32[]{:S(2)}, u32[]{:S(2)}) collective-permute-start(bf16[192,2048]{1,0:T(8,128)(2,1)} %get-tuple-element.140), channel_id=1, source_target_pairs={{0,8},{8,16},{16,24},{24,28},{28,20},{20,12},{12,4},{4,0},{1,9},{9... | collective-permute-start | bytes 2359304 | tf_op jit(solution)/shard_map/ppermute | solution.py:471
  643.4 20.8 %collective-permute-start.28 = (bf16[192,2048]{1,0:T(8,128)(2,1)}, bf16[192,2048]{1,0:T(8,128)(2,1)}, u32[]{:S(2)}, u32[]{:S(2)}) collective-permute-start(bf16[192,2048]{1,0:T(8,128)(2,1)} %get-tuple-element.141), channel_id=1, source_target_pairs={{0,4},{8,0},{16,8},{24,16},{28,24},{20,28},{12,20},{4,12},{1,5},{9... | collective-permute-start | bytes 2359304 | tf_op jit(solution)/shard_map/ppermute | solution.py:471
  649.3 40.2 %collective-permute-start.31 = (bf16[192,3072]{1,0:T(8,128)(2,1)}, bf16[192,3072]{1,0:T(8,128)(2,1)}, u32[]{:S(2)}, u32[]{:S(2)}) collective-permute-start(bf16[192,3072]{1,0:T(8,128)(2,1)} %get-tuple-element.131), channel_id=1, source_target_pairs={{0,4},{8,0},{16,8},{24,16},{28,24},{20,28},{12,20},{4,12},{1,5},{9... | collective-permute-start | bytes 3538952 | tf_op jit(solution)/shard_map/ppermute | solution.py:471
  650.8 38.7 %collective-permute-start.30 = (bf16[192,3072]{1,0:T(8,128)(2,1)}, bf16[192,3072]{1,0:T(8,128)(2,1)}, u32[]{:S(2)}, u32[]{:S(2)}) collective-permute-start(bf16[192,3072]{1,0:T(8,128)(2,1)} %get-tuple-element.130), channel_id=1, source_target_pairs={{0,8},{8,16},{16,24},{24,28},{28,20},{20,12},{12,4},{4,0},{1,9},{9... | collective-permute-start | bytes 3538952 | tf_op jit(solution)/shard_map/ppermute | solution.py:471
  666.7 36.1 %collective-permute-start.29 = (bf16[192,2048]{1,0:T(8,128)(2,1)S(1)}, bf16[192,2048]{1,0:T(8,128)(2,1)S(1)}, u32[]{:S(2)}, u32[]{:S(2)}) collective-permute-start(bf16[192,2048]{1,0:T(8,128)(2,1)S(1)} %get-tuple-element.139), channel_id=1, source_target_pairs={{0,4},{8,0},{16,8},{24,16},{28,24},{20,28},{12,20},{4,12},{1,5},{9... | collective-permute-start | bytes 2359304 | tf_op jit(solution)/shard_map/ppermute | solution.py:471
  668.4 34.3 %collective-permute-start.25 = (bf16[192,2048]{1,0:T(8,128)(2,1)S(1)}, bf16[192,2048]{1,0:T(8,128)(2,1)S(1)}, u32[]{:S(2)}, u32[]{:S(2)}) collective-permute-start(bf16[192,2048]{1,0:T(8,128)(2,1)S(1)} %get-tuple-element.138), channel_id=1, source_target_pairs={{0,8},{8,16},{16,24},{24,28},{28,20},{20,12},{12,4},{4,0},{1,9},{9... | collective-permute-start | bytes 2359304 | tf_op jit(solution)/shard_map/ppermute | solution.py:471
  (66 other events, 1232.3 us)
Sparse Core Ops, SparseCore 0:
  9.6 49.0 all-gather.4
  60.3 46.3 all-gather.6
  197.1 54.6 reduce-scatter.4
  255.8 46.3 all-gather.8
  353.1 58.3 reduce-scatter.6
  418.6 46.3 all-gather.10
  582.3 54.4 reduce-scatter.10
  639.4 58.3 reduce-scatter.8

commit v3 on v2

--- a/solution.py
+++ b/solution.py
@@ -38,20 +38,21 @@
     return beta, inv_sq
 
 
-def prep_kernel(heads, q_ref, k_ref, u_ref, r_ref, near_ref, q0_ref, kp_ref, inv_ref, t_ref):
+def prep_kernel(heads, chunks, table_ref, *refs):
+    q_refs, k_refs, u_refs, r_refs = (refs[n * chunks : (n + 1) * chunks] for n in range(4))
+    near_ref, q0_ref, kp_ref, inv_ref, t_ref = refs[4 * chunks :]
     rows, cols = iotas()
     strict = rows > cols
     lower = rows >= cols
     diff = rows ^ cols
     eye = jnp.where(rows == cols, 1.0, 0.0).astype(f32)
     eye_b = eye.astype(bf16)
-    chunks = q_ref.shape[0] // BLOCK
     items = [(c, h) for c in range(chunks) for h in range(heads)]
     state = []
     for c, h in items:
-        rs, cs = pl.ds(c * BLOCK, BLOCK), pl.ds(h * BLOCK, BLOCK)
-        q, k, u = q_ref[rs, cs], k_ref[rs, cs], u_ref[rs, cs]
-        beta, inv_sq = strengths(u, r_ref[rs, h : h + 1].astype(f32))
+        cs = pl.ds(h * BLOCK, BLOCK)
+        q, k, u = q_refs[c][:, cs], k_refs[c][:, cs], u_refs[c][:, cs]
+        beta, inv_sq = strengths(u, r_refs[c][:, h : h + 1].astype(f32))
         bp = beta * inv_sq
         big = mm_rt(jnp.concatenate([u, q], axis=0), jnp.concatenate([u, k], axis=0))
         gram = big[:BLOCK, :BLOCK]
@@ -86,7 +87,7 @@
 
 
 def fwd_kernel(
-    heads, depth, scale, first_ref, q0_ref, near_ref, kp_ref, v_ref, o_ref, linv_ref, e_ref, cur_ref, s_ref, m_ref, acc_ref
+    heads, depth, scale, first_ref, table_ref, slot_ref, q0_ref, near_ref, kp_ref, v_ref, o_ref, linv_ref, e_ref, cur_ref, s_ref, m_ref, acc_ref
 ):
     i = pl.program_id(0)
     first = first_ref[i]
@@ -119,7 +120,7 @@
         m_ref[h] = e0
         eb = e0.astype(bf16)
         e_ref[0, 0, h] = eb
-        v = v_ref[pl.ds(pl.multiple_of(i * BLOCK, BLOCK), BLOCK), h * BLOCK : (h + 1) * BLOCK]
+        v = v_ref[pl.ds(pl.multiple_of(table_ref[i] * BLOCK, BLOCK), BLOCK), h * BLOCK : (h + 1) * BLOCK]
         acc_ref[h] = mm(eb, v)
     for d in range(1, depth):
 
@@ -131,7 +132,7 @@
                 m_ref[h] = m_ref[h] + e
                 eb = e.astype(bf16)
                 e_ref[0, d, h] = eb
-                v = v_ref[pl.ds(pl.multiple_of(j * BLOCK, BLOCK), BLOCK), h * BLOCK : (h + 1) * BLOCK]
+                v = v_ref[pl.ds(pl.multiple_of(table_ref[j] * BLOCK, BLOCK), BLOCK), h * BLOCK : (h + 1) * BLOCK]
                 acc_ref[h] = acc_ref[h] + mm(eb, v)
 
     for h in range(heads):
@@ -141,11 +142,11 @@
         linv_ref[:, cs] = jnp.broadcast_to(linv, (BLOCK, BLOCK))
 
 
-def bwd_kernel(heads, depth, scale, last_ref, *refs):
+def bwd_kernel(heads, depth, scale, last_ref, table_ref, slot_ref, *refs):
     (do_ref, o_ref, linv_ref, q_ref, k_ref, v_ref, u_ref, r_ref, kp_ref, inv_ref, t_ref) = refs[:11]
     e_refs = refs[11 : 11 + depth]
     cur_refs = refs[11 + depth : 10 + 2 * depth]
-    out_ref, dop_ref, del_ref, g_ref, dv_ref, acc_ref = refs[10 + 2 * depth :]
+    out_ref, dop_ref, del_ref, g_ref, dv_ref, acc_ref = refs[-6:]
     j = pl.program_id(0)
     last = last_ref[j]
     rows, cols = iotas()
@@ -160,8 +161,9 @@
             rs = pl.ds(c * BLOCK, BLOCK)
             for h in range(heads):
                 cs = slice(h * BLOCK, (h + 1) * BLOCK)
-                dop = do_ref[rs, cs].astype(f32) * linv_ref[rs, cs]
-                delta = jnp.sum(dop * o_ref[rs, cs].astype(f32), axis=1, keepdims=True)
+                there = pl.ds(pl.multiple_of(slot_ref[c] * BLOCK, BLOCK), BLOCK)
+                dop = do_ref[there, cs].astype(f32) * linv_ref[rs, cs]
+                delta = jnp.sum(dop * o_ref[there, cs].astype(f32), axis=1, keepdims=True)
                 dop_ref[rs, cs] = dop.astype(bf16)
                 del_ref[rs, cs] = jnp.broadcast_to(delta, (BLOCK, BLOCK))
                 g_ref[c, h] = jnp.zeros((BLOCK, BLOCK), bf16)
@@ -237,51 +239,66 @@
     out_ref[:, 4 * width :] = dr_all.astype(bf16)
 
 
-def attention_prep(proj, heads):
-    total = proj.shape[0]
-    count = total // BLOCK
+def attention_prep(proj, table, heads):
+    count = table.shape[0]
     width = heads * BLOCK
     step = 2
-    wide = lambda col: pl.BlockSpec((step * BLOCK, width), lambda i: (i, col))
-    tile = lambda n: pl.BlockSpec((step, heads, BLOCK, n), lambda i: (i, 0, 0, 0))
+
+    def rows(c, n, col):
+        return pl.BlockSpec((BLOCK, n), lambda i, t: (t[i * step + c], col))
+
+    tile = lambda n: pl.BlockSpec((step, heads, BLOCK, n), lambda i, t: (i, 0, 0, 0))
     shape = lambda n, t: jax.ShapeDtypeStruct((count, heads, BLOCK, n), t)
+    spec = pltpu.PrefetchScalarGridSpec(
+        num_scalar_prefetch=1,
+        grid=(count // step,),
+        in_specs=[rows(c, width, col) for col in (0, 1, 3) for c in range(step)]
+        + [rows(c, BLOCK, 4 * heads) for c in range(step)],
+        out_specs=[
+            tile(BLOCK),
+            pl.BlockSpec((step * BLOCK, width), lambda i, t: (i, 0)),
+            tile(2 * BLOCK),
+            tile(BLOCK),
+            tile(2 * BLOCK),
+        ],
+    )
     return pl.pallas_call(
-        functools.partial(prep_kernel, heads),
-        grid=(count // step,),
-        in_specs=[wide(0), wide(1), wide(3), pl.BlockSpec((step * BLOCK, BLOCK), lambda i: (i, 4 * heads))],
-        out_specs=[tile(BLOCK), pl.BlockSpec((step * BLOCK, width), lambda i: (i, 0)), tile(2 * BLOCK), tile(BLOCK), tile(2 * BLOCK)],
+        functools.partial(prep_kernel, heads, step),
+        grid_spec=spec,
         out_shape=[
             shape(BLOCK, f32),
-            jax.ShapeDtypeStruct((total, width), bf16),
+            jax.ShapeDtypeStruct((count * BLOCK, width), bf16),
             shape(2 * BLOCK, bf16),
             shape(BLOCK, bf16),
             shape(2 * BLOCK, bf16),
         ],
-        cost_estimate=pl.CostEstimate(flops=count * heads * 22 * 2 * BLOCK**3 * 4, bytes_accessed=20 * total * width, transcendentals=0),
+        cost_estimate=pl.CostEstimate(
+            flops=count * heads * 45 * BLOCK**3, bytes_accessed=6 * count * BLOCK * width, transcendentals=0
+        ),
         name="attn_prep",
-    )(proj, proj, proj, proj)
-
-
-def attention_fwd(proj, prep, first, heads, depth):
+    )(table, *([proj] * (4 * step)))
+
+
+def attention_fwd(proj, prep, first, table, slot, heads):
     near, q0, kp, _, _ = prep
-    total = proj.shape[0]
-    count = total // BLOCK
+    count = table.shape[0]
+    depth = count
     width = heads * BLOCK
     scale = float(BLOCK) ** -0.5
     spec = pltpu.PrefetchScalarGridSpec(
-        num_scalar_prefetch=1,
+        num_scalar_prefetch=3,
         grid=(count,),
         in_specs=[
-            pl.BlockSpec((BLOCK, width), lambda i, f: (i, 0)),
-            pl.BlockSpec((1, heads, BLOCK, BLOCK), lambda i, f: (i, 0, 0, 0)),
-            pl.BlockSpec((count, heads, BLOCK, 2 * BLOCK), lambda i, f: (0, 0, 0, 0)),
-            pl.BlockSpec((total, width), lambda i, f: (0, 2)),
+            pl.BlockSpec((BLOCK, width), lambda i, f, t, w: (i, 0)),
+            pl.BlockSpec((1, heads, BLOCK, BLOCK), lambda i, f, t, w: (i, 0, 0, 0)),
+            pl.BlockSpec((count, heads, BLOCK, 2 * BLOCK), lambda i, f, t, w: (0, 0, 0, 0)),
+            pl.BlockSpec((proj.shape[0], width), lambda i, f, t, w: (0, 2)),
         ],
         out_specs=[
-            pl.BlockSpec((BLOCK, width), lambda i, f: (i, 0)),
-            pl.BlockSpec((BLOCK, width), lambda i, f: (i, 0)),
-            pl.BlockSpec((1, depth, heads, BLOCK, BLOCK), lambda i, f: (i, 0, 0, 0, 0)),
-            pl.BlockSpec((1, depth - 1, heads, BLOCK, BLOCK), lambda i, f: (i, 0, 0, 0, 0)),
+            pl.BlockSpec((BLOCK, width), lambda i, f, t, w: (w[i], 0)),
+            pl.BlockSpec((BLOCK, width), lambda i, f, t, w: (i, 0)),
+            pl.BlockSpec((1, depth, heads, BLOCK, BLOCK), lambda i, f, t, w: (i, 0, 0, 0, 0)),
+            pl.BlockSpec((1, depth - 1, heads, BLOCK, BLOCK), lambda i, f, t, w: (i, 0, 0, 0, 0)),
         ],
         scratch_shapes=[
             pltpu.VMEM((depth, heads, BLOCK, BLOCK), f32),
@@ -293,51 +310,61 @@
         functools.partial(fwd_kernel, heads, depth, scale),
         grid_spec=spec,
         out_shape=[
-            jax.ShapeDtypeStruct((total, width), bf16),
-            jax.ShapeDtypeStruct((total, width), f32),
+            jax.ShapeDtypeStruct((count * BLOCK, width), bf16),
+            jax.ShapeDtypeStruct((count * BLOCK, width), f32),
             jax.ShapeDtypeStruct((count, depth, heads, BLOCK, BLOCK), bf16),
             jax.ShapeDtypeStruct((count, depth - 1, heads, BLOCK, BLOCK), bf16),
         ],
-        cost_estimate=pl.CostEstimate(flops=count * heads * 24 * 2 * BLOCK**3 * 4, bytes_accessed=20 * total * width, transcendentals=0),
+        cost_estimate=pl.CostEstimate(
+            flops=count * heads * 48 * BLOCK**3, bytes_accessed=6 * count * BLOCK * width, transcendentals=0
+        ),
         name="attn_fwd",
-    )(first, q0, near, kp, proj)
-
-
-def attention_bwd(proj, prep, saved, d_mixed, last, heads, depth):
+    )(first, table, slot, q0, near, kp, proj)
+
+
+def attention_bwd(proj, prep, saved, d_mixed, last, table, slot, heads, filled):
     _, _, kp, inv, t_all = prep
     mixed, linv, e_all, cur_all = saved
-    total = proj.shape[0]
-    count = total // BLOCK
+    count = table.shape[0]
+    depth = count
+    total = count * BLOCK
     width = heads * BLOCK
     scale = float(BLOCK) ** -0.5
-    full = lambda: pl.BlockSpec((total, width), lambda j, f: (0, 0))
-    wide = lambda col: pl.BlockSpec((BLOCK, width), lambda j, f: (j, col))
-    tile = lambda n: pl.BlockSpec((1, heads, BLOCK, n), lambda j, f: (j, 0, 0, 0))
+    full = lambda: pl.BlockSpec((total, width), lambda j, f, t, w: (0, 0))
+    wide = lambda col: pl.BlockSpec((BLOCK, width), lambda j, f, t, w: (t[j], col))
+    tile = lambda n: pl.BlockSpec((1, heads, BLOCK, n), lambda j, f, t, w: (j, 0, 0, 0))
 
     def diagonal(d, slot):
         return pl.BlockSpec(
-            (1, 1, heads, BLOCK, BLOCK), lambda j, f: (jnp.minimum(j + d, count - 1), slot, 0, 0, 0)
+            (1, 1, heads, BLOCK, BLOCK), lambda j, f, t, w: (jnp.minimum(j + d, count - 1), slot, 0, 0, 0)
         )
 
+    in_specs = [
+        full(),
+        full(),
+        full(),
+        wide(0),
+        wide(1),
+        wide(2),
+        wide(3),
+        pl.BlockSpec((BLOCK, BLOCK), lambda j, f, t, w: (t[j], 4 * heads)),
+        tile(2 * BLOCK),
+        tile(BLOCK),
+        tile(2 * BLOCK),
+    ]
+    in_specs += [diagonal(d, d) for d in range(depth)] + [diagonal(d, d - 1) for d in range(1, depth)]
+    operands = [last, table, slot, d_mixed, mixed, linv, proj, proj, proj, proj, proj, kp, inv, t_all]
+    operands += [e_all] * depth + [cur_all] * (depth - 1)
+    aliases = {}
+    if filled is not None:
+        aliases = {len(operands): 0}
+        in_specs.append(pl.BlockSpec(memory_space=pl.ANY))
+        operands.append(filled)
     spec = pltpu.PrefetchScalarGridSpec(
-        num_scalar_prefetch=1,
+        num_scalar_prefetch=3,
         grid=(count,),
-        in_specs=[
-            full(),
-            full(),
-            full(),
-            wide(0),
-            wide(1),
-            wide(2),
-            wide(3),
-            pl.BlockSpec((BLOCK, BLOCK), lambda j, f: (j, 4 * heads)),
-            tile(2 * BLOCK),
-            tile(BLOCK),
-            tile(2 * BLOCK),
-        ]
-        + [diagonal(d, d) for d in range(depth)]
-        + [diagonal(d, d - 1) for d in range(1, depth)],
-        out_specs=pl.BlockSpec((BLOCK, 4 * width + BLOCK), lambda j, f: (j, 0)),
+        in_specs=in_specs,
+        out_specs=pl.BlockSpec((BLOCK, 4 * width + BLOCK), lambda j, f, t, w: (t[j], 0)),
         scratch_shapes=[
             pltpu.VMEM((total, width), bf16),
             pltpu.VMEM((total, width), f32),
@@ -349,26 +376,137 @@
     return pl.pallas_call(
         functools.partial(bwd_kernel, heads, depth, scale),
         grid_spec=spec,
-        out_shape=jax.ShapeDtypeStruct((total, 4 * width + BLOCK), bf16),
-        cost_estimate=pl.CostEstimate(flops=count * heads * 60 * 2 * BLOCK**3 * 4, bytes_accessed=40 * total * width, transcendentals=0),
+        out_shape=jax.ShapeDtypeStruct((proj.shape[0], 4 * width + BLOCK), bf16),
+        input_output_aliases=aliases,
+        cost_estimate=pl.CostEstimate(
+            flops=count * heads * 120 * BLOCK**3, bytes_accessed=8 * total * width, transcendentals=0
+        ),
         name="attn_bwd",
-    )(last, d_mixed, mixed, linv, proj, proj, proj, proj, proj, kp, inv, t_all, *([e_all] * depth), *([cur_all] * (depth - 1)))
-
-
-def block_tables(packing, begins):
-    bins, bin_rows = packing.shape
-    per_bin = bin_rows // BLOCK
-    place = packing[:, ::BLOCK].reshape(-1) // BLOCK
-    start = begins[:, ::BLOCK] // BLOCK + jnp.arange(bins, dtype=jnp.int32)[:, None] * per_bin
-    start = start.reshape(-1)
-    count = bins * per_bin
-    slots = jnp.arange(count, dtype=jnp.int32)
-    onehot = place[:, None] == slots[None, :]
-    start_place = jnp.sum(jnp.where(start[:, None] == slots[None, :], place[None, :], 0), axis=1)
-    first = jnp.sum(jnp.where(onehot, start_place[:, None], 0), axis=0).astype(jnp.int32)
-    member = first[None, :] == first[:, None]
-    last = jnp.max(jnp.where(member, slots[None, :], 0), axis=1).astype(jnp.int32)
-    return first, last, per_bin
+    )(*operands)
+
+
+def gather_kernel(group, table_ref, *refs):
+    outs = refs[-(len(refs) // (group + 1)) :]
+    for m, dst in enumerate(outs):
+        for c in range(group):
+            dst[c * BLOCK : (c + 1) * BLOCK, :] = refs[m * group + c][...]
+
+
+def gather_blocks(x, tables, group):
+    streams, count = tables.shape
+    cols = x.shape[1]
+
+    def source(m, c):
+        return pl.BlockSpec((BLOCK, cols), lambda i, t: (t[m * count + i * group + c], 0))
+
+    spec = pltpu.PrefetchScalarGridSpec(
+        num_scalar_prefetch=1,
+        grid=(count // group,),
+        in_specs=[source(m, c) for m in range(streams) for c in range(group)],
+        out_specs=[pl.BlockSpec((group * BLOCK, cols), lambda i, t: (i, 0))] * streams,
+    )
+    return pl.pallas_call(
+        functools.partial(gather_kernel, group),
+        grid_spec=spec,
+        out_shape=[jax.ShapeDtypeStruct((count * BLOCK, cols), x.dtype)] * streams,
+        cost_estimate=pl.CostEstimate(flops=0, bytes_accessed=4 * streams * count * BLOCK * cols, transcendentals=0),
+        name="gather_blocks",
+    )(tables.reshape(-1), *([x] * (group * streams)))
+
+
+def pick_kernel(bounds, table_ref, *refs):
+    at = table_ref[pl.program_id(0)]
+    for n, (low, high) in enumerate(bounds):
+
+        @pl.when((at >= low) & (at < high))
+        def _():
+            refs[-1][...] = refs[n][...]
+
+
+def pick_blocks(parts, table):
+    cols = parts[0].shape[1]
+    bounds, low = [], 0
+    for part in parts:
+        bounds.append((low, low + part.shape[0] // BLOCK))
+        low = bounds[-1][1]
+
+    def source(low, high):
+        return pl.BlockSpec((BLOCK, cols), lambda i, t: (jnp.clip(t[i] - low, 0, high - low - 1), 0))
+
+    spec = pltpu.PrefetchScalarGridSpec(
+        num_scalar_prefetch=1,
+        grid=(table.shape[0],),
+        in_specs=[source(*bound) for bound in bounds],
+        out_specs=pl.BlockSpec((BLOCK, cols), lambda i, t: (i, 0)),
+    )
+    return pl.pallas_call(
+        functools.partial(pick_kernel, bounds),
+        grid_spec=spec,
+        out_shape=jax.ShapeDtypeStruct((table.shape[0] * BLOCK, cols), parts[0].dtype),
+        cost_estimate=pl.CostEstimate(flops=0, bytes_accessed=4 * table.shape[0] * BLOCK * cols, transcendentals=0),
+        name="pick_blocks",
+    )(table, *parts)
+
+
+def place_kernel(count, rows, spot_ref, *refs):
+    pieces, out, bufs, sem_in, sem_out = refs[:count], refs[count], refs[count + 1], refs[count + 2], refs[count + 3]
+    loads = [pltpu.make_async_copy(pieces[n], bufs.at[n], sem_in.at[n]) for n in range(count)]
+    for load in loads:
+        load.start()
+    stores = []
+    for n in range(count):
+        loads[n].wait()
+        to = out.at[pl.ds(pl.multiple_of(spot_ref[n] * rows, rows), rows), :]
+        stores.append(pltpu.make_async_copy(bufs.at[n], to, sem_out.at[n]))
+        stores[n].start()
+    for store in stores:
+        store.wait()
+
+
+def place_pieces(pieces, spots, count):
+    rows, cols = pieces[0].shape
+    held = len(pieces)
+    dtype = pieces[0].dtype
+    spec = pltpu.PrefetchScalarGridSpec(
+        num_scalar_prefetch=1,
+        grid=(1,),
+        in_specs=[pl.BlockSpec(memory_space=pl.ANY)] * held,
+        out_specs=pl.BlockSpec(memory_space=pl.ANY),
+        scratch_shapes=[
+            pltpu.VMEM((held, rows, cols), dtype),
+            pltpu.SemaphoreType.DMA((held,)),
+            pltpu.SemaphoreType.DMA((held,)),
+        ],
+    )
+    where = jnp.concatenate([jnp.reshape(spot, (1,)) for spot in spots]).astype(jnp.int32)
+    return pl.pallas_call(
+        functools.partial(place_kernel, held, rows),
+        grid_spec=spec,
+        out_shape=jax.ShapeDtypeStruct((count * rows, cols), dtype),
+        cost_estimate=pl.CostEstimate(flops=0, bytes_accessed=4 * held * rows * cols, transcendentals=0),
+        name="place_pieces",
+    )(where, *pieces)
+
+
+def open_kernel(spot_ref, x_ref, out_ref):
+    out_ref[...] = x_ref[...]
+
+
+def open_buffer(x, spot, count):
+    rows, cols = x.shape
+    spec = pltpu.PrefetchScalarGridSpec(
+        num_scalar_prefetch=1,
+        grid=(2,),
+        in_specs=[pl.BlockSpec((rows // 2, cols), lambda i, t: (i, 0))],
+        out_specs=pl.BlockSpec((rows // 2, cols), lambda i, t: (2 * t[0] + i, 0)),
+    )
+    return pl.pallas_call(
+        open_kernel,
+        grid_spec=spec,
+        out_shape=jax.ShapeDtypeStruct((count * rows, cols), x.dtype),
+        cost_estimate=pl.CostEstimate(flops=0, bytes_accessed=4 * rows * cols, transcendentals=0),
+        name="open_buffer",
+    )(jnp.reshape(spot, (1,)).astype(jnp.int32), x)
 
 
 def rows_contract(a, b):
@@ -396,18 +534,21 @@
 def ring_tables(axis):
     count = lax.axis_size(axis)
     order = ring_order(count)
-    place = [order.index(i) for i in range(count)]
     right = [(order[p], order[(p + 1) % count]) for p in range(count)]
     left = [(order[p], order[(p - 1) % count]) for p in range(count)]
-    spot = jnp.asarray(place, jnp.int32)[lax.axis_index(axis)]
-    owners = jnp.asarray(order, jnp.int32)
-    owner = lambda shift: owners[(spot + shift) % count]
+    me = lax.axis_index(axis)
+    spot = jnp.where(me % 2 == 0, me // 2, count - 1 - me // 2)
+
+    def owner(shift):
+        at = (spot + shift + count) % count
+        return jnp.where(at < count // 2, 2 * at, 2 * (count - 1 - at) + 1)
+
     return count, right, left, owner
 
 
 class RingGather:
-    def __init__(self, x, axis):
-        self.axis, self.x = axis, x
+    def __init__(self, x, axis, whole=False):
+        self.axis, self.x, self.whole = axis, x, whole
         self.count, self.right, self.left, self.owner = ring_tables(axis)
         self.moving = (x, x)
         self.hops = []
@@ -434,10 +575,16 @@
             self.hop()
         rows = self.x.shape[0]
         put = lax.dynamic_update_slice_in_dim
-        out = put(jnp.zeros((self.count * rows, self.x.shape[1]), self.x.dtype), self.x, self.owner(0) * rows, 0)
+        pieces, spots = [self.x], [self.owner(0)]
         for s, (from_left, from_right) in enumerate(self.hops[:-1], 1):
-            out = put(out, from_left, self.owner(-s) * rows, 0)
-            out = put(out, from_right, self.owner(s) * rows, 0)
+            pieces += [from_left, from_right]
+            spots += [self.owner(-s), self.owner(s)]
+        if self.whole:
+            out = place_pieces(pieces, spots, self.count)
+        else:
+            out = open_buffer(self.x, spots[0], self.count)
+            for piece, spot in zip(pieces[1:], spots[1:]):
+                out = put(out, piece, spot * rows, 0)
         far = self.owner(self.count // 2) * rows
         out = put(out, self.hops[-1][0], far, 0)
         return put(out, self.hops[-1][1], far + rows // 2, 0)
@@ -447,7 +594,7 @@
     def __init__(self, parts, axis):
         self.axis, self.parts = axis, parts
         self.count, self.right, self.left, self.owner = ring_tables(axis)
-        self.rows = parts.shape[0] // self.count
+        self.rows = parts[0].shape[0] // self.count
         self.top = self.count // 2
         self.done = 0
         half = self.rows // 2
@@ -455,7 +602,8 @@
 
     def piece(self, shift, start=0, size=None):
         size = self.rows if size is None else size
-        return lax.dynamic_slice_in_dim(self.parts, self.owner(shift) * self.rows + start, size, 0)
+        at = self.owner(shift) * self.rows + start
+        return jnp.concatenate([lax.dynamic_slice_in_dim(part, at, size, 0) for part in self.parts], axis=1)
 
     def hop(self):
         to_right, to_left = self.moving
@@ -494,8 +642,31 @@
     return total
 
 
-def after(x, *others):
-    return lax.optimization_barrier((x,) + others)[0]
+SLOTS = (0, 2, 1, 3)
+
+
+def across(x):
+    return lax.ppermute(x, "tp", [(i, i ^ 2) for i in range(4)])
+
+
+def beside(x):
+    return lax.ppermute(x, "tp", [(i, i ^ 1) for i in range(4)])
+
+
+def share(rows):
+    size = rows.shape[0] // 4
+    other = beside(rows[2 * size :])
+    pair = rows[: 2 * size].astype(f32) + other.astype(f32)
+    return pair[:size], across(pair[size:].astype(bf16))
+
+
+def spread(x):
+    pair = jnp.concatenate([x, across(x)], axis=0)
+    return jnp.concatenate([pair, beside(pair)], axis=0)
+
+
+def together(*values):
+    return lax.optimization_barrier(values)
 
 
 def local(
@@ -515,94 +686,211 @@
     pack_index,
     seq_start,
 ):
-    first, last, depth = block_tables(pack_index[0], seq_start[0])
+    packing, begins = pack_index[0], seq_start[0]
+    bins, bin_rows = packing.shape
+    per_bin = bin_rows // BLOCK
+    streams = range(bins)
     width = w_query.shape[1]
     heads = w_beta.shape[1]
     hidden_width = w_gate.shape[1]
     shard = w_query.shape[0]
+    ranks = 4
+    assert lax.axis_size("tp") == ranks
+    half = bin_rows // ranks
+    per_half = half // BLOCK
+    me = lax.axis_index("tp")
+
+    given = packing[:, ::BLOCK] // BLOCK
+    per_own = bins * per_half
+    table = given
+    first = begins[:, ::BLOCK] // BLOCK
+    spots = jnp.arange(per_bin, dtype=jnp.int32)
+    last = jnp.max(jnp.where(first[:, :, None] == first[:, None, :], spots[None, None, :], 0), axis=2)
+    away = me ^ (spots // per_half)
+    slot = ((away // 2) + 2 * (away % 2)) * per_half + spots % per_half
+    places = jnp.arange(bins, dtype=jnp.int32)[:, None] * per_bin + slot[None, :]
+    blocks = jnp.arange(bins * per_bin, dtype=jnp.int32)
+    inverse = jnp.sum(jnp.where(given.reshape(-1)[:, None] == blocks[None, :], places.reshape(-1)[:, None], 0), axis=0)
+    slotted = jnp.sum(jnp.where(slot[None, :, None] == spots[None, None, :], given[:, :, None], 0), axis=1)
+    packed = jnp.sum(jnp.where(given.reshape(-1)[:, None] == blocks[None, :], blocks[:, None], 0), axis=0)
+    mine = (blocks // per_own == me) & (blocks >= 0)
+    pull = jnp.arange(per_own, dtype=jnp.int32)[:, None] == jnp.where(mine, blocks % per_own, -1)[None, :]
+    own_places = jnp.sum(jnp.where(pull, inverse[None, :], 0), axis=1)
+    own_packed = jnp.sum(jnp.where(pull, packed[None, :], 0), axis=1)
+    origin = me ^ (own_packed % per_bin // per_half)
+    own_spots = ((origin // 2) + 2 * (origin % 2)) * per_own + own_packed // per_bin * per_half + own_packed % per_half
+    tables = (table.astype(jnp.int32), first, last, slot, slotted, own_places, own_spots)
+
     extras = jnp.concatenate(
         [w_beta, gain_attn[:, None], gain_ffn[:, None], jnp.zeros((shard, BLOCK - heads - 2), bf16)], axis=1
     )
-    attn_pack = jnp.concatenate([w_query, w_key, w_value, w_house, extras, w_out], axis=1)
+    attn_pack = jnp.concatenate([w_query, w_key, w_value, w_house, extras], axis=1)
     ffn_pack = jnp.concatenate([w_gate, w_up, w_down], axis=1)
     full_tokens = lax.all_gather(tokens, "tp", axis=0, tiled=True)
-    attn_full = RingGather(attn_pack, "fsdp").finish()
-    ffn_ring = RingGather(after(ffn_pack, attn_full), "fsdp")
+    attn_ring = RingGather(attn_pack, "fsdp")
+    attn_ring.hop()
+    table, first, last, slot, slotted, own_places, own_spots = attn_ring.before(*tables)
+    while len(attn_ring.hops) < attn_ring.count // 2 - 1:
+        attn_ring.hop()
+    full_tokens, out_shard, cotangent = attn_ring.before(full_tokens, w_out, cotangent)
+    w_in, ffn_pack, out_shard, cotangent = together(attn_ring.finish(), ffn_pack, out_shard, cotangent)
+    ffn_ring = RingGather(ffn_pack, "fsdp", True)
     ffn_ring.hop()
-    full_cot = lax.all_gather(after(cotangent, full_tokens), "tp", axis=0, tiled=True)
-    proj_width = 4 * width + BLOCK
-    w_in = attn_full[:, :proj_width]
-    full_out = attn_full[:, proj_width:]
+    x_rows = gather_blocks(full_tokens, slotted[:, :per_half], per_half)
+    full_out = lax.all_gather(out_shard, "fsdp", axis=0, tiled=True)
+    full_cot = lax.all_gather(cotangent, "tp", axis=0, tiled=True)
     pick = (jnp.arange(BLOCK)[None, :] == heads + jnp.arange(8)[:, None]).astype(bf16)
-    gain_rows = cols_contract(pick, attn_full[:, 4 * width : proj_width])
+    gain_rows = cols_contract(pick, w_in[:, 4 * width :])
     gain_one, gain_two = gain_rows[0], gain_rows[1]
 
     all_unit, _ = unit_rows(full_tokens.astype(f32))
     normed = (all_unit * gain_one).astype(bf16)
     proj = jnp.dot(normed, w_in, preferred_element_type=f32).astype(bf16)
-    proj = ffn_ring.before(proj)
-    ffn_ring.hop()
-    prep = list(attention_prep(proj, heads))
+
+    def attend(m):
+        prep = attention_prep(proj, table[m], heads)
+        return prep, lambda prep: attention_fwd(proj, prep, first[m], table[m], slot, heads)
+
+    preps, saved, hidden_in, unit_two, scale_two, normed_two = [], [], [], [], [], []
+
+    def close(m, own, far):
+        hidden_in.append(x_rows[m].astype(f32) + own + far.astype(f32))
+        unit, scale = unit_rows(hidden_in[m])
+        unit_two.append(unit)
+        scale_two.append(scale)
+        return (unit * gain_two).astype(bf16)
+
+    prep, run = attend(0)
+    prep = list(prep)
     prep[0] = ffn_ring.before(prep[0])
     ffn_ring.hop()
-    saved = attention_fwd(proj, prep, first, heads, depth)
-    mixed, full_cot = ffn_ring.before(saved[0], full_cot)
+    preps.append(prep)
+    saved.append(list(run(prep)))
+    rows = ffn_ring.before(cols_contract(saved[0][0], full_out).astype(bf16))
+    ffn_ring.hop()
+    attn_own, attn_far = share(rows)
+    proj, attn_own = together(proj, attn_own)
+    prep, run = attend(1)
+    prep = list(prep)
+    prep[0], attn_far = ffn_ring.before(prep[0], attn_far)
+    while len(ffn_ring.hops) < ffn_ring.count // 2:
+        ffn_ring.hop()
+    preps.append(prep)
+    normed_own = close(0, attn_own, attn_far)
+    normed_far = across(normed_own)
+    prep[0], normed_own = together(prep[0], normed_own)
+    saved.append(list(run(prep)))
+    saved[1][0], normed_far, full_cot = together(saved[1][0], normed_far, full_cot)
+    pair = jnp.concatenate([normed_own, normed_far], axis=0)
+    normed_two.append(jnp.concatenate([pair, beside(pair)], axis=0))
+    attn_own, attn_far = share(cols_contract(saved[1][0], full_out).astype(bf16))
+    attn_own, full_cot, ffn_ring.x = together(attn_own, full_cot, ffn_ring.x)
     ffn_full = ffn_ring.finish()
-    attn_part = lax.psum_scatter(
-        cols_contract(mixed, full_out).astype(bf16), "tp", scatter_dimension=0, tiled=True
-    ).astype(f32)
-    x_own = tokens.astype(f32)
-    unit_one, scale_one = unit_rows(x_own)
-    hidden_in = x_own + attn_part
-    unit_two, scale_two = unit_rows(hidden_in)
-    normed_two = lax.all_gather((unit_two * gain_two).astype(bf16), "tp", axis=0, tiled=True)
-    gate_pre = jnp.dot(normed_two, ffn_full[:, :hidden_width], preferred_element_type=f32)
-    up_part = jnp.dot(normed_two, ffn_full[:, hidden_width : 2 * hidden_width], preferred_element_type=f32)
-    full_down = ffn_full[:, 2 * hidden_width :]
-    hidden = (jax.nn.silu(gate_pre) * up_part).astype(bf16)
-    ffn_rows = cols_contract(hidden, full_down).astype(bf16)
-    grad_hidden = jnp.dot(full_cot, full_down, preferred_element_type=f32)
-    sigma = jax.nn.sigmoid(gate_pre)
-    grad_gate = (grad_hidden * up_part * sigma * (1.0 + gate_pre * (1.0 - sigma))).astype(bf16)
-    grad_up = (grad_hidden * jax.nn.silu(gate_pre)).astype(bf16)
-    gate_up = jnp.concatenate([grad_gate, grad_up], axis=1)
-    grad_two = lax.psum_scatter(
-        cols_contract(gate_up, ffn_full[:, : 2 * hidden_width]).astype(bf16), "tp", scatter_dimension=0, tiled=True
-    ).astype(f32)
-    ffn_grads = jnp.concatenate(
-        [rows_contract(normed_two, gate_up), rows_contract(full_cot, hidden)], axis=1
-    ).astype(bf16)
-    ffn_back = RingScatter(ffn_grads, "fsdp")
+    cot_rows = list(gather_blocks(full_cot, slotted, 4))
+
+    full_gate, full_up = ffn_full[:, :hidden_width], ffn_full[:, hidden_width : 2 * hidden_width]
+    full_gate_up, full_down = ffn_full[:, : 2 * hidden_width], ffn_full[:, 2 * hidden_width :]
+    hidden, gate_up, back = [], [], []
+
+    def ffn(m, rows, middle):
+        gate_pre = jnp.dot(rows, full_gate, preferred_element_type=f32)
+        up_part = jnp.dot(rows, full_up, preferred_element_type=f32)
+        cot_rows[m] = middle(cot_rows[m])
+        hidden.append((jax.nn.silu(gate_pre) * up_part).astype(bf16))
+        grad_hidden = jnp.dot(cot_rows[m], full_down, preferred_element_type=f32)
+        sigma = jax.nn.sigmoid(gate_pre)
+        grad_gate = (grad_hidden * up_part * sigma * (1.0 + gate_pre * (1.0 - sigma))).astype(bf16)
+        grad_up = (grad_hidden * jax.nn.silu(gate_pre)).astype(bf16)
+        gate_up.append(jnp.concatenate([grad_gate, grad_up], axis=1))
+
+    def ffn_back_rows(m):
+        return cols_contract(gate_up[m], full_gate_up).astype(bf16)
+
+    flying = {}
+
+    def middle(rows):
+        rows, own, far = together(rows, attn_own, attn_far)
+        mine = close(1, own, far)
+        flying[0], flying[1] = mine, across(mine)
+        return rows
+
+    ffn(0, normed_two[0], middle)
+    normed_own, normed_far = flying[0], flying[1]
+    rows, normed_own, normed_far = together(ffn_back_rows(0), normed_own, normed_far)
+    back_own, back_far = share(rows)
+    pair = jnp.concatenate([normed_own, normed_far], axis=0)
+    normed_two.append(jnp.concatenate([pair, beside(pair)], axis=0))
+    grad_attn = []
+
+    def close_back(m, own, far):
+        norm_two_grad = norm_back(own + far.astype(f32), unit_two[m], scale_two[m], gain_two)
+        cot_own = cot_rows[m][:half].astype(f32)
+        return (cot_own + norm_two_grad).astype(bf16)
+
+    def middle_back(rows):
+        rows, own, far = together(rows, back_own, back_far)
+        mine = close_back(0, own, far)
+        flying[0], flying[1] = mine, across(mine)
+        return rows
+
+    ffn(1, normed_two[1], middle_back)
+    dh_own, dh_far = flying[0], flying[1]
+    rows, dh_own, dh_far = together(ffn_back_rows(1), dh_own, dh_far)
+    back_own, back_far = share(rows)
+    back_own, normed_two[0], normed_two[1] = together(back_own, *normed_two)
+    grads_in = sum(rows_contract(normed_two[m], gate_up[m]) for m in streams)
+    grads_in, dh_far = together(grads_in.astype(bf16), dh_far)
+    pair = jnp.concatenate([dh_own, dh_far], axis=0)
+    grad_attn.append(jnp.concatenate([pair, beside(pair)], axis=0))
+    grads_down = sum(rows_contract(cot_rows[m], hidden[m]) for m in streams).astype(bf16)
+    grads_down, back_far = together(grads_down, back_far)
+    ffn_back = RingScatter([grads_in, grads_down], "fsdp")
     ffn_back.hop()
-    grad_two, mixed = ffn_back.before(grad_two, mixed)
+    dh_own = close_back(1, back_own, back_far)
+    dh_far = across(dh_own)
+    hidden[0], hidden[1], dh_own = together(*hidden, dh_own)
+    y_parts = list(ffn_back.before(*[cols_contract(hidden[m], full_down).astype(bf16) for m in streams]))
     ffn_back.hop()
-    norm_two_grad = norm_back(grad_two, unit_two, scale_two, gain_two)
-    grad_hidden_in = cotangent.astype(f32) + norm_two_grad
-    grad_attn = lax.all_gather(grad_hidden_in.astype(bf16), "tp", axis=0, tiled=True)
-    ffn_part = lax.psum_scatter(after(ffn_rows, grad_attn), "tp", scatter_dimension=0, tiled=True).astype(f32)
-    out_y = (hidden_in + ffn_part).astype(bf16)
-    grad_out = rows_contract(grad_attn, mixed)
-    d_mixed = jnp.dot(grad_attn, full_out, preferred_element_type=f32).astype(bf16)
-    d_mixed, grad_out = ffn_back.before(d_mixed, grad_out)
+    ffn_parts = [share(part) for part in y_parts]
+    d_mixed = jnp.dot(grad_attn[0], full_out, preferred_element_type=f32).astype(bf16)
+    y_own, y_far = [p[0] for p in ffn_parts], [p[1] for p in ffn_parts]
+    d_mixed, y_own[0], y_own[1] = together(d_mixed, *y_own)
+    d_proj = attention_bwd(proj, preps[0], saved[0], d_mixed, last[0], table[0], slot, heads, None)
+    d_proj, dh_far, y_far[0], y_far[1] = ffn_back.before(d_proj, dh_far, *y_far)
     ffn_back.hop()
-    d_proj = attention_bwd(proj, prep, saved, d_mixed, last, heads, depth)
-    d_proj = ffn_back.before(d_proj)
-    attn_grads = jnp.concatenate([rows_contract(normed, d_proj), grad_out], axis=1).astype(bf16)
-    attn_back = RingScatter(attn_grads, "fsdp")
+    pair = jnp.concatenate([dh_own, dh_far], axis=0)
+    grad_attn.append(jnp.concatenate([pair, beside(pair)], axis=0))
+    d_mixed = jnp.dot(grad_attn[1], full_out, preferred_element_type=f32).astype(bf16)
+    y_rows = jnp.concatenate(
+        [(hidden_in[m] + y_own[m] + y_far[m].astype(f32)).astype(bf16) for m in streams], axis=0
+    )
+    grad_out = sum(rows_contract(grad_attn[m], saved[m][0]) for m in streams).astype(bf16)
+    d_mixed, grad_out, y_rows = together(d_mixed, grad_out, y_rows)
+    y_across = across(y_rows)
+    d_proj = attention_bwd(proj, preps[1], saved[1], d_mixed, last[1], table[1], slot, heads, d_proj)
+    d_proj, y_across = ffn_back.before(d_proj, y_across)
+    ffn_back.hop()
+    attn_grads, d_proj, y_rows = together(rows_contract(normed, d_proj).astype(bf16), d_proj, y_rows)
+    attn_back = RingScatter([attn_grads, grad_out], "fsdp")
     attn_back.hop()
-    d_proj = after(d_proj, attn_grads)
-    grad_one = lax.psum_scatter(
-        cols_contract(d_proj, w_in).astype(bf16), "tp", scatter_dimension=0, tiled=True
-    ).astype(f32)
+    y_pair = jnp.concatenate([y_rows, y_across], axis=0)
+    rows_one, y_other = attn_back.before(cols_contract(d_proj, w_in).astype(bf16), beside(y_pair))
+    grad_one = lax.psum_scatter(rows_one, "tp", scatter_dimension=0, tiled=True).astype(f32)
+    ffn_sum = ffn_back.finish()
+    attn_back.hop()
+    ffn_sum = attn_back.before(ffn_sum)
+    attn_back.hop()
+    out_y = pick_blocks([y_rows, y_across, y_other], own_spots)
+    grad_one = attn_back.before(grad_one)
+    attn_sum = attn_back.finish()
+    unit_one, scale_one = unit_rows(tokens.astype(f32))
     norm_one_grad = norm_back(grad_one, unit_one, scale_one, gain_one)
-    out_dx = (grad_hidden_in + norm_one_grad).astype(bf16)
-    ffn_sum = ffn_back.finish()
-    attn_sum = attn_back.finish()
-    own = lambda grads, weights: jnp.sum(grads * weights.astype(f32), axis=1)
-    own_one = own(attn_sum[:, : 4 * width], attn_pack[:, : 4 * width]) + own(
+    out_dx = (pick_blocks(grad_attn, own_places).astype(f32) + norm_one_grad).astype(bf16)
+    dots = lambda grads, weights: jnp.sum(grads * weights.astype(f32), axis=1)
+    own_one = dots(attn_sum[:, : 4 * width], attn_pack[:, : 4 * width]) + dots(
         attn_sum[:, 4 * width : 4 * width + heads], w_beta
     )
-    own_two = own(ffn_sum[:, : 2 * hidden_width], ffn_pack[:, : 2 * hidden_width])
+    own_two = dots(ffn_sum[:, : 2 * hidden_width], ffn_pack[:, : 2 * hidden_width])
     gains = tp_sum(jnp.stack([own_one, own_two])) / jnp.stack([gain_attn, gain_ffn]).astype(f32)
     return (
         out_y,
@@ -612,7 +900,7 @@
         attn_sum[:, 2 * width : 3 * width],
         attn_sum[:, 3 * width : 4 * width],
         attn_sum[:, 4 * width : 4 * width + heads],
-        attn_sum[:, proj_width:],
+        attn_sum[:, 4 * width + BLOCK :],
         ffn_sum[:, :hidden_width],
         ffn_sum[:, hidden_width : 2 * hidden_width],
         ffn_sum[:, 2 * hidden_width :],

time: 726 us -> 679 us (0.935)
  waiting for transfers between devices: 267 us -> 125 us
  local copies, waits for them, and re-layouts: 33.4 us -> 76.8 us
  starting transfers between devices: 37 us -> 59.9 us
  Pallas kernels: 145 us -> 167 us
  other arithmetic: 43.9 us -> 57.3 us
  between operations: 28.9 us -> 15.6 us
    reduce_scatter x4 -> x1, waiting for transfers between devices: 79.8 us -> 0.01 us  [local(): lax.psum_scatter(rows_one, 'tp', scatter_dimension=0, tiled=True)]
    all_gather x3 -> x2, waiting for transfers between devices: 47 us -> 0.02 us  [the longest x1 0.02 us: local(): full_out = lax.all_gather(out_shard, 'fsdp', axis=0, tiled=True)]
    pallas_call x1 -> x8, Pallas kernels: 29.9 us -> 61.2 us  [the longest x2 34.2 us: attention_prep(): pl.pallas_call(functools.partial(prep_kernel, heads, step), grid_spec=spe...]
    ppermute x0 -> x22, waiting for transfers between devices: none -> 24.8 us  [the longest x11 22.2 us: across(): return lax.ppermute(x, 'tp', [(i, i ^ 2) for i in range(4)])]
    all_gather x1, waiting for transfers between devices: 23.8 us -> 0.01 us  [local(): full_tokens = lax.all_gather(tokens, 'tp', axis=0, tiled=True)]
    ppermute x0 -> x22, starting transfers between devices: none -> 12.4 us  [the longest x11 10.6 us: across(): return lax.ppermute(x, 'tp', [(i, i ^ 2) for i in range(4)])]
    unnamed x112 -> x222, local copies, waits for them, and re-layouts: 10.1 us -> 21.6 us
    dynamic_slice x2 -> x8, local copies, waits for them, and re-layouts: 1.22 us -> 12.7 us  [piece(): lax.dynamic_slice_in_dim(part, at, size, 0)]
  transfers between devices with their start and end apart: 43 -> 61, of which waited for: 21 -> 25; matrix products, arithmetic and copies ran while one was open for 20% -> 37% of each run, Pallas kernels for 20% -> 25%
where the time goes in v3:
time: 679 us; the launch traced here: 670 us
  matrix products  168 us (25%)
  Pallas kernels  167 us (25%)
  waiting for transfers between devices  125 us (18%)
  local copies, waits for them, and re-layouts  76.8 us (11%)
  starting transfers between devices  59.9 us (9%)
  other arithmetic  57.3 us (8%)
  between operations  15.6 us (2%)
    pallas_call x2, Pallas kernels, attention_bwd(): pl.pallas_call(functools.partial(bwd_kernel, heads, depth, scale), grid_s...  74.5 us
    dot_general x7, matrix products, rows_contract(): lax.dot_general(a, b, (((0,), (0,)), ((), ())), preferred_element_type=f32)  50.9 us
    dot_general x8, matrix products, cols_contract(): lax.dot_general(a, b, (((1,), (1,)), ((), ())), preferred_element_type=f32)  49.1 us
    pallas_call x2, Pallas kernels, attention_prep(): pl.pallas_call(functools.partial(prep_kernel, heads, step), grid_spec=spe...  34.2 us
    ppermute x8, waiting for transfers between devices, hop(): lax.ppermute(from_left, self.axis, self.right)  32.3 us
    ppermute x8, waiting for transfers between devices, hop(): lax.ppermute(to_right, self.axis, self.right)  31.9 us
    pallas_call x2, Pallas kernels, attention_fwd(): pl.pallas_call(functools.partial(fwd_kernel, heads, depth, scale), grid_s...  31.5 us
    ppermute x8, waiting for transfers between devices, hop(): lax.ppermute(to_left, self.axis, self.left)  26.7 us
  transfers between devices with their start and end apart: 61, of which 25 were waited for; matrix products, arithmetic and copies ran while one was open for 37% of the time, Pallas kernels for 25%

profile of v3, /device:TPU:0, one launch (start us, length us, event | category | flops | bytes accessed | tf_op | source)
XLA Modules:
  0.0 669.7 jit_solution(11845621888900875999)
XLA Ops:
  18.6 10.4 %collective-permute-done = bf16[192,1664]{1,0:T(8,128)(2,1)S(1)} collective-permute-done((bf16[192,1664]{1,0:T(8,128)(2,1)S(1)}, bf16[192,1664]{1,0:T(8,128)(2,1)S(1)}, u32[]{:S(2)}, u32[]{:S(2)}) %collective-permute-start) | collective-permute-done | bytes 639008 | tf_op jit(solution)/shard_map/ppermute | solution.py:562
  36.5 9.1 %collective-permute-done.2 = bf16[192,1664]{1,0:T(8,128)(2,1)} collective-permute-done((bf16[192,1664]{1,0:T(8,128)(2,1)S(1)}, bf16[192,1664]{1,0:T(8,128)(2,1)}, u32[]{:S(2)}, u32[]{:S(2)}) %collective-permute-start.2) | collective-permute-done | bytes 639008 | tf_op jit(solution)/shard_map/ppermute | solution.py:562
  52.5 7.5 %collective-permute-done.3 = bf16[192,1664]{1,0:T(8,128)(2,1)S(1)} collective-permute-done((bf16[192,1664]{1,0:T(8,128)(2,1)}, bf16[192,1664]{1,0:T(8,128)(2,1)S(1)}, u32[]{:S(2)}, u32[]{:S(2)}) %collective-permute-start.3) | collective-permute-done | bytes 639008 | tf_op jit(solution)/shard_map/ppermute | solution.py:562
  79.3 16.4 %convolution_convert_fusion.refs_0_.refs_1_.refs_2_.refs_3_.refs_4_.refs_5_.refs_6_.refs_7_.v_ref = bf16[2048,1664]{1,0:T(8,128)(2,1)} fusion(bf16[1536,1664]{1,0:T(8,128)(2,1)} %constant_dynamic-update-slice_fusion.14, bf16[2048,1536]{1,0:T(8,128)(2,1)S(1)} %copy-done, f32[1536]{0:T(1024)S(1)} %get-tuple-element.283, f32[2048]{0:T(1024)S(1)} %add_rsqrt_fusion), kind=kOutput, calls=%fused_computation.6 | convolution fusion | flops 10484973568 | bytes 18233344 | tf_op jit(solution)/shard_map/dot_general | solution.py:748
  95.6 17.0 %attn_prep.2 = (f32[8,3,128,128]{3,2,1,0:T(8,128)}, bf16[1024,384]{1,0:T(8,128)(2,1)}, bf16[8,3,128,256]{3,2,1,0:T(8,128)(2,1)}, bf16[8,3,128,128]{3,2,1,0:T(8,128)(2,1)}, bf16[8,3,128,256]{3,2,1,0:T(8,128)(2,1)}) custom-call(s32[8]{0:T(128)} %get-tuple-element.360.table_ref, ...), custom_call_target="tpu_custom_call" | custom-call | flops 2264924160 | bytes 2359296 | tf_op jit(solution)/shard_map/attn_prep/pallas_call | solution.py:265
  119.2 18.8 %attn_fwd.2 = (bf16[1024,384]{1,0:T(8,128)(2,1)}, f32[1024,384]{1,0:T(8,128)}, bf16[8,8,3,128,128]{4,3,2,1,0:T(8,128)(2,1)}, bf16[8,7,3,128,128]{4,3,2,1,0:T(8,128)(2,1)}) custom-call(s32[8]{0:T(128)} %get-tuple-element.358.first_ref, s32[8]{0:T(128)} %get-tuple-element.360.table_ref, s32[8]{0:T(128)} %copy-done.73, ...), custom_call_target="tpu_custom_call" | custom-call | flops 2415919104 | bytes 2359296 | tf_op jit(solution)/shard_map/attn_fwd/pallas_call | solution.py:309
  151.2 17.1 %attn_prep.3 = (f32[8,3,128,128]{3,2,1,0:T(8,128)}, bf16[1024,384]{1,0:T(8,128)(2,1)}, bf16[8,3,128,256]{3,2,1,0:T(8,128)(2,1)}, bf16[8,3,128,128]{3,2,1,0:T(8,128)(2,1)}, bf16[8,3,128,256]{3,2,1,0:T(8,128)(2,1)}) custom-call(s32[8]{0:T(128)} %get-tuple-element.361.table_ref, ...), custom_call_target="tpu_custom_call" | custom-call | flops 2264924160 | bytes 2359296 | tf_op jit(solution)/shard_map/attn_prep/pallas_call | solution.py:265
  172.2 7.5 %collective-permute-done.15 = bf16[256,1536]{1,0:T(8,128)(2,1)} collective-permute-done((bf16[256,1536]{1,0:T(8,128)(2,1)}, bf16[256,1536]{1,0:T(8,128)(2,1)}, u32[]{:S(2)}, u32[]{:S(2)}) %collective-permute-start.15) | collective-permute-done | bytes 786464 | tf_op jit(solution)/shard_map/ppermute | solution.py:649
  182.1 12.7 %attn_fwd.3 = (bf16[1024,384]{1,0:T(8,128)(2,1)}, f32[1024,384]{1,0:T(8,128)}, bf16[8,8,3,128,128]{4,3,2,1,0:T(8,128)(2,1)}, bf16[8,7,3,128,128]{4,3,2,1,0:T(8,128)(2,1)}) custom-call(s32[8]{0:T(128)} %get-tuple-element.359.first_ref, s32[8]{0:T(128)} %get-tuple-element.361.table_ref, s32[8]{0:T(128)} %copy-done.73, ...), custom_call_target="tpu_custom_call" | custom-call | flops 2415919104 | bytes 2359296 | tf_op jit(solution)/shard_map/attn_fwd/pallas_call | solution.py:309
  194.8 6.3 collective-permute-done.16
  222.6 5.4 gather_blocks.3
  228.0 7.3 %place_pieces.1 = bf16[1536,3072]{1,0:T(8,128)(2,1)} custom-call(s32[7]{0:T(128)} %concatenate.120.spot_ref, bf16[192,3072]{1,0:T(8,128)(2,1)} %copy-done.13, bf16[192,3072]{1,0:T(8,128)(2,1)} %copy-done.41, bf16[192,3072]{1,0:T(8,128)(2,1)} %copy-done.42, bf16[192,3072]{1,0:T(8,128)(2,1)} %collective-permute-done.10.refs_3_, ...), custom_call_target="tpu_custom_call" | custom-call | bytes 16515072 | tf_op jit(solution)/shard_map/place_pieces/pallas_call | solution.py:482
  242.1 8.5 %fusion.26 = f32[1024,1024]{0,1:T(8,128)} fusion(bf16[1024,1536]{1,0:T(8,128)(2,1)} %constant_dynamic-update-slice_fusion, bf16[1536,3072]{1,0:T(8,128)(2,1)} %constant_dynamic-update-slice_fusion.12), kind=kOutput, calls=%fused_computation.53 | convolution fusion | flops 3221225472 | bytes 10485760 | tf_op jit(solution)/shard_map/dot_general | solution.py:796
  253.2 5.1 fusion.39
  258.3 9.8 %multiply_convert_fusion.1 = (bf16[1024,1024]{0,1:T(8,128)(2,1)}, bf16[1024,1024]{0,1:T(8,128)(2,1)S(1)}, bf16[1024,1024]{0,1:T(8,128)(2,1)}) fusion(f32[1024,1024]{0,1:T(8,128)} %fusion.26, f32[1024,1024]{0,1:T(8,128)} %fusion.39, bf16[1024,1536]{1,0:T(8,128)(2,1)} %constant_dynamic-update-slice_fusion, bf16[1536,3072]{1,0:T(8,128)(2,1)S(1)} %bitcast.61), kind=kOutput, calls=%fused_computation.17 | convolution fusion | flops 3236954112 | bytes 20971520 | tf_op jit(solution)/shard_map/dot_general | solution.py:797
  268.1 9.0 %fusion.9 = bf16[1024,1536]{1,0:T(8,128)(2,1)S(1)} fusion(bf16[1536,3072]{1,0:T(8,128)(2,1)S(1)} %bitcast.61, bf16[1024,1024]{0,1:T(8,128)(2,1)} %get-tuple-element.297, bf16[1024,1024]{0,1:T(8,128)(2,1)S(1)} %get-tuple-element.296), kind=kOutput, calls=%fused_computation.28 | convolution fusion | flops 6452412416 | bytes 13631488 | tf_op jit(solution)/shard_map/dot_general | solution.py:517
  287.4 8.2 %fusion.24 = f32[1024,1024]{0,1:T(8,128)} fusion(bf16[1024,1536]{1,0:T(8,128)(2,1)S(1)} %constant_dynamic-update-slice_fusion.3, bf16[1536,3072]{1,0:T(8,128)(2,1)} %constant_dynamic-update-slice_fusion.12), kind=kOutput, calls=%fused_computation.51 | convolution fusion | flops 3221225472 | bytes 10485760 | tf_op jit(solution)/shard_map/dot_general | solution.py:796
  295.6 8.5 %collective-permute-done.24 = bf16[256,1536]{1,0:T(8,128)(2,1)S(1)} collective-permute-done((bf16[256,1536]{1,0:T(8,128)(2,1)S(1)}, bf16[256,1536]{1,0:T(8,128)(2,1)S(1)}, u32[]{:S(2)}, u32[]{:S(2)}) %collective-permute-start.24) | collective-permute-done | bytes 786464 | tf_op jit(solution)/shard_map/ppermute | solution.py:649
  304.1 5.0 fusion.37
  312.5 9.5 %multiply_convert_fusion = (bf16[1024,1024]{0,1:T(8,128)(2,1)S(1)}, bf16[1024,1024]{0,1:T(8,128)(2,1)S(1)}, bf16[1024,1024]{0,1:T(8,128)(2,1)}) fusion(f32[1024,1024]{0,1:T(8,128)} %fusion.24, f32[1024,1024]{0,1:T(8,128)} %fusion.37, bf16[1024,1536]{1,0:T(8,128)(2,1)} %copy-done.67, bf16[1536,3072]{1,0:T(8,128)(2,1)S(1)} %bitcast.63), kind=kOutput, calls=%fused_computation.16 | convolution fusion | flops 3236954112 | bytes 20971520 | tf_op jit(solution)/shard_map/dot_general | solution.py:797
  322.0 9.3 %fusion.12 = bf16[1024,1536]{1,0:T(8,128)(2,1)S(1)} fusion(bf16[1536,3072]{1,0:T(8,128)(2,1)S(1)} %bitcast.63, bf16[1024,1024]{0,1:T(8,128)(2,1)} %get-tuple-element.300, bf16[1024,1024]{0,1:T(8,128)(2,1)S(1)} %get-tuple-element.299), kind=kOutput, calls=%fused_computation.29 | convolution fusion | flops 6452412416 | bytes 13631488 | tf_op jit(solution)/shard_map/dot_general | solution.py:517
  344.4 9.5 %fusion.32 = f32[1536,2048]{1,0:T(8,128)} fusion(bf16[1024,1536]{1,0:T(8,128)(2,1)S(1)} %copy-done.68, bf16[1024,1024]{0,1:T(8,128)(2,1)S(1)} %copy-done.95, bf16[1024,1024]{0,1:T(8,128)(2,1)S(1)} %copy-done.94), kind=kOutput, calls=%fused_computation.59 | convolution fusion | flops 6450839552 | bytes 19922944 | tf_op jit(solution)/shard_map/dot_general | solution.py:513
  354.0 11.4 %add_convert_fusion = bf16[1536,2048]{1,0:T(8,128)(2,1)S(1)} fusion(f32[1536,2048]{1,0:T(8,128)} %fusion.32, bf16[1024,1536]{1,0:T(8,128)(2,1)} %constant_dynamic-update-slice_fusion, bf16[1024,1024]{0,1:T(8,128)(2,1)} %get-tuple-element.297, bf16[1024,1024]{0,1:T(8,128)(2,1)} %copy-done.96), kind=kOutput, calls=%fused_computation.5 | convolution fusion | flops 6457131008 | bytes 26214400 | tf_op jit(solution)/shard_map/dot_general | solution.py:513
  387.7 8.7 %collective-permute-done.30 = bf16[96,3072]{1,0:T(8,128)(2,1)S(1)} collective-permute-done((bf16[96,3072]{1,0:T(8,128)(2,1)S(1)}, bf16[96,3072]{1,0:T(8,128)(2,1)S(1)}, u32[]{:S(2)}, u32[]{:S(2)}) %collective-permute-start.30) | collective-permute-done | bytes 589856 | tf_op jit(solution)/shard_map/ppermute | solution.py:619
  412.9 42.8 %attn_bwd.2.refs_26_ = bf16[2048,1664]{1,0:T(8,128)(2,1)} custom-call(s32[8]{0:T(128)} %get-tuple-element.357.last_ref, s32[8]{0:T(128)} %get-tuple-element.360.table_ref, s32[8]{0:T(128)} %copy-done.73, bf16[1024,384]{1,0:T(8,128)(2,1)} %convolution_convert_fusion.8.refs_0_, bf16[1024,384]{1,0:T(8,128)(2,1)} %get-tuple-element.148.refs_1_, ...), custom_call_target="tpu_custom_call" | custom-call | flops 6039797760 | bytes 3145728 | tf_op jit(solution)/shard_map/attn_bwd/pallas_call | solution.py:376
  480.6 31.7 %attn_bwd.3 = bf16[2048,1664]{1,0:T(8,128)(2,1)} custom-call(s32[8]{0:T(128)} %get-tuple-element.356.last_ref, s32[8]{0:T(128)} %get-tuple-element.361.table_ref, s32[8]{0:T(128)} %copy-done.73, bf16[1024,384]{1,0:T(8,128)(2,1)} %convolution_convert_fusion.7.refs_0_, bf16[1024,384]{1,0:T(8,128)(2,1)} %get-tuple-element.164.refs_1_, ...), custom_call_target="tpu_custom_call", output_to_operand_aliasing={{}: (29, {})} | custom-call | flops 6039797760 | bytes 3145728 | tf_op jit(solution)/shard_map/attn_bwd/pallas_call | solution.py:376
  512.4 16.8 %convolution_convert_fusion.2 = bf16[1536,1664]{1,0:T(8,128)(2,1)S(1)} fusion(bf16[2048,1664]{1,0:T(8,128)(2,1)} %attn_bwd.3, bf16[2048,1536]{1,0:T(8,128)(2,1)} %all-gather.4.cloned.1.call-done.refs_0_.refs_1_.refs_2_.refs_3_, f32[1536]{0:T(1024)S(1)} %copy-done.70, f32[2048]{0:T(1024)S(1)} %copy-done.76), kind=kOutput, calls=%fused_computation.8 | convolution fusion | flops 10484121600 | bytes 18233344 | tf_op jit(solution)/shard_map/dot_general | solution.py:513
  534.5 11.4 %collective-permute-start.44 = (bf16[96,2048]{1,0:T(8,128)(2,1)S(1)}, bf16[96,2048]{1,0:T(8,128)(2,1)S(1)}, u32[]{:S(2)}, u32[]{:S(2)}) collective-permute-start(bf16[96,2048]{1,0:T(8,128)(2,1)S(1)} %pad_maximum_fusion.20), channel_id=1, source_target_pairs={{0,4},{8,0},{16,8},{24,16},{28,24},{20,28},{12,20},{4,12},{1,5},{9... | collective-permute-start | bytes 1179656 | tf_op jit(solution)/shard_map/ppermute | solution.py:619
  546.2 15.1 %convolution_convert_fusion.1 = bf16[2048,1536]{1,0:T(8,128)(2,1)} fusion(bf16[2048,1664]{1,0:T(8,128)(2,1)S(1)} %copy-done.5, bf16[1536,1664]{1,0:T(8,128)(2,1)} %constant_dynamic-update-slice_fusion.14), kind=kOutput, calls=%fused_computation.7 | convolution fusion | flops 10472128512 | bytes 18219008 | tf_op jit(solution)/shard_map/dot_general | solution.py:517
  578.1 18.2 %collective-permute-done.48 = bf16[192,3072]{1,0:T(8,128)(2,1)S(1)} collective-permute-done((bf16[192,3072]{1,0:T(8,128)(2,1)S(1)}, bf16[192,3072]{1,0:T(8,128)(2,1)S(1)}, u32[]{:S(2)}, u32[]{:S(2)}) %collective-permute-start.48) | collective-permute-done | bytes 1179680 | tf_op jit(solution)/shard_map/ppermute | solution.py:619
  600.3 14.0 %collective-permute-done.47 = bf16[192,2048]{1,0:T(8,128)(2,1)S(1)} collective-permute-done((bf16[192,2048]{1,0:T(8,128)(2,1)S(1)}, bf16[192,2048]{1,0:T(8,128)(2,1)S(1)}, u32[]{:S(2)}, u32[]{:S(2)}) %collective-permute-start.47) | collective-permute-done | bytes 786464 | tf_op jit(solution)/shard_map/ppermute | solution.py:619
  644.5 11.0 %collective-permute-done.52 = bf16[192,2048]{1,0:T(8,128)(2,1)S(1)} collective-permute-done((bf16[192,2048]{1,0:T(8,128)(2,1)S(1)}, bf16[192,2048]{1,0:T(8,128)(2,1)S(1)}, u32[]{:S(2)}, u32[]{:S(2)}) %collective-permute-start.52) | collective-permute-done | bytes 786464 | tf_op jit(solution)/shard_map/ppermute | solution.py:619
  (506 shorter events, 255.0 us)
Async XLA Ops:
  7.2 54.1 %all-gather.4.cloned.1.call-start = ((), (), s32[]{:S(2)}) async-start(), calls=%async_computation.1 | async-start | bytes 7864320 | tf_op jit(solution)/shard_map/all_gather | solution.py:729
  7.9 130.1 %all-gather.6.cloned.1.call-start = ((), (), s32[]{:S(2)}) async-start(), calls=%async_computation.2 | async-start | bytes 1327104 | tf_op jit(solution)/shard_map/all_gather | solution.py:740
  70.8 130.2 %all-gather.8.cloned.1.call-start = ((), (), s32[]{:S(2)}) async-start(), calls=%async_computation.3 | async-start | bytes 7864320 | tf_op jit(solution)/shard_map/all_gather | solution.py:741
  71.5 562.3 %reduce-scatter.2.cloned.1.call-start = ((), (), s32[]{:S(2)}) async-start(), calls=%async_computation.4 | async-start | bytes 7864320 | tf_op jit(solution)/shard_map/reduce_scatter | solution.py:878
  75.9 37.0 %collective-permute-start.8 = (bf16[192,3072]{1,0:T(8,128)(2,1)S(1)}, bf16[192,3072]{1,0:T(8,128)(2,1)S(1)}, u32[]{:S(2)}, u32[]{:S(2)}) collective-permute-start(bf16[192,3072]{1,0:T(8,128)(2,1)S(1)} %pad_maximum_fusion.12.refs_0_), channel_id=1, source_target_pairs={{0,8},{8,16},{16,24},{24,28},{28,20},{20,12},{12,4},{4,0},{1,9},{9... | collective-permute-start | bytes 3538952 | tf_op jit(solution)/shard_map/ppermute | solution.py:562
  77.4 38.3 %collective-permute-start.9 = (bf16[192,3072]{1,0:T(8,128)(2,1)S(1)}, bf16[192,3072]{1,0:T(8,128)(2,1)S(1)}, u32[]{:S(2)}, u32[]{:S(2)}) collective-permute-start(bf16[192,3072]{1,0:T(8,128)(2,1)S(1)} %pad_maximum_fusion.12.refs_0_), channel_id=1, source_target_pairs={{0,4},{8,0},{16,8},{24,16},{28,24},{20,28},{12,20},{4,12},{1,5},{9... | collective-permute-start | bytes 3538952 | tf_op jit(solution)/shard_map/ppermute | solution.py:563
  115.8 25.6 %collective-permute-start.10 = (bf16[192,3072]{1,0:T(8,128)(2,1)S(1)}, bf16[192,3072]{1,0:T(8,128)(2,1)}, u32[]{:S(2)}, u32[]{:S(2)}) collective-permute-start(bf16[192,3072]{1,0:T(8,128)(2,1)S(1)} %collective-permute-done.8.refs_1_), channel_id=1, source_target_pairs={{0,8},{8,16},{16,24},{24,28},{28,20},{20,12},{12,4},{4,0},{1,9},{9... | collective-permute-start | bytes 3538952 | tf_op jit(solution)/shard_map/ppermute | solution.py:562
  118.5 22.9 %collective-permute-start.11 = (bf16[192,3072]{1,0:T(8,128)(2,1)S(1)}, bf16[192,3072]{1,0:T(8,128)(2,1)}, u32[]{:S(2)}, u32[]{:S(2)}) collective-permute-start(bf16[192,3072]{1,0:T(8,128)(2,1)S(1)} %collective-permute-done.9.refs_2_), channel_id=1, source_target_pairs={{0,4},{8,0},{16,8},{24,16},{28,24},{20,28},{12,20},{4,12},{1,5},{9... | collective-permute-start | bytes 3538952 | tf_op jit(solution)/shard_map/ppermute | solution.py:563
  141.6 28.7 %collective-permute-start.13 = (bf16[192,3072]{1,0:T(8,128)(2,1)}, bf16[192,3072]{1,0:T(8,128)(2,1)}, u32[]{:S(2)}, u32[]{:S(2)}) collective-permute-start(bf16[192,3072]{1,0:T(8,128)(2,1)} %collective-permute-done.10.refs_3_), channel_id=1, source_target_pairs={{0,8},{8,16},{16,24},{24,28},{28,20},{20,12},{12,4},{4,0},{1,9},{9... | collective-permute-start | bytes 3538952 | tf_op jit(solution)/shard_map/ppermute | solution.py:562
  143.9 28.4 %collective-permute-start.14 = (bf16[192,3072]{1,0:T(8,128)(2,1)}, bf16[192,3072]{1,0:T(8,128)(2,1)}, u32[]{:S(2)}, u32[]{:S(2)}) collective-permute-start(bf16[192,3072]{1,0:T(8,128)(2,1)} %collective-permute-done.11.refs_4_), channel_id=1, source_target_pairs={{0,4},{8,0},{16,8},{24,16},{28,24},{20,28},{12,20},{4,12},{1,5},{9... | collective-permute-start | bytes 3538952 | tf_op jit(solution)/shard_map/ppermute | solution.py:563
  146.6 33.1 %collective-permute-start.15 = (bf16[256,1536]{1,0:T(8,128)(2,1)}, bf16[256,1536]{1,0:T(8,128)(2,1)}, u32[]{:S(2)}, u32[]{:S(2)}) collective-permute-start(bf16[256,1536]{1,0:T(8,128)(2,1)} %slice.409), channel_id=1, source_target_pairs={{0,2},{1,3},{2,0},{3,1},{4,6},{5,7},{6,4},{7,5},{8,10},{9,11},{10,... | collective-permute-start | bytes 2359304 | tf_op jit(solution)/shard_map/ppermute | solution.py:649
  210.4 25.0 %collective-permute-start.19 = (bf16[96,3072]{1,0:T(8,128)(2,1)}, bf16[96,3072]{1,0:T(8,128)(2,1)}, u32[]{:S(2)}, u32[]{:S(2)}) collective-permute-start(bf16[96,3072]{1,0:T(8,128)(2,1)} %slice.237), channel_id=1, source_target_pairs={{0,8},{8,16},{16,24},{24,28},{28,20},{20,12},{12,4},{4,0},{1,9},{9... | collective-permute-start | bytes 1769480 | tf_op jit(solution)/shard_map/ppermute | solution.py:562
  213.9 23.4 %collective-permute-start.20 = (bf16[96,3072]{1,0:T(8,128)(2,1)}, bf16[96,3072]{1,0:T(8,128)(2,1)}, u32[]{:S(2)}, u32[]{:S(2)}) collective-permute-start(bf16[96,3072]{1,0:T(8,128)(2,1)} %slice.238), channel_id=1, source_target_pairs={{0,4},{8,0},{16,8},{24,16},{28,24},{20,28},{12,20},{4,12},{1,5},{9... | collective-permute-start | bytes 1769480 | tf_op jit(solution)/shard_map/ppermute | solution.py:563
  216.1 23.2 %collective-permute-start.21 = (bf16[512,1536]{1,0:T(8,128)(2,1)}, bf16[512,1536]{1,0:T(8,128)(2,1)}, u32[]{:S(2)}, u32[]{:S(2)}) collective-permute-start(bf16[512,1536]{1,0:T(8,128)(2,1)} %pad_maximum_fusion.7), channel_id=1, source_target_pairs={{0,1},{1,0},{2,3},{3,2},{4,5},{5,4},{6,7},{7,6},{8,9},{9,8},{10,11... | collective-permute-start | bytes 4718600 | tf_op jit(solution)/shard_map/ppermute | solution.py:653
  221.4 29.1 %collective-permute-start.18 = (bf16[256,1536]{1,0:T(8,128)(2,1)S(1)}, bf16[256,1536]{1,0:T(8,128)(2,1)S(1)}, u32[]{:S(2)}, u32[]{:S(2)}) collective-permute-start(bf16[256,1536]{1,0:T(8,128)(2,1)S(1)} %slice.408), channel_id=1, source_target_pairs={{0,2},{1,3},{2,0},{3,1},{4,6},{5,7},{6,4},{7,5},{8,10},{9,11},{10,... | collective-permute-start | bytes 2359304 | tf_op jit(solution)/shard_map/ppermute | solution.py:649
  252.3 24.9 %collective-permute-start.22 = (bf16[256,1536]{1,0:T(8,128)(2,1)S(1)}, bf16[256,1536]{1,0:T(8,128)(2,1)S(1)}, u32[]{:S(2)}, u32[]{:S(2)}) collective-permute-start(bf16[256,1536]{1,0:T(8,128)(2,1)S(1)} %multiply_convert_fusion.6), channel_id=1, source_target_pairs={{0,2},{1,3},{2,0},{3,1},{4,6},{5,7},{6,4},{7,5},{8,10},{9,11},{10,... | collective-permute-start | bytes 2359304 | tf_op jit(solution)/shard_map/ppermute | solution.py:649
  342.4 26.9 %collective-permute-start.28 = (bf16[256,1536]{1,0:T(8,128)(2,1)}, bf16[256,1536]{1,0:T(8,128)(2,1)S(1)}, u32[]{:S(2)}, u32[]{:S(2)}) collective-permute-start(bf16[256,1536]{1,0:T(8,128)(2,1)} %slice.406), channel_id=1, source_target_pairs={{0,2},{1,3},{2,0},{3,1},{4,6},{5,7},{6,4},{7,5},{8,10},{9,11},{10,... | collective-permute-start | bytes 2359304 | tf_op jit(solution)/shard_map/ppermute | solution.py:649
  365.6 38.0 %collective-permute-start.33 = (bf16[512,1536]{1,0:T(8,128)(2,1)S(1)}, bf16[512,1536]{1,0:T(8,128)(2,1)S(1)}, u32[]{:S(2)}, u32[]{:S(2)}) collective-permute-start(bf16[512,1536]{1,0:T(8,128)(2,1)S(1)} %pad_maximum_fusion.9), channel_id=1, source_target_pairs={{0,1},{1,0},{2,3},{3,2},{4,5},{5,4},{6,7},{7,6},{8,9},{9,8},{10,11... | collective-permute-start | bytes 4718600 | tf_op jit(solution)/shard_map/ppermute | solution.py:653
  375.9 79.8 %collective-permute-start.36 = (bf16[256,1536]{1,0:T(8,128)(2,1)S(1)}, bf16[256,1536]{1,0:T(8,128)(2,1)}, u32[]{:S(2)}, u32[]{:S(2)}) collective-permute-start(bf16[256,1536]{1,0:T(8,128)(2,1)S(1)} %add_convert_fusion.4), channel_id=1, source_target_pairs={{0,2},{1,3},{2,0},{3,1},{4,6},{5,7},{6,4},{7,5},{8,10},{9,11},{10,... | collective-permute-start | bytes 2359304 | tf_op jit(solution)/shard_map/ppermute | solution.py:649
  401.4 54.4 %collective-permute-start.32 = (bf16[192,3072]{1,0:T(8,128)(2,1)}, bf16[192,3072]{1,0:T(8,128)(2,1)}, u32[]{:S(2)}, u32[]{:S(2)}) collective-permute-start(bf16[192,3072]{1,0:T(8,128)(2,1)} %pad_maximum_fusion.13), channel_id=1, source_target_pairs={{0,4},{8,0},{16,8},{24,16},{28,24},{20,28},{12,20},{4,12},{1,5},{9... | collective-permute-start | bytes 3538952 | tf_op jit(solution)/shard_map/ppermute | solution.py:619
  403.6 52.2 %collective-permute-start.31 = (bf16[192,3072]{1,0:T(8,128)(2,1)}, bf16[192,3072]{1,0:T(8,128)(2,1)}, u32[]{:S(2)}, u32[]{:S(2)}) collective-permute-start(bf16[192,3072]{1,0:T(8,128)(2,1)} %fusion.46), channel_id=1, source_target_pairs={{0,8},{8,16},{16,24},{24,28},{28,20},{20,12},{12,4},{4,0},{1,9},{9... | collective-permute-start | bytes 3538952 | tf_op jit(solution)/shard_map/ppermute | solution.py:619
  406.6 49.1 %collective-permute-start.38 = (bf16[256,1536]{1,0:T(8,128)(2,1)}, bf16[256,1536]{1,0:T(8,128)(2,1)}, u32[]{:S(2)}, u32[]{:S(2)}) collective-permute-start(bf16[256,1536]{1,0:T(8,128)(2,1)} %slice.404), channel_id=1, source_target_pairs={{0,2},{1,3},{2,0},{3,1},{4,6},{5,7},{6,4},{7,5},{8,10},{9,11},{10,... | collective-permute-start | bytes 2359304 | tf_op jit(solution)/shard_map/ppermute | solution.py:649
  409.0 46.7 %collective-permute-start.37 = (bf16[256,1536]{1,0:T(8,128)(2,1)}, bf16[256,1536]{1,0:T(8,128)(2,1)}, u32[]{:S(2)}, u32[]{:S(2)}) collective-permute-start(bf16[256,1536]{1,0:T(8,128)(2,1)} %slice.405), channel_id=1, source_target_pairs={{0,2},{1,3},{2,0},{3,1},{4,6},{5,7},{6,4},{7,5},{8,10},{9,11},{10,... | collective-permute-start | bytes 2359304 | tf_op jit(solution)/shard_map/ppermute | solution.py:649
  461.3 51.0 %collective-permute-start.40 = (bf16[192,3072]{1,0:T(8,128)(2,1)}, bf16[192,3072]{1,0:T(8,128)(2,1)}, u32[]{:S(2)}, u32[]{:S(2)}) collective-permute-start(bf16[192,3072]{1,0:T(8,128)(2,1)} %maximum_add_fusion.1), channel_id=1, source_target_pairs={{0,4},{8,0},{16,8},{24,16},{28,24},{20,28},{12,20},{4,12},{1,5},{9... | collective-permute-start | bytes 3538952 | tf_op jit(solution)/shard_map/ppermute | solution.py:619
  475.0 37.3 %collective-permute-start.42 = (bf16[512,1536]{1,0:T(8,128)(2,1)S(1)}, bf16[512,1536]{1,0:T(8,128)(2,1)S(1)}, u32[]{:S(2)}, u32[]{:S(2)}) collective-permute-start(bf16[512,1536]{1,0:T(8,128)(2,1)S(1)} %pad_maximum_fusion.11.refs_0_), channel_id=1, source_target_pairs={{0,2},{1,3},{2,0},{3,1},{4,6},{5,7},{6,4},{7,5},{8,10},{9,11},{10,... | collective-permute-start | bytes 4718600 | tf_op jit(solution)/shard_map/ppermute | solution.py:649
  478.7 33.7 %collective-permute-start.39 = (bf16[192,3072]{1,0:T(8,128)(2,1)}, bf16[192,3072]{1,0:T(8,128)(2,1)}, u32[]{:S(2)}, u32[]{:S(2)}) collective-permute-start(bf16[192,3072]{1,0:T(8,128)(2,1)} %maximum_add_fusion), channel_id=1, source_target_pairs={{0,8},{8,16},{16,24},{24,28},{28,20},{20,12},{12,4},{4,0},{1,9},{9... | collective-permute-start | bytes 3538952 | tf_op jit(solution)/shard_map/ppermute | solution.py:619
  531.2 30.3 %collective-permute-start.45 = (bf16[1024,1536]{1,0:T(8,128)(2,1)}, bf16[1024,1536]{1,0:T(8,128)(2,1)}, u32[]{:S(2)}, u32[]{:S(2)}) collective-permute-start(bf16[1024,1536]{1,0:T(8,128)(2,1)} %pad_maximum_fusion.2), channel_id=1, source_target_pairs={{0,1},{1,0},{2,3},{3,2},{4,5},{5,4},{6,7},{7,6},{8,9},{9,8},{10,11... | collective-permute-start | bytes 9437192 | tf_op jit(solution)/shard_map/ppermute | solution.py:653
  534.5 26.8 %collective-permute-start.44 = (bf16[96,2048]{1,0:T(8,128)(2,1)S(1)}, bf16[96,2048]{1,0:T(8,128)(2,1)S(1)}, u32[]{:S(2)}, u32[]{:S(2)}) collective-permute-start(bf16[96,2048]{1,0:T(8,128)(2,1)S(1)} %pad_maximum_fusion.20), channel_id=1, source_target_pairs={{0,4},{8,0},{16,8},{24,16},{28,24},{20,28},{12,20},{4,12},{1,5},{9... | collective-permute-start | bytes 1179656 | tf_op jit(solution)/shard_map/ppermute | solution.py:619
  567.4 28.9 %collective-permute-start.48 = (bf16[192,3072]{1,0:T(8,128)(2,1)S(1)}, bf16[192,3072]{1,0:T(8,128)(2,1)S(1)}, u32[]{:S(2)}, u32[]{:S(2)}) collective-permute-start(bf16[192,3072]{1,0:T(8,128)(2,1)S(1)} %maximum_add_fusion.2), channel_id=1, source_target_pairs={{0,8},{8,16},{16,24},{24,28},{28,20},{20,12},{12,4},{4,0},{1,9},{9... | collective-permute-start | bytes 3538952 | tf_op jit(solution)/shard_map/ppermute | solution.py:619
  569.5 28.9 %collective-permute-start.49 = (bf16[192,3072]{1,0:T(8,128)(2,1)S(1)}, bf16[192,3072]{1,0:T(8,128)(2,1)S(1)}, u32[]{:S(2)}, u32[]{:S(2)}) collective-permute-start(bf16[192,3072]{1,0:T(8,128)(2,1)S(1)} %maximum_add_fusion.3), channel_id=1, source_target_pairs={{0,4},{8,0},{16,8},{24,16},{28,24},{20,28},{12,20},{4,12},{1,5},{9... | collective-permute-start | bytes 3538952 | tf_op jit(solution)/shard_map/ppermute | solution.py:619
  575.6 38.8 %collective-permute-start.47 = (bf16[192,2048]{1,0:T(8,128)(2,1)S(1)}, bf16[192,2048]{1,0:T(8,128)(2,1)S(1)}, u32[]{:S(2)}, u32[]{:S(2)}) collective-permute-start(bf16[192,2048]{1,0:T(8,128)(2,1)S(1)} %pad_maximum_fusion.14), channel_id=1, source_target_pairs={{0,4},{8,0},{16,8},{24,16},{28,24},{20,28},{12,20},{4,12},{1,5},{9... | collective-permute-start | bytes 2359304 | tf_op jit(solution)/shard_map/ppermute | solution.py:619
  578.0 36.3 %collective-permute-start.46 = (bf16[192,2048]{1,0:T(8,128)(2,1)S(1)}, bf16[192,2048]{1,0:T(8,128)(2,1)S(1)}, u32[]{:S(2)}, u32[]{:S(2)}) collective-permute-start(bf16[192,2048]{1,0:T(8,128)(2,1)S(1)} %fusion.49), channel_id=1, source_target_pairs={{0,8},{8,16},{16,24},{24,28},{28,20},{20,12},{12,4},{4,0},{1,9},{9... | collective-permute-start | bytes 2359304 | tf_op jit(solution)/shard_map/ppermute | solution.py:619
  (139 other events, 1371.2 us)
Sparse Core Ops, SparseCore 0:
  9.6 49.0 all-gather.3
  70.9 46.1 all-gather.5
  118.7 58.8 all-gather.7
  561.6 56.6 reduce-scatter.1

commit v4 on v3

--- a/solution.py
+++ b/solution.py
@@ -29,6 +29,12 @@
     rows = lax.broadcasted_iota(jnp.int32, (BLOCK, BLOCK), 0)
     cols = lax.broadcasted_iota(jnp.int32, (BLOCK, BLOCK), 1)
     return rows, cols
+
+
+def lockstep(tasks):
+    tasks = list(tasks)
+    while tasks:
+        tasks = [task for task in tasks if next(task, None) is not None]
 
 
 def strengths(u, r_col):
@@ -184,58 +190,77 @@
         def _():
             i = j + d
             there = pl.ds(pl.multiple_of(i * BLOCK, BLOCK), BLOCK)
-            for h in range(heads):
+            def far(h):
                 cs = slice(h * BLOCK, (h + 1) * BLOCK)
                 dop = dop_ref[there, cs]
                 e = e_refs[d][0, 0, h]
                 dp = mm_rt(dop, v_ref[:, cs])
+                yield 1
+                dv_ref[h] = dv_ref[h] + mm_lt(e, dop)
+                yield 1
                 ds = (e.astype(f32) * (dp - del_ref[there, cs]) * scale).astype(bf16)
-                dv_ref[h] = dv_ref[h] + mm_lt(e, dop)
                 dsg = jnp.concatenate([ds, g_ref[i, h]], axis=1)
+                yield 1
                 acc_ref[h] = acc_ref[h] + mm_lt(cur_refs[d - 1][0, 0, h], dsg)
+                yield 1
                 g_ref[i, h] = mm_rt(dsg, kp_ref[0, h]).astype(bf16)
+
+            lockstep(far(h) for h in range(heads))
 
     lane = cols
     dr_all = jnp.zeros((BLOCK, BLOCK), f32)
     width = heads * BLOCK
-    for h in range(heads):
+    drs = {}
+
+    def local_part(h):
         cs = slice(h * BLOCK, (h + 1) * BLOCK)
         q, k, u = q_ref[:, cs], k_ref[:, cs], u_ref[:, cs]
-        beta, inv_sq = strengths(u, r_ref[:, h : h + 1].astype(f32))
-        bp = beta * inv_sq
         kq = mm_rt(u, jnp.concatenate([k, q], axis=0))
+        yield 1
         e_s = jnp.where(strict, kq[:, :BLOCK], 0.0).astype(bf16)
         a_t = jnp.where(upper, kq[:, BLOCK:], 0.0).astype(bf16)
         dn = near[h]
-        dq = g_ref[j, h]
         acc = acc_ref[h]
-        bmat = jnp.concatenate([jnp.concatenate([dn, dq], axis=1), acc.astype(bf16)], axis=0)
+        bmat = jnp.concatenate([jnp.concatenate([dn, g_ref[j, h]], axis=1), acc.astype(bf16)], axis=0)
         yz = mm(jnp.concatenate([a_t, u], axis=1), bmat).astype(bf16)
+        yield 1
         ru = mm_rt(jnp.concatenate([e_s, u], axis=1), bmat)
+        beta, inv_sq = strengths(u, r_ref[:, h : h + 1].astype(f32))
+        bp = beta * inv_sq
+        yield 1
         inv = inv_ref[0, h]
         left = mm_lt(inv, yz) * (-bp)
+        yield 1
         right = -mm(inv, (ru * bp).astype(bf16))
+        yield 1
         d_s = jnp.where(strict, -mm_rt(left.astype(bf16), t_ref[0, h]), 0.0).astype(bf16)
         d_e = jnp.where(strict, left[:, :BLOCK], 0.0).astype(bf16)
         d_at = jnp.where(upper, right[:, :BLOCK], 0.0).astype(bf16)
+        du = left[:, BLOCK:] + right[:, BLOCK:]
+        yield 1
         d_a = d_at.astype(f32).T.astype(bf16)
         uk = jnp.concatenate([u, k], axis=0)
+        dq_o = g_ref[j, h].astype(f32) + mm(jnp.concatenate([d_a, dn], axis=1), uk)
+        out_ref[:, cs] = dq_o.astype(bf16)
+        yield 1
         uq = jnp.concatenate([u, q], axis=0)
-        du = left[:, BLOCK:] + right[:, BLOCK:]
+        dk_o = acc_ref[h][:, :BLOCK].T + mm_lt(jnp.concatenate([d_e, dn], axis=0), uq)
+        out_ref[:, width + h * BLOCK : width + (h + 1) * BLOCK] = dk_o.astype(bf16)
+        yield 1
         du = du + mm(jnp.concatenate([d_s, d_e], axis=1), uk)
         d_st = d_s.astype(f32).T.astype(bf16)
         du = du + mm(jnp.concatenate([d_st, d_at], axis=1), uq)
-        dq_o = dq.astype(f32) + mm(jnp.concatenate([d_a, dn], axis=1), uk)
-        dk_o = acc[:, :BLOCK].T + mm_lt(jnp.concatenate([d_e, dn], axis=0), uq)
+        yield 1
         uf = u.astype(f32)
         rad = jnp.sum(uf * du, axis=1, keepdims=True)
         du = du - (inv_sq * rad) * uf
-        dr = 0.5 * rad * (1.0 - 0.5 * beta)
-        dr_all = jnp.where(lane == h, dr, dr_all)
-        out_ref[:, cs] = dq_o.astype(bf16)
-        out_ref[:, width + h * BLOCK : width + (h + 1) * BLOCK] = dk_o.astype(bf16)
+        drs[h] = 0.5 * rad * (1.0 - 0.5 * beta)
         out_ref[:, 2 * width + h * BLOCK : 2 * width + (h + 1) * BLOCK] = dv_ref[h].astype(bf16)
         out_ref[:, 3 * width + h * BLOCK : 3 * width + (h + 1) * BLOCK] = du.astype(bf16)
+
+    lockstep(local_part(h) for h in range(heads))
+    for h in range(heads):
+        dr_all = jnp.where(lane == h, drs[h], dr_all)
     out_ref[:, 4 * width :] = dr_all.astype(bf16)
 
 
@@ -414,38 +439,66 @@
     )(tables.reshape(-1), *([x] * (group * streams)))
 
 
-def pick_kernel(bounds, table_ref, *refs):
-    at = table_ref[pl.program_id(0)]
-    for n, (low, high) in enumerate(bounds):
-
-        @pl.when((at >= low) & (at < high))
-        def _():
-            refs[-1][...] = refs[n][...]
-
-
-def pick_blocks(parts, table):
-    cols = parts[0].shape[1]
-    bounds, low = [], 0
-    for part in parts:
-        bounds.append((low, low + part.shape[0] // BLOCK))
-        low = bounds[-1][1]
-
-    def source(low, high):
-        return pl.BlockSpec((BLOCK, cols), lambda i, t: (jnp.clip(t[i] - low, 0, high - low - 1), 0))
-
+def pick_kernel(bounds, picks, table_ref, *refs):
+    total = sum(len(part) for part in bounds)
+    parts, outs = refs[:total], refs[total:-3]
+    held, load_sem, store_sem = refs[-3:]
+    stores = []
+    base = 0
+    for group, limits in enumerate(bounds):
+        for n in range(picks):
+            slot = group * picks + n
+            at = table_ref[slot]
+            for p, (low, high) in enumerate(limits):
+
+                @pl.when((at >= low) & (at < high))
+                def _():
+                    rows = pl.ds(pl.multiple_of((at - low) * BLOCK, BLOCK), BLOCK)
+                    pltpu.make_async_copy(parts[base + p].at[rows, :], held.at[slot], load_sem.at[slot]).start()
+
+        base += len(limits)
+    for group in range(len(bounds)):
+        for n in range(picks):
+            slot = group * picks + n
+            rows = pl.ds(n * BLOCK, BLOCK)
+            pltpu.make_async_copy(outs[group].at[rows, :], held.at[slot], load_sem.at[slot]).wait()
+            stores.append(pltpu.make_async_copy(held.at[slot], outs[group].at[rows, :], store_sem.at[slot]))
+            stores[-1].start()
+    for store in stores:
+        store.wait()
+
+
+def pick_blocks(groups, tables):
+    picks = tables[0].shape[0]
+    cols = groups[0][0].shape[1]
+    dtype = groups[0][0].dtype
+    bounds = []
+    for parts in groups:
+        limits, low = [], 0
+        for part in parts:
+            limits.append((low, low + part.shape[0] // BLOCK))
+            low = limits[-1][1]
+        bounds.append(limits)
+    flat = [part for parts in groups for part in parts]
+    slots = picks * len(groups)
     spec = pltpu.PrefetchScalarGridSpec(
         num_scalar_prefetch=1,
-        grid=(table.shape[0],),
-        in_specs=[source(*bound) for bound in bounds],
-        out_specs=pl.BlockSpec((BLOCK, cols), lambda i, t: (i, 0)),
+        grid=(1,),
+        in_specs=[pl.BlockSpec(memory_space=pl.ANY)] * len(flat),
+        out_specs=[pl.BlockSpec(memory_space=pl.ANY)] * len(groups),
+        scratch_shapes=[
+            pltpu.VMEM((slots, BLOCK, cols), dtype),
+            pltpu.SemaphoreType.DMA((slots,)),
+            pltpu.SemaphoreType.DMA((slots,)),
+        ],
     )
     return pl.pallas_call(
-        functools.partial(pick_kernel, bounds),
+        functools.partial(pick_kernel, bounds, picks),
         grid_spec=spec,
-        out_shape=jax.ShapeDtypeStruct((table.shape[0] * BLOCK, cols), parts[0].dtype),
-        cost_estimate=pl.CostEstimate(flops=0, bytes_accessed=4 * table.shape[0] * BLOCK * cols, transcendentals=0),
+        out_shape=[jax.ShapeDtypeStruct((picks * BLOCK, cols), dtype)] * len(groups),
+        cost_estimate=pl.CostEstimate(flops=0, bytes_accessed=4 * slots * BLOCK * cols, transcendentals=0),
         name="pick_blocks",
-    )(table, *parts)
+    )(jnp.concatenate(tables).astype(jnp.int32), *flat)
 
 
 def place_kernel(count, rows, spot_ref, *refs):
@@ -628,6 +681,137 @@
         while self.done < self.top:
             self.hop()
         return self.piece(0).astype(f32) + self.moving[0].astype(f32) + self.moving[1].astype(f32)
+
+
+def ring_kernel(axis, count, rows, widths, *refs):
+    held = len(widths)
+    parts, outs = refs[:held], refs[held : 2 * held]
+    own_buf, send_buf, recv_buf, load_sem, send_sem, recv_sem = refs[2 * held :]
+    me = lax.axis_index(axis)
+    odd = me % 2
+    spot = (1 - odd) * (me // 2) + odd * (count - 1 - me // 2)
+
+    def owner(shift):
+        at = (spot + shift + count) % count
+        upper = at // (count // 2)
+        return (1 - upper) * (2 * at) + upper * (2 * (count - 1 - at) + 1)
+
+    top = count // 2
+    cut = rows // 32 * 16
+    ways = ((1, owner(1)), (-1, owner(-1)))
+    barrier = pltpu.get_barrier_semaphore()
+    for _, peer in ways:
+        pl.semaphore_signal(barrier, inc=1, device_id={axis: peer}, device_id_type=pl.DeviceIdType.MESH)
+
+    def load(shift, slot):
+        copies = []
+        at = pl.multiple_of(owner(shift) * rows, rows)
+        col = 0
+        for n, width in enumerate(widths):
+            copies.append(
+                pltpu.make_async_copy(
+                    parts[n].at[pl.ds(at, rows), :],
+                    own_buf.at[slot, :, pl.ds(col, width)],
+                    load_sem.at[slot, n],
+                )
+            )
+            col += width
+        for copy in copies:
+            copy.start()
+        return copies
+
+    slots = {top: 0, 0: 2 * top - 1}
+    for s in range(1, top):
+        slots[s], slots[-s] = 2 * s - 1, 2 * s
+    loads = {}
+    for shift in [top] + [t * s for s in range(top - 1, 0, -1) for t in (1, -1)] + [0]:
+        loads[shift] = load(shift, slots[shift])
+    for copy in loads[top]:
+        copy.wait()
+    pl.semaphore_wait(barrier, 2)
+    halves = ((0, cut), (cut, rows - cut))
+    sent = []
+
+    def push(way, hop, part, src):
+        start, size = halves[part]
+        copy = pltpu.make_async_remote_copy(
+            src_ref=src,
+            dst_ref=recv_buf.at[way, hop, pl.ds(start, size), :],
+            send_sem=send_sem.at[way, hop, part],
+            recv_sem=recv_sem.at[way, hop, part],
+            device_id={axis: ways[way][1]},
+            device_id_type=pl.DeviceIdType.MESH,
+        )
+        copy.start()
+        sent.append(copy)
+        return copy
+
+    flying = {}
+    for way in range(2):
+        start, size = halves[way]
+        flying[way, way] = push(way, 0, way, own_buf.at[slots[top], pl.ds(start, size), :])
+    for hop in range(1, top):
+        shift = top - hop
+        order = [(way, 1 - way) for way in range(2)] + [(way, way) for way in range(2)]
+        for way, part in order:
+            sign = ways[way][0]
+            start, size = halves[part]
+            slot = slots[sign * shift]
+            if part == 1 - way:
+                for copy in loads[sign * shift]:
+                    copy.wait()
+            area = pl.ds(start, size)
+            if hop == 1 and part == 1 - way:
+                flying[way, part] = push(way, hop, part, own_buf.at[slot, area, :])
+                continue
+            flying[way, part].wait_recv()
+            total = own_buf[slot, area, :].astype(f32) + recv_buf[way, hop - 1, area, :].astype(f32)
+            send_buf[way, hop - 1, area, :] = total.astype(bf16)
+            flying[way, part] = push(way, hop, part, send_buf.at[way, hop - 1, area, :])
+    for copy in loads[0]:
+        copy.wait()
+    for part in range(2):
+        start, size = halves[part]
+        area = pl.ds(start, size)
+        for way in range(2):
+            flying[way, part].wait_recv()
+        col = 0
+        for n, width in enumerate(widths):
+            cols = pl.ds(col, width)
+            outs[n][area, :] = (
+                own_buf[slots[0], area, cols].astype(f32)
+                + recv_buf[0, top - 1, area, cols].astype(f32)
+                + recv_buf[1, top - 1, area, cols].astype(f32)
+            )
+            col += width
+    for copy in sent:
+        copy.wait_send()
+
+
+def ring_sum(parts, axis):
+    count = lax.axis_size(axis)
+    rows = parts[0].shape[0] // count
+    widths = [part.shape[1] for part in parts]
+    cols = sum(widths)
+    top = count // 2
+    sent = (2 * top - 1) * rows * cols * 2
+    return pl.pallas_call(
+        functools.partial(ring_kernel, axis, count, rows, widths),
+        in_specs=[pl.BlockSpec(memory_space=pl.ANY)] * len(parts),
+        out_specs=[pl.BlockSpec(memory_space=pltpu.VMEM)] * len(parts),
+        out_shape=[jax.ShapeDtypeStruct((rows, width), f32) for width in widths],
+        scratch_shapes=[
+            pltpu.VMEM((count, rows, cols), bf16),
+            pltpu.VMEM((2, top - 1, rows, cols), bf16),
+            pltpu.VMEM((2, top, rows, cols), bf16),
+            pltpu.SemaphoreType.DMA((count, len(parts))),
+            pltpu.SemaphoreType.DMA((2, top, 2)),
+            pltpu.SemaphoreType.DMA((2, top, 2)),
+        ],
+        compiler_params=pltpu.CompilerParams(collective_id=0, has_side_effects=True),
+        cost_estimate=pl.CostEstimate(flops=0, bytes_accessed=4 * count * rows * cols, transcendentals=0),
+        name="ring_sum",
+    )(*parts)
 
 
 def tp_sum(x):
@@ -725,19 +909,22 @@
         [w_beta, gain_attn[:, None], gain_ffn[:, None], jnp.zeros((shard, BLOCK - heads - 2), bf16)], axis=1
     )
     attn_pack = jnp.concatenate([w_query, w_key, w_value, w_house, extras], axis=1)
-    ffn_pack = jnp.concatenate([w_gate, w_up, w_down], axis=1)
+    ffn_pack = jnp.concatenate([w_gate, w_up], axis=1)
     full_tokens = lax.all_gather(tokens, "tp", axis=0, tiled=True)
     attn_ring = RingGather(attn_pack, "fsdp")
     attn_ring.hop()
     table, first, last, slot, slotted, own_places, own_spots = attn_ring.before(*tables)
     while len(attn_ring.hops) < attn_ring.count // 2 - 1:
         attn_ring.hop()
-    full_tokens, out_shard, cotangent = attn_ring.before(full_tokens, w_out, cotangent)
-    w_in, ffn_pack, out_shard, cotangent = together(attn_ring.finish(), ffn_pack, out_shard, cotangent)
+    full_tokens, out_shard, down_shard, cotangent = attn_ring.before(full_tokens, w_out, w_down, cotangent)
+    w_in, ffn_pack, out_shard, down_shard, cotangent = together(
+        attn_ring.finish(), ffn_pack, out_shard, down_shard, cotangent
+    )
     ffn_ring = RingGather(ffn_pack, "fsdp", True)
     ffn_ring.hop()
     x_rows = gather_blocks(full_tokens, slotted[:, :per_half], per_half)
     full_out = lax.all_gather(out_shard, "fsdp", axis=0, tiled=True)
+    full_down = lax.all_gather(down_shard, "fsdp", axis=0, tiled=True)
     full_cot = lax.all_gather(cotangent, "tp", axis=0, tiled=True)
     pick = (jnp.arange(BLOCK)[None, :] == heads + jnp.arange(8)[:, None]).astype(bf16)
     gain_rows = cols_contract(pick, w_in[:, 4 * width :])
@@ -789,7 +976,7 @@
     cot_rows = list(gather_blocks(full_cot, slotted, 4))
 
     full_gate, full_up = ffn_full[:, :hidden_width], ffn_full[:, hidden_width : 2 * hidden_width]
-    full_gate_up, full_down = ffn_full[:, : 2 * hidden_width], ffn_full[:, 2 * hidden_width :]
+    full_gate_up = ffn_full
     hidden, gate_up, back = [], [], []
 
     def ffn(m, rows, middle):
@@ -838,26 +1025,23 @@
     rows, dh_own, dh_far = together(ffn_back_rows(1), dh_own, dh_far)
     back_own, back_far = share(rows)
     back_own, normed_two[0], normed_two[1] = together(back_own, *normed_two)
-    grads_in = sum(rows_contract(normed_two[m], gate_up[m]) for m in streams)
-    grads_in, dh_far = together(grads_in.astype(bf16), dh_far)
+    grads_down = sum(rows_contract(cot_rows[m], hidden[m]) for m in streams)
+    grads_down, dh_far, gate_up[0], gate_up[1] = together(grads_down.astype(bf16), dh_far, *gate_up)
+    sum_down = lax.psum_scatter(grads_down, "fsdp", scatter_dimension=0, tiled=True)
     pair = jnp.concatenate([dh_own, dh_far], axis=0)
     grad_attn.append(jnp.concatenate([pair, beside(pair)], axis=0))
-    grads_down = sum(rows_contract(cot_rows[m], hidden[m]) for m in streams).astype(bf16)
-    grads_down, back_far = together(grads_down, back_far)
-    ffn_back = RingScatter([grads_in, grads_down], "fsdp")
-    ffn_back.hop()
+    grads_in = sum(rows_contract(normed_two[m], gate_up[m]) for m in streams)
+    grads_in, back_far = together(grads_in.astype(bf16), back_far)
+    sum_in = lax.psum_scatter(grads_in, "fsdp", scatter_dimension=0, tiled=True)
     dh_own = close_back(1, back_own, back_far)
     dh_far = across(dh_own)
     hidden[0], hidden[1], dh_own = together(*hidden, dh_own)
-    y_parts = list(ffn_back.before(*[cols_contract(hidden[m], full_down).astype(bf16) for m in streams]))
-    ffn_back.hop()
-    ffn_parts = [share(part) for part in y_parts]
+    ffn_parts = [share(cols_contract(hidden[m], full_down).astype(bf16)) for m in streams]
     d_mixed = jnp.dot(grad_attn[0], full_out, preferred_element_type=f32).astype(bf16)
     y_own, y_far = [p[0] for p in ffn_parts], [p[1] for p in ffn_parts]
     d_mixed, y_own[0], y_own[1] = together(d_mixed, *y_own)
     d_proj = attention_bwd(proj, preps[0], saved[0], d_mixed, last[0], table[0], slot, heads, None)
-    d_proj, dh_far, y_far[0], y_far[1] = ffn_back.before(d_proj, dh_far, *y_far)
-    ffn_back.hop()
+    d_proj, dh_far, y_far[0], y_far[1] = together(d_proj, dh_far, *y_far)
     pair = jnp.concatenate([dh_own, dh_far], axis=0)
     grad_attn.append(jnp.concatenate([pair, beside(pair)], axis=0))
     d_mixed = jnp.dot(grad_attn[1], full_out, preferred_element_type=f32).astype(bf16)
@@ -868,29 +1052,26 @@
     d_mixed, grad_out, y_rows = together(d_mixed, grad_out, y_rows)
     y_across = across(y_rows)
     d_proj = attention_bwd(proj, preps[1], saved[1], d_mixed, last[1], table[1], slot, heads, d_proj)
-    d_proj, y_across = ffn_back.before(d_proj, y_across)
-    ffn_back.hop()
+    d_proj, sum_down = together(d_proj, sum_down)
     attn_grads, d_proj, y_rows = together(rows_contract(normed, d_proj).astype(bf16), d_proj, y_rows)
-    attn_back = RingScatter([attn_grads, grad_out], "fsdp")
-    attn_back.hop()
     y_pair = jnp.concatenate([y_rows, y_across], axis=0)
-    rows_one, y_other = attn_back.before(cols_contract(d_proj, w_in).astype(bf16), beside(y_pair))
-    grad_one = lax.psum_scatter(rows_one, "tp", scatter_dimension=0, tiled=True).astype(f32)
-    ffn_sum = ffn_back.finish()
-    attn_back.hop()
-    ffn_sum = attn_back.before(ffn_sum)
-    attn_back.hop()
-    out_y = pick_blocks([y_rows, y_across, y_other], own_spots)
-    grad_one = attn_back.before(grad_one)
-    attn_sum = attn_back.finish()
+    rows_one, y_other, attn_grads, sum_in = together(
+        cols_contract(d_proj, w_in).astype(bf16), beside(y_pair), attn_grads, sum_in
+    )
+    grad_one = lax.psum_scatter(rows_one, "tp", scatter_dimension=0, tiled=True)
+    dh_own, out_y = pick_blocks([grad_attn, [y_rows, y_across, y_other]], [own_places, own_spots])
+    attn_grads, dh_own, out_y = together(attn_grads, dh_own, out_y)
+    attn_sum, grad_out = ring_sum([attn_grads, grad_out], "fsdp")
+    sum_in, sum_down = sum_in.astype(f32), sum_down.astype(f32)
+    grad_one = grad_one.astype(f32)
     unit_one, scale_one = unit_rows(tokens.astype(f32))
     norm_one_grad = norm_back(grad_one, unit_one, scale_one, gain_one)
-    out_dx = (pick_blocks(grad_attn, own_places).astype(f32) + norm_one_grad).astype(bf16)
+    out_dx = (dh_own.astype(f32) + norm_one_grad).astype(bf16)
     dots = lambda grads, weights: jnp.sum(grads * weights.astype(f32), axis=1)
     own_one = dots(attn_sum[:, : 4 * width], attn_pack[:, : 4 * width]) + dots(
         attn_sum[:, 4 * width : 4 * width + heads], w_beta
     )
-    own_two = dots(ffn_sum[:, : 2 * hidden_width], ffn_pack[:, : 2 * hidden_width])
+    own_two = dots(sum_in, ffn_pack)
     gains = tp_sum(jnp.stack([own_one, own_two])) / jnp.stack([gain_attn, gain_ffn]).astype(f32)
     return (
         out_y,
@@ -900,10 +1081,10 @@
         attn_sum[:, 2 * width : 3 * width],
         attn_sum[:, 3 * width : 4 * width],
         attn_sum[:, 4 * width : 4 * width + heads],
-        attn_sum[:, 4 * width + BLOCK :],
-        ffn_sum[:, :hidden_width],
-        ffn_sum[:, hidden_width : 2 * hidden_width],
-        ffn_sum[:, 2 * hidden_width :],
+        grad_out,
+        sum_in[:, :hidden_width],
+        sum_in[:, hidden_width:],
+        sum_down,
         gains[0],
         gains[1],
     )

time: 679 us -> 656 us (0.966)
  Pallas kernels: 167 us -> 206 us
  starting transfers between devices: 59.9 us -> 32.6 us
  waiting for transfers between devices: 125 us -> 106 us
  local copies, waits for them, and re-layouts: 76.8 us -> 62.4 us
    pallas_call x2, Pallas kernels: 9.13 us -> 71.3 us  [the longest x1 67.8 us: ring_sum(): pl.pallas_call(functools.partial(ring_kernel, axis, count, rows, widths),...]
    ppermute x16 -> x0, waiting for transfers between devices: 58.6 us -> none  [the longest x8 31.9 us: hop(): lax.ppermute(to_right, self.axis, self.right)]
    ppermute x11, waiting for transfers between devices: 22.2 us -> 60.4 us  [across(): return lax.ppermute(x, 'tp', [(i, i ^ 2) for i in range(4)])]
    ppermute x16 -> x0, starting transfers between devices: 26.7 us -> none  [the longest x8 22 us: hop(): lax.ppermute(to_left, self.axis, self.left)]
    pallas_call x2, Pallas kernels: 74.5 us -> 53.2 us  [attention_bwd(): pl.pallas_call(functools.partial(bwd_kernel, heads, depth, scale), grid_s...]
    add x12 -> x0, other arithmetic: 16.6 us -> none  [the longest x8 14.1 us: hop(): to_right, to_left = (a + to_right, b + to_left)]
    dynamic_slice x8 -> x0, local copies, waits for them, and re-layouts: 12.7 us -> none  [piece(): lax.dynamic_slice_in_dim(part, at, size, 0)]
    ppermute x8, starting transfers between devices: 15.9 us -> 4.32 us  [hop(): lax.ppermute(from_left, self.axis, self.right)]
  transfers between devices with their start and end apart: 61 -> 48, of which waited for: 25 -> 14; matrix products, arithmetic and copies ran while one was open for 37% -> 40% of each run, Pallas kernels for 25% -> 32%
where the time goes in v4:
time: 656 us; the launch traced here: 644 us
  Pallas kernels  206 us (31%)
  matrix products  170 us (26%)
  waiting for transfers between devices  106 us (16%)
  local copies, waits for them, and re-layouts  62.4 us (10%)
  other arithmetic  50.6 us (8%)
  starting transfers between devices  32.6 us (5%)
  between operations  16 us (2%)
    pallas_call x1, Pallas kernels, ring_sum(): pl.pallas_call(functools.partial(ring_kernel, axis, count, rows, widths),...  67.8 us
    ppermute x11, waiting for transfers between devices, across(): return lax.ppermute(x, 'tp', [(i, i ^ 2) for i in range(4)])  60.4 us
    dot_general x7, matrix products, rows_contract(): lax.dot_general(a, b, (((0,), (0,)), ((), ())), preferred_element_type=f32)  55.3 us
    pallas_call x2, Pallas kernels, attention_bwd(): pl.pallas_call(functools.partial(bwd_kernel, heads, depth, scale), grid_s...  53.2 us
    dot_general x8, matrix products, cols_contract(): lax.dot_general(a, b, (((1,), (1,)), ((), ())), preferred_element_type=f32)  45.3 us
    pallas_call x2, Pallas kernels, attention_prep(): pl.pallas_call(functools.partial(prep_kernel, heads, step), grid_spec=spe...  34.3 us
    pallas_call x2, Pallas kernels, attention_fwd(): pl.pallas_call(functools.partial(fwd_kernel, heads, depth, scale), grid_s...  31.2 us
    ppermute x8, waiting for transfers between devices, hop(): lax.ppermute(from_left, self.axis, self.right)  26.5 us
  transfers between devices with their start and end apart: 48, of which 14 were waited for; matrix products, arithmetic and copies ran while one was open for 40% of the time, Pallas kernels for 32%

profile of v4, /device:TPU:0, one launch (start us, length us, event | category | flops | bytes accessed | tf_op | source)
XLA Modules:
  0.0 643.5 jit_solution(15266580950917525311)
XLA Ops:
  18.8 10.3 %collective-permute-done.1 = bf16[192,1664]{1,0:T(8,128)(2,1)S(1)} collective-permute-done((bf16[192,1664]{1,0:T(8,128)(2,1)S(1)}, bf16[192,1664]{1,0:T(8,128)(2,1)S(1)}, u32[]{:S(2)}, u32[]{:S(2)}) %collective-permute-start.1) | collective-permute-done | bytes 639008 | tf_op jit(solution)/shard_map/ppermute | solution.py:616
  36.4 9.1 %collective-permute-done.2 = bf16[192,1664]{1,0:T(8,128)(2,1)S(1)} collective-permute-done((bf16[192,1664]{1,0:T(8,128)(2,1)S(1)}, bf16[192,1664]{1,0:T(8,128)(2,1)S(1)}, u32[]{:S(2)}, u32[]{:S(2)}) %collective-permute-start.2) | collective-permute-done | bytes 639008 | tf_op jit(solution)/shard_map/ppermute | solution.py:615
  51.3 8.4 %collective-permute-done.3 = bf16[192,1664]{1,0:T(8,128)(2,1)S(1)} collective-permute-done((bf16[192,1664]{1,0:T(8,128)(2,1)S(1)}, bf16[192,1664]{1,0:T(8,128)(2,1)S(1)}, u32[]{:S(2)}, u32[]{:S(2)}) %collective-permute-start.3) | collective-permute-done | bytes 639008 | tf_op jit(solution)/shard_map/ppermute | solution.py:615
  64.7 5.0 collective-permute-done.6
  80.2 16.3 %convolution_convert_fusion.refs_0_.refs_1_.refs_2_.refs_3_.refs_4_.refs_5_.refs_6_.refs_7_.v_ref = bf16[2048,1664]{1,0:T(8,128)(2,1)} fusion(bf16[1536,1664]{1,0:T(8,128)(2,1)} %constant_dynamic-update-slice_fusion.14, bf16[2048,1536]{1,0:T(8,128)(2,1)S(1)} %copy-done, f32[1536]{0:T(1024)S(1)} %get-tuple-element.277, f32[2048]{0:T(1024)S(1)} %add_rsqrt_fusion), kind=kOutput, calls=%fused_computation.6 | convolution fusion | flops 10484973568 | bytes 18233344 | tf_op jit(solution)/shard_map/dot_general | solution.py:935
  96.5 17.1 %attn_prep.2 = (f32[8,3,128,128]{3,2,1,0:T(8,128)}, bf16[1024,384]{1,0:T(8,128)(2,1)}, bf16[8,3,128,256]{3,2,1,0:T(8,128)(2,1)}, bf16[8,3,128,128]{3,2,1,0:T(8,128)(2,1)}, bf16[8,3,128,256]{3,2,1,0:T(8,128)(2,1)}) custom-call(s32[8]{0:T(128)} %get-tuple-element.312.table_ref, ...), custom_call_target="tpu_custom_call" | custom-call | flops 2264924160 | bytes 2359296 | tf_op jit(solution)/shard_map/attn_prep/pallas_call | solution.py:290
  116.5 18.8 %attn_fwd.2 = (bf16[1024,384]{1,0:T(8,128)(2,1)}, f32[1024,384]{1,0:T(8,128)}, bf16[8,8,3,128,128]{4,3,2,1,0:T(8,128)(2,1)}, bf16[8,7,3,128,128]{4,3,2,1,0:T(8,128)(2,1)}) custom-call(s32[8]{0:T(128)} %get-tuple-element.311.first_ref, s32[8]{0:T(128)} %get-tuple-element.312.table_ref, s32[8]{0:T(128)} %copy-done.54, ...), custom_call_target="tpu_custom_call" | custom-call | flops 2415919104 | bytes 2359296 | tf_op jit(solution)/shard_map/attn_fwd/pallas_call | solution.py:334
  148.1 17.1 %attn_prep.3 = (f32[8,3,128,128]{3,2,1,0:T(8,128)}, bf16[1024,384]{1,0:T(8,128)(2,1)}, bf16[8,3,128,256]{3,2,1,0:T(8,128)(2,1)}, bf16[8,3,128,128]{3,2,1,0:T(8,128)(2,1)}, bf16[8,3,128,256]{3,2,1,0:T(8,128)(2,1)}) custom-call(s32[8]{0:T(128)} %get-tuple-element.313.table_ref, ...), custom_call_target="tpu_custom_call" | custom-call | flops 2264924160 | bytes 2359296 | tf_op jit(solution)/shard_map/attn_prep/pallas_call | solution.py:290
  165.2 11.2 %collective-permute-done.15 = bf16[256,1536]{1,0:T(8,128)(2,1)} collective-permute-done((bf16[256,1536]{1,0:T(8,128)(2,1)}, bf16[256,1536]{1,0:T(8,128)(2,1)}, u32[]{:S(2)}, u32[]{:S(2)}) %collective-permute-start.15) | collective-permute-done | bytes 786464 | tf_op jit(solution)/shard_map/ppermute | solution.py:833
  178.8 12.5 %attn_fwd.3 = (bf16[1024,384]{1,0:T(8,128)(2,1)}, f32[1024,384]{1,0:T(8,128)}, bf16[8,8,3,128,128]{4,3,2,1,0:T(8,128)(2,1)}, bf16[8,7,3,128,128]{4,3,2,1,0:T(8,128)(2,1)}) custom-call(s32[8]{0:T(128)} %get-tuple-element.310.first_ref, s32[8]{0:T(128)} %get-tuple-element.313.table_ref, s32[8]{0:T(128)} %copy-done.54, ...), custom_call_target="tpu_custom_call" | custom-call | flops 2415919104 | bytes 2359296 | tf_op jit(solution)/shard_map/attn_fwd/pallas_call | solution.py:334
  191.3 6.5 %collective-permute-done.16 = bf16[256,1536]{1,0:T(8,128)(2,1)S(1)} collective-permute-done((bf16[256,1536]{1,0:T(8,128)(2,1)S(1)}, bf16[256,1536]{1,0:T(8,128)(2,1)S(1)}, u32[]{:S(2)}, u32[]{:S(2)}) %collective-permute-start.16) | collective-permute-done | bytes 786464 | tf_op jit(solution)/shard_map/ppermute | solution.py:833
  216.9 5.5 place_pieces.1
  222.5 5.4 gather_blocks.3
  232.2 5.2 collective-permute-done.20
  241.8 8.4 %fusion.16 = f32[1024,1024]{0,1:T(8,128)} fusion(bf16[1024,1536]{1,0:T(8,128)(2,1)} %constant_dynamic-update-slice_fusion, bf16[1536,2048]{1,0:T(8,128)(2,1)} %constant_dynamic-update-slice_fusion.12), kind=kOutput, calls=%fused_computation.50 | convolution fusion | flops 3221225472 | bytes 10485760 | tf_op jit(solution)/shard_map/dot_general | solution.py:984
  253.3 8.4 %fusion.39 = f32[1024,1024]{0,1:T(8,128)} fusion(bf16[1024,1536]{1,0:T(8,128)(2,1)} %get-tuple-element.172, bf16[1536,1024]{1,0:T(8,128)(2,1)} %all-gather.11.cloned.1.call-done), kind=kOutput, calls=%fused_computation.207 | convolution fusion | flops 3221225472 | bytes 10485760 | tf_op jit(solution)/shard_map/dot_general | solution.py:987
  261.7 9.8 %multiply_convert_fusion.4 = (bf16[1024,1024]{0,1:T(8,128)(2,1)S(1)}, bf16[1024,1024]{0,1:T(8,128)(2,1)S(1)}, bf16[1024,1024]{0,1:T(8,128)(2,1)}) fusion(f32[1024,1024]{0,1:T(8,128)} %fusion.39, f32[1024,1024]{0,1:T(8,128)} %fusion.16, bf16[1024,1536]{1,0:T(8,128)(2,1)S(1)} %copy-done.47, bf16[1536,2048]{1,0:T(8,128)(2,1)} %constant_dynamic-update-slice_fusion.12), kind=kOutput, calls=%fused_computation.18 | convolution fusion | flops 3236954112 | bytes 20971520 | tf_op jit(solution)/shard_map/dot_general | solution.py:983
  271.6 7.3 %convolution_convert_fusion.4 = bf16[1024,1536]{1,0:T(8,128)(2,1)S(1)} fusion(bf16[1536,2048]{1,0:T(8,128)(2,1)S(1)} %bitcast.69, bf16[1024,1024]{0,1:T(8,128)(2,1)S(1)} %get-tuple-element.293, bf16[1024,1024]{0,1:T(8,128)(2,1)S(1)} %get-tuple-element.292), kind=kOutput, calls=%fused_computation.25 | convolution fusion | flops 6452412416 | bytes 13631488 | tf_op jit(solution)/shard_map/dot_general | solution.py:570
  285.6 5.1 fusion.14
  290.7 12.5 %collective-permute-done.25 = bf16[256,1536]{1,0:T(8,128)(2,1)S(1)} collective-permute-done((bf16[256,1536]{1,0:T(8,128)(2,1)S(1)}, bf16[256,1536]{1,0:T(8,128)(2,1)S(1)}, u32[]{:S(2)}, u32[]{:S(2)}) %collective-permute-start.25) | collective-permute-done | bytes 786464 | tf_op jit(solution)/shard_map/ppermute | solution.py:833
  307.4 5.0 fusion.40
  312.4 8.6 %multiply_convert_fusion.1 = (bf16[1024,1024]{0,1:T(8,128)(2,1)S(1)}, bf16[1024,1024]{0,1:T(8,128)(2,1)S(1)}, bf16[1024,1024]{0,1:T(8,128)(2,1)S(1)}) fusion(f32[1024,1024]{0,1:T(8,128)} %fusion.40, f32[1024,1024]{0,1:T(8,128)} %fusion.14, bf16[1024,1536]{1,0:T(8,128)(2,1)} %copy-done.48, bf16[1536,2048]{1,0:T(8,128)(2,1)S(1)} %bitcast.69), kind=kOutput, calls=%fused_computation.13 | convolution fusion | flops 3236954112 | bytes 20971520 | tf_op jit(solution)/shard_map/dot_general | solution.py:983
  321.0 7.3 %convolution_convert_fusion.3 = bf16[1024,1536]{1,0:T(8,128)(2,1)S(1)} fusion(bf16[1536,2048]{1,0:T(8,128)(2,1)S(1)} %bitcast.69, bf16[1024,1024]{0,1:T(8,128)(2,1)S(1)} %get-tuple-element.290, bf16[1024,1024]{0,1:T(8,128)(2,1)S(1)} %get-tuple-element.289), kind=kOutput, calls=%fused_computation.24 | convolution fusion | flops 6452412416 | bytes 13631488 | tf_op jit(solution)/shard_map/dot_general | solution.py:570
  349.7 9.7 %fusion.42 = f32[1536,2048]{1,0:T(8,128)} fusion(bf16[1024,1536]{1,0:T(8,128)(2,1)S(1)} %copy-done.49, bf16[1024,2048]{0,1:T(8,128)(2,1)S(1)} %copy-done.21), kind=kOutput, calls=%fused_computation.210 | convolution fusion | flops 6442450944 | bytes 19922944 | tf_op jit(solution)/shard_map/dot_general | solution.py:566
  359.4 12.6 %add_convert_fusion = bf16[1536,2048]{1,0:T(8,128)(2,1)} fusion(f32[1536,2048]{1,0:T(8,128)} %fusion.42, bf16[1024,1536]{1,0:T(8,128)(2,1)} %constant_dynamic-update-slice_fusion, bf16[1024,2048]{0,1:T(8,128)(2,1)S(1)} %copy-done.20), kind=kOutput, calls=%fused_computation.5 | convolution fusion | flops 6448742400 | bytes 26214400 | tf_op jit(solution)/shard_map/dot_general | solution.py:566
  409.3 30.9 %attn_bwd.2.refs_26_ = bf16[2048,1664]{1,0:T(8,128)(2,1)} custom-call(s32[8]{0:T(128)} %get-tuple-element.308.last_ref, s32[8]{0:T(128)} %get-tuple-element.312.table_ref, s32[8]{0:T(128)} %copy-done.54, bf16[1024,384]{1,0:T(8,128)(2,1)} %convolution_convert_fusion.10.refs_0_, bf16[1024,384]{1,0:T(8,128)(2,1)} %get-tuple-element.145.refs_1_, ...), custom_call_target="tpu_custom_call" | custom-call | flops 6039797760 | bytes 3145728 | tf_op jit(solution)/shard_map/attn_bwd/pallas_call | solution.py:401
  440.2 12.6 %collective-permute-done.34 = bf16[256,1536]{1,0:T(8,128)(2,1)} collective-permute-done((bf16[256,1536]{1,0:T(8,128)(2,1)}, bf16[256,1536]{1,0:T(8,128)(2,1)}, u32[]{:S(2)}, u32[]{:S(2)}) %collective-permute-start.34) | collective-permute-done | bytes 786464 | tf_op jit(solution)/shard_map/ppermute | solution.py:833
  468.8 22.3 %attn_bwd.3 = bf16[2048,1664]{1,0:T(8,128)(2,1)} custom-call(s32[8]{0:T(128)} %get-tuple-element.309.last_ref, s32[8]{0:T(128)} %get-tuple-element.313.table_ref, s32[8]{0:T(128)} %copy-done.54, bf16[1024,384]{1,0:T(8,128)(2,1)} %convolution_convert_fusion.9.refs_0_, bf16[1024,384]{1,0:T(8,128)(2,1)} %get-tuple-element.164.refs_1_, ...), custom_call_target="tpu_custom_call", output_to_operand_aliasing={{}: (29, {})} | custom-call | flops 6039797760 | bytes 3145728 | tf_op jit(solution)/shard_map/attn_bwd/pallas_call | solution.py:401
  492.0 18.0 %convolution_convert_fusion.2.refs_0_ = bf16[1536,1664]{1,0:T(8,128)(2,1)} fusion(bf16[2048,1664]{1,0:T(8,128)(2,1)} %attn_bwd.3, bf16[2048,1536]{1,0:T(8,128)(2,1)} %all-gather.5.cloned.1.call-done.refs_0_.refs_1_.refs_2_.refs_3_, f32[1536]{0:T(1024)S(1)} %copy-done.51, f32[2048]{0:T(1024)S(1)} %copy-done.57), kind=kOutput, calls=%fused_computation.8 | convolution fusion | flops 10484121600 | bytes 18233344 | tf_op jit(solution)/shard_map/dot_general | solution.py:566
  510.0 17.6 %collective-permute-done.36.refs_3_ = bf16[512,1536]{1,0:T(8,128)(2,1)S(1)} collective-permute-done((bf16[512,1536]{1,0:T(8,128)(2,1)S(1)}, bf16[512,1536]{1,0:T(8,128)(2,1)S(1)}, u32[]{:S(2)}, u32[]{:S(2)}) %collective-permute-start.36) | collective-permute-done | bytes 1572896 | tf_op jit(solution)/shard_map/ppermute | solution.py:833
  529.9 15.4 %convolution_convert_fusion.1 = bf16[2048,1536]{1,0:T(8,128)(2,1)} fusion(bf16[2048,1664]{1,0:T(8,128)(2,1)S(1)} %copy-done.5, bf16[1536,1664]{1,0:T(8,128)(2,1)} %constant_dynamic-update-slice_fusion.14), kind=kOutput, calls=%fused_computation.7 | convolution fusion | flops 10472128512 | bytes 18219008 | tf_op jit(solution)/shard_map/dot_general | solution.py:570
  553.2 67.8 %ring_sum.1 = (f32[192,1664]{1,0:T(8,128)}, f32[192,384]{1,0:T(8,128)}) custom-call(bf16[1536,1664]{1,0:T(8,128)(2,1)} %convolution_convert_fusion.2.refs_0_, bf16[1536,384]{1,0:T(8,128)(2,1)} %fusion.13.refs_1_), custom_call_target="tpu_custom_call" | custom-call | bytes 12582912 | tf_op jit(solution)/shard_map/ring_sum/pallas_call | solution.py:798
  (398 shorter events, 200.0 us)
Async XLA Ops:
  7.2 53.5 %all-gather.5.cloned.1.call-start = ((), (), s32[]{:S(2)}) async-start(), calls=%async_computation.3 | async-start | bytes 7864320 | tf_op jit(solution)/shard_map/all_gather | solution.py:913
  7.9 127.4 %all-gather.7.cloned.1.call-start = ((), (), s32[]{:S(2)}) async-start(), calls=%async_computation.4 | async-start | bytes 1327104 | tf_op jit(solution)/shard_map/all_gather | solution.py:926
  11.6 17.5 %collective-permute-start.1 = (bf16[192,1664]{1,0:T(8,128)(2,1)S(1)}, bf16[192,1664]{1,0:T(8,128)(2,1)S(1)}, u32[]{:S(2)}, u32[]{:S(2)}) collective-permute-start(bf16[192,1664]{1,0:T(8,128)(2,1)S(1)} %concatenate.55.x_ref), channel_id=1, source_target_pairs={{0,4},{8,0},{16,8},{24,16},{28,24},{20,28},{12,20},{4,12},{1,5},{9... | collective-permute-start | bytes 1916936 | tf_op jit(solution)/shard_map/ppermute | solution.py:616
  14.6 15.8 %collective-permute-start = (bf16[192,1664]{1,0:T(8,128)(2,1)S(1)}, bf16[192,1664]{1,0:T(8,128)(2,1)S(1)}, u32[]{:S(2)}, u32[]{:S(2)}) collective-permute-start(bf16[192,1664]{1,0:T(8,128)(2,1)S(1)} %concatenate.55.x_ref), channel_id=1, source_target_pairs={{0,8},{8,16},{16,24},{24,28},{28,20},{20,12},{12,4},{4,0},{1,9},{9... | collective-permute-start | bytes 1916936 | tf_op jit(solution)/shard_map/ppermute | solution.py:615
  71.2 126.6 %all-gather.9.cloned.1.call-start = ((), (), s32[]{:S(2)}) async-start(), calls=%async_computation.5 | async-start | bytes 7864320 | tf_op jit(solution)/shard_map/all_gather | solution.py:928
  71.9 181.3 %all-gather.11.cloned.1.call-start = ((), (), s32[]{:S(2)}) async-start(), calls=%async_computation.6 | async-start | bytes 3538944 | tf_op jit(solution)/shard_map/all_gather | solution.py:927
  76.8 36.8 %collective-permute-start.9 = (bf16[192,2048]{1,0:T(8,128)(2,1)S(1)}, bf16[192,2048]{1,0:T(8,128)(2,1)S(1)}, u32[]{:S(2)}, u32[]{:S(2)}) collective-permute-start(bf16[192,2048]{1,0:T(8,128)(2,1)S(1)} %pad_maximum_fusion.8.refs_0_), channel_id=1, source_target_pairs={{0,4},{8,0},{16,8},{24,16},{28,24},{20,28},{12,20},{4,12},{1,5},{9... | collective-permute-start | bytes 2359304 | tf_op jit(solution)/shard_map/ppermute | solution.py:616
  78.4 35.3 %collective-permute-start.8 = (bf16[192,2048]{1,0:T(8,128)(2,1)S(1)}, bf16[192,2048]{1,0:T(8,128)(2,1)S(1)}, u32[]{:S(2)}, u32[]{:S(2)}) collective-permute-start(bf16[192,2048]{1,0:T(8,128)(2,1)S(1)} %pad_maximum_fusion.8.refs_0_), channel_id=1, source_target_pairs={{0,8},{8,16},{16,24},{24,28},{28,20},{20,12},{12,4},{4,0},{1,9},{9... | collective-permute-start | bytes 2359304 | tf_op jit(solution)/shard_map/ppermute | solution.py:615
  113.7 24.9 %collective-permute-start.10 = (bf16[192,2048]{1,0:T(8,128)(2,1)S(1)}, bf16[192,2048]{1,0:T(8,128)(2,1)}, u32[]{:S(2)}, u32[]{:S(2)}) collective-permute-start(bf16[192,2048]{1,0:T(8,128)(2,1)S(1)} %collective-permute-done.8.refs_1_), channel_id=1, source_target_pairs={{0,8},{8,16},{16,24},{24,28},{28,20},{20,12},{12,4},{4,0},{1,9},{9... | collective-permute-start | bytes 2359304 | tf_op jit(solution)/shard_map/ppermute | solution.py:615
  114.2 24.4 %collective-permute-start.11 = (bf16[192,2048]{1,0:T(8,128)(2,1)S(1)}, bf16[192,2048]{1,0:T(8,128)(2,1)}, u32[]{:S(2)}, u32[]{:S(2)}) collective-permute-start(bf16[192,2048]{1,0:T(8,128)(2,1)S(1)} %collective-permute-done.9.refs_2_), channel_id=1, source_target_pairs={{0,4},{8,0},{16,8},{24,16},{28,24},{20,28},{12,20},{4,12},{1,5},{9... | collective-permute-start | bytes 2359304 | tf_op jit(solution)/shard_map/ppermute | solution.py:616
  138.8 26.4 %collective-permute-start.12 = (bf16[192,2048]{1,0:T(8,128)(2,1)}, bf16[192,2048]{1,0:T(8,128)(2,1)}, u32[]{:S(2)}, u32[]{:S(2)}) collective-permute-start(bf16[192,2048]{1,0:T(8,128)(2,1)} %collective-permute-done.10.refs_3_), channel_id=1, source_target_pairs={{0,8},{8,16},{16,24},{24,28},{28,20},{20,12},{12,4},{4,0},{1,9},{9... | collective-permute-start | bytes 2359304 | tf_op jit(solution)/shard_map/ppermute | solution.py:615
  138.9 26.3 %collective-permute-start.13 = (bf16[192,2048]{1,0:T(8,128)(2,1)}, bf16[192,2048]{1,0:T(8,128)(2,1)}, u32[]{:S(2)}, u32[]{:S(2)}) collective-permute-start(bf16[192,2048]{1,0:T(8,128)(2,1)} %collective-permute-done.11.refs_4_), channel_id=1, source_target_pairs={{0,4},{8,0},{16,8},{24,16},{28,24},{20,28},{12,20},{4,12},{1,5},{9... | collective-permute-start | bytes 2359304 | tf_op jit(solution)/shard_map/ppermute | solution.py:616
  143.8 32.6 %collective-permute-start.15 = (bf16[256,1536]{1,0:T(8,128)(2,1)}, bf16[256,1536]{1,0:T(8,128)(2,1)}, u32[]{:S(2)}, u32[]{:S(2)}) collective-permute-start(bf16[256,1536]{1,0:T(8,128)(2,1)} %slice.294), channel_id=1, source_target_pairs={{0,2},{1,3},{2,0},{3,1},{4,6},{5,7},{6,4},{7,5},{8,10},{9,11},{10,... | collective-permute-start | bytes 2359304 | tf_op jit(solution)/shard_map/ppermute | solution.py:833
  178.4 19.4 %collective-permute-start.16 = (bf16[256,1536]{1,0:T(8,128)(2,1)S(1)}, bf16[256,1536]{1,0:T(8,128)(2,1)S(1)}, u32[]{:S(2)}, u32[]{:S(2)}) collective-permute-start(bf16[256,1536]{1,0:T(8,128)(2,1)S(1)} %multiply_convert_fusion.7), channel_id=1, source_target_pairs={{0,2},{1,3},{2,0},{3,1},{4,6},{5,7},{6,4},{7,5},{8,10},{9,11},{10,... | collective-permute-start | bytes 2359304 | tf_op jit(solution)/shard_map/ppermute | solution.py:833
  178.7 312.4 %reduce-scatter.4.cloned.1.call-start = ((), (), s32[]{:S(2)}) async-start(), calls=%async_computation.7 | async-start | bytes 3538944 | tf_op jit(solution)/shard_map/reduce_scatter | solution.py:1030
  208.1 29.3 %collective-permute-start.20 = (bf16[96,2048]{1,0:T(8,128)(2,1)S(1)}, bf16[96,2048]{1,0:T(8,128)(2,1)}, u32[]{:S(2)}, u32[]{:S(2)}) collective-permute-start(bf16[96,2048]{1,0:T(8,128)(2,1)S(1)} %slice.196), channel_id=1, source_target_pairs={{0,4},{8,0},{16,8},{24,16},{28,24},{20,28},{12,20},{4,12},{1,5},{9... | collective-permute-start | bytes 1179656 | tf_op jit(solution)/shard_map/ppermute | solution.py:616
  209.6 20.8 %collective-permute-start.19 = (bf16[96,2048]{1,0:T(8,128)(2,1)}, bf16[96,2048]{1,0:T(8,128)(2,1)}, u32[]{:S(2)}, u32[]{:S(2)}) collective-permute-start(bf16[96,2048]{1,0:T(8,128)(2,1)} %slice.195), channel_id=1, source_target_pairs={{0,8},{8,16},{16,24},{24,28},{28,20},{20,12},{12,4},{4,0},{1,9},{9... | collective-permute-start | bytes 1179656 | tf_op jit(solution)/shard_map/ppermute | solution.py:615
  211.8 27.3 %collective-permute-start.17 = (bf16[512,1536]{1,0:T(8,128)(2,1)}, bf16[512,1536]{1,0:T(8,128)(2,1)}, u32[]{:S(2)}, u32[]{:S(2)}) collective-permute-start(bf16[512,1536]{1,0:T(8,128)(2,1)} %pad_maximum_fusion.3), channel_id=1, source_target_pairs={{0,1},{1,0},{2,3},{3,2},{4,5},{5,4},{6,7},{7,6},{8,9},{9,8},{10,11... | collective-permute-start | bytes 4718600 | tf_op jit(solution)/shard_map/ppermute | solution.py:837
  216.6 33.6 %collective-permute-start.21 = (bf16[256,1536]{1,0:T(8,128)(2,1)}, bf16[256,1536]{1,0:T(8,128)(2,1)}, u32[]{:S(2)}, u32[]{:S(2)}) collective-permute-start(bf16[256,1536]{1,0:T(8,128)(2,1)} %slice.293), channel_id=1, source_target_pairs={{0,2},{1,3},{2,0},{3,1},{4,6},{5,7},{6,4},{7,5},{8,10},{9,11},{10,... | collective-permute-start | bytes 2359304 | tf_op jit(solution)/shard_map/ppermute | solution.py:833
  253.2 25.7 %collective-permute-start.22 = (bf16[256,1536]{1,0:T(8,128)(2,1)S(1)}, bf16[256,1536]{1,0:T(8,128)(2,1)S(1)}, u32[]{:S(2)}, u32[]{:S(2)}) collective-permute-start(bf16[256,1536]{1,0:T(8,128)(2,1)S(1)} %multiply_convert_fusion.6), channel_id=1, source_target_pairs={{0,2},{1,3},{2,0},{3,1},{4,6},{5,7},{6,4},{7,5},{8,10},{9,11},{10,... | collective-permute-start | bytes 2359304 | tf_op jit(solution)/shard_map/ppermute | solution.py:833
  283.4 19.8 %collective-permute-start.25 = (bf16[256,1536]{1,0:T(8,128)(2,1)S(1)}, bf16[256,1536]{1,0:T(8,128)(2,1)S(1)}, u32[]{:S(2)}, u32[]{:S(2)}) collective-permute-start(bf16[256,1536]{1,0:T(8,128)(2,1)S(1)} %slice.292), channel_id=1, source_target_pairs={{0,2},{1,3},{2,0},{3,1},{4,6},{5,7},{6,4},{7,5},{8,10},{9,11},{10,... | collective-permute-start | bytes 2359304 | tf_op jit(solution)/shard_map/ppermute | solution.py:833
  305.6 26.3 %collective-permute-start.26 = (bf16[256,1536]{1,0:T(8,128)(2,1)S(1)}, bf16[256,1536]{1,0:T(8,128)(2,1)S(1)}, u32[]{:S(2)}, u32[]{:S(2)}) collective-permute-start(bf16[256,1536]{1,0:T(8,128)(2,1)S(1)} %add_convert_fusion.5), channel_id=1, source_target_pairs={{0,2},{1,3},{2,0},{3,1},{4,6},{5,7},{6,4},{7,5},{8,10},{9,11},{10,... | collective-permute-start | bytes 2359304 | tf_op jit(solution)/shard_map/ppermute | solution.py:833
  342.3 203.0 %reduce-scatter.6.cloned.1.call-start = ((), (), s32[]{:S(2)}) async-start(), calls=%async_computation.8 | async-start | bytes 7077888 | tf_op jit(solution)/shard_map/reduce_scatter | solution.py:1035
  343.6 47.1 %collective-permute-start.29 = (bf16[512,1536]{1,0:T(8,128)(2,1)}, bf16[512,1536]{1,0:T(8,128)(2,1)}, u32[]{:S(2)}, u32[]{:S(2)}) collective-permute-start(bf16[512,1536]{1,0:T(8,128)(2,1)} %pad_maximum_fusion.5), channel_id=1, source_target_pairs={{0,1},{1,0},{2,3},{3,2},{4,5},{5,4},{6,7},{7,6},{8,9},{9,8},{10,11... | collective-permute-start | bytes 4718600 | tf_op jit(solution)/shard_map/ppermute | solution.py:837
  348.2 23.7 %collective-permute-start.28 = (bf16[256,1536]{1,0:T(8,128)(2,1)}, bf16[256,1536]{1,0:T(8,128)(2,1)}, u32[]{:S(2)}, u32[]{:S(2)}) collective-permute-start(bf16[256,1536]{1,0:T(8,128)(2,1)} %slice.291), channel_id=1, source_target_pairs={{0,2},{1,3},{2,0},{3,1},{4,6},{5,7},{6,4},{7,5},{8,10},{9,11},{10,... | collective-permute-start | bytes 2359304 | tf_op jit(solution)/shard_map/ppermute | solution.py:833
  382.5 17.7 %collective-permute-start.30 = (bf16[512,1536]{1,0:T(8,128)(2,1)}, bf16[512,1536]{1,0:T(8,128)(2,1)}, u32[]{:S(2)}, u32[]{:S(2)}) collective-permute-start(bf16[512,1536]{1,0:T(8,128)(2,1)} %slice.244), channel_id=1, source_target_pairs={{0,1},{1,0},{2,3},{3,2},{4,5},{5,4},{6,7},{7,6},{8,9},{9,8},{10,11... | collective-permute-start | bytes 4718600 | tf_op jit(solution)/shard_map/ppermute | solution.py:837
  393.4 237.6 %reduce-scatter.8.cloned.1.call-start = ((), (), s32[]{:S(2)}) async-start(), calls=%async_computation.9 | async-start | bytes 7864320 | tf_op jit(solution)/shard_map/reduce_scatter | solution.py:1061
  399.4 40.7 %collective-permute-start.32 = (bf16[256,1536]{1,0:T(8,128)(2,1)S(1)}, bf16[256,1536]{1,0:T(8,128)(2,1)S(1)}, u32[]{:S(2)}, u32[]{:S(2)}) collective-permute-start(bf16[256,1536]{1,0:T(8,128)(2,1)S(1)} %copy-done.13), channel_id=1, source_target_pairs={{0,2},{1,3},{2,0},{3,1},{4,6},{5,7},{6,4},{7,5},{8,10},{9,11},{10,... | collective-permute-start | bytes 2359304 | tf_op jit(solution)/shard_map/ppermute | solution.py:833
  403.3 36.9 %collective-permute-start.33 = (bf16[256,1536]{1,0:T(8,128)(2,1)}, bf16[256,1536]{1,0:T(8,128)(2,1)}, u32[]{:S(2)}, u32[]{:S(2)}) collective-permute-start(bf16[256,1536]{1,0:T(8,128)(2,1)} %slice.290), channel_id=1, source_target_pairs={{0,2},{1,3},{2,0},{3,1},{4,6},{5,7},{6,4},{7,5},{8,10},{9,11},{10,... | collective-permute-start | bytes 2359304 | tf_op jit(solution)/shard_map/ppermute | solution.py:833
  407.3 45.5 %collective-permute-start.34 = (bf16[256,1536]{1,0:T(8,128)(2,1)}, bf16[256,1536]{1,0:T(8,128)(2,1)}, u32[]{:S(2)}, u32[]{:S(2)}) collective-permute-start(bf16[256,1536]{1,0:T(8,128)(2,1)} %slice.289), channel_id=1, source_target_pairs={{0,2},{1,3},{2,0},{3,1},{4,6},{5,7},{6,4},{7,5},{8,10},{9,11},{10,... | collective-permute-start | bytes 2359304 | tf_op jit(solution)/shard_map/ppermute | solution.py:833
  491.2 36.5 %collective-permute-start.36 = (bf16[512,1536]{1,0:T(8,128)(2,1)S(1)}, bf16[512,1536]{1,0:T(8,128)(2,1)S(1)}, u32[]{:S(2)}, u32[]{:S(2)}) collective-permute-start(bf16[512,1536]{1,0:T(8,128)(2,1)S(1)} %pad_maximum_fusion.7.refs_2_), channel_id=1, source_target_pairs={{0,2},{1,3},{2,0},{3,1},{4,6},{5,7},{6,4},{7,5},{8,10},{9,11},{10,... | collective-permute-start | bytes 4718600 | tf_op jit(solution)/shard_map/ppermute | solution.py:833
  529.8 15.5 %collective-permute-start.37 = (bf16[1024,1536]{1,0:T(8,128)(2,1)}, bf16[1024,1536]{1,0:T(8,128)(2,1)}, u32[]{:S(2)}, u32[]{:S(2)}) collective-permute-start(bf16[1024,1536]{1,0:T(8,128)(2,1)} %pad_maximum_fusion.2), channel_id=1, source_target_pairs={{0,1},{1,0},{2,3},{3,2},{4,5},{5,4},{6,7},{7,6},{8,9},{9,8},{10,11... | collective-permute-start | bytes 9437192 | tf_op jit(solution)/shard_map/ppermute | solution.py:837
  (97 other events, 1224.2 us)
Sparse Core Ops, SparseCore 0:
  9.6 49.0 all-gather.4
  71.3 42.7 all-gather.6
  115.7 57.9 all-gather.8
  178.9 67.2 all-gather.10
  342.4 78.0 reduce-scatter.3
  424.0 117.0 reduce-scatter.5
  545.5 66.4 reduce-scatter.7

commit v5 on v4

--- a/solution.py
+++ b/solution.py
@@ -67,29 +67,57 @@
         n0 = big[BLOCK:, BLOCK:]
         low = jnp.where(strict, gram * bp, 0.0)
         eu = jnp.concatenate([e_s * bp, u.astype(f32) * bp], axis=1).astype(bf16)
-        state.append([q, k, u, a_s.astype(bf16), n0, low, eu, eye - jnp.where(diff < 2, low, 0.0)])
-    size = 2
-    while size < BLOCK:
-        sel = (diff >= size) & (diff < 2 * size)
-        prods = []
-        for st in state:
-            xb = st[7].astype(bf16)
-            prods.append((xb, mm(jnp.where(sel, st[5], 0.0).astype(bf16), xb)))
-        for st, (xb, y) in zip(state, prods):
-            st[7] = st[7] - mm(xb, y.astype(bf16))
-        size *= 2
-    for (c, h), (q, k, u, a_b, n0, low, eu, x) in zip(items, state):
+        start = (eye - jnp.where(diff < 2, low, 0.0)).astype(bf16)
+        state.append([q, k, u, a_s.astype(bf16), n0, low.astype(bf16), eu, start])
+    def invert(st, delay):
+        for _ in range(delay):
+            yield 1
+        size = 2
+        while size < BLOCK:
+            sel = jnp.where((diff >= size) & (diff < 2 * size), 1.0, 0.0).astype(bf16)
+            if size < 16:
+                y = mm(st[5] * sel, st[7]).astype(bf16)
+                yield 1
+                st[7] = st[7] - mm(st[7], y).astype(bf16)
+            else:
+                groups = range(size, BLOCK, 2 * size)
+                odd = lambda x: jnp.concatenate([x[g : g + size] for g in groups], axis=0)
+                blank = jnp.zeros((size, BLOCK), bf16)
+                y = mm(odd(st[5]) * odd(sel), st[7]).astype(bf16)
+                yield 1
+                pieces = []
+                for n in range(len(groups)):
+                    pieces += [blank, y[n * size : (n + 1) * size]]
+                rows_odd = odd(st[7])
+                fresh = rows_odd - mm(rows_odd, jnp.concatenate(pieces, axis=0)).astype(bf16)
+                pieces = []
+                for n, g in enumerate(groups):
+                    pieces += [st[7][g - size : g], fresh[n * size : (n + 1) * size]]
+                st[7] = jnp.concatenate(pieces, axis=0)
+            yield 1
+            size *= 2
+
+    lockstep(invert(st, n % 2) for n, st in enumerate(state))
+    def close(item, st, delay):
+        for _ in range(delay):
+            yield 1
+        c, h = item
+        q, k, u, a_b, n0, low, eu, x = st
         rs, cs = pl.ds(c * BLOCK, BLOCK), pl.ds(h * BLOCK, BLOCK)
-        xb = x.astype(bf16)
-        t = mm(xb, eu).astype(bf16)
+        t = mm(x, eu).astype(bf16)
+        inv_ref[c, h] = x
+        t_ref[c, h] = t
+        yield 1
         top = mm(a_b, t)
+        yield 1
         bot = mm_lt(u, t)
-        inv_ref[c, h] = xb
-        t_ref[c, h] = t
         near_ref[c, h] = n0 - top[:, :BLOCK]
         q0_ref[rs, cs] = (q.astype(f32) - top[:, BLOCK:]).astype(bf16)
+        yield 1
         ket = mm_rt(eye_b, k) - bot[:, :BLOCK]
         kp_ref[c, h] = jnp.concatenate([ket, eye - bot[:, BLOCK:]], axis=1).astype(bf16)
+
+    lockstep(close(item, st, 0) for n, (item, st) in enumerate(zip(items, state)))
 
 
 def fwd_kernel(
@@ -128,18 +156,18 @@
         e_ref[0, 0, h] = eb
         v = v_ref[pl.ds(pl.multiple_of(table_ref[i] * BLOCK, BLOCK), BLOCK), h * BLOCK : (h + 1) * BLOCK]
         acc_ref[h] = mm(eb, v)
-    for d in range(1, depth):
-
-        @pl.when(i - d >= first)
-        def _():
-            j = i - d
-            for h in range(heads):
-                e = jnp.exp((s_ref[d, h] - peaks[h]) * scale)
-                m_ref[h] = m_ref[h] + e
-                eb = e.astype(bf16)
-                e_ref[0, d, h] = eb
-                v = v_ref[pl.ds(pl.multiple_of(table_ref[j] * BLOCK, BLOCK), BLOCK), h * BLOCK : (h + 1) * BLOCK]
-                acc_ref[h] = acc_ref[h] + mm(eb, v)
+    def weigh(d, carry):
+        j = i - d
+        at = pl.ds(pl.multiple_of(table_ref[j] * BLOCK, BLOCK), BLOCK)
+        for h in range(heads):
+            e = jnp.exp((s_ref[d, h] - peaks[h]) * scale)
+            m_ref[h] = m_ref[h] + e
+            eb = e.astype(bf16)
+            e_ref[0, d, h] = eb
+            acc_ref[h] = acc_ref[h] + mm(eb, v_ref[at, h * BLOCK : (h + 1) * BLOCK])
+        return carry
+
+    lax.fori_loop(1, i - first + 1, weigh, 0)
 
     for h in range(heads):
         linv = 1.0 / jnp.sum(m_ref[h], axis=1, keepdims=True)
@@ -267,7 +295,7 @@
 def attention_prep(proj, table, heads):
     count = table.shape[0]
     width = heads * BLOCK
-    step = 2
+    step = 4
 
     def rows(c, n, col):
         return pl.BlockSpec((BLOCK, n), lambda i, t: (t[i * step + c], col))
@@ -788,6 +816,107 @@
         copy.wait_send()
 
 
+def spread_kernel(axis, count, rows, widths, *refs):
+    held = len(widths)
+    parts, out = refs[:held], refs[held]
+    own_buf, left_buf, right_buf, load_sem, store_sem, send_sem, recv_sem = refs[held + 1 :]
+    me = lax.axis_index(axis)
+    odd = me % 2
+    spot = (1 - odd) * (me // 2) + odd * (count - 1 - me // 2)
+
+    def owner(shift):
+        at = (spot + shift + count) % count
+        upper = at // (count // 2)
+        return (1 - upper) * (2 * at) + upper * (2 * (count - 1 - at) + 1)
+
+    top = count // 2
+    cut = rows // 32 * 16
+    halves = ((0, cut), (cut, rows - cut))
+    peers = (owner(1), owner(-1))
+    barrier = pltpu.get_barrier_semaphore()
+    for peer in peers:
+        pl.semaphore_signal(barrier, inc=1, device_id={axis: peer}, device_id_type=pl.DeviceIdType.MESH)
+    loads, col = [], 0
+    for n, width in enumerate(widths):
+        loads.append(pltpu.make_async_copy(parts[n], own_buf.at[:, pl.ds(col, width)], load_sem.at[n]))
+        loads[-1].start()
+        col += width
+    for load in loads:
+        load.wait()
+    pl.semaphore_wait(barrier, 2)
+    bufs = (left_buf, right_buf)
+    flying, sent, stores = {}, [], []
+
+    def push(way, hop, part, src):
+        start, size = halves[part]
+        copy = pltpu.make_async_remote_copy(
+            src_ref=src,
+            dst_ref=bufs[way].at[hop, pl.ds(start, size), :],
+            send_sem=send_sem.at[way, hop, part],
+            recv_sem=recv_sem.at[way, hop, part],
+            device_id={axis: peers[way]},
+            device_id_type=pl.DeviceIdType.MESH,
+        )
+        copy.start()
+        sent.append(copy)
+        flying[way, hop, part] = copy
+
+    def store(src, shift, part, sem):
+        start, size = halves[part]
+        at = pl.multiple_of(owner(shift) * rows + start, 16)
+        stores.append(pltpu.make_async_copy(src, out.at[pl.ds(at, size), :], sem))
+        stores[-1].start()
+
+    for part in range(2):
+        for way in range(2):
+            start, size = halves[part]
+            push(way, 0, part, own_buf.at[pl.ds(start, size), :])
+    for part in range(2):
+        start, size = halves[part]
+        store(own_buf.at[pl.ds(start, size), :], 0, part, store_sem.at[2, 0, part])
+    for hop in range(top):
+        for part in range(2):
+            for way in range(2):
+                if hop == top - 1 and part != way:
+                    continue
+                start, size = halves[part]
+                here = bufs[way].at[hop, pl.ds(start, size), :]
+                flying[way, hop, part].wait_recv()
+                if hop + 1 < top - 1 or (hop + 1 == top - 1 and part == way):
+                    push(way, hop + 1, part, here)
+                store(here, -(hop + 1) if way == 0 else hop + 1, part, store_sem.at[way, hop, part])
+    for copy in sent:
+        copy.wait_send()
+    for copy in stores:
+        copy.wait()
+
+
+def ring_spread(parts, axis):
+    count = lax.axis_size(axis)
+    rows = parts[0].shape[0]
+    widths = [part.shape[1] for part in parts]
+    cols = sum(widths)
+    top = count // 2
+    return pl.pallas_call(
+        functools.partial(spread_kernel, axis, count, rows, widths),
+        in_specs=[pl.BlockSpec(memory_space=pl.ANY)] * len(parts),
+        out_specs=pl.BlockSpec(memory_space=pl.ANY),
+        out_shape=jax.ShapeDtypeStruct((count * rows, cols), bf16),
+        scratch_shapes=[
+            pltpu.VMEM((rows, cols), bf16),
+            pltpu.VMEM((top, rows, cols), bf16),
+            pltpu.VMEM((top, rows, cols), bf16),
+            pltpu.SemaphoreType.DMA((len(parts),)),
+            pltpu.SemaphoreType.DMA((3, top, 2)),
+            pltpu.SemaphoreType.DMA((2, top, 2)),
+            pltpu.SemaphoreType.DMA((2, top, 2)),
+        ],
+        compiler_params=pltpu.CompilerParams(collective_id=1, has_side_effects=True),
+        cost_estimate=pl.CostEstimate(flops=0, bytes_accessed=4 * count * rows * cols, transcendentals=0),
+        name="ring_spread",
+    )(*parts)
+
+
 def ring_sum(parts, axis):
     count = lax.axis_size(axis)
     rows = parts[0].shape[0] // count
@@ -903,29 +1032,28 @@
     own_packed = jnp.sum(jnp.where(pull, packed[None, :], 0), axis=1)
     origin = me ^ (own_packed % per_bin // per_half)
     own_spots = ((origin // 2) + 2 * (origin % 2)) * per_own + own_packed // per_bin * per_half + own_packed % per_half
-    tables = (table.astype(jnp.int32), first, last, slot, slotted, own_places, own_spots)
+    holder = me ^ (slotted // per_own)
+    cot_table = ((holder // 2) + 2 * (holder % 2)) * per_own + slotted % per_own
+    tables = (table.astype(jnp.int32), first, last, slot, slotted, own_places, own_spots, cot_table)
 
     extras = jnp.concatenate(
         [w_beta, gain_attn[:, None], gain_ffn[:, None], jnp.zeros((shard, BLOCK - heads - 2), bf16)], axis=1
     )
-    attn_pack = jnp.concatenate([w_query, w_key, w_value, w_house, extras], axis=1)
     ffn_pack = jnp.concatenate([w_gate, w_up], axis=1)
     full_tokens = lax.all_gather(tokens, "tp", axis=0, tiled=True)
-    attn_ring = RingGather(attn_pack, "fsdp")
-    attn_ring.hop()
-    table, first, last, slot, slotted, own_places, own_spots = attn_ring.before(*tables)
-    while len(attn_ring.hops) < attn_ring.count // 2 - 1:
-        attn_ring.hop()
-    full_tokens, out_shard, down_shard, cotangent = attn_ring.before(full_tokens, w_out, w_down, cotangent)
-    w_in, ffn_pack, out_shard, down_shard, cotangent = together(
-        attn_ring.finish(), ffn_pack, out_shard, down_shard, cotangent
+    tables = together(*tables)
+    table, first, last, slot, slotted, own_places, own_spots, cot_table = tables
+    ffn_pack, slotted = together(ffn_pack, slotted)
+    w_in = ring_spread([w_query, w_key, w_value, w_house, extras], "fsdp")
+    full_tokens, w_in, ffn_pack, out_shard, down_shard, cotangent, table, first, last, slot, own_places, own_spots = together(
+        full_tokens, w_in, ffn_pack, w_out, w_down, cotangent, table, first, last, slot, own_places, own_spots
     )
     ffn_ring = RingGather(ffn_pack, "fsdp", True)
     ffn_ring.hop()
     x_rows = gather_blocks(full_tokens, slotted[:, :per_half], per_half)
     full_out = lax.all_gather(out_shard, "fsdp", axis=0, tiled=True)
     full_down = lax.all_gather(down_shard, "fsdp", axis=0, tiled=True)
-    full_cot = lax.all_gather(cotangent, "tp", axis=0, tiled=True)
+    cot_far = across(cotangent)
     pick = (jnp.arange(BLOCK)[None, :] == heads + jnp.arange(8)[:, None]).astype(bf16)
     gain_rows = cols_contract(pick, w_in[:, 4 * width :])
     gain_one, gain_two = gain_rows[0], gain_rows[1]
@@ -953,6 +1081,8 @@
     ffn_ring.hop()
     preps.append(prep)
     saved.append(list(run(prep)))
+    saved[0][0], cot_far = together(saved[0][0], cot_far)
+    cot_parts = [cotangent, cot_far, beside(cotangent), beside(cot_far)]
     rows = ffn_ring.before(cols_contract(saved[0][0], full_out).astype(bf16))
     ffn_ring.hop()
     attn_own, attn_far = share(rows)
@@ -967,13 +1097,13 @@
     normed_far = across(normed_own)
     prep[0], normed_own = together(prep[0], normed_own)
     saved.append(list(run(prep)))
-    saved[1][0], normed_far, full_cot = together(saved[1][0], normed_far, full_cot)
+    saved[1][0], normed_far, cot_parts[2], cot_parts[3] = together(saved[1][0], normed_far, *cot_parts[2:])
     pair = jnp.concatenate([normed_own, normed_far], axis=0)
     normed_two.append(jnp.concatenate([pair, beside(pair)], axis=0))
     attn_own, attn_far = share(cols_contract(saved[1][0], full_out).astype(bf16))
-    attn_own, full_cot, ffn_ring.x = together(attn_own, full_cot, ffn_ring.x)
+    attn_own, cot_parts[3], ffn_ring.x = together(attn_own, cot_parts[3], ffn_ring.x)
     ffn_full = ffn_ring.finish()
-    cot_rows = list(gather_blocks(full_cot, slotted, 4))
+    cot_rows = list(pick_blocks([cot_parts] * bins, list(cot_table)))
 
     full_gate, full_up = ffn_full[:, :hidden_width], ffn_full[:, hidden_width : 2 * hidden_width]
     full_gate_up = ffn_full
@@ -1014,20 +1144,16 @@
         cot_own = cot_rows[m][:half].astype(f32)
         return (cot_own + norm_two_grad).astype(bf16)
 
-    def middle_back(rows):
-        rows, own, far = together(rows, back_own, back_far)
-        mine = close_back(0, own, far)
-        flying[0], flying[1] = mine, across(mine)
-        return rows
-
-    ffn(1, normed_two[1], middle_back)
-    dh_own, dh_far = flying[0], flying[1]
+    ffn(1, normed_two[1], lambda rows: rows)
+    gate_up[1], back_own, back_far = together(gate_up[1], back_own, back_far)
+    dh_own = close_back(0, back_own, back_far)
+    dh_far = across(dh_own)
+    grads_down = sum(rows_contract(cot_rows[m], hidden[m]) for m in streams)
+    grads_down, gate_up[1] = together(grads_down.astype(bf16), gate_up[1])
+    sum_down = lax.psum_scatter(grads_down, "fsdp", scatter_dimension=0, tiled=True)
     rows, dh_own, dh_far = together(ffn_back_rows(1), dh_own, dh_far)
     back_own, back_far = share(rows)
     back_own, normed_two[0], normed_two[1] = together(back_own, *normed_two)
-    grads_down = sum(rows_contract(cot_rows[m], hidden[m]) for m in streams)
-    grads_down, dh_far, gate_up[0], gate_up[1] = together(grads_down.astype(bf16), dh_far, *gate_up)
-    sum_down = lax.psum_scatter(grads_down, "fsdp", scatter_dimension=0, tiled=True)
     pair = jnp.concatenate([dh_own, dh_far], axis=0)
     grad_attn.append(jnp.concatenate([pair, beside(pair)], axis=0))
     grads_in = sum(rows_contract(normed_two[m], gate_up[m]) for m in streams)
@@ -1041,25 +1167,26 @@
     y_own, y_far = [p[0] for p in ffn_parts], [p[1] for p in ffn_parts]
     d_mixed, y_own[0], y_own[1] = together(d_mixed, *y_own)
     d_proj = attention_bwd(proj, preps[0], saved[0], d_mixed, last[0], table[0], slot, heads, None)
-    d_proj, dh_far, y_far[0], y_far[1] = together(d_proj, dh_far, *y_far)
+    d_proj, dh_far, y_far[0] = together(d_proj, dh_far, y_far[0])
     pair = jnp.concatenate([dh_own, dh_far], axis=0)
     grad_attn.append(jnp.concatenate([pair, beside(pair)], axis=0))
     d_mixed = jnp.dot(grad_attn[1], full_out, preferred_element_type=f32).astype(bf16)
-    y_rows = jnp.concatenate(
-        [(hidden_in[m] + y_own[m] + y_far[m].astype(f32)).astype(bf16) for m in streams], axis=0
-    )
+    finish_y = lambda m: (hidden_in[m] + y_own[m] + y_far[m].astype(f32)).astype(bf16)
+    y_rows = [finish_y(0)]
     grad_out = sum(rows_contract(grad_attn[m], saved[m][0]) for m in streams).astype(bf16)
-    d_mixed, grad_out, y_rows = together(d_mixed, grad_out, y_rows)
-    y_across = across(y_rows)
+    d_mixed, grad_out, y_rows[0] = together(d_mixed, grad_out, y_rows[0])
+    y_across = [across(y_rows[0])]
     d_proj = attention_bwd(proj, preps[1], saved[1], d_mixed, last[1], table[1], slot, heads, d_proj)
-    d_proj, sum_down = together(d_proj, sum_down)
-    attn_grads, d_proj, y_rows = together(rows_contract(normed, d_proj).astype(bf16), d_proj, y_rows)
-    y_pair = jnp.concatenate([y_rows, y_across], axis=0)
-    rows_one, y_other, attn_grads, sum_in = together(
-        cols_contract(d_proj, w_in).astype(bf16), beside(y_pair), attn_grads, sum_in
+    d_proj, sum_down, y_across[0], y_far[1] = together(d_proj, sum_down, y_across[0], y_far[1])
+    y_rows.append(finish_y(1))
+    y_across.append(across(y_rows[1]))
+    attn_grads, d_proj, y_across[1] = together(rows_contract(normed, d_proj).astype(bf16), d_proj, y_across[1])
+    y_pair = jnp.concatenate([*y_rows, *y_across], axis=0)
+    rows_one, y_other, attn_grads = together(
+        cols_contract(d_proj, w_in).astype(bf16), beside(y_pair), attn_grads
     )
     grad_one = lax.psum_scatter(rows_one, "tp", scatter_dimension=0, tiled=True)
-    dh_own, out_y = pick_blocks([grad_attn, [y_rows, y_across, y_other]], [own_places, own_spots])
+    dh_own, out_y = pick_blocks([grad_attn, [*y_rows, *y_across, y_other]], [own_places, own_spots])
     attn_grads, dh_own, out_y = together(attn_grads, dh_own, out_y)
     attn_sum, grad_out = ring_sum([attn_grads, grad_out], "fsdp")
     sum_in, sum_down = sum_in.astype(f32), sum_down.astype(f32)
@@ -1068,8 +1195,9 @@
     norm_one_grad = norm_back(grad_one, unit_one, scale_one, gain_one)
     out_dx = (dh_own.astype(f32) + norm_one_grad).astype(bf16)
     dots = lambda grads, weights: jnp.sum(grads * weights.astype(f32), axis=1)
-    own_one = dots(attn_sum[:, : 4 * width], attn_pack[:, : 4 * width]) + dots(
-        attn_sum[:, 4 * width : 4 * width + heads], w_beta
+    own_one = dots(attn_sum[:, 4 * width : 4 * width + heads], w_beta) + sum(
+        dots(attn_sum[:, n * width : (n + 1) * width], weight)
+        for n, weight in enumerate((w_query, w_key, w_value, w_house))
     )
     own_two = dots(sum_in, ffn_pack)
     gains = tp_sum(jnp.stack([own_one, own_two])) / jnp.stack([gain_attn, gain_ffn]).astype(f32)

time: 656 us -> 619 us (0.944)
  waiting for transfers between devices: 106 us -> 29.5 us
  Pallas kernels: 206 us -> 255 us
    pallas_call x1, Pallas kernels: 1.84 us -> 55.6 us  [ring_spread(): pl.pallas_call(functools.partial(spread_kernel, axis, count, rows, widths...]
    ppermute x11 -> x13, waiting for transfers between devices: 60.4 us -> 18 us  [across(): return lax.ppermute(x, 'tp', [(i, i ^ 2) for i in range(4)])]
    ppermute x8 -> x4, waiting for transfers between devices: 26.5 us -> 0.21 us  [hop(): lax.ppermute(from_left, self.axis, self.right)]
    pallas_call x2, Pallas kernels: 34.3 us -> 21.2 us  [attention_prep(): pl.pallas_call(functools.partial(prep_kernel, heads, step), grid_spec=spe...]
    ppermute x8 -> x4, starting transfers between devices: 13.8 us -> 3.26 us  [hop(): lax.ppermute(from_right, self.axis, self.left)]
    ppermute x8 -> x4, waiting for transfers between devices: 16.5 us -> 8.81 us  [hop(): lax.ppermute(from_right, self.axis, self.left)]
    dynamic_update_slice x6 -> x0, local copies, waits for them, and re-layouts: 6.59 us -> none  [finish(): out = put(out, piece, spot * rows, 0)]
    unnamed x167 -> x171, local copies, waits for them, and re-layouts: 19.8 us -> 23.2 us
  transfers between devices with their start and end apart: 48 -> 43, of which waited for: 14 -> 8; matrix products, arithmetic and copies ran while one was open for 40% -> 42% of each run, Pallas kernels for 32% -> 42%
where the time goes in v5:
time: 619 us; the launch traced here: 609 us
  Pallas kernels  255 us (41%)
  matrix products  169 us (27%)
  local copies, waits for them, and re-layouts  56.5 us (9%)
  other arithmetic  56 us (9%)
  waiting for transfers between devices  29.5 us (5%)
  starting transfers between devices  26.4 us (4%)
  between operations  16 us (3%)
    pallas_call x1, Pallas kernels, ring_sum(): pl.pallas_call(functools.partial(ring_kernel, axis, count, rows, widths),...  71.3 us
    pallas_call x2, Pallas kernels, attention_bwd(): pl.pallas_call(functools.partial(bwd_kernel, heads, depth, scale), grid_s...  55.8 us
    pallas_call x1, Pallas kernels, ring_spread(): pl.pallas_call(functools.partial(spread_kernel, axis, count, rows, widths...  55.6 us
    dot_general x7, matrix products, rows_contract(): lax.dot_general(a, b, (((0,), (0,)), ((), ())), preferred_element_type=f32)  52.8 us
    dot_general x8, matrix products, cols_contract(): lax.dot_general(a, b, (((1,), (1,)), ((), ())), preferred_element_type=f32)  49 us
    pallas_call x2, Pallas kernels, attention_fwd(): pl.pallas_call(functools.partial(fwd_kernel, heads, depth, scale), grid_s...  32.8 us
    unnamed x171, local copies, waits for them, and re-layouts  23.2 us
    pallas_call x2, Pallas kernels, attention_prep(): pl.pallas_call(functools.partial(prep_kernel, heads, step), grid_spec=spe...  21.2 us
  transfers between devices with their start and end apart: 43, of which 8 were waited for; matrix products, arithmetic and copies ran while one was open for 42% of the time, Pallas kernels for 42%

profile of v5, /device:TPU:0, one launch (start us, length us, event | category | flops | bytes accessed | tf_op | source)
XLA Modules:
  0.0 608.7 jit_solution(4490442994076754401)
XLA Ops:
  16.4 55.6 %ring_spread.1 = bf16[1536,1664]{1,0:T(8,128)(2,1)} custom-call(bf16[192,384]{1,0:T(8,128)(2,1)} %refs_0_.1, bf16[192,384]{1,0:T(8,128)(2,1)} %refs_1_.1, bf16[192,384]{1,0:T(8,128)(2,1)} %refs_2_.1, bf16[192,384]{1,0:T(8,128)(2,1)} %refs_3_.1, bf16[192,128]{1,0:T(8,128)(2,1)} %maximum_maximum_fusion.refs_4_), custom_call_target="tpu_custom_call" | custom-call | bytes 10223616 | tf_op jit(solution)/shard_map/ring_spread/pallas_call | solution.py:900
  74.2 4.2 fusion
  81.3 16.4 %convolution_convert_fusion.refs_0_.refs_1_.refs_2_.refs_3_.refs_4_.refs_5_.refs_6_.refs_7_.refs_8_.refs_9_.refs_10_.refs_11_.refs_12_.refs_13_.refs_14_.refs_15_.v_ref = bf16[2048,1664]{1,0:T(8,128)(2,1)} fusion(bf16[1536,1664]{1,0:T(8,128)(2,1)} %ring_spread.1, bf16[2048,1536]{1,0:T(8,128)(2,1)S(1)} %copy-done, f32[1536]{0:T(1024)S(1)} %get-tuple-element.283, ...), kind=kOutput, calls=%fused_computation.6 | convolution fusion | flops 10484973568 | bytes 18233344 | tf_op jit(solution)/shard_map/dot_general | solution.py:1063
  98.3 10.5 %attn_prep.2 = (f32[8,3,128,128]{3,2,1,0:T(8,128)}, bf16[1024,384]{1,0:T(8,128)(2,1)}, bf16[8,3,128,256]{3,2,1,0:T(8,128)(2,1)}, bf16[8,3,128,128]{3,2,1,0:T(8,128)(2,1)}, bf16[8,3,128,256]{3,2,1,0:T(8,128)(2,1)}) custom-call(s32[8]{0:T(128)} %get-tuple-element.330.table_ref, ...), custom_call_target="tpu_custom_call" | custom-call | flops 2264924160 | bytes 2359296 | tf_op jit(solution)/shard_map/attn_prep/pallas_call | solution.py:318
  111.5 18.7 %attn_fwd.2 = (bf16[1024,384]{1,0:T(8,128)(2,1)}, f32[1024,384]{1,0:T(8,128)}, bf16[8,8,3,128,128]{4,3,2,1,0:T(8,128)(2,1)}, bf16[8,7,3,128,128]{4,3,2,1,0:T(8,128)(2,1)}) custom-call(s32[8]{0:T(128)} %get-tuple-element.329.first_ref, s32[8]{0:T(128)} %get-tuple-element.330.table_ref, s32[8]{0:T(128)} %copy-done.56, ...), custom_call_target="tpu_custom_call" | custom-call | flops 2415919104 | bytes 2359296 | tf_op jit(solution)/shard_map/attn_fwd/pallas_call | solution.py:362
  145.1 10.7 %attn_prep.3 = (f32[8,3,128,128]{3,2,1,0:T(8,128)}, bf16[1024,384]{1,0:T(8,128)(2,1)}, bf16[8,3,128,256]{3,2,1,0:T(8,128)(2,1)}, bf16[8,3,128,128]{3,2,1,0:T(8,128)(2,1)}, bf16[8,3,128,256]{3,2,1,0:T(8,128)(2,1)}) custom-call(s32[8]{0:T(128)} %get-tuple-element.331.table_ref, ...), custom_call_target="tpu_custom_call" | custom-call | flops 2264924160 | bytes 2359296 | tf_op jit(solution)/shard_map/attn_prep/pallas_call | solution.py:318
  155.8 4.3 collective-permute-done.8
  162.8 14.1 %attn_fwd.3 = (bf16[1024,384]{1,0:T(8,128)(2,1)}, f32[1024,384]{1,0:T(8,128)}, bf16[8,8,3,128,128]{4,3,2,1,0:T(8,128)(2,1)}, bf16[8,7,3,128,128]{4,3,2,1,0:T(8,128)(2,1)}) custom-call(s32[8]{0:T(128)} %get-tuple-element.328.first_ref, s32[8]{0:T(128)} %get-tuple-element.331.table_ref, s32[8]{0:T(128)} %copy-done.56, ...), custom_call_target="tpu_custom_call" | custom-call | flops 2415919104 | bytes 2359296 | tf_op jit(solution)/shard_map/attn_fwd/pallas_call | solution.py:362
  176.9 4.1 collective-permute-done.9
  200.3 5.6 place_pieces.1
  205.9 6.2 %pick_blocks.2 = (bf16[1024,1536]{1,0:T(8,128)(2,1)}, bf16[1024,1536]{1,0:T(8,128)(2,1)}) custom-call(s32[16]{0:T(128)} %pad_add_fusion.table_ref, bf16[512,1536]{1,0:T(8,128)(2,1)} %refs_4_, bf16[512,1536]{1,0:T(8,128)(2,1)} %collective-permute-done.4.refs_1_.refs_5_, bf16[512,1536]{1,0:T(8,128)(2,1)} %collective-permute-done.10.refs_2_.refs_6_, ...), custom_call_target="tpu_custom_call" | custom-call | bytes 12582912 | tf_op jit(solution)/shard_map/pick_blocks/pallas_call | solution.py:523
  214.1 8.8 %collective-permute-done.15 = bf16[96,2048]{1,0:T(8,128)(2,1)} collective-permute-done((bf16[96,2048]{1,0:T(8,128)(2,1)S(1)}, bf16[96,2048]{1,0:T(8,128)(2,1)}, u32[]{:S(2)}, u32[]{:S(2)}) %collective-permute-start.15) | collective-permute-done | bytes 393248 | tf_op jit(solution)/shard_map/ppermute | solution.py:644
  227.3 8.4 %fusion.16 = f32[1024,1024]{0,1:T(8,128)} fusion(bf16[1024,1536]{1,0:T(8,128)(2,1)} %constant_dynamic-update-slice_fusion, bf16[1536,2048]{1,0:T(8,128)(2,1)} %constant_dynamic-update-slice_fusion.12), kind=kOutput, calls=%fused_computation.50 | convolution fusion | flops 3221225472 | bytes 10485760 | tf_op jit(solution)/shard_map/dot_general | solution.py:1114
  239.7 8.5 %fusion.43 = f32[1024,1024]{0,1:T(8,128)} fusion(bf16[1024,1536]{1,0:T(8,128)(2,1)} %get-tuple-element.180, bf16[1536,1024]{1,0:T(8,128)(2,1)} %all-gather.8.cloned.1.call-done), kind=kOutput, calls=%fused_computation.220 | convolution fusion | flops 3221225472 | bytes 10485760 | tf_op jit(solution)/shard_map/dot_general | solution.py:1117
  248.2 9.8 %multiply_convert_fusion.4 = (bf16[1024,1024]{0,1:T(8,128)(2,1)S(1)}, bf16[1024,1024]{0,1:T(8,128)(2,1)}, bf16[1024,1024]{0,1:T(8,128)(2,1)}) fusion(f32[1024,1024]{0,1:T(8,128)} %fusion.43, f32[1024,1024]{0,1:T(8,128)S(1)} %copy-done.69, bf16[1024,1536]{1,0:T(8,128)(2,1)S(1)} %copy-done.48, bf16[1536,2048]{1,0:T(8,128)(2,1)} %constant_dynamic-update-slice_fusion.12), kind=kOutput, calls=%fused_computation.18 | convolution fusion | flops 3236954112 | bytes 20971520 | tf_op jit(solution)/shard_map/dot_general | solution.py:1113
  258.0 9.0 %convolution_convert_fusion.4 = bf16[1024,1536]{1,0:T(8,128)(2,1)S(1)} fusion(bf16[1536,2048]{1,0:T(8,128)(2,1)S(1)} %bitcast.75, bf16[1024,1024]{0,1:T(8,128)(2,1)} %get-tuple-element.307, bf16[1024,1024]{0,1:T(8,128)(2,1)S(1)} %get-tuple-element.306), kind=kOutput, calls=%fused_computation.25 | convolution fusion | flops 6452412416 | bytes 13631488 | tf_op jit(solution)/shard_map/dot_general | solution.py:598
  269.9 5.0 fusion.45
  279.5 5.0 fusion.14
  284.5 8.8 %multiply_convert_fusion.1 = (bf16[1024,1024]{0,1:T(8,128)(2,1)S(1)}, bf16[1024,1024]{0,1:T(8,128)(2,1)S(1)}, bf16[1024,1024]{0,1:T(8,128)(2,1)S(1)}) fusion(f32[1024,1024]{0,1:T(8,128)} %fusion.45, f32[1024,1024]{0,1:T(8,128)} %fusion.14, bf16[1024,1536]{1,0:T(8,128)(2,1)} %copy-done.50, bf16[1536,2048]{1,0:T(8,128)(2,1)S(1)} %bitcast.75), kind=kOutput, calls=%fused_computation.13 | convolution fusion | flops 3236954112 | bytes 20971520 | tf_op jit(solution)/shard_map/dot_general | solution.py:1113
  293.3 3.5 fusion.44
  300.9 4.9 add_convert_fusion.1
  310.4 9.0 %convolution_convert_fusion.3 = bf16[1024,1536]{1,0:T(8,128)(2,1)S(1)} fusion(bf16[1024,2048]{0,1:T(8,128)(2,1)S(1)} %copy-done.19, bf16[1536,2048]{1,0:T(8,128)(2,1)} %constant_dynamic-update-slice_fusion.12), kind=kOutput, calls=%fused_computation.24 | convolution fusion | flops 6444023808 | bytes 13631488 | tf_op jit(solution)/shard_map/dot_general | solution.py:598
  319.5 8.7 %collective-permute-done.21 = bf16[256,1536]{1,0:T(8,128)(2,1)S(1)} collective-permute-done((bf16[256,1536]{1,0:T(8,128)(2,1)S(1)}, bf16[256,1536]{1,0:T(8,128)(2,1)S(1)}, u32[]{:S(2)}, u32[]{:S(2)}) %collective-permute-start.21) | collective-permute-done | bytes 786464 | tf_op jit(solution)/shard_map/ppermute | solution.py:962
  338.4 9.6 %fusion.46 = f32[1536,2048]{1,0:T(8,128)} fusion(bf16[1024,1536]{1,0:T(8,128)(2,1)S(1)} %copy-done.51, bf16[1024,2048]{0,1:T(8,128)(2,1)S(1)} %copy-done.20), kind=kOutput, calls=%fused_computation.223 | convolution fusion | flops 6442450944 | bytes 19922944 | tf_op jit(solution)/shard_map/dot_general | solution.py:594
  348.0 12.4 %add_convert_fusion = bf16[1536,2048]{1,0:T(8,128)(2,1)} fusion(f32[1536,2048]{1,0:T(8,128)} %fusion.46, bf16[1024,1536]{1,0:T(8,128)(2,1)S(1)} %copy-done.49, bf16[1024,1024]{0,1:T(8,128)(2,1)} %get-tuple-element.307, bf16[1024,1024]{0,1:T(8,128)(2,1)S(1)} %copy-done.75), kind=kOutput, calls=%fused_computation.5 | convolution fusion | flops 6457131008 | bytes 26214400 | tf_op jit(solution)/shard_map/dot_general | solution.py:594
  365.7 3.7 convolution_convert_fusion.8
  372.7 3.9 convolution_convert_fusion.7
  392.5 30.9 %attn_bwd.2.refs_26_ = bf16[2048,1664]{1,0:T(8,128)(2,1)} custom-call(s32[8]{0:T(128)} %get-tuple-element.324.last_ref, s32[8]{0:T(128)} %get-tuple-element.330.table_ref, s32[8]{0:T(128)} %copy-done.56, bf16[1024,384]{1,0:T(8,128)(2,1)} %convolution_convert_fusion.10.refs_0_, bf16[1024,384]{1,0:T(8,128)(2,1)} %get-tuple-element.151.refs_1_, ...), custom_call_target="tpu_custom_call" | custom-call | flops 6039797760 | bytes 3145728 | tf_op jit(solution)/shard_map/attn_bwd/pallas_call | solution.py:429
  441.0 24.9 %attn_bwd.3 = bf16[2048,1664]{1,0:T(8,128)(2,1)} custom-call(s32[8]{0:T(128)} %get-tuple-element.325.last_ref, s32[8]{0:T(128)} %get-tuple-element.331.table_ref, s32[8]{0:T(128)} %copy-done.56, bf16[1024,384]{1,0:T(8,128)(2,1)} %convolution_convert_fusion.9.refs_0_, bf16[1024,384]{1,0:T(8,128)(2,1)} %get-tuple-element.170.refs_1_, ...), custom_call_target="tpu_custom_call", output_to_operand_aliasing={{}: (29, {})} | custom-call | flops 6039797760 | bytes 3145728 | tf_op jit(solution)/shard_map/attn_bwd/pallas_call | solution.py:429
  468.7 17.6 %convolution_convert_fusion.2.refs_0_ = bf16[1536,1664]{1,0:T(8,128)(2,1)} fusion(bf16[2048,1664]{1,0:T(8,128)(2,1)} %attn_bwd.3, bf16[2048,1536]{1,0:T(8,128)(2,1)} %all-gather.4.cloned.1.call-done.refs_0_.refs_1_.refs_2_.refs_3_, f32[1536]{0:T(1024)S(1)} %copy-done.53, f32[2048]{0:T(1024)S(1)} %copy-done.59), kind=kOutput, calls=%fused_computation.8 | convolution fusion | flops 10484121600 | bytes 18233344 | tf_op jit(solution)/shard_map/dot_general | solution.py:594
  490.5 15.4 %convolution_convert_fusion.1 = bf16[2048,1536]{1,0:T(8,128)(2,1)} fusion(bf16[2048,1664]{1,0:T(8,128)(2,1)S(1)} %bitcast.73, bf16[1536,1664]{1,0:T(8,128)(2,1)} %ring_spread.1), kind=kOutput, calls=%fused_computation.7 | convolution fusion | flops 10472128512 | bytes 18219008 | tf_op jit(solution)/shard_map/dot_general | solution.py:598
  512.8 71.3 %ring_sum.1 = (f32[192,1664]{1,0:T(8,128)}, f32[192,384]{1,0:T(8,128)}) custom-call(bf16[1536,1664]{1,0:T(8,128)(2,1)} %convolution_convert_fusion.2.refs_0_, bf16[1536,384]{1,0:T(8,128)(2,1)} %fusion.13.refs_1_), custom_call_target="tpu_custom_call" | custom-call | bytes 12582912 | tf_op jit(solution)/shard_map/ring_sum/pallas_call | solution.py:927
  (382 shorter events, 163.0 us)
Async XLA Ops:
  7.2 64.8 %all-gather.4.cloned.1.call-start = ((), (), s32[]{:S(2)}) async-start(), calls=%async_computation.3 | async-start | bytes 7864320 | tf_op jit(solution)/shard_map/all_gather | solution.py:1043
  7.9 122.3 %all-gather.6.cloned.1.call-start = ((), (), s32[]{:S(2)}) async-start(), calls=%async_computation.4 | async-start | bytes 1327104 | tf_op jit(solution)/shard_map/all_gather | solution.py:1054
  72.0 36.8 %collective-permute-start.1 = (bf16[192,2048]{1,0:T(8,128)(2,1)S(1)}, bf16[192,2048]{1,0:T(8,128)(2,1)S(1)}, u32[]{:S(2)}, u32[]{:S(2)}) collective-permute-start(bf16[192,2048]{1,0:T(8,128)(2,1)S(1)} %pad_maximum_fusion.9.refs_0_), channel_id=1, source_target_pairs={{0,4},{8,0},{16,8},{24,16},{28,24},{20,28},{12,20},{4,12},{1,5},{9... | collective-permute-start | bytes 2359304 | tf_op jit(solution)/shard_map/ppermute | solution.py:644
  72.5 36.4 %collective-permute-start = (bf16[192,2048]{1,0:T(8,128)(2,1)S(1)}, bf16[192,2048]{1,0:T(8,128)(2,1)S(1)}, u32[]{:S(2)}, u32[]{:S(2)}) collective-permute-start(bf16[192,2048]{1,0:T(8,128)(2,1)S(1)} %pad_maximum_fusion.9.refs_0_), channel_id=1, source_target_pairs={{0,8},{8,16},{16,24},{24,28},{28,20},{20,12},{12,4},{4,0},{1,9},{9... | collective-permute-start | bytes 2359304 | tf_op jit(solution)/shard_map/ppermute | solution.py:643
  74.1 165.6 %all-gather.8.cloned.1.call-start = ((), (), s32[]{:S(2)}) async-start(), calls=%async_computation.5 | async-start | bytes 3538944 | tf_op jit(solution)/shard_map/all_gather | solution.py:1055
  79.7 50.4 %collective-permute-start.4 = (bf16[512,1536]{1,0:T(8,128)(2,1)}, bf16[512,1536]{1,0:T(8,128)(2,1)}, u32[]{:S(2)}, u32[]{:S(2)}) collective-permute-start(bf16[512,1536]{1,0:T(8,128)(2,1)} %refs_4_), channel_id=1, source_target_pairs={{0,2},{1,3},{2,0},{3,1},{4,6},{5,7},{6,4},{7,5},{8,10},{9,11},{10,... | collective-permute-start | bytes 4718600 | tf_op jit(solution)/shard_map/ppermute | solution.py:962
  108.9 24.7 %collective-permute-start.2 = (bf16[192,2048]{1,0:T(8,128)(2,1)S(1)}, bf16[192,2048]{1,0:T(8,128)(2,1)}, u32[]{:S(2)}, u32[]{:S(2)}) collective-permute-start(bf16[192,2048]{1,0:T(8,128)(2,1)S(1)} %collective-permute-done.refs_1_), channel_id=1, source_target_pairs={{0,8},{8,16},{16,24},{24,28},{28,20},{20,12},{12,4},{4,0},{1,9},{9... | collective-permute-start | bytes 2359304 | tf_op jit(solution)/shard_map/ppermute | solution.py:643
  110.4 23.1 %collective-permute-start.3 = (bf16[192,2048]{1,0:T(8,128)(2,1)S(1)}, bf16[192,2048]{1,0:T(8,128)(2,1)}, u32[]{:S(2)}, u32[]{:S(2)}) collective-permute-start(bf16[192,2048]{1,0:T(8,128)(2,1)S(1)} %collective-permute-done.1.refs_2_), channel_id=1, source_target_pairs={{0,4},{8,0},{16,8},{24,16},{28,24},{20,28},{12,20},{4,12},{1,5},{9... | collective-permute-start | bytes 2359304 | tf_op jit(solution)/shard_map/ppermute | solution.py:644
  133.8 22.0 %collective-permute-start.5 = (bf16[192,2048]{1,0:T(8,128)(2,1)}, bf16[192,2048]{1,0:T(8,128)(2,1)S(1)}, u32[]{:S(2)}, u32[]{:S(2)}) collective-permute-start(bf16[192,2048]{1,0:T(8,128)(2,1)} %collective-permute-done.2.refs_3_), channel_id=1, source_target_pairs={{0,8},{8,16},{16,24},{24,28},{28,20},{20,12},{12,4},{4,0},{1,9},{9... | collective-permute-start | bytes 2359304 | tf_op jit(solution)/shard_map/ppermute | solution.py:643
  133.8 22.0 %collective-permute-start.6 = (bf16[192,2048]{1,0:T(8,128)(2,1)}, bf16[192,2048]{1,0:T(8,128)(2,1)S(1)}, u32[]{:S(2)}, u32[]{:S(2)}) collective-permute-start(bf16[192,2048]{1,0:T(8,128)(2,1)} %collective-permute-done.3.refs_4_), channel_id=1, source_target_pairs={{0,4},{8,0},{16,8},{24,16},{28,24},{20,28},{12,20},{4,12},{1,5},{9... | collective-permute-start | bytes 2359304 | tf_op jit(solution)/shard_map/ppermute | solution.py:644
  140.3 19.9 %collective-permute-start.8 = (bf16[256,1536]{1,0:T(8,128)(2,1)}, bf16[256,1536]{1,0:T(8,128)(2,1)}, u32[]{:S(2)}, u32[]{:S(2)}) collective-permute-start(bf16[256,1536]{1,0:T(8,128)(2,1)} %slice.283), channel_id=1, source_target_pairs={{0,2},{1,3},{2,0},{3,1},{4,6},{5,7},{6,4},{7,5},{8,10},{9,11},{10,... | collective-permute-start | bytes 2359304 | tf_op jit(solution)/shard_map/ppermute | solution.py:962
  141.4 35.5 %collective-permute-start.10 = (bf16[512,1536]{1,0:T(8,128)(2,1)}, bf16[512,1536]{1,0:T(8,128)(2,1)}, u32[]{:S(2)}, u32[]{:S(2)}) collective-permute-start(bf16[512,1536]{1,0:T(8,128)(2,1)} %refs_4_), channel_id=1, source_target_pairs={{0,1},{1,0},{2,3},{3,2},{4,5},{5,4},{6,7},{7,6},{8,9},{9,8},{10,11... | collective-permute-start | bytes 4718600 | tf_op jit(solution)/shard_map/ppermute | solution.py:966
  144.6 32.3 %collective-permute-start.11 = (bf16[512,1536]{1,0:T(8,128)(2,1)}, bf16[512,1536]{1,0:T(8,128)(2,1)}, u32[]{:S(2)}, u32[]{:S(2)}) collective-permute-start(bf16[512,1536]{1,0:T(8,128)(2,1)} %collective-permute-done.4.refs_1_.refs_5_), channel_id=1, source_target_pairs={{0,1},{1,0},{2,3},{3,2},{4,5},{5,4},{6,7},{7,6},{8,9},{9,8},{10,11... | collective-permute-start | bytes 4718600 | tf_op jit(solution)/shard_map/ppermute | solution.py:966
  162.2 18.8 %collective-permute-start.9 = (bf16[256,1536]{1,0:T(8,128)(2,1)S(1)}, bf16[256,1536]{1,0:T(8,128)(2,1)S(1)}, u32[]{:S(2)}, u32[]{:S(2)}) collective-permute-start(bf16[256,1536]{1,0:T(8,128)(2,1)S(1)} %multiply_convert_fusion.7), channel_id=1, source_target_pairs={{0,2},{1,3},{2,0},{3,1},{4,6},{5,7},{6,4},{7,5},{8,10},{9,11},{10,... | collective-permute-start | bytes 2359304 | tf_op jit(solution)/shard_map/ppermute | solution.py:962
  162.8 303.2 %reduce-scatter.4.cloned.1.call-start = ((), (), s32[]{:S(2)}) async-start(), calls=%async_computation.6 | async-start | bytes 3538944 | tf_op jit(solution)/shard_map/reduce_scatter | solution.py:1153
  191.3 31.6 %collective-permute-start.15 = (bf16[96,2048]{1,0:T(8,128)(2,1)S(1)}, bf16[96,2048]{1,0:T(8,128)(2,1)}, u32[]{:S(2)}, u32[]{:S(2)}) collective-permute-start(bf16[96,2048]{1,0:T(8,128)(2,1)S(1)} %slice.187), channel_id=1, source_target_pairs={{0,4},{8,0},{16,8},{24,16},{28,24},{20,28},{12,20},{4,12},{1,5},{9... | collective-permute-start | bytes 1179656 | tf_op jit(solution)/shard_map/ppermute | solution.py:644
  191.4 20.9 %collective-permute-start.14 = (bf16[96,2048]{1,0:T(8,128)(2,1)}, bf16[96,2048]{1,0:T(8,128)(2,1)}, u32[]{:S(2)}, u32[]{:S(2)}) collective-permute-start(bf16[96,2048]{1,0:T(8,128)(2,1)} %slice.186), channel_id=1, source_target_pairs={{0,8},{8,16},{16,24},{24,28},{28,20},{20,12},{12,4},{4,0},{1,9},{9... | collective-permute-start | bytes 1179656 | tf_op jit(solution)/shard_map/ppermute | solution.py:643
  195.0 29.6 %collective-permute-start.12 = (bf16[512,1536]{1,0:T(8,128)(2,1)}, bf16[512,1536]{1,0:T(8,128)(2,1)}, u32[]{:S(2)}, u32[]{:S(2)}) collective-permute-start(bf16[512,1536]{1,0:T(8,128)(2,1)} %pad_maximum_fusion.5), channel_id=1, source_target_pairs={{0,1},{1,0},{2,3},{3,2},{4,5},{5,4},{6,7},{7,6},{8,9},{9,8},{10,11... | collective-permute-start | bytes 4718600 | tf_op jit(solution)/shard_map/ppermute | solution.py:966
  199.7 36.1 %collective-permute-start.16 = (bf16[256,1536]{1,0:T(8,128)(2,1)}, bf16[256,1536]{1,0:T(8,128)(2,1)}, u32[]{:S(2)}, u32[]{:S(2)}) collective-permute-start(bf16[256,1536]{1,0:T(8,128)(2,1)} %slice.282), channel_id=1, source_target_pairs={{0,2},{1,3},{2,0},{3,1},{4,6},{5,7},{6,4},{7,5},{8,10},{9,11},{10,... | collective-permute-start | bytes 2359304 | tf_op jit(solution)/shard_map/ppermute | solution.py:962
  238.7 28.4 %collective-permute-start.17 = (bf16[256,1536]{1,0:T(8,128)(2,1)S(1)}, bf16[256,1536]{1,0:T(8,128)(2,1)S(1)}, u32[]{:S(2)}, u32[]{:S(2)}) collective-permute-start(bf16[256,1536]{1,0:T(8,128)(2,1)S(1)} %multiply_convert_fusion.6), channel_id=1, source_target_pairs={{0,2},{1,3},{2,0},{3,1},{4,6},{5,7},{6,4},{7,5},{8,10},{9,11},{10,... | collective-permute-start | bytes 2359304 | tf_op jit(solution)/shard_map/ppermute | solution.py:962
  276.6 29.3 %collective-permute-start.20 = (bf16[256,1536]{1,0:T(8,128)(2,1)}, bf16[256,1536]{1,0:T(8,128)(2,1)}, u32[]{:S(2)}, u32[]{:S(2)}) collective-permute-start(bf16[256,1536]{1,0:T(8,128)(2,1)} %slice.281), channel_id=1, source_target_pairs={{0,2},{1,3},{2,0},{3,1},{4,6},{5,7},{6,4},{7,5},{8,10},{9,11},{10,... | collective-permute-start | bytes 2359304 | tf_op jit(solution)/shard_map/ppermute | solution.py:962
  309.4 18.7 %collective-permute-start.21 = (bf16[256,1536]{1,0:T(8,128)(2,1)S(1)}, bf16[256,1536]{1,0:T(8,128)(2,1)S(1)}, u32[]{:S(2)}, u32[]{:S(2)}) collective-permute-start(bf16[256,1536]{1,0:T(8,128)(2,1)S(1)} %add_convert_fusion.5), channel_id=1, source_target_pairs={{0,2},{1,3},{2,0},{3,1},{4,6},{5,7},{6,4},{7,5},{8,10},{9,11},{10,... | collective-permute-start | bytes 2359304 | tf_op jit(solution)/shard_map/ppermute | solution.py:962
  330.0 258.3 %reduce-scatter.8.cloned.1.call-start = ((), (), s32[]{:S(2)}) async-start(), calls=%async_computation.8 | async-start | bytes 7077888 | tf_op jit(solution)/shard_map/reduce_scatter | solution.py:1161
  331.3 47.1 %collective-permute-start.24 = (bf16[512,1536]{1,0:T(8,128)(2,1)}, bf16[512,1536]{1,0:T(8,128)(2,1)}, u32[]{:S(2)}, u32[]{:S(2)}) collective-permute-start(bf16[512,1536]{1,0:T(8,128)(2,1)} %pad_maximum_fusion.7), channel_id=1, source_target_pairs={{0,1},{1,0},{2,3},{3,2},{4,5},{5,4},{6,7},{7,6},{8,9},{9,8},{10,11... | collective-permute-start | bytes 4718600 | tf_op jit(solution)/shard_map/ppermute | solution.py:966
  337.5 23.0 %collective-permute-start.23 = (bf16[256,1536]{1,0:T(8,128)(2,1)}, bf16[256,1536]{1,0:T(8,128)(2,1)}, u32[]{:S(2)}, u32[]{:S(2)}) collective-permute-start(bf16[256,1536]{1,0:T(8,128)(2,1)} %slice.280), channel_id=1, source_target_pairs={{0,2},{1,3},{2,0},{3,1},{4,6},{5,7},{6,4},{7,5},{8,10},{9,11},{10,... | collective-permute-start | bytes 2359304 | tf_op jit(solution)/shard_map/ppermute | solution.py:962
  383.2 40.2 %collective-permute-start.27 = (bf16[256,1536]{1,0:T(8,128)(2,1)}, bf16[256,1536]{1,0:T(8,128)(2,1)}, u32[]{:S(2)}, u32[]{:S(2)}) collective-permute-start(bf16[256,1536]{1,0:T(8,128)(2,1)} %add_convert_fusion.4), channel_id=1, source_target_pairs={{0,2},{1,3},{2,0},{3,1},{4,6},{5,7},{6,4},{7,5},{8,10},{9,11},{10,... | collective-permute-start | bytes 2359304 | tf_op jit(solution)/shard_map/ppermute | solution.py:962
  384.0 212.3 %reduce-scatter.6.cloned.1.call-start = ((), (), s32[]{:S(2)}) async-start(), calls=%async_computation.7 | async-start | bytes 7864320 | tf_op jit(solution)/shard_map/reduce_scatter | solution.py:1188
  387.5 35.8 %collective-permute-start.28 = (bf16[256,1536]{1,0:T(8,128)(2,1)}, bf16[256,1536]{1,0:T(8,128)(2,1)}, u32[]{:S(2)}, u32[]{:S(2)}) collective-permute-start(bf16[256,1536]{1,0:T(8,128)(2,1)} %slice.279), channel_id=1, source_target_pairs={{0,2},{1,3},{2,0},{3,1},{4,6},{5,7},{6,4},{7,5},{8,10},{9,11},{10,... | collective-permute-start | bytes 2359304 | tf_op jit(solution)/shard_map/ppermute | solution.py:962
  427.4 38.5 %collective-permute-start.31 = (bf16[256,1536]{1,0:T(8,128)(2,1)}, bf16[256,1536]{1,0:T(8,128)(2,1)}, u32[]{:S(2)}, u32[]{:S(2)}) collective-permute-start(bf16[256,1536]{1,0:T(8,128)(2,1)} %slice.278), channel_id=1, source_target_pairs={{0,2},{1,3},{2,0},{3,1},{4,6},{5,7},{6,4},{7,5},{8,10},{9,11},{10,... | collective-permute-start | bytes 2359304 | tf_op jit(solution)/shard_map/ppermute | solution.py:962
  439.8 26.2 %collective-permute-start.30 = (bf16[256,1536]{1,0:T(8,128)(2,1)}, bf16[256,1536]{1,0:T(8,128)(2,1)}, u32[]{:S(2)}, u32[]{:S(2)}) collective-permute-start(bf16[256,1536]{1,0:T(8,128)(2,1)} %add_convert_fusion.3.refs_2_), channel_id=1, source_target_pairs={{0,2},{1,3},{2,0},{3,1},{4,6},{5,7},{6,4},{7,5},{8,10},{9,11},{10,... | collective-permute-start | bytes 2359304 | tf_op jit(solution)/shard_map/ppermute | solution.py:962
  467.7 19.5 %collective-permute-start.32 = (bf16[256,1536]{1,0:T(8,128)(2,1)S(1)}, bf16[256,1536]{1,0:T(8,128)(2,1)S(1)}, u32[]{:S(2)}, u32[]{:S(2)}) collective-permute-start(bf16[256,1536]{1,0:T(8,128)(2,1)S(1)} %add_convert_fusion.2.refs_3_), channel_id=1, source_target_pairs={{0,2},{1,3},{2,0},{3,1},{4,6},{5,7},{6,4},{7,5},{8,10},{9,11},{10,... | collective-permute-start | bytes 2359304 | tf_op jit(solution)/shard_map/ppermute | solution.py:962
  490.5 15.5 %collective-permute-start.33 = (bf16[1024,1536]{1,0:T(8,128)(2,1)}, bf16[1024,1536]{1,0:T(8,128)(2,1)}, u32[]{:S(2)}, u32[]{:S(2)}) collective-permute-start(bf16[1024,1536]{1,0:T(8,128)(2,1)} %pad_maximum_fusion.2), channel_id=1, source_target_pairs={{0,1},{1,0},{2,3},{3,2},{4,5},{5,4},{6,7},{7,6},{8,9},{9,8},{10,11... | collective-permute-start | bytes 9437192 | tf_op jit(solution)/shard_map/ppermute | solution.py:966
  (94 other events, 996.2 us)
Sparse Core Ops, SparseCore 0:
  9.6 49.0 all-gather.3
  74.2 44.0 all-gather.5
  162.9 65.1 all-gather.7
  330.1 74.7 reduce-scatter.3
  408.4 120.3 reduce-scatter.7
  531.1 62.9 reduce-scatter.5

commit v6 on v5

--- a/solution.py
+++ b/solution.py
@@ -438,35 +438,6 @@
     )(*operands)
 
 
-def gather_kernel(group, table_ref, *refs):
-    outs = refs[-(len(refs) // (group + 1)) :]
-    for m, dst in enumerate(outs):
-        for c in range(group):
-            dst[c * BLOCK : (c + 1) * BLOCK, :] = refs[m * group + c][...]
-
-
-def gather_blocks(x, tables, group):
-    streams, count = tables.shape
-    cols = x.shape[1]
-
-    def source(m, c):
-        return pl.BlockSpec((BLOCK, cols), lambda i, t: (t[m * count + i * group + c], 0))
-
-    spec = pltpu.PrefetchScalarGridSpec(
-        num_scalar_prefetch=1,
-        grid=(count // group,),
-        in_specs=[source(m, c) for m in range(streams) for c in range(group)],
-        out_specs=[pl.BlockSpec((group * BLOCK, cols), lambda i, t: (i, 0))] * streams,
-    )
-    return pl.pallas_call(
-        functools.partial(gather_kernel, group),
-        grid_spec=spec,
-        out_shape=[jax.ShapeDtypeStruct((count * BLOCK, cols), x.dtype)] * streams,
-        cost_estimate=pl.CostEstimate(flops=0, bytes_accessed=4 * streams * count * BLOCK * cols, transcendentals=0),
-        name="gather_blocks",
-    )(tables.reshape(-1), *([x] * (group * streams)))
-
-
 def pick_kernel(bounds, picks, table_ref, *refs):
     total = sum(len(part) for part in bounds)
     parts, outs = refs[:total], refs[total:-3]
@@ -496,8 +467,8 @@
         store.wait()
 
 
-def pick_blocks(groups, tables):
-    picks = tables[0].shape[0]
+def pick_blocks(groups, table):
+    picks = table.shape[0] // len(groups)
     cols = groups[0][0].shape[1]
     dtype = groups[0][0].dtype
     bounds = []
@@ -526,7 +497,7 @@
         out_shape=[jax.ShapeDtypeStruct((picks * BLOCK, cols), dtype)] * len(groups),
         cost_estimate=pl.CostEstimate(flops=0, bytes_accessed=4 * slots * BLOCK * cols, transcendentals=0),
         name="pick_blocks",
-    )(jnp.concatenate(tables).astype(jnp.int32), *flat)
+    )(table, *flat)
 
 
 def place_kernel(count, rows, spot_ref, *refs):
@@ -947,11 +918,12 @@
     count = lax.axis_size("tp")
     me = lax.axis_index("tp")
     pieces = [x] + [lax.ppermute(x, "tp", [(i, (i + s) % count) for i in range(count)]) for s in range(1, count)]
-    stacked = jnp.stack(pieces)
-    slots = (me - jnp.arange(count, dtype=jnp.int32)) % count
     total = jnp.zeros_like(x)
     for r in range(count):
-        total = total + jnp.sum(jnp.where((slots == r)[:, None, None], stacked, 0.0), axis=0)
+        chosen = pieces[0]
+        for step in range(1, count):
+            chosen = jnp.where((me - step) % count == r, pieces[step], chosen)
+        total = total + chosen
     return total
 
 
@@ -1034,7 +1006,9 @@
     own_spots = ((origin // 2) + 2 * (origin % 2)) * per_own + own_packed // per_bin * per_half + own_packed % per_half
     holder = me ^ (slotted // per_own)
     cot_table = ((holder // 2) + 2 * (holder % 2)) * per_own + slotted % per_own
-    tables = (table.astype(jnp.int32), first, last, slot, slotted, own_places, own_spots, cot_table)
+    x_table = slotted[:, :per_half].reshape(-1)
+    end_table = jnp.concatenate([own_places, own_spots]).astype(jnp.int32)
+    tables = (table.astype(jnp.int32), first, last, slot, x_table, end_table, cot_table.reshape(-1))
 
     extras = jnp.concatenate(
         [w_beta, gain_attn[:, None], gain_ffn[:, None], jnp.zeros((shard, BLOCK - heads - 2), bf16)], axis=1
@@ -1042,15 +1016,15 @@
     ffn_pack = jnp.concatenate([w_gate, w_up], axis=1)
     full_tokens = lax.all_gather(tokens, "tp", axis=0, tiled=True)
     tables = together(*tables)
-    table, first, last, slot, slotted, own_places, own_spots, cot_table = tables
-    ffn_pack, slotted = together(ffn_pack, slotted)
+    table, first, last, slot, x_table, end_table, cot_table = tables
     w_in = ring_spread([w_query, w_key, w_value, w_house, extras], "fsdp")
-    full_tokens, w_in, ffn_pack, out_shard, down_shard, cotangent, table, first, last, slot, own_places, own_spots = together(
-        full_tokens, w_in, ffn_pack, w_out, w_down, cotangent, table, first, last, slot, own_places, own_spots
+    full_tokens, w_in, ffn_pack, out_shard, down_shard, cotangent, *tables = together(
+        full_tokens, w_in, ffn_pack, w_out, w_down, cotangent, *tables
     )
+    table, first, last, slot, x_table, end_table, cot_table = tables
     ffn_ring = RingGather(ffn_pack, "fsdp", True)
     ffn_ring.hop()
-    x_rows = gather_blocks(full_tokens, slotted[:, :per_half], per_half)
+    x_rows = pick_blocks([[full_tokens]] * bins, x_table)
     full_out = lax.all_gather(out_shard, "fsdp", axis=0, tiled=True)
     full_down = lax.all_gather(down_shard, "fsdp", axis=0, tiled=True)
     cot_far = across(cotangent)
@@ -1097,13 +1071,13 @@
     normed_far = across(normed_own)
     prep[0], normed_own = together(prep[0], normed_own)
     saved.append(list(run(prep)))
-    saved[1][0], normed_far, cot_parts[2], cot_parts[3] = together(saved[1][0], normed_far, *cot_parts[2:])
+    saved[1][0], normed_far, cot_parts[2], cot_parts[3] = ffn_ring.before(saved[1][0], normed_far, *cot_parts[2:])
     pair = jnp.concatenate([normed_own, normed_far], axis=0)
     normed_two.append(jnp.concatenate([pair, beside(pair)], axis=0))
     attn_own, attn_far = share(cols_contract(saved[1][0], full_out).astype(bf16))
     attn_own, cot_parts[3], ffn_ring.x = together(attn_own, cot_parts[3], ffn_ring.x)
     ffn_full = ffn_ring.finish()
-    cot_rows = list(pick_blocks([cot_parts] * bins, list(cot_table)))
+    cot_rows = list(pick_blocks([cot_parts] * bins, cot_table))
 
     full_gate, full_up = ffn_full[:, :hidden_width], ffn_full[:, hidden_width : 2 * hidden_width]
     full_gate_up = ffn_full
@@ -1145,19 +1119,20 @@
         return (cot_own + norm_two_grad).astype(bf16)
 
     ffn(1, normed_two[1], lambda rows: rows)
-    gate_up[1], back_own, back_far = together(gate_up[1], back_own, back_far)
+    gate_up[1], hidden[1], back_own, back_far = together(gate_up[1], hidden[1], back_own, back_far)
     dh_own = close_back(0, back_own, back_far)
+    hidden[1], dh_own = together(hidden[1], dh_own)
     dh_far = across(dh_own)
     grads_down = sum(rows_contract(cot_rows[m], hidden[m]) for m in streams)
     grads_down, gate_up[1] = together(grads_down.astype(bf16), gate_up[1])
     sum_down = lax.psum_scatter(grads_down, "fsdp", scatter_dimension=0, tiled=True)
-    rows, dh_own, dh_far = together(ffn_back_rows(1), dh_own, dh_far)
+    rows, dh_own = together(ffn_back_rows(1), dh_own)
     back_own, back_far = share(rows)
     back_own, normed_two[0], normed_two[1] = together(back_own, *normed_two)
+    grads_in = sum(rows_contract(normed_two[m], gate_up[m]) for m in streams)
+    grads_in, back_far, dh_far = together(grads_in.astype(bf16), back_far, dh_far)
     pair = jnp.concatenate([dh_own, dh_far], axis=0)
     grad_attn.append(jnp.concatenate([pair, beside(pair)], axis=0))
-    grads_in = sum(rows_contract(normed_two[m], gate_up[m]) for m in streams)
-    grads_in, back_far = together(grads_in.astype(bf16), back_far)
     sum_in = lax.psum_scatter(grads_in, "fsdp", scatter_dimension=0, tiled=True)
     dh_own = close_back(1, back_own, back_far)
     dh_far = across(dh_own)
@@ -1181,12 +1156,10 @@
     y_rows.append(finish_y(1))
     y_across.append(across(y_rows[1]))
     attn_grads, d_proj, y_across[1] = together(rows_contract(normed, d_proj).astype(bf16), d_proj, y_across[1])
-    y_pair = jnp.concatenate([*y_rows, *y_across], axis=0)
-    rows_one, y_other, attn_grads = together(
-        cols_contract(d_proj, w_in).astype(bf16), beside(y_pair), attn_grads
-    )
+    y_other = [beside(part) for part in (*y_rows, *y_across)]
+    rows_one, attn_grads, *y_other = together(cols_contract(d_proj, w_in).astype(bf16), attn_grads, *y_other)
     grad_one = lax.psum_scatter(rows_one, "tp", scatter_dimension=0, tiled=True)
-    dh_own, out_y = pick_blocks([grad_attn, [*y_rows, *y_across, y_other]], [own_places, own_spots])
+    dh_own, out_y = pick_blocks([grad_attn, [*y_rows, *y_across, *y_other]], end_table)
     attn_grads, dh_own, out_y = together(attn_grads, dh_own, out_y)
     attn_sum, grad_out = ring_sum([attn_grads, grad_out], "fsdp")
     sum_in, sum_down = sum_in.astype(f32), sum_down.astype(f32)

time: 619 us -> 597 us (0.964)
  Pallas kernels: 255 us -> 243 us
  waiting for transfers between devices: 29.5 us -> 21.1 us
    ppermute x4, waiting for transfers between devices: 8.81 us -> 0.01 us  [hop(): lax.ppermute(from_right, self.axis, self.left)]
    pallas_call x1, Pallas kernels: 71.3 us -> 64 us  [ring_sum(): pl.pallas_call(functools.partial(ring_kernel, axis, count, rows, widths),...]
    pallas_call x2 -> x3, Pallas kernels: 9.67 us -> 12.5 us  [pick_blocks(): pl.pallas_call(functools.partial(pick_kernel, bounds, picks), grid_spec=s...]
    unnamed x171 -> x167, local copies, waits for them, and re-layouts: 23.2 us -> 25.8 us
  transfers between devices with their start and end apart: 43 -> 46, of which waited for: 8 -> 8; matrix products, arithmetic and copies ran while one was open for 42% -> 40% of each run, Pallas kernels for 42% -> 41%
where the time goes in v6:
time: 597 us; the launch traced here: 587 us
  Pallas kernels  243 us (41%)
  matrix products  170 us (28%)
  local copies, waits for them, and re-layouts  57.9 us (10%)
  other arithmetic  51.5 us (9%)
  starting transfers between devices  28 us (5%)
  waiting for transfers between devices  21.1 us (4%)
  between operations  15.9 us (3%)
    pallas_call x1, Pallas kernels, ring_sum(): pl.pallas_call(functools.partial(ring_kernel, axis, count, rows, widths),...  64 us
    pallas_call x1, Pallas kernels, ring_spread(): pl.pallas_call(functools.partial(spread_kernel, axis, count, rows, widths...  55.6 us
    pallas_call x2, Pallas kernels, attention_bwd(): pl.pallas_call(functools.partial(bwd_kernel, heads, depth, scale), grid_s...  53.1 us
    dot_general x7, matrix products, rows_contract(): lax.dot_general(a, b, (((0,), (0,)), ((), ())), preferred_element_type=f32)  53 us
    dot_general x8, matrix products, cols_contract(): lax.dot_general(a, b, (((1,), (1,)), ((), ())), preferred_element_type=f32)  48.7 us
    pallas_call x2, Pallas kernels, attention_fwd(): pl.pallas_call(functools.partial(fwd_kernel, heads, depth, scale), grid_s...  31.1 us
    unnamed x167, local copies, waits for them, and re-layouts  25.8 us
    pallas_call x2, Pallas kernels, attention_prep(): pl.pallas_call(functools.partial(prep_kernel, heads, step), grid_spec=spe...  21.2 us
  transfers between devices with their start and end apart: 46, of which 8 were waited for; matrix products, arithmetic and copies ran while one was open for 40% of the time, Pallas kernels for 41%

profile of v6, /device:TPU:0, one launch (start us, length us, event | category | flops | bytes accessed | tf_op | source)
XLA Modules:
  0.0 587.3 jit_solution(16251691847478821837)
XLA Ops:
  16.0 55.6 %ring_spread.1 = bf16[1536,1664]{1,0:T(8,128)(2,1)} custom-call(bf16[192,384]{1,0:T(8,128)(2,1)} %refs_0_.1, bf16[192,384]{1,0:T(8,128)(2,1)} %refs_1_.1, bf16[192,384]{1,0:T(8,128)(2,1)} %refs_2_.1, bf16[192,384]{1,0:T(8,128)(2,1)} %refs_3_.1, bf16[192,128]{1,0:T(8,128)(2,1)} %maximum_maximum_fusion.refs_4_), custom_call_target="tpu_custom_call" | custom-call | bytes 10223616 | tf_op jit(solution)/shard_map/ring_spread/pallas_call | solution.py:871
  73.9 4.2 fusion
  81.1 16.4 %convolution_convert_fusion.refs_0_.refs_1_.refs_2_.refs_3_.refs_4_.refs_5_.refs_6_.refs_7_.refs_8_.refs_9_.refs_10_.refs_11_.refs_12_.refs_13_.refs_14_.refs_15_.v_ref = bf16[2048,1664]{1,0:T(8,128)(2,1)} fusion(bf16[1536,1664]{1,0:T(8,128)(2,1)} %ring_spread.1, bf16[2048,1536]{1,0:T(8,128)(2,1)S(1)} %copy-done, f32[1536]{0:T(1024)S(1)} %get-tuple-element.295, ...), kind=kOutput, calls=%fused_computation.6 | convolution fusion | flops 10484973568 | bytes 18233344 | tf_op jit(solution)/shard_map/dot_general | solution.py:1037
  98.1 10.5 %attn_prep.2 = (f32[8,3,128,128]{3,2,1,0:T(8,128)}, bf16[1024,384]{1,0:T(8,128)(2,1)}, bf16[8,3,128,256]{3,2,1,0:T(8,128)(2,1)}, bf16[8,3,128,128]{3,2,1,0:T(8,128)(2,1)}, bf16[8,3,128,256]{3,2,1,0:T(8,128)(2,1)}) custom-call(s32[8]{0:T(128)} %get-tuple-element.334.table_ref, ...), custom_call_target="tpu_custom_call" | custom-call | flops 2264924160 | bytes 2359296 | tf_op jit(solution)/shard_map/attn_prep/pallas_call | solution.py:318
  111.2 18.7 %attn_fwd.2 = (bf16[1024,384]{1,0:T(8,128)(2,1)}, f32[1024,384]{1,0:T(8,128)}, bf16[8,8,3,128,128]{4,3,2,1,0:T(8,128)(2,1)}, bf16[8,7,3,128,128]{4,3,2,1,0:T(8,128)(2,1)}) custom-call(s32[8]{0:T(128)} %get-tuple-element.333.first_ref, s32[8]{0:T(128)} %get-tuple-element.334.table_ref, s32[8]{0:T(128)} %copy-done.55, ...), custom_call_target="tpu_custom_call" | custom-call | flops 2415919104 | bytes 2359296 | tf_op jit(solution)/shard_map/attn_fwd/pallas_call | solution.py:362
  144.1 10.7 %attn_prep.3 = (f32[8,3,128,128]{3,2,1,0:T(8,128)}, bf16[1024,384]{1,0:T(8,128)(2,1)}, bf16[8,3,128,256]{3,2,1,0:T(8,128)(2,1)}, bf16[8,3,128,128]{3,2,1,0:T(8,128)(2,1)}, bf16[8,3,128,256]{3,2,1,0:T(8,128)(2,1)}) custom-call(s32[8]{0:T(128)} %get-tuple-element.335.table_ref, ...), custom_call_target="tpu_custom_call" | custom-call | flops 2264924160 | bytes 2359296 | tf_op jit(solution)/shard_map/attn_prep/pallas_call | solution.py:318
  154.8 5.2 collective-permute-done.8
  165.6 12.4 %attn_fwd.3 = (bf16[1024,384]{1,0:T(8,128)(2,1)}, f32[1024,384]{1,0:T(8,128)}, bf16[8,8,3,128,128]{4,3,2,1,0:T(8,128)(2,1)}, bf16[8,7,3,128,128]{4,3,2,1,0:T(8,128)(2,1)}) custom-call(s32[8]{0:T(128)} %get-tuple-element.332.first_ref, s32[8]{0:T(128)} %get-tuple-element.335.table_ref, s32[8]{0:T(128)} %copy-done.55, ...), custom_call_target="tpu_custom_call" | custom-call | flops 2415919104 | bytes 2359296 | tf_op jit(solution)/shard_map/attn_fwd/pallas_call | solution.py:362
  180.9 3.3 convolution_convert_fusion.5
  194.9 5.6 place_pieces.1
  200.5 6.2 %pick_blocks.4 = (bf16[1024,1536]{1,0:T(8,128)(2,1)}, bf16[1024,1536]{1,0:T(8,128)(2,1)}) custom-call(s32[16]{0:T(128)} %get-tuple-element.182.table_ref, bf16[512,1536]{1,0:T(8,128)(2,1)} %refs_4_, bf16[512,1536]{1,0:T(8,128)(2,1)} %collective-permute-done.4.refs_1_.refs_5_, bf16[512,1536]{1,0:T(8,128)(2,1)} %collective-permute-done.12.refs_2_.refs_6_, ...), custom_call_target="tpu_custom_call" | custom-call | bytes 12582912 | tf_op jit(solution)/shard_map/pick_blocks/pallas_call | solution.py:494
  212.9 8.3 %fusion.16 = f32[1024,1024]{0,1:T(8,128)} fusion(bf16[1024,1536]{1,0:T(8,128)(2,1)} %constant_dynamic-update-slice_fusion, bf16[1536,2048]{1,0:T(8,128)(2,1)} %constant_dynamic-update-slice_fusion.12), kind=kOutput, calls=%fused_computation.49 | convolution fusion | flops 3221225472 | bytes 10485760 | tf_op jit(solution)/shard_map/dot_general | solution.py:1088
  226.6 8.5 %fusion.42 = f32[1024,1024]{0,1:T(8,128)} fusion(bf16[1024,1536]{1,0:T(8,128)(2,1)} %get-tuple-element.189, bf16[1536,1024]{1,0:T(8,128)(2,1)} %all-gather.8.cloned.1.call-done), kind=kOutput, calls=%fused_computation.203 | convolution fusion | flops 3221225472 | bytes 10485760 | tf_op jit(solution)/shard_map/dot_general | solution.py:1091
  235.1 9.8 %multiply_convert_fusion.4 = (bf16[1024,1024]{0,1:T(8,128)(2,1)S(1)}, bf16[1024,1024]{0,1:T(8,128)(2,1)}, bf16[1024,1024]{0,1:T(8,128)(2,1)}) fusion(f32[1024,1024]{0,1:T(8,128)} %fusion.42, f32[1024,1024]{0,1:T(8,128)S(1)} %copy-done.65, bf16[1024,1536]{1,0:T(8,128)(2,1)S(1)} %copy-done.47, bf16[1536,2048]{1,0:T(8,128)(2,1)} %constant_dynamic-update-slice_fusion.12), kind=kOutput, calls=%fused_computation.18 | convolution fusion | flops 3236954112 | bytes 20971520 | tf_op jit(solution)/shard_map/dot_general | solution.py:1087
  244.9 9.0 %convolution_convert_fusion.4 = bf16[1024,1536]{1,0:T(8,128)(2,1)S(1)} fusion(bf16[1536,2048]{1,0:T(8,128)(2,1)S(1)} %bitcast.67, bf16[1024,1024]{0,1:T(8,128)(2,1)} %get-tuple-element.316, bf16[1024,1024]{0,1:T(8,128)(2,1)S(1)} %get-tuple-element.315), kind=kOutput, calls=%fused_computation.25 | convolution fusion | flops 6452412416 | bytes 13631488 | tf_op jit(solution)/shard_map/dot_general | solution.py:569
  256.7 5.0 fusion.41
  265.7 5.0 fusion.18
  270.8 9.7 %multiply_convert_fusion = (bf16[1024,1024]{0,1:T(8,128)(2,1)}, bf16[1024,1024]{0,1:T(8,128)(2,1)S(1)}, bf16[1024,1024]{0,1:T(8,128)(2,1)S(1)}) fusion(f32[1024,1024]{0,1:T(8,128)} %fusion.18, f32[1024,1024]{0,1:T(8,128)} %fusion.41, bf16[1024,1536]{1,0:T(8,128)(2,1)} %copy-done.49, bf16[1536,2048]{1,0:T(8,128)(2,1)S(1)} %bitcast.67), kind=kOutput, calls=%fused_computation.12 | convolution fusion | flops 3236954112 | bytes 20971520 | tf_op jit(solution)/shard_map/dot_general | solution.py:1088
  286.6 3.6 fusion.43
  290.2 5.2 add_convert_fusion.1
  295.3 10.2 %convolution_convert_fusion.3 = bf16[1024,1536]{1,0:T(8,128)(2,1)S(1)} fusion(bf16[1024,2048]{0,1:T(8,128)(2,1)} %pad_maximum_fusion.1, bf16[1536,2048]{1,0:T(8,128)(2,1)} %constant_dynamic-update-slice_fusion.12), kind=kOutput, calls=%fused_computation.24 | convolution fusion | flops 6444023808 | bytes 13631488 | tf_op jit(solution)/shard_map/dot_general | solution.py:569
  316.6 9.7 %fusion.44 = f32[1536,2048]{1,0:T(8,128)} fusion(bf16[1024,1536]{1,0:T(8,128)(2,1)S(1)} %copy-done.50, bf16[1024,2048]{0,1:T(8,128)(2,1)S(1)} %copy-done.16), kind=kOutput, calls=%fused_computation.205 | convolution fusion | flops 6442450944 | bytes 19922944 | tf_op jit(solution)/shard_map/dot_general | solution.py:565
  326.3 12.3 %add_convert_fusion = bf16[1536,2048]{1,0:T(8,128)(2,1)} fusion(f32[1536,2048]{1,0:T(8,128)} %fusion.44, bf16[1024,1536]{1,0:T(8,128)(2,1)S(1)} %copy-done.48, bf16[1024,1024]{0,1:T(8,128)(2,1)} %get-tuple-element.316, bf16[1024,1024]{0,1:T(8,128)(2,1)S(1)} %copy-done.71), kind=kOutput, calls=%fused_computation.5 | convolution fusion | flops 6457131008 | bytes 26214400 | tf_op jit(solution)/shard_map/dot_general | solution.py:565
  338.7 5.8 collective-permute-done.22
  349.5 3.7 convolution_convert_fusion.8
  355.6 3.7 convolution_convert_fusion.7
  382.7 30.8 %attn_bwd.2.refs_26_ = bf16[2048,1664]{1,0:T(8,128)(2,1)} custom-call(s32[8]{0:T(128)} %get-tuple-element.330.last_ref, s32[8]{0:T(128)} %get-tuple-element.334.table_ref, s32[8]{0:T(128)} %copy-done.55, bf16[1024,384]{1,0:T(8,128)(2,1)} %convolution_convert_fusion.10.refs_0_, bf16[1024,384]{1,0:T(8,128)(2,1)} %get-tuple-element.156.refs_1_, ...), custom_call_target="tpu_custom_call" | custom-call | flops 6039797760 | bytes 3145728 | tf_op jit(solution)/shard_map/attn_bwd/pallas_call | solution.py:429
  431.3 22.3 %attn_bwd.3 = bf16[2048,1664]{1,0:T(8,128)(2,1)} custom-call(s32[8]{0:T(128)} %get-tuple-element.331.last_ref, s32[8]{0:T(128)} %get-tuple-element.335.table_ref, s32[8]{0:T(128)} %copy-done.55, bf16[1024,384]{1,0:T(8,128)(2,1)} %convolution_convert_fusion.9.refs_0_, bf16[1024,384]{1,0:T(8,128)(2,1)} %get-tuple-element.177.refs_1_, ...), custom_call_target="tpu_custom_call", output_to_operand_aliasing={{}: (29, {})} | custom-call | flops 6039797760 | bytes 3145728 | tf_op jit(solution)/shard_map/attn_bwd/pallas_call | solution.py:429
  458.7 17.5 %convolution_convert_fusion.2.refs_0_ = bf16[1536,1664]{1,0:T(8,128)(2,1)} fusion(bf16[2048,1664]{1,0:T(8,128)(2,1)} %attn_bwd.3, bf16[2048,1536]{1,0:T(8,128)(2,1)} %all-gather.4.cloned.1.call-done.refs_0_.refs_1_, f32[1536]{0:T(1024)S(1)} %copy-done.52, f32[2048]{0:T(1024)S(1)} %copy-done.58), kind=kOutput, calls=%fused_computation.8 | convolution fusion | flops 10484121600 | bytes 18233344 | tf_op jit(solution)/shard_map/dot_general | solution.py:565
  477.4 14.1 %convolution_convert_fusion.1 = bf16[2048,1536]{1,0:T(8,128)(2,1)} fusion(bf16[2048,1664]{1,0:T(8,128)(2,1)S(1)} %bitcast.65, bf16[1536,1664]{1,0:T(8,128)(2,1)S(1)} %bitcast.69), kind=kOutput, calls=%fused_computation.7 | convolution fusion | flops 10472128512 | bytes 18219008 | tf_op jit(solution)/shard_map/dot_general | solution.py:569
  495.8 3.5 pick_blocks.5
  499.3 64.0 %ring_sum.1 = (f32[192,1664]{1,0:T(8,128)}, f32[192,384]{1,0:T(8,128)}) custom-call(bf16[1536,1664]{1,0:T(8,128)(2,1)} %convolution_convert_fusion.2.refs_0_, bf16[1536,384]{1,0:T(8,128)(2,1)} %fusion.13.refs_1_), custom_call_target="tpu_custom_call" | custom-call | bytes 12582912 | tf_op jit(solution)/shard_map/ring_sum/pallas_call | solution.py:898
  (376 shorter events, 161.0 us)
Async XLA Ops:
  7.2 64.6 %all-gather.4.cloned.1.call-start = ((), (), s32[]{:S(2)}) async-start(), calls=%async_computation.3 | async-start | bytes 7864320 | tf_op jit(solution)/shard_map/all_gather | solution.py:1017
  7.9 122.0 %all-gather.6.cloned.1.call-start = ((), (), s32[]{:S(2)}) async-start(), calls=%async_computation.4 | async-start | bytes 1327104 | tf_op jit(solution)/shard_map/all_gather | solution.py:1028
  71.8 36.8 %collective-permute-start.1 = (bf16[192,2048]{1,0:T(8,128)(2,1)S(1)}, bf16[192,2048]{1,0:T(8,128)(2,1)S(1)}, u32[]{:S(2)}, u32[]{:S(2)}) collective-permute-start(bf16[192,2048]{1,0:T(8,128)(2,1)S(1)} %pad_maximum_fusion.8.refs_0_), channel_id=1, source_target_pairs={{0,4},{8,0},{16,8},{24,16},{28,24},{20,28},{12,20},{4,12},{1,5},{9... | collective-permute-start | bytes 2359304 | tf_op jit(solution)/shard_map/ppermute | solution.py:615
  72.3 36.3 %collective-permute-start = (bf16[192,2048]{1,0:T(8,128)(2,1)S(1)}, bf16[192,2048]{1,0:T(8,128)(2,1)S(1)}, u32[]{:S(2)}, u32[]{:S(2)}) collective-permute-start(bf16[192,2048]{1,0:T(8,128)(2,1)S(1)} %pad_maximum_fusion.8.refs_0_), channel_id=1, source_target_pairs={{0,8},{8,16},{16,24},{24,28},{28,20},{20,12},{12,4},{4,0},{1,9},{9... | collective-permute-start | bytes 2359304 | tf_op jit(solution)/shard_map/ppermute | solution.py:614
  73.9 152.7 %all-gather.8.cloned.1.call-start = ((), (), s32[]{:S(2)}) async-start(), calls=%async_computation.5 | async-start | bytes 3538944 | tf_op jit(solution)/shard_map/all_gather | solution.py:1029
  79.5 50.4 %collective-permute-start.4 = (bf16[512,1536]{1,0:T(8,128)(2,1)}, bf16[512,1536]{1,0:T(8,128)(2,1)}, u32[]{:S(2)}, u32[]{:S(2)}) collective-permute-start(bf16[512,1536]{1,0:T(8,128)(2,1)} %refs_4_), channel_id=1, source_target_pairs={{0,2},{1,3},{2,0},{3,1},{4,6},{5,7},{6,4},{7,5},{8,10},{9,11},{10,... | collective-permute-start | bytes 4718600 | tf_op jit(solution)/shard_map/ppermute | solution.py:934
  108.6 24.7 %collective-permute-start.2 = (bf16[192,2048]{1,0:T(8,128)(2,1)S(1)}, bf16[192,2048]{1,0:T(8,128)(2,1)}, u32[]{:S(2)}, u32[]{:S(2)}) collective-permute-start(bf16[192,2048]{1,0:T(8,128)(2,1)S(1)} %collective-permute-done.refs_1_), channel_id=1, source_target_pairs={{0,8},{8,16},{16,24},{24,28},{28,20},{20,12},{12,4},{4,0},{1,9},{9... | collective-permute-start | bytes 2359304 | tf_op jit(solution)/shard_map/ppermute | solution.py:614
  110.2 23.2 %collective-permute-start.3 = (bf16[192,2048]{1,0:T(8,128)(2,1)S(1)}, bf16[192,2048]{1,0:T(8,128)(2,1)}, u32[]{:S(2)}, u32[]{:S(2)}) collective-permute-start(bf16[192,2048]{1,0:T(8,128)(2,1)S(1)} %collective-permute-done.1.refs_2_), channel_id=1, source_target_pairs={{0,4},{8,0},{16,8},{24,16},{28,24},{20,28},{12,20},{4,12},{1,5},{9... | collective-permute-start | bytes 2359304 | tf_op jit(solution)/shard_map/ppermute | solution.py:615
  133.5 21.2 %collective-permute-start.5 = (bf16[192,2048]{1,0:T(8,128)(2,1)}, bf16[192,2048]{1,0:T(8,128)(2,1)S(1)}, u32[]{:S(2)}, u32[]{:S(2)}) collective-permute-start(bf16[192,2048]{1,0:T(8,128)(2,1)} %collective-permute-done.2.refs_3_), channel_id=1, source_target_pairs={{0,8},{8,16},{16,24},{24,28},{28,20},{20,12},{12,4},{4,0},{1,9},{9... | collective-permute-start | bytes 2359304 | tf_op jit(solution)/shard_map/ppermute | solution.py:614
  133.6 21.2 %collective-permute-start.6 = (bf16[192,2048]{1,0:T(8,128)(2,1)}, bf16[192,2048]{1,0:T(8,128)(2,1)S(1)}, u32[]{:S(2)}, u32[]{:S(2)}) collective-permute-start(bf16[192,2048]{1,0:T(8,128)(2,1)} %collective-permute-done.3.refs_4_), channel_id=1, source_target_pairs={{0,4},{8,0},{16,8},{24,16},{28,24},{20,28},{12,20},{4,12},{1,5},{9... | collective-permute-start | bytes 2359304 | tf_op jit(solution)/shard_map/ppermute | solution.py:615
  140.1 19.9 %collective-permute-start.8 = (bf16[256,1536]{1,0:T(8,128)(2,1)}, bf16[256,1536]{1,0:T(8,128)(2,1)}, u32[]{:S(2)}, u32[]{:S(2)}) collective-permute-start(bf16[256,1536]{1,0:T(8,128)(2,1)} %slice.283), channel_id=1, source_target_pairs={{0,2},{1,3},{2,0},{3,1},{4,6},{5,7},{6,4},{7,5},{8,10},{9,11},{10,... | collective-permute-start | bytes 2359304 | tf_op jit(solution)/shard_map/ppermute | solution.py:934
  140.6 37.4 %collective-permute-start.12 = (bf16[512,1536]{1,0:T(8,128)(2,1)}, bf16[512,1536]{1,0:T(8,128)(2,1)}, u32[]{:S(2)}, u32[]{:S(2)}) collective-permute-start(bf16[512,1536]{1,0:T(8,128)(2,1)} %refs_4_), channel_id=1, source_target_pairs={{0,1},{1,0},{2,3},{3,2},{4,5},{5,4},{6,7},{7,6},{8,9},{9,8},{10,11... | collective-permute-start | bytes 4718600 | tf_op jit(solution)/shard_map/ppermute | solution.py:938
  143.5 34.5 %collective-permute-start.13 = (bf16[512,1536]{1,0:T(8,128)(2,1)}, bf16[512,1536]{1,0:T(8,128)(2,1)}, u32[]{:S(2)}, u32[]{:S(2)}) collective-permute-start(bf16[512,1536]{1,0:T(8,128)(2,1)} %collective-permute-done.4.refs_1_.refs_5_), channel_id=1, source_target_pairs={{0,1},{1,0},{2,3},{3,2},{4,5},{5,4},{6,7},{7,6},{8,9},{9,8},{10,11... | collective-permute-start | bytes 4718600 | tf_op jit(solution)/shard_map/ppermute | solution.py:938
  162.1 18.8 %collective-permute-start.11 = (bf16[256,1536]{1,0:T(8,128)(2,1)S(1)}, bf16[256,1536]{1,0:T(8,128)(2,1)S(1)}, u32[]{:S(2)}, u32[]{:S(2)}) collective-permute-start(bf16[256,1536]{1,0:T(8,128)(2,1)S(1)} %multiply_convert_fusion.7), channel_id=1, source_target_pairs={{0,2},{1,3},{2,0},{3,1},{4,6},{5,7},{6,4},{7,5},{8,10},{9,11},{10,... | collective-permute-start | bytes 2359304 | tf_op jit(solution)/shard_map/ppermute | solution.py:934
  163.5 14.5 %collective-permute-start.9 = (bf16[96,2048]{1,0:T(8,128)(2,1)S(1)}, bf16[96,2048]{1,0:T(8,128)(2,1)}, u32[]{:S(2)}, u32[]{:S(2)}) collective-permute-start(bf16[96,2048]{1,0:T(8,128)(2,1)S(1)} %slice.182), channel_id=1, source_target_pairs={{0,8},{8,16},{16,24},{24,28},{28,20},{20,12},{12,4},{4,0},{1,9},{9... | collective-permute-start | bytes 1179656 | tf_op jit(solution)/shard_map/ppermute | solution.py:614
  165.5 288.2 %reduce-scatter.4.cloned.1.call-start = ((), (), s32[]{:S(2)}) async-start(), calls=%async_computation.6 | async-start | bytes 3538944 | tf_op jit(solution)/shard_map/reduce_scatter | solution.py:1128
  189.2 21.0 %collective-permute-start.14 = (bf16[512,1536]{1,0:T(8,128)(2,1)}, bf16[512,1536]{1,0:T(8,128)(2,1)}, u32[]{:S(2)}, u32[]{:S(2)}) collective-permute-start(bf16[512,1536]{1,0:T(8,128)(2,1)} %pad_maximum_fusion.4), channel_id=1, source_target_pairs={{0,1},{1,0},{2,3},{3,2},{4,5},{5,4},{6,7},{7,6},{8,9},{9,8},{10,11... | collective-permute-start | bytes 4718600 | tf_op jit(solution)/shard_map/ppermute | solution.py:938
  194.4 26.9 %collective-permute-start.16 = (bf16[256,1536]{1,0:T(8,128)(2,1)}, bf16[256,1536]{1,0:T(8,128)(2,1)}, u32[]{:S(2)}, u32[]{:S(2)}) collective-permute-start(bf16[256,1536]{1,0:T(8,128)(2,1)} %slice.282), channel_id=1, source_target_pairs={{0,2},{1,3},{2,0},{3,1},{4,6},{5,7},{6,4},{7,5},{8,10},{9,11},{10,... | collective-permute-start | bytes 2359304 | tf_op jit(solution)/shard_map/ppermute | solution.py:934
  224.1 29.8 %collective-permute-start.17 = (bf16[256,1536]{1,0:T(8,128)(2,1)S(1)}, bf16[256,1536]{1,0:T(8,128)(2,1)S(1)}, u32[]{:S(2)}, u32[]{:S(2)}) collective-permute-start(bf16[256,1536]{1,0:T(8,128)(2,1)S(1)} %multiply_convert_fusion.6), channel_id=1, source_target_pairs={{0,2},{1,3},{2,0},{3,1},{4,6},{5,7},{6,4},{7,5},{8,10},{9,11},{10,... | collective-permute-start | bytes 2359304 | tf_op jit(solution)/shard_map/ppermute | solution.py:934
  262.4 20.6 %collective-permute-start.20 = (bf16[256,1536]{1,0:T(8,128)(2,1)S(1)}, bf16[256,1536]{1,0:T(8,128)(2,1)S(1)}, u32[]{:S(2)}, u32[]{:S(2)}) collective-permute-start(bf16[256,1536]{1,0:T(8,128)(2,1)S(1)} %slice.281), channel_id=1, source_target_pairs={{0,2},{1,3},{2,0},{3,1},{4,6},{5,7},{6,4},{7,5},{8,10},{9,11},{10,... | collective-permute-start | bytes 2359304 | tf_op jit(solution)/shard_map/ppermute | solution.py:934
  307.3 31.3 %collective-permute-start.23 = (bf16[256,1536]{1,0:T(8,128)(2,1)}, bf16[256,1536]{1,0:T(8,128)(2,1)}, u32[]{:S(2)}, u32[]{:S(2)}) collective-permute-start(bf16[256,1536]{1,0:T(8,128)(2,1)} %add_convert_fusion.5), channel_id=1, source_target_pairs={{0,2},{1,3},{2,0},{3,1},{4,6},{5,7},{6,4},{7,5},{8,10},{9,11},{10,... | collective-permute-start | bytes 2359304 | tf_op jit(solution)/shard_map/ppermute | solution.py:934
  308.0 259.5 %reduce-scatter.8.cloned.1.call-start = ((), (), s32[]{:S(2)}) async-start(), calls=%async_computation.8 | async-start | bytes 7077888 | tf_op jit(solution)/shard_map/reduce_scatter | solution.py:1136
  315.7 28.8 %collective-permute-start.22 = (bf16[256,1536]{1,0:T(8,128)(2,1)}, bf16[256,1536]{1,0:T(8,128)(2,1)}, u32[]{:S(2)}, u32[]{:S(2)}) collective-permute-start(bf16[256,1536]{1,0:T(8,128)(2,1)} %slice.280), channel_id=1, source_target_pairs={{0,2},{1,3},{2,0},{3,1},{4,6},{5,7},{6,4},{7,5},{8,10},{9,11},{10,... | collective-permute-start | bytes 2359304 | tf_op jit(solution)/shard_map/ppermute | solution.py:934
  366.6 46.9 %collective-permute-start.27 = (bf16[256,1536]{1,0:T(8,128)(2,1)}, bf16[256,1536]{1,0:T(8,128)(2,1)}, u32[]{:S(2)}, u32[]{:S(2)}) collective-permute-start(bf16[256,1536]{1,0:T(8,128)(2,1)} %add_convert_fusion.4), channel_id=1, source_target_pairs={{0,2},{1,3},{2,0},{3,1},{4,6},{5,7},{6,4},{7,5},{8,10},{9,11},{10,... | collective-permute-start | bytes 2359304 | tf_op jit(solution)/shard_map/ppermute | solution.py:934
  367.2 207.7 %reduce-scatter.6.cloned.1.call-start = ((), (), s32[]{:S(2)}) async-start(), calls=%async_computation.7 | async-start | bytes 7864320 | tf_op jit(solution)/shard_map/reduce_scatter | solution.py:1161
  372.9 40.7 %collective-permute-start.28 = (bf16[256,1536]{1,0:T(8,128)(2,1)}, bf16[256,1536]{1,0:T(8,128)(2,1)}, u32[]{:S(2)}, u32[]{:S(2)}) collective-permute-start(bf16[256,1536]{1,0:T(8,128)(2,1)} %slice.279), channel_id=1, source_target_pairs={{0,2},{1,3},{2,0},{3,1},{4,6},{5,7},{6,4},{7,5},{8,10},{9,11},{10,... | collective-permute-start | bytes 2359304 | tf_op jit(solution)/shard_map/ppermute | solution.py:934
  417.6 36.0 %collective-permute-start.31 = (bf16[256,1536]{1,0:T(8,128)(2,1)}, bf16[256,1536]{1,0:T(8,128)(2,1)}, u32[]{:S(2)}, u32[]{:S(2)}) collective-permute-start(bf16[256,1536]{1,0:T(8,128)(2,1)} %slice.278), channel_id=1, source_target_pairs={{0,2},{1,3},{2,0},{3,1},{4,6},{5,7},{6,4},{7,5},{8,10},{9,11},{10,... | collective-permute-start | bytes 2359304 | tf_op jit(solution)/shard_map/ppermute | solution.py:934
  430.7 23.9 %collective-permute-start.30 = (bf16[256,1536]{1,0:T(8,128)(2,1)}, bf16[256,1536]{1,0:T(8,128)(2,1)}, u32[]{:S(2)}, u32[]{:S(2)}) collective-permute-start(bf16[256,1536]{1,0:T(8,128)(2,1)} %add_convert_fusion.3.refs_2_), channel_id=1, source_target_pairs={{0,2},{1,3},{2,0},{3,1},{4,6},{5,7},{6,4},{7,5},{8,10},{9,11},{10,... | collective-permute-start | bytes 2359304 | tf_op jit(solution)/shard_map/ppermute | solution.py:934
  431.3 60.2 %collective-permute-start.33 = (bf16[256,1536]{1,0:T(8,128)(2,1)}, bf16[256,1536]{1,0:T(8,128)(2,1)}, u32[]{:S(2)}, u32[]{:S(2)}) collective-permute-start(bf16[256,1536]{1,0:T(8,128)(2,1)} %add_convert_fusion.3.refs_2_), channel_id=1, source_target_pairs={{0,1},{1,0},{2,3},{3,2},{4,5},{5,4},{6,7},{7,6},{8,9},{9,8},{10,11... | collective-permute-start | bytes 2359304 | tf_op jit(solution)/shard_map/ppermute | solution.py:938
  457.2 34.3 %collective-permute-start.34 = (bf16[256,1536]{1,0:T(8,128)(2,1)}, bf16[256,1536]{1,0:T(8,128)(2,1)S(1)}, u32[]{:S(2)}, u32[]{:S(2)}) collective-permute-start(bf16[256,1536]{1,0:T(8,128)(2,1)} %add_convert_fusion.2.refs_3_), channel_id=1, source_target_pairs={{0,1},{1,0},{2,3},{3,2},{4,5},{5,4},{6,7},{7,6},{8,9},{9,8},{10,11... | collective-permute-start | bytes 2359304 | tf_op jit(solution)/shard_map/ppermute | solution.py:938
  457.2 20.2 %collective-permute-start.32 = (bf16[256,1536]{1,0:T(8,128)(2,1)}, bf16[256,1536]{1,0:T(8,128)(2,1)S(1)}, u32[]{:S(2)}, u32[]{:S(2)}) collective-permute-start(bf16[256,1536]{1,0:T(8,128)(2,1)} %add_convert_fusion.2.refs_3_), channel_id=1, source_target_pairs={{0,2},{1,3},{2,0},{3,1},{4,6},{5,7},{6,4},{7,5},{8,10},{9,11},{10,... | collective-permute-start | bytes 2359304 | tf_op jit(solution)/shard_map/ppermute | solution.py:934
  476.1 15.4 %collective-permute-start.35 = (bf16[256,1536]{1,0:T(8,128)(2,1)}, bf16[256,1536]{1,0:T(8,128)(2,1)}, u32[]{:S(2)}, u32[]{:S(2)}) collective-permute-start(bf16[256,1536]{1,0:T(8,128)(2,1)} %collective-permute-done.30.refs_4_), channel_id=1, source_target_pairs={{0,1},{1,0},{2,3},{3,2},{4,5},{5,4},{6,7},{7,6},{8,9},{9,8},{10,11... | collective-permute-start | bytes 2359304 | tf_op jit(solution)/shard_map/ppermute | solution.py:938
  (95 other events, 1109.4 us)
Sparse Core Ops, SparseCore 0:
  9.6 49.0 all-gather.3
  74.0 43.9 all-gather.5
  165.7 60.8 all-gather.7
  308.1 73.1 reduce-scatter.3
  384.7 117.0 reduce-scatter.7
  504.2 59.2 reduce-scatter.5

commit v7 on v6

--- a/solution.py
+++ b/solution.py
@@ -1010,9 +1010,10 @@
     end_table = jnp.concatenate([own_places, own_spots]).astype(jnp.int32)
     tables = (table.astype(jnp.int32), first, last, slot, x_table, end_table, cot_table.reshape(-1))
 
-    extras = jnp.concatenate(
-        [w_beta, gain_attn[:, None], gain_ffn[:, None], jnp.zeros((shard, BLOCK - heads - 2), bf16)], axis=1
-    )
+    lanes = lax.broadcasted_iota(jnp.int32, (shard, BLOCK), 1)
+    extras = jnp.pad(w_beta, ((0, 0), (0, BLOCK - heads)))
+    extras = jnp.where(lanes == heads, gain_attn[:, None], extras)
+    extras = jnp.where(lanes == heads + 1, gain_ffn[:, None], extras)
     ffn_pack = jnp.concatenate([w_gate, w_up], axis=1)
     full_tokens = lax.all_gather(tokens, "tp", axis=0, tiled=True)
     tables = together(*tables)
@@ -1122,22 +1123,26 @@
     gate_up[1], hidden[1], back_own, back_far = together(gate_up[1], hidden[1], back_own, back_far)
     dh_own = close_back(0, back_own, back_far)
     hidden[1], dh_own = together(hidden[1], dh_own)
-    dh_far = across(dh_own)
     grads_down = sum(rows_contract(cot_rows[m], hidden[m]) for m in streams)
     grads_down, gate_up[1] = together(grads_down.astype(bf16), gate_up[1])
     sum_down = lax.psum_scatter(grads_down, "fsdp", scatter_dimension=0, tiled=True)
     rows, dh_own = together(ffn_back_rows(1), dh_own)
     back_own, back_far = share(rows)
     back_own, normed_two[0], normed_two[1] = together(back_own, *normed_two)
-    grads_in = sum(rows_contract(normed_two[m], gate_up[m]) for m in streams)
-    grads_in, back_far, dh_far = together(grads_in.astype(bf16), back_far, dh_far)
-    pair = jnp.concatenate([dh_own, dh_far], axis=0)
-    grad_attn.append(jnp.concatenate([pair, beside(pair)], axis=0))
+    grads_in, dh_own = together(rows_contract(normed_two[0], gate_up[0]), dh_own)
+    dh_far = across(dh_own)
+    grads_in = grads_in + sum(rows_contract(normed_two[m], gate_up[m]) for m in streams[1:])
+    grads_in, back_far = together(grads_in.astype(bf16), back_far)
+    early_own, early_far = dh_own, dh_far
     sum_in = lax.psum_scatter(grads_in, "fsdp", scatter_dimension=0, tiled=True)
     dh_own = close_back(1, back_own, back_far)
     dh_far = across(dh_own)
     hidden[0], hidden[1], dh_own = together(*hidden, dh_own)
-    ffn_parts = [share(cols_contract(hidden[m], full_down).astype(bf16)) for m in streams]
+    y_parts = [cols_contract(hidden[m], full_down).astype(bf16) for m in streams]
+    y_parts[0], y_parts[1], early_far = together(*y_parts, early_far)
+    ffn_parts = [share(part) for part in y_parts]
+    pair = jnp.concatenate([early_own, early_far], axis=0)
+    grad_attn.append(jnp.concatenate([pair, beside(pair)], axis=0))
     d_mixed = jnp.dot(grad_attn[0], full_out, preferred_element_type=f32).astype(bf16)
     y_own, y_far = [p[0] for p in ffn_parts], [p[1] for p in ffn_parts]
     d_mixed, y_own[0], y_own[1] = together(d_mixed, *y_own)

time: 597 us -> 591 us (0.990)
  waiting for transfers between devices: 21.1 us -> 14.8 us
    ppermute x13, waiting for transfers between devices: 15.9 us -> 9.45 us  [across(): return lax.ppermute(x, 'tp', [(i, i ^ 2) for i in range(4)])]
    unnamed x167 -> x169, local copies, waits for them, and re-layouts: 25.8 us -> 26 us
  transfers between devices with their start and end apart: 46 -> 46, of which waited for: 8 -> 7; matrix products, arithmetic and copies ran while one was open for 40% -> 40% of each run, Pallas kernels for 41% -> 42%
where the time goes in v7:
time: 591 us; the launch traced here: 582 us
  Pallas kernels  246 us (42%)
  matrix products  170 us (29%)
  local copies, waits for them, and re-layouts  55.7 us (9%)
  other arithmetic  52.1 us (9%)
  starting transfers between devices  28.1 us (5%)
  between operations  15.9 us (3%)
  waiting for transfers between devices  14.8 us (3%)
    pallas_call x1, Pallas kernels, ring_sum(): pl.pallas_call(functools.partial(ring_kernel, axis, count, rows, widths),...  65.8 us
    pallas_call x1, Pallas kernels, ring_spread(): pl.pallas_call(functools.partial(spread_kernel, axis, count, rows, widths...  55.6 us
    pallas_call x2, Pallas kernels, attention_bwd(): pl.pallas_call(functools.partial(bwd_kernel, heads, depth, scale), grid_s...  53.5 us
    dot_general x7, matrix products, rows_contract(): lax.dot_general(a, b, (((0,), (0,)), ((), ())), preferred_element_type=f32)  52.8 us
    dot_general x8, matrix products, cols_contract(): lax.dot_general(a, b, (((1,), (1,)), ((), ())), preferred_element_type=f32)  48.5 us
    pallas_call x2, Pallas kernels, attention_fwd(): pl.pallas_call(functools.partial(fwd_kernel, heads, depth, scale), grid_s...  31.4 us
    unnamed x169, local copies, waits for them, and re-layouts  26 us
    pallas_call x2, Pallas kernels, attention_prep(): pl.pallas_call(functools.partial(prep_kernel, heads, step), grid_spec=spe...  21.2 us
  transfers between devices with their start and end apart: 46, of which 7 were waited for; matrix products, arithmetic and copies ran while one was open for 40% of the time, Pallas kernels for 42%

profile of v7, /device:TPU:0, one launch (start us, length us, event | category | flops | bytes accessed | tf_op | source)
XLA Modules:
  0.0 581.8 jit_solution(18192503365993977906)
XLA Ops:
  15.2 55.6 %ring_spread.1 = bf16[1536,1664]{1,0:T(8,128)(2,1)} custom-call(bf16[192,384]{1,0:T(8,128)(2,1)} %refs_0_.1, bf16[192,384]{1,0:T(8,128)(2,1)} %refs_1_.1, bf16[192,384]{1,0:T(8,128)(2,1)} %refs_2_.1, bf16[192,384]{1,0:T(8,128)(2,1)} %refs_3_.1, bf16[192,128]{1,0:T(8,128)(2,1)} %select_select_fusion.refs_4_), custom_call_target="tpu_custom_call" | custom-call | bytes 10223616 | tf_op jit(solution)/shard_map/ring_spread/pallas_call | solution.py:871
  73.1 4.2 fusion
  80.2 16.4 %convolution_convert_fusion.refs_0_.refs_1_.refs_2_.refs_3_.refs_4_.refs_5_.refs_6_.refs_7_.refs_8_.refs_9_.refs_10_.refs_11_.refs_12_.refs_13_.refs_14_.refs_15_.v_ref = bf16[2048,1664]{1,0:T(8,128)(2,1)} fusion(bf16[1536,1664]{1,0:T(8,128)(2,1)} %ring_spread.1, bf16[2048,1536]{1,0:T(8,128)(2,1)S(1)} %copy-done, f32[1536]{0:T(1024)S(1)} %get-tuple-element.290, ...), kind=kOutput, calls=%fused_computation.6 | convolution fusion | flops 10484973568 | bytes 18233344 | tf_op jit(solution)/shard_map/dot_general | solution.py:1038
  97.2 10.5 %attn_prep.2 = (f32[8,3,128,128]{3,2,1,0:T(8,128)}, bf16[1024,384]{1,0:T(8,128)(2,1)}, bf16[8,3,128,256]{3,2,1,0:T(8,128)(2,1)}, bf16[8,3,128,128]{3,2,1,0:T(8,128)(2,1)}, bf16[8,3,128,256]{3,2,1,0:T(8,128)(2,1)}) custom-call(s32[8]{0:T(128)} %get-tuple-element.329.table_ref, ...), custom_call_target="tpu_custom_call" | custom-call | flops 2264924160 | bytes 2359296 | tf_op jit(solution)/shard_map/attn_prep/pallas_call | solution.py:318
  110.3 18.7 %attn_fwd.2 = (bf16[1024,384]{1,0:T(8,128)(2,1)}, f32[1024,384]{1,0:T(8,128)}, bf16[8,8,3,128,128]{4,3,2,1,0:T(8,128)(2,1)}, bf16[8,7,3,128,128]{4,3,2,1,0:T(8,128)(2,1)}) custom-call(s32[8]{0:T(128)} %get-tuple-element.328.first_ref, s32[8]{0:T(128)} %get-tuple-element.329.table_ref, s32[8]{0:T(128)} %copy-done.55, ...), custom_call_target="tpu_custom_call" | custom-call | flops 2415919104 | bytes 2359296 | tf_op jit(solution)/shard_map/attn_fwd/pallas_call | solution.py:362
  143.2 10.7 %attn_prep.3 = (f32[8,3,128,128]{3,2,1,0:T(8,128)}, bf16[1024,384]{1,0:T(8,128)(2,1)}, bf16[8,3,128,256]{3,2,1,0:T(8,128)(2,1)}, bf16[8,3,128,128]{3,2,1,0:T(8,128)(2,1)}, bf16[8,3,128,256]{3,2,1,0:T(8,128)(2,1)}) custom-call(s32[8]{0:T(128)} %get-tuple-element.330.table_ref, ...), custom_call_target="tpu_custom_call" | custom-call | flops 2264924160 | bytes 2359296 | tf_op jit(solution)/shard_map/attn_prep/pallas_call | solution.py:318
  153.9 5.2 collective-permute-done.8
  164.7 12.7 %attn_fwd.3 = (bf16[1024,384]{1,0:T(8,128)(2,1)}, f32[1024,384]{1,0:T(8,128)}, bf16[8,8,3,128,128]{4,3,2,1,0:T(8,128)(2,1)}, bf16[8,7,3,128,128]{4,3,2,1,0:T(8,128)(2,1)}) custom-call(s32[8]{0:T(128)} %get-tuple-element.327.first_ref, s32[8]{0:T(128)} %get-tuple-element.330.table_ref, s32[8]{0:T(128)} %copy-done.55, ...), custom_call_target="tpu_custom_call" | custom-call | flops 2415919104 | bytes 2359296 | tf_op jit(solution)/shard_map/attn_fwd/pallas_call | solution.py:362
  180.0 3.3 convolution_convert_fusion.5
  194.0 5.5 place_pieces.1
  199.5 6.1 %pick_blocks.4 = (bf16[1024,1536]{1,0:T(8,128)(2,1)}, bf16[1024,1536]{1,0:T(8,128)(2,1)}) custom-call(s32[16]{0:T(128)} %get-tuple-element.186.table_ref, bf16[512,1536]{1,0:T(8,128)(2,1)} %refs_4_, bf16[512,1536]{1,0:T(8,128)(2,1)} %collective-permute-done.4.refs_1_.refs_5_, bf16[512,1536]{1,0:T(8,128)(2,1)} %collective-permute-done.12.refs_2_.refs_6_, ...), custom_call_target="tpu_custom_call" | custom-call | bytes 12582912 | tf_op jit(solution)/shard_map/pick_blocks/pallas_call | solution.py:494
  211.8 8.5 %fusion.16 = f32[1024,1024]{0,1:T(8,128)} fusion(bf16[1024,1536]{1,0:T(8,128)(2,1)} %constant_dynamic-update-slice_fusion, bf16[1536,2048]{1,0:T(8,128)(2,1)} %constant_dynamic-update-slice_fusion.12), kind=kOutput, calls=%fused_computation.49 | convolution fusion | flops 3221225472 | bytes 10485760 | tf_op jit(solution)/shard_map/dot_general | solution.py:1089
  224.8 8.5 %fusion.43 = f32[1024,1024]{0,1:T(8,128)} fusion(bf16[1024,1536]{1,0:T(8,128)(2,1)} %get-tuple-element.193, bf16[1536,1024]{1,0:T(8,128)(2,1)} %all-gather.8.cloned.1.call-done), kind=kOutput, calls=%fused_computation.206 | convolution fusion | flops 3221225472 | bytes 10485760 | tf_op jit(solution)/shard_map/dot_general | solution.py:1092
  233.3 9.8 %multiply_convert_fusion.4 = (bf16[1024,1024]{0,1:T(8,128)(2,1)S(1)}, bf16[1024,1024]{0,1:T(8,128)(2,1)}, bf16[1024,1024]{0,1:T(8,128)(2,1)}) fusion(f32[1024,1024]{0,1:T(8,128)} %fusion.43, f32[1024,1024]{0,1:T(8,128)S(1)} %copy-done.65, bf16[1024,1536]{1,0:T(8,128)(2,1)S(1)} %copy-done.47, bf16[1536,2048]{1,0:T(8,128)(2,1)} %constant_dynamic-update-slice_fusion.12), kind=kOutput, calls=%fused_computation.18 | convolution fusion | flops 3236954112 | bytes 20971520 | tf_op jit(solution)/shard_map/dot_general | solution.py:1088
  243.2 9.0 %convolution_convert_fusion.4 = bf16[1024,1536]{1,0:T(8,128)(2,1)S(1)} fusion(bf16[1536,2048]{1,0:T(8,128)(2,1)S(1)} %bitcast.67, bf16[1024,1024]{0,1:T(8,128)(2,1)} %get-tuple-element.311, bf16[1024,1024]{0,1:T(8,128)(2,1)S(1)} %get-tuple-element.310), kind=kOutput, calls=%fused_computation.25 | convolution fusion | flops 6452412416 | bytes 13631488 | tf_op jit(solution)/shard_map/dot_general | solution.py:569
  255.1 5.0 fusion.42
  263.6 5.0 fusion.18
  268.6 9.7 %multiply_convert_fusion = (bf16[1024,1024]{0,1:T(8,128)(2,1)}, bf16[1024,1024]{0,1:T(8,128)(2,1)S(1)}, bf16[1024,1024]{0,1:T(8,128)(2,1)S(1)}) fusion(f32[1024,1024]{0,1:T(8,128)} %fusion.18, f32[1024,1024]{0,1:T(8,128)} %fusion.42, bf16[1024,1536]{1,0:T(8,128)(2,1)} %copy-done.49, bf16[1536,2048]{1,0:T(8,128)(2,1)S(1)} %bitcast.67), kind=kOutput, calls=%fused_computation.12 | convolution fusion | flops 3236954112 | bytes 20971520 | tf_op jit(solution)/shard_map/dot_general | solution.py:1089
  284.4 3.6 fusion.44
  288.0 5.1 add_convert_fusion.1
  293.2 10.2 %convolution_convert_fusion.3 = bf16[1024,1536]{1,0:T(8,128)(2,1)S(1)} fusion(bf16[1024,2048]{0,1:T(8,128)(2,1)} %pad_maximum_fusion.1, bf16[1536,2048]{1,0:T(8,128)(2,1)} %constant_dynamic-update-slice_fusion.12), kind=kOutput, calls=%fused_computation.24 | convolution fusion | flops 6444023808 | bytes 13631488 | tf_op jit(solution)/shard_map/dot_general | solution.py:569
  305.2 3.5 collective-permute-done.21
  314.4 9.8 %fusion.22 = f32[1536,2048]{1,0:T(8,128)} fusion(bf16[1024,1536]{1,0:T(8,128)(2,1)S(1)} %copy-done.48, bf16[1024,1024]{0,1:T(8,128)(2,1)S(1)} %copy-done.72, bf16[1024,1024]{0,1:T(8,128)(2,1)S(1)} %copy-done.71), kind=kOutput, calls=%fused_computation.55 | convolution fusion | flops 6450839552 | bytes 19922944 | tf_op jit(solution)/shard_map/dot_general | solution.py:565
  325.2 11.6 %add_convert_fusion = bf16[1536,2048]{1,0:T(8,128)(2,1)} fusion(f32[1536,2048]{1,0:T(8,128)} %fusion.22, bf16[1024,1536]{1,0:T(8,128)(2,1)S(1)} %copy-done.50, bf16[1024,2048]{0,1:T(8,128)(2,1)S(1)} %copy-done.16), kind=kOutput, calls=%fused_computation.5 | convolution fusion | flops 6448742400 | bytes 26214400 | tf_op jit(solution)/shard_map/dot_general | solution.py:565
  342.2 3.7 convolution_convert_fusion.8
  345.9 3.7 convolution_convert_fusion.7
  375.4 30.8 %attn_bwd.2.refs_26_ = bf16[2048,1664]{1,0:T(8,128)(2,1)} custom-call(s32[8]{0:T(128)} %get-tuple-element.325.last_ref, s32[8]{0:T(128)} %get-tuple-element.329.table_ref, s32[8]{0:T(128)} %copy-done.55, bf16[1024,384]{1,0:T(8,128)(2,1)} %convolution_convert_fusion.10.refs_0_, bf16[1024,384]{1,0:T(8,128)(2,1)} %get-tuple-element.160.refs_1_, ...), custom_call_target="tpu_custom_call" | custom-call | flops 6039797760 | bytes 3145728 | tf_op jit(solution)/shard_map/attn_bwd/pallas_call | solution.py:429
  424.1 22.7 %attn_bwd.3 = bf16[2048,1664]{1,0:T(8,128)(2,1)} custom-call(s32[8]{0:T(128)} %get-tuple-element.326.last_ref, s32[8]{0:T(128)} %get-tuple-element.330.table_ref, s32[8]{0:T(128)} %copy-done.55, bf16[1024,384]{1,0:T(8,128)(2,1)} %convolution_convert_fusion.9.refs_0_, bf16[1024,384]{1,0:T(8,128)(2,1)} %get-tuple-element.181.refs_1_, ...), custom_call_target="tpu_custom_call", output_to_operand_aliasing={{}: (29, {})} | custom-call | flops 6039797760 | bytes 3145728 | tf_op jit(solution)/shard_map/attn_bwd/pallas_call | solution.py:429
  451.2 18.0 %convolution_convert_fusion.2.refs_0_ = bf16[1536,1664]{1,0:T(8,128)(2,1)} fusion(bf16[2048,1664]{1,0:T(8,128)(2,1)} %attn_bwd.3, bf16[2048,1536]{1,0:T(8,128)(2,1)} %all-gather.4.cloned.1.call-done.refs_0_.refs_1_, f32[1536]{0:T(1024)S(1)} %copy-done.52, f32[2048]{0:T(1024)S(1)} %copy-done.58), kind=kOutput, calls=%fused_computation.8 | convolution fusion | flops 10484121600 | bytes 18233344 | tf_op jit(solution)/shard_map/dot_general | solution.py:565
  470.1 14.0 %convolution_convert_fusion.1 = bf16[2048,1536]{1,0:T(8,128)(2,1)} fusion(bf16[2048,1664]{1,0:T(8,128)(2,1)S(1)} %bitcast.65, bf16[1536,1664]{1,0:T(8,128)(2,1)S(1)} %bitcast.69), kind=kOutput, calls=%fused_computation.7 | convolution fusion | flops 10472128512 | bytes 18219008 | tf_op jit(solution)/shard_map/dot_general | solution.py:569
  488.4 3.5 pick_blocks.5
  491.9 65.8 %ring_sum.1 = (f32[192,1664]{1,0:T(8,128)}, f32[192,384]{1,0:T(8,128)}) custom-call(bf16[1536,1664]{1,0:T(8,128)(2,1)} %convolution_convert_fusion.2.refs_0_, bf16[1536,384]{1,0:T(8,128)(2,1)} %fusion.13.refs_1_), custom_call_target="tpu_custom_call" | custom-call | bytes 12582912 | tf_op jit(solution)/shard_map/ring_sum/pallas_call | solution.py:898
  (375 shorter events, 155.5 us)
Async XLA Ops:
  7.2 63.7 %all-gather.4.cloned.1.call-start = ((), (), s32[]{:S(2)}) async-start(), calls=%async_computation.3 | async-start | bytes 7864320 | tf_op jit(solution)/shard_map/all_gather | solution.py:1018
  7.9 121.2 %all-gather.6.cloned.1.call-start = ((), (), s32[]{:S(2)}) async-start(), calls=%async_computation.4 | async-start | bytes 1327104 | tf_op jit(solution)/shard_map/all_gather | solution.py:1029
  70.9 36.8 %collective-permute-start.1 = (bf16[192,2048]{1,0:T(8,128)(2,1)S(1)}, bf16[192,2048]{1,0:T(8,128)(2,1)S(1)}, u32[]{:S(2)}, u32[]{:S(2)}) collective-permute-start(bf16[192,2048]{1,0:T(8,128)(2,1)S(1)} %pad_maximum_fusion.8.refs_0_), channel_id=1, source_target_pairs={{0,4},{8,0},{16,8},{24,16},{28,24},{20,28},{12,20},{4,12},{1,5},{9... | collective-permute-start | bytes 2359304 | tf_op jit(solution)/shard_map/ppermute | solution.py:615
  71.4 36.3 %collective-permute-start = (bf16[192,2048]{1,0:T(8,128)(2,1)S(1)}, bf16[192,2048]{1,0:T(8,128)(2,1)S(1)}, u32[]{:S(2)}, u32[]{:S(2)}) collective-permute-start(bf16[192,2048]{1,0:T(8,128)(2,1)S(1)} %pad_maximum_fusion.8.refs_0_), channel_id=1, source_target_pairs={{0,8},{8,16},{16,24},{24,28},{28,20},{20,12},{12,4},{4,0},{1,9},{9... | collective-permute-start | bytes 2359304 | tf_op jit(solution)/shard_map/ppermute | solution.py:614
  73.0 151.8 %all-gather.8.cloned.1.call-start = ((), (), s32[]{:S(2)}) async-start(), calls=%async_computation.5 | async-start | bytes 3538944 | tf_op jit(solution)/shard_map/all_gather | solution.py:1030
  78.6 50.4 %collective-permute-start.4 = (bf16[512,1536]{1,0:T(8,128)(2,1)}, bf16[512,1536]{1,0:T(8,128)(2,1)}, u32[]{:S(2)}, u32[]{:S(2)}) collective-permute-start(bf16[512,1536]{1,0:T(8,128)(2,1)} %refs_4_), channel_id=1, source_target_pairs={{0,2},{1,3},{2,0},{3,1},{4,6},{5,7},{6,4},{7,5},{8,10},{9,11},{10,... | collective-permute-start | bytes 4718600 | tf_op jit(solution)/shard_map/ppermute | solution.py:934
  107.7 24.7 %collective-permute-start.2 = (bf16[192,2048]{1,0:T(8,128)(2,1)S(1)}, bf16[192,2048]{1,0:T(8,128)(2,1)}, u32[]{:S(2)}, u32[]{:S(2)}) collective-permute-start(bf16[192,2048]{1,0:T(8,128)(2,1)S(1)} %collective-permute-done.refs_1_), channel_id=1, source_target_pairs={{0,8},{8,16},{16,24},{24,28},{28,20},{20,12},{12,4},{4,0},{1,9},{9... | collective-permute-start | bytes 2359304 | tf_op jit(solution)/shard_map/ppermute | solution.py:614
  109.3 23.1 %collective-permute-start.3 = (bf16[192,2048]{1,0:T(8,128)(2,1)S(1)}, bf16[192,2048]{1,0:T(8,128)(2,1)}, u32[]{:S(2)}, u32[]{:S(2)}) collective-permute-start(bf16[192,2048]{1,0:T(8,128)(2,1)S(1)} %collective-permute-done.1.refs_2_), channel_id=1, source_target_pairs={{0,4},{8,0},{16,8},{24,16},{28,24},{20,28},{12,20},{4,12},{1,5},{9... | collective-permute-start | bytes 2359304 | tf_op jit(solution)/shard_map/ppermute | solution.py:615
  132.6 21.2 %collective-permute-start.5 = (bf16[192,2048]{1,0:T(8,128)(2,1)}, bf16[192,2048]{1,0:T(8,128)(2,1)S(1)}, u32[]{:S(2)}, u32[]{:S(2)}) collective-permute-start(bf16[192,2048]{1,0:T(8,128)(2,1)} %collective-permute-done.2.refs_3_), channel_id=1, source_target_pairs={{0,8},{8,16},{16,24},{24,28},{28,20},{20,12},{12,4},{4,0},{1,9},{9... | collective-permute-start | bytes 2359304 | tf_op jit(solution)/shard_map/ppermute | solution.py:614
  132.7 21.2 %collective-permute-start.6 = (bf16[192,2048]{1,0:T(8,128)(2,1)}, bf16[192,2048]{1,0:T(8,128)(2,1)S(1)}, u32[]{:S(2)}, u32[]{:S(2)}) collective-permute-start(bf16[192,2048]{1,0:T(8,128)(2,1)} %collective-permute-done.3.refs_4_), channel_id=1, source_target_pairs={{0,4},{8,0},{16,8},{24,16},{28,24},{20,28},{12,20},{4,12},{1,5},{9... | collective-permute-start | bytes 2359304 | tf_op jit(solution)/shard_map/ppermute | solution.py:615
  139.2 19.9 %collective-permute-start.8 = (bf16[256,1536]{1,0:T(8,128)(2,1)}, bf16[256,1536]{1,0:T(8,128)(2,1)}, u32[]{:S(2)}, u32[]{:S(2)}) collective-permute-start(bf16[256,1536]{1,0:T(8,128)(2,1)} %slice.279), channel_id=1, source_target_pairs={{0,2},{1,3},{2,0},{3,1},{4,6},{5,7},{6,4},{7,5},{8,10},{9,11},{10,... | collective-permute-start | bytes 2359304 | tf_op jit(solution)/shard_map/ppermute | solution.py:934
  139.7 37.7 %collective-permute-start.12 = (bf16[512,1536]{1,0:T(8,128)(2,1)}, bf16[512,1536]{1,0:T(8,128)(2,1)}, u32[]{:S(2)}, u32[]{:S(2)}) collective-permute-start(bf16[512,1536]{1,0:T(8,128)(2,1)} %refs_4_), channel_id=1, source_target_pairs={{0,1},{1,0},{2,3},{3,2},{4,5},{5,4},{6,7},{7,6},{8,9},{9,8},{10,11... | collective-permute-start | bytes 4718600 | tf_op jit(solution)/shard_map/ppermute | solution.py:938
  142.6 34.8 %collective-permute-start.13 = (bf16[512,1536]{1,0:T(8,128)(2,1)}, bf16[512,1536]{1,0:T(8,128)(2,1)}, u32[]{:S(2)}, u32[]{:S(2)}) collective-permute-start(bf16[512,1536]{1,0:T(8,128)(2,1)} %collective-permute-done.4.refs_1_.refs_5_), channel_id=1, source_target_pairs={{0,1},{1,0},{2,3},{3,2},{4,5},{5,4},{6,7},{7,6},{8,9},{9,8},{10,11... | collective-permute-start | bytes 4718600 | tf_op jit(solution)/shard_map/ppermute | solution.py:938
  161.2 18.8 %collective-permute-start.11 = (bf16[256,1536]{1,0:T(8,128)(2,1)S(1)}, bf16[256,1536]{1,0:T(8,128)(2,1)S(1)}, u32[]{:S(2)}, u32[]{:S(2)}) collective-permute-start(bf16[256,1536]{1,0:T(8,128)(2,1)S(1)} %multiply_convert_fusion.7), channel_id=1, source_target_pairs={{0,2},{1,3},{2,0},{3,1},{4,6},{5,7},{6,4},{7,5},{8,10},{9,11},{10,... | collective-permute-start | bytes 2359304 | tf_op jit(solution)/shard_map/ppermute | solution.py:934
  162.6 14.8 %collective-permute-start.9 = (bf16[96,2048]{1,0:T(8,128)(2,1)S(1)}, bf16[96,2048]{1,0:T(8,128)(2,1)}, u32[]{:S(2)}, u32[]{:S(2)}) collective-permute-start(bf16[96,2048]{1,0:T(8,128)(2,1)S(1)} %slice.182), channel_id=1, source_target_pairs={{0,8},{8,16},{16,24},{24,28},{28,20},{20,12},{12,4},{4,0},{1,9},{9... | collective-permute-start | bytes 1179656 | tf_op jit(solution)/shard_map/ppermute | solution.py:614
  164.6 282.3 %reduce-scatter.4.cloned.1.call-start = ((), (), s32[]{:S(2)}) async-start(), calls=%async_computation.6 | async-start | bytes 3538944 | tf_op jit(solution)/shard_map/reduce_scatter | solution.py:1128
  188.2 20.9 %collective-permute-start.14 = (bf16[512,1536]{1,0:T(8,128)(2,1)}, bf16[512,1536]{1,0:T(8,128)(2,1)}, u32[]{:S(2)}, u32[]{:S(2)}) collective-permute-start(bf16[512,1536]{1,0:T(8,128)(2,1)} %pad_maximum_fusion.4), channel_id=1, source_target_pairs={{0,1},{1,0},{2,3},{3,2},{4,5},{5,4},{6,7},{7,6},{8,9},{9,8},{10,11... | collective-permute-start | bytes 4718600 | tf_op jit(solution)/shard_map/ppermute | solution.py:938
  193.4 26.9 %collective-permute-start.16 = (bf16[256,1536]{1,0:T(8,128)(2,1)}, bf16[256,1536]{1,0:T(8,128)(2,1)}, u32[]{:S(2)}, u32[]{:S(2)}) collective-permute-start(bf16[256,1536]{1,0:T(8,128)(2,1)} %slice.278), channel_id=1, source_target_pairs={{0,2},{1,3},{2,0},{3,1},{4,6},{5,7},{6,4},{7,5},{8,10},{9,11},{10,... | collective-permute-start | bytes 2359304 | tf_op jit(solution)/shard_map/ppermute | solution.py:934
  223.2 29.0 %collective-permute-start.17 = (bf16[256,1536]{1,0:T(8,128)(2,1)S(1)}, bf16[256,1536]{1,0:T(8,128)(2,1)S(1)}, u32[]{:S(2)}, u32[]{:S(2)}) collective-permute-start(bf16[256,1536]{1,0:T(8,128)(2,1)S(1)} %multiply_convert_fusion.6), channel_id=1, source_target_pairs={{0,2},{1,3},{2,0},{3,1},{4,6},{5,7},{6,4},{7,5},{8,10},{9,11},{10,... | collective-permute-start | bytes 2359304 | tf_op jit(solution)/shard_map/ppermute | solution.py:934
  260.7 20.1 %collective-permute-start.20 = (bf16[256,1536]{1,0:T(8,128)(2,1)S(1)}, bf16[256,1536]{1,0:T(8,128)(2,1)S(1)}, u32[]{:S(2)}, u32[]{:S(2)}) collective-permute-start(bf16[256,1536]{1,0:T(8,128)(2,1)S(1)} %slice.277), channel_id=1, source_target_pairs={{0,2},{1,3},{2,0},{3,1},{4,6},{5,7},{6,4},{7,5},{8,10},{9,11},{10,... | collective-permute-start | bytes 2359304 | tf_op jit(solution)/shard_map/ppermute | solution.py:934
  305.2 256.7 %reduce-scatter.8.cloned.1.call-start = ((), (), s32[]{:S(2)}) async-start(), calls=%async_computation.8 | async-start | bytes 7077888 | tf_op jit(solution)/shard_map/reduce_scatter | solution.py:1137
  313.4 23.4 %collective-permute-start.22 = (bf16[256,1536]{1,0:T(8,128)(2,1)}, bf16[256,1536]{1,0:T(8,128)(2,1)}, u32[]{:S(2)}, u32[]{:S(2)}) collective-permute-start(bf16[256,1536]{1,0:T(8,128)(2,1)} %slice.276), channel_id=1, source_target_pairs={{0,2},{1,3},{2,0},{3,1},{4,6},{5,7},{6,4},{7,5},{8,10},{9,11},{10,... | collective-permute-start | bytes 2359304 | tf_op jit(solution)/shard_map/ppermute | solution.py:934
  324.2 26.0 %collective-permute-start.23 = (bf16[256,1536]{1,0:T(8,128)(2,1)}, bf16[256,1536]{1,0:T(8,128)(2,1)}, u32[]{:S(2)}, u32[]{:S(2)}) collective-permute-start(bf16[256,1536]{1,0:T(8,128)(2,1)} %add_convert_fusion.5), channel_id=1, source_target_pairs={{0,2},{1,3},{2,0},{3,1},{4,6},{5,7},{6,4},{7,5},{8,10},{9,11},{10,... | collective-permute-start | bytes 2359304 | tf_op jit(solution)/shard_map/ppermute | solution.py:934
  358.9 47.4 %collective-permute-start.27 = (bf16[256,1536]{1,0:T(8,128)(2,1)}, bf16[256,1536]{1,0:T(8,128)(2,1)}, u32[]{:S(2)}, u32[]{:S(2)}) collective-permute-start(bf16[256,1536]{1,0:T(8,128)(2,1)} %add_convert_fusion.4), channel_id=1, source_target_pairs={{0,2},{1,3},{2,0},{3,1},{4,6},{5,7},{6,4},{7,5},{8,10},{9,11},{10,... | collective-permute-start | bytes 2359304 | tf_op jit(solution)/shard_map/ppermute | solution.py:934
  359.9 209.5 %reduce-scatter.6.cloned.1.call-start = ((), (), s32[]{:S(2)}) async-start(), calls=%async_computation.7 | async-start | bytes 7864320 | tf_op jit(solution)/shard_map/reduce_scatter | solution.py:1166
  369.7 36.5 %collective-permute-start.28 = (bf16[256,1536]{1,0:T(8,128)(2,1)}, bf16[256,1536]{1,0:T(8,128)(2,1)}, u32[]{:S(2)}, u32[]{:S(2)}) collective-permute-start(bf16[256,1536]{1,0:T(8,128)(2,1)} %slice.275), channel_id=1, source_target_pairs={{0,2},{1,3},{2,0},{3,1},{4,6},{5,7},{6,4},{7,5},{8,10},{9,11},{10,... | collective-permute-start | bytes 2359304 | tf_op jit(solution)/shard_map/ppermute | solution.py:934
  410.4 36.5 %collective-permute-start.31 = (bf16[256,1536]{1,0:T(8,128)(2,1)}, bf16[256,1536]{1,0:T(8,128)(2,1)}, u32[]{:S(2)}, u32[]{:S(2)}) collective-permute-start(bf16[256,1536]{1,0:T(8,128)(2,1)} %slice.274), channel_id=1, source_target_pairs={{0,2},{1,3},{2,0},{3,1},{4,6},{5,7},{6,4},{7,5},{8,10},{9,11},{10,... | collective-permute-start | bytes 2359304 | tf_op jit(solution)/shard_map/ppermute | solution.py:934
  423.2 24.1 %collective-permute-start.30 = (bf16[256,1536]{1,0:T(8,128)(2,1)}, bf16[256,1536]{1,0:T(8,128)(2,1)}, u32[]{:S(2)}, u32[]{:S(2)}) collective-permute-start(bf16[256,1536]{1,0:T(8,128)(2,1)} %add_convert_fusion.3.refs_2_), channel_id=1, source_target_pairs={{0,2},{1,3},{2,0},{3,1},{4,6},{5,7},{6,4},{7,5},{8,10},{9,11},{10,... | collective-permute-start | bytes 2359304 | tf_op jit(solution)/shard_map/ppermute | solution.py:934
  424.1 60.0 %collective-permute-start.33 = (bf16[256,1536]{1,0:T(8,128)(2,1)}, bf16[256,1536]{1,0:T(8,128)(2,1)}, u32[]{:S(2)}, u32[]{:S(2)}) collective-permute-start(bf16[256,1536]{1,0:T(8,128)(2,1)} %add_convert_fusion.3.refs_2_), channel_id=1, source_target_pairs={{0,1},{1,0},{2,3},{3,2},{4,5},{5,4},{6,7},{7,6},{8,9},{9,8},{10,11... | collective-permute-start | bytes 2359304 | tf_op jit(solution)/shard_map/ppermute | solution.py:938
  449.9 34.2 %collective-permute-start.34 = (bf16[256,1536]{1,0:T(8,128)(2,1)}, bf16[256,1536]{1,0:T(8,128)(2,1)S(1)}, u32[]{:S(2)}, u32[]{:S(2)}) collective-permute-start(bf16[256,1536]{1,0:T(8,128)(2,1)} %add_convert_fusion.2.refs_3_), channel_id=1, source_target_pairs={{0,1},{1,0},{2,3},{3,2},{4,5},{5,4},{6,7},{7,6},{8,9},{9,8},{10,11... | collective-permute-start | bytes 2359304 | tf_op jit(solution)/shard_map/ppermute | solution.py:938
  450.1 20.0 %collective-permute-start.32 = (bf16[256,1536]{1,0:T(8,128)(2,1)}, bf16[256,1536]{1,0:T(8,128)(2,1)S(1)}, u32[]{:S(2)}, u32[]{:S(2)}) collective-permute-start(bf16[256,1536]{1,0:T(8,128)(2,1)} %add_convert_fusion.2.refs_3_), channel_id=1, source_target_pairs={{0,2},{1,3},{2,0},{3,1},{4,6},{5,7},{6,4},{7,5},{8,10},{9,11},{10,... | collective-permute-start | bytes 2359304 | tf_op jit(solution)/shard_map/ppermute | solution.py:934
  469.2 14.9 %collective-permute-start.35 = (bf16[256,1536]{1,0:T(8,128)(2,1)}, bf16[256,1536]{1,0:T(8,128)(2,1)}, u32[]{:S(2)}, u32[]{:S(2)}) collective-permute-start(bf16[256,1536]{1,0:T(8,128)(2,1)} %collective-permute-done.30.refs_4_), channel_id=1, source_target_pairs={{0,1},{1,0},{2,3},{3,2},{4,5},{5,4},{6,7},{7,6},{8,9},{9,8},{10,11... | collective-permute-start | bytes 2359304 | tf_op jit(solution)/shard_map/ppermute | solution.py:938
  (96 other events, 1102.3 us)
Sparse Core Ops, SparseCore 0:
  9.6 49.0 all-gather.3
  73.1 43.8 all-gather.5
  164.8 59.5 all-gather.7
  305.3 73.1 reduce-scatter.3
  381.9 119.5 reduce-scatter.7
  503.9 61.3 reduce-scatter.5
